TPU v7x, 32 devices: a whole 2x2x4 slice. The times are simulated.
32 devices in a mesh: seq: 16 (over z, x, core), head: 2 (over y).
Axes of the slice: x: 2, y: 2, z: 4, core: 2. Of those that a mesh axis runs over, the one named last changes fastest.
Arguments:
- frames: bfloat16 [6144, 1536], P('seq'), may hold values from -6 to 6
- time_token: bfloat16 [6, 1536], replicated, may hold values from -6 to 6
- prompt: bfloat16 [6, 128, 768], replicated, may hold values from -6 to 6
- clip_ids: int32 [6144], replicated, may hold values from 0 to 5, as said below
- norm1_gain: float32 [1536], P('seq'), may hold values from 0.5 to 1.5
- norm2_gain: float32 [1536], P('seq'), may hold values from 0.5 to 1.5
- norm3_gain: float32 [1536], P('seq'), may hold values from 0.5 to 1.5
- query_weight: float32 [1536, 1536], P('seq', 'head'), may hold values from -0.15625 to 0.15625
- key_weight: float32 [1536, 1536], P('seq', 'head'), may hold values from -0.15625 to 0.15625
- value_weight: float32 [1536, 1536], P('seq', 'head'), may hold values from -0.15625 to 0.15625
- out_weight: float32 [1536, 1536], P('seq', 'head'), may hold values from -1.75 to 1.75
- cross_query: float32 [1536, 1536], P('seq', 'head'), may hold values from -0.15625 to 0.15625
- cross_key: float32 [768, 1536], P('seq', 'head'), may hold values from -0.21875 to 0.21875
- cross_value: float32 [768, 1536], P('seq', 'head'), may hold values from -0.21875 to 0.21875
- cross_out: float32 [1536, 1536], P('seq', 'head'), may hold values from -1.25 to 1.25
- gate_weight: float32 [1536, 6144], P('seq', 'head'), may hold values from -0.15625 to 0.15625
- up_weight: float32 [1536, 6144], P('seq', 'head'), may hold values from -0.15625 to 0.15625
- down_weight: float32 [1536, 6144], P('seq', 'head'), may hold values from -0.078125 to 0.078125
- gate_bias: float32 [6144], P('head'), may hold values from -3 to 3
- up_bias: float32 [6144], P('head'), may hold values from -3 to 3
- down_bias: float32 [1536], P('seq'), may hold values from -2 to 2
- out_grad: bfloat16 [6144, 1536], P('seq'), may hold values from -6 to 6
Outputs:
- result: bfloat16 [6144, 1536], P('seq')
- frames_grad: bfloat16 [6144, 1536], P('seq')
- time_grad: float32 [6, 1536], replicated
- norm1_gain_grad: float32 [1536], P('seq')
- norm2_gain_grad: float32 [1536], P('seq')
- norm3_gain_grad: float32 [1536], P('seq')
- query_weight_grad: float32 [1536, 1536], P('seq', 'head')
- key_weight_grad: float32 [1536, 1536], P('seq', 'head')
- value_weight_grad: float32 [1536, 1536], P('seq', 'head')
- out_weight_grad: float32 [1536, 1536], P('seq', 'head')
- cross_query_grad: float32 [1536, 1536], P('seq', 'head')
- cross_key_grad: float32 [768, 1536], P('seq', 'head')
- cross_value_grad: float32 [768, 1536], P('seq', 'head')
- cross_out_grad: float32 [1536, 1536], P('seq', 'head')
- gate_weight_grad: float32 [1536, 6144], P('seq', 'head')
- up_weight_grad: float32 [1536, 6144], P('seq', 'head')
- down_weight_grad: float32 [1536, 6144], P('seq', 'head')
- gate_bias_grad: float32 [6144], P('head')
- up_bias_grad: float32 [6144], P('head')
- down_bias_grad: float32 [1536], P('seq')
Inputs may be any that keep to these rules, and one draw needn't show every extreme that they name: `clip_ids`: never falls from one frame to the next, starts at 0 and takes every value up to 5; each clip covers 2 * 256 frames or more, and one covers exactly 512; no clip starts at a nonzero multiple of 384.
All inputs are finite; a program needn't handle non-finite values.
Results may differ from a plain program's by a relative error of at most 0.025.
Values may be sent and summed in bfloat16 or wider, within the bound.
A program may use at most 320 MiB of HBM per device.

v0:
```python
from functools import reduce

import jax
import jax.numpy as jnp
from jax import lax
from jax.sharding import PartitionSpec as P

HD = 64
ROT = 32
HALF = 256


EPS = 1e-05
NEG = -1e30


def extended(block, sides, width):
    for axis, dim in sides:
        count = lax.axis_size(axis)
        forward = [(i, i + 1) for i in range(count - 1)]
        backward = [(target, source) for source, target in forward]
        low = lax.ppermute(
            lax.slice_in_dim(block, block.shape[dim] - width, None, axis=dim), axis, forward
        )
        high = lax.ppermute(lax.slice_in_dim(block, 0, width, axis=dim), axis, backward)
        block = jnp.concatenate([low, block, high], axis=dim)
    return block


def passed_along(value, axis, steps):
    count = lax.axis_size(axis)
    first, last = (max(0, -steps), min(count, count - steps))
    return lax.ppermute(value, axis, [(source, source + steps) for source in range(first, last)])


def layer_norm_parts(values, gain):
    average = jnp.mean(values, axis=-1, keepdims=True)
    centered = values - average
    spread = jnp.mean(centered * centered, axis=-1, keepdims=True)
    inverse = lax.rsqrt(spread + EPS)
    normal = centered * inverse
    return (normal * gain, normal, inverse)


def norm_back(grad_out, normal, inverse, gain):
    shaped = grad_out * gain
    return (
        shaped
        - jnp.mean(shaped, axis=-1, keepdims=True)
        - normal * jnp.mean(shaped * normal, axis=-1, keepdims=True)
    ) * inverse


def angles(positions):
    ladder = jnp.arange(ROT // 2, dtype=jnp.float32)
    frequency = 10000.0 ** (-2.0 * ladder / ROT)
    phases = positions.astype(jnp.float32)[:, None] * frequency[None, :]
    return (jnp.cos(phases), jnp.sin(phases))


def rotate(values, cos_table, sin_table):
    shaped = values.reshape(values.shape[0], -1, HD)
    rot_half = ROT // 2
    leading = shaped[:, :, :rot_half]
    trailing = shaped[:, :, rot_half:ROT]
    cos_row = cos_table[:, None, :]
    sin_row = sin_table[:, None, :]
    turned = jnp.concatenate(
        [
            leading * cos_row - trailing * sin_row,
            trailing * cos_row + leading * sin_row,
            shaped[:, :, ROT:],
        ],
        axis=-1,
    )
    return turned.reshape(values.shape)


def product(matrix_a, matrix_b):
    return jnp.dot(matrix_a, matrix_b, preferred_element_type=jnp.float32)


def product_t(matrix_a, matrix_b):
    return lax.dot_general(
        matrix_a, matrix_b, (((1,), (1,)), ((), ())), preferred_element_type=jnp.float32
    )


def product_tn(matrix_a, matrix_b):
    return lax.dot_general(
        matrix_a, matrix_b, (((0,), (0,)), ((), ())), preferred_element_type=jnp.float32
    )


def exact_t(matrix_a, matrix_b):
    return lax.dot_general(
        matrix_a,
        matrix_b,
        (((1,), (1,)), ((), ())),
        precision=lax.Precision.HIGHEST,
        preferred_element_type=jnp.float32,
    )


def exact_tn(matrix_a, matrix_b):
    return lax.dot_general(
        matrix_a,
        matrix_b,
        (((0,), (0,)), ((), ())),
        precision=lax.Precision.HIGHEST,
        preferred_element_type=jnp.float32,
    )


def score_parts(query_h, key_parts, score_scale):
    return [
        jnp.where(
            visible[None],
            jnp.einsum("qhd,khd->hqk", query_h, key_h, preferred_element_type=jnp.float32)
            * score_scale,
            NEG,
        )
        for key_h, value_h, visible in key_parts
    ]


def attend_forward(query_h, key_parts, score_scale):
    scores = score_parts(query_h, key_parts, score_scale)
    row_peak = reduce(jnp.maximum, [jnp.max(score_part, axis=-1) for score_part in scores])
    exp_parts = [jnp.exp(score_part - row_peak[:, :, None]) for score_part in scores]
    row_total = reduce(jnp.add, [jnp.sum(exp_part, axis=-1) for exp_part in exp_parts])
    attn_mixed = reduce(
        jnp.add,
        [
            jnp.einsum(
                "hqk,khd->qhd",
                (exp_part / row_total[:, :, None]).astype(jnp.bfloat16),
                key_part[1],
                preferred_element_type=jnp.float32,
            )
            for exp_part, key_part in zip(exp_parts, key_parts)
        ],
    )
    return (attn_mixed, row_peak + jnp.log(row_total))


def attend_backward(query_h, key_parts, score_scale, log_total, grad_h):
    scores = score_parts(query_h, key_parts, score_scale)
    prob_parts = [jnp.exp(score_part - log_total[:, :, None]) for score_part in scores]
    dprob_parts = [
        jnp.einsum("qhd,khd->hqk", grad_h, key_part[1], preferred_element_type=jnp.float32)
        for key_part in key_parts
    ]
    row_dot = reduce(
        jnp.add,
        [
            jnp.sum(prob_part * dprob_part, axis=-1)
            for prob_part, dprob_part in zip(prob_parts, dprob_parts)
        ],
    )
    dscore_parts = [
        (prob_part * (dprob_part - row_dot[:, :, None])).astype(jnp.bfloat16)
        for prob_part, dprob_part in zip(prob_parts, dprob_parts)
    ]
    grad_query = (
        reduce(
            jnp.add,
            [
                jnp.einsum(
                    "hqk,khd->qhd", dscore_part, key_part[0], preferred_element_type=jnp.float32
                )
                for dscore_part, key_part in zip(dscore_parts, key_parts)
            ],
        )
        * score_scale
    )
    grad_keys = [
        jnp.einsum("hqk,qhd->khd", dscore_part, query_h, preferred_element_type=jnp.float32)
        * score_scale
        for dscore_part in dscore_parts
    ]
    grad_values = [
        jnp.einsum(
            "hqk,qhd->khd",
            prob_part.astype(jnp.bfloat16),
            grad_h,
            preferred_element_type=jnp.float32,
        )
        for prob_part in prob_parts
    ]
    return (grad_query, grad_keys, grad_values)


def per_device(
    frames,
    time_token,
    prompt,
    clip_ids,
    norm1_gain,
    norm2_gain,
    norm3_gain,
    query_weight,
    key_weight,
    value_weight,
    out_weight,
    cross_query,
    cross_key,
    cross_value,
    cross_out,
    gate_weight,
    up_weight,
    down_weight,
    gate_bias,
    up_bias,
    down_bias,
    out_grad,
):
    local_rows = frames.shape[0]
    clip_total = time_token.shape[0]
    ctx_tokens = prompt.shape[1]
    slot_count = local_rows // (2 * HALF) + 2
    seq_index = lax.axis_index("seq")
    head_index = lax.axis_index("head")
    first_row = seq_index * local_rows
    score_scale = HD ** (-0.5)
    block_rows = min(local_rows, 2 * HALF)
    block_count = local_rows // block_rows
    window = block_rows + 2 * HALF
    block_indices = jnp.arange(block_count, dtype=jnp.int32)

    def branch_total(partial_sum):
        return lax.psum(partial_sum.astype(jnp.bfloat16), "head").astype(jnp.float32)

    def back_total(partial_sum):
        return lax.psum(partial_sum.astype(jnp.bfloat16), "head").astype(jnp.float32)

    (
        gain_one,
        gain_two,
        gain_three,
        w_query,
        w_key,
        w_value,
        w_out,
        c_query,
        c_key,
        c_value,
        c_out,
        w_gate,
        w_up,
        w_down,
        b_down,
    ) = (
        lax.all_gather(norm1_gain.astype(jnp.bfloat16), "seq", axis=0, tiled=True),
        lax.all_gather(norm2_gain.astype(jnp.bfloat16), "seq", axis=0, tiled=True),
        lax.all_gather(norm3_gain.astype(jnp.bfloat16), "seq", axis=0, tiled=True),
        lax.all_gather(query_weight.astype(jnp.bfloat16), "seq", axis=0, tiled=True),
        lax.all_gather(key_weight.astype(jnp.bfloat16), "seq", axis=0, tiled=True),
        lax.all_gather(value_weight.astype(jnp.bfloat16), "seq", axis=0, tiled=True),
        lax.all_gather(out_weight.astype(jnp.bfloat16), "seq", axis=0, tiled=True),
        lax.all_gather(cross_query.astype(jnp.bfloat16), "seq", axis=0, tiled=True),
        lax.all_gather(cross_key.astype(jnp.bfloat16), "seq", axis=0, tiled=True),
        lax.all_gather(cross_value.astype(jnp.bfloat16), "seq", axis=0, tiled=True),
        lax.all_gather(cross_out.astype(jnp.bfloat16), "seq", axis=0, tiled=True),
        lax.all_gather(gate_weight.astype(jnp.bfloat16), "seq", axis=0, tiled=True),
        lax.all_gather(up_weight.astype(jnp.bfloat16), "seq", axis=0, tiled=True),
        lax.all_gather(down_weight.astype(jnp.bfloat16), "seq", axis=0, tiled=True),
        lax.all_gather(down_bias.astype(jnp.bfloat16), "seq", axis=0, tiled=True),
    )
    gain_one_f = gain_one.astype(jnp.float32)
    gain_two_f = gain_two.astype(jnp.float32)
    positions = first_row + jnp.arange(local_rows, dtype=jnp.int32)
    cos_table, sin_table = angles(positions)
    padded_ids = jnp.pad(clip_ids, (HALF, HALF), constant_values=-1)
    own_ids = lax.dynamic_slice_in_dim(clip_ids, first_row, local_rows)
    near_ids = lax.dynamic_slice_in_dim(padded_ids, first_row, local_rows + 2 * HALF)
    base_clip = jnp.minimum(own_ids[0], clip_total - slot_count)
    own_slot = own_ids - base_clip
    slot_range = jnp.arange(slot_count, dtype=jnp.int32)
    frames_f = frames.astype(jnp.float32)
    normed_out, normal_one, inverse_one = layer_norm_parts(frames_f, gain_one_f)
    normed_one = normed_out.astype(jnp.bfloat16)
    query_rows = rotate(product(normed_one, w_query), cos_table, sin_table).astype(jnp.bfloat16)
    key_rows = rotate(product(normed_one, w_key), cos_table, sin_table).astype(jnp.bfloat16)
    value_rows = product(normed_one, w_value).astype(jnp.bfloat16)
    local_width = query_rows.shape[1]
    head_count = local_width // HD
    near = extended(jnp.stack([key_rows, value_rows]), (("seq", 1),), HALF)
    near_key_h = near[0].reshape(local_rows + 2 * HALF, head_count, HD)
    near_value_h = near[1].reshape(local_rows + 2 * HALF, head_count, HD)
    query_all_h = query_rows.reshape(local_rows, head_count, HD)
    stamp_rows = lax.dynamic_slice_in_dim(time_token, base_clip, slot_count, 0).astype(jnp.float32)
    stamp_out, stamp_normal, stamp_inverse = layer_norm_parts(stamp_rows, gain_one_f)
    stamp_normed = stamp_out.astype(jnp.bfloat16)
    stamp_key_h = (
        product(stamp_normed, w_key).astype(jnp.bfloat16).reshape(slot_count, head_count, HD)
    )
    stamp_value_h = (
        product(stamp_normed, w_value).astype(jnp.bfloat16).reshape(slot_count, head_count, HD)
    )

    def self_parts(block_index):
        row_start = block_index * block_rows
        query_pos = row_start + jnp.arange(block_rows, dtype=jnp.int32)
        key_pos = row_start - HALF + jnp.arange(window, dtype=jnp.int32)
        visible = (own_ids[:, None] == near_ids[None, :]) & (
            jnp.abs(query_pos[:, None] - key_pos[None, :]) <= HALF
        )
        own_stamp = own_slot[:, None] == slot_range[None, :]
        return (
            query_all_h,
            [(near_key_h, near_value_h, visible), (stamp_key_h, stamp_value_h, own_stamp)],
        )

    def self_forward(block_index):
        query_h, key_parts = self_parts(block_index)
        attn_mixed, log_total = attend_forward(query_h, key_parts, score_scale)
        return (attn_mixed.reshape(block_rows, local_width).astype(jnp.bfloat16), log_total)

    attn_blocks, self_logs = lax.map(self_forward, block_indices)
    attn_mixed = attn_blocks.reshape(local_rows, local_width)
    h_one = frames_f + branch_total(product_t(attn_mixed, w_out))
    middle_out, normal_two, inverse_two = layer_norm_parts(h_one, gain_two_f)
    normed_two = middle_out.astype(jnp.bfloat16)
    cross_rows = product(normed_two, c_query).astype(jnp.bfloat16)
    cross_all_h = cross_rows.reshape(local_rows, head_count, HD)
    context_rows = lax.dynamic_slice_in_dim(prompt, base_clip, slot_count, 0).reshape(
        slot_count * ctx_tokens, prompt.shape[2]
    )
    ctx_key_h = (
        product(context_rows, c_key)
        .astype(jnp.bfloat16)
        .reshape(slot_count * ctx_tokens, head_count, HD)
    )
    ctx_value_h = (
        product(context_rows, c_value)
        .astype(jnp.bfloat16)
        .reshape(slot_count * ctx_tokens, head_count, HD)
    )
    key_slot = jnp.arange(slot_count * ctx_tokens, dtype=jnp.int32) // ctx_tokens

    def cross_parts(block_index):
        row_start = block_index * block_rows
        visible = own_slot[:, None] == key_slot[None, :]
        return (cross_all_h, [(ctx_key_h, ctx_value_h, visible)])

    def cross_forward(block_index):
        query_h, key_parts = cross_parts(block_index)
        cross_mix, log_total = attend_forward(query_h, key_parts, score_scale)
        return (cross_mix.reshape(block_rows, local_width).astype(jnp.bfloat16), log_total)

    cross_blocks, cross_logs = lax.map(cross_forward, block_indices)
    cross_mixed = cross_blocks.reshape(local_rows, local_width)
    h_two = h_one + branch_total(product_t(cross_mixed, c_out))
    gain_three_f = gain_three.astype(jnp.float32)
    third_out, normal_three, inverse_three = layer_norm_parts(h_two, gain_three_f)
    normed_three = third_out.astype(jnp.bfloat16)
    gate_pre = product(normed_three, w_gate) + gate_bias
    up_pre = product(normed_three, w_up) + up_bias
    hidden = (jax.nn.silu(gate_pre) * up_pre).astype(jnp.bfloat16)
    result = (h_two + branch_total(product_t(hidden, w_down)) + b_down.astype(jnp.float32)).astype(
        jnp.bfloat16
    )
    grad_top = out_grad.astype(jnp.float32)
    grad_hidden = product(out_grad, w_down)
    sigmoid_gate = jax.nn.sigmoid(gate_pre)
    grad_up = (grad_hidden * gate_pre * sigmoid_gate).astype(jnp.bfloat16)
    grad_gate = (
        grad_hidden * up_pre * sigmoid_gate * (1.0 + gate_pre * (1.0 - sigmoid_gate))
    ).astype(jnp.bfloat16)
    gate_bias_local = jnp.sum(grad_gate.astype(jnp.float32), axis=0)
    up_bias_local = jnp.sum(grad_up.astype(jnp.float32), axis=0)
    grad_normed_three = back_total(product_t(grad_gate, w_gate) + product_t(grad_up, w_up))
    glu_terms = (
        product_tn(normed_three, grad_gate),
        product_tn(normed_three, grad_up),
        product_tn(out_grad, hidden),
        jnp.sum(grad_normed_three * normal_three, axis=0),
        jnp.sum(grad_top, axis=0),
    )
    grad_h_two = grad_top + norm_back(grad_normed_three, normal_three, inverse_three, gain_three_f)
    grad_two_low = grad_h_two.astype(jnp.bfloat16)
    grad_cross_mixed = product(grad_two_low, c_out).astype(jnp.bfloat16)
    cross_out_term = product_tn(grad_two_low, cross_mixed)
    grad_cross_h = grad_cross_mixed.reshape(local_rows, head_count, HD)

    def cross_step(ctx_grads, block_index):
        query_h, key_parts = cross_parts(block_index)
        grad_query, grad_keys, grad_values = attend_backward(
            query_h, key_parts, score_scale, cross_logs[block_index], grad_cross_h
        )
        return (ctx_grads + jnp.stack([grad_keys[0], grad_values[0]]), grad_query)

    ctx_grads, grad_cross_q = lax.scan(
        cross_step,
        jnp.zeros((2, slot_count * ctx_tokens, head_count, HD), jnp.float32),
        block_indices,
    )
    grad_cross_query = grad_cross_q.reshape(local_rows, local_width).astype(jnp.bfloat16)
    context_float = context_rows.astype(jnp.float32)
    cross_key_term = exact_tn(context_float, ctx_grads[0].reshape(-1, local_width))
    cross_value_term = exact_tn(context_float, ctx_grads[1].reshape(-1, local_width))
    cross_query_term = product_tn(normed_two, grad_cross_query)
    grad_normed_two = back_total(product_t(grad_cross_query, c_query))
    gain_two_term = jnp.sum(grad_normed_two * normal_two, axis=0)
    grad_h_one = grad_h_two + norm_back(grad_normed_two, normal_two, inverse_two, gain_two_f)
    grad_one_low = grad_h_one.astype(jnp.bfloat16)
    grad_attn = product(grad_one_low, w_out).astype(jnp.bfloat16)
    out_term = product_tn(grad_one_low, attn_mixed)
    grad_attn_h = grad_attn.reshape(local_rows, head_count, HD)

    def self_step(grad_state, block_index):
        near_grads, stamp_grads = grad_state
        query_h, key_parts = self_parts(block_index)
        row_start = block_index * block_rows
        grad_query, grad_keys, grad_values = attend_backward(
            query_h, key_parts, score_scale, self_logs[block_index], grad_attn_h
        )
        prior = near_grads
        near_grads = prior + jnp.stack([grad_keys[0], grad_values[0]])
        stamp_grads = stamp_grads + jnp.stack([grad_keys[1], grad_values[1]])
        return ((near_grads, stamp_grads), grad_query)

    start_state = (
        jnp.zeros((2, local_rows + 2 * HALF, head_count, HD), jnp.float32),
        jnp.zeros((2, slot_count, head_count, HD), jnp.float32),
    )
    (near_grads, stamp_grads), grad_query_blocks = lax.scan(self_step, start_state, block_indices)
    near_grads = near_grads.reshape(2, local_rows + 2 * HALF, local_width)
    from_above = passed_along(near_grads[:, :HALF].astype(jnp.bfloat16), "seq", -1).astype(
        jnp.float32
    )
    from_below = passed_along(
        near_grads[:, HALF + local_rows :].astype(jnp.bfloat16), "seq", 1
    ).astype(jnp.float32)
    own_grads = (
        near_grads[:, HALF : HALF + local_rows]
        + jnp.pad(from_below, ((0, 0), (0, local_rows - HALF), (0, 0)))
        + jnp.pad(from_above, ((0, 0), (local_rows - HALF, 0), (0, 0)))
    )
    grad_query_rows = rotate(
        grad_query_blocks.reshape(local_rows, local_width), cos_table, -sin_table
    ).astype(jnp.bfloat16)
    grad_key_rows = rotate(own_grads[0], cos_table, -sin_table).astype(jnp.bfloat16)
    grad_value_rows = own_grads[1].astype(jnp.bfloat16)
    stamp_key_grad = stamp_grads[0].reshape(slot_count, local_width)
    stamp_value_grad = stamp_grads[1].reshape(slot_count, local_width)
    stamp_float = stamp_normed.astype(jnp.float32)
    query_term = product_tn(normed_one, grad_query_rows)
    key_term = product_tn(normed_one, grad_key_rows) + exact_tn(stamp_float, stamp_key_grad)
    value_term = product_tn(normed_one, grad_value_rows) + exact_tn(stamp_float, stamp_value_grad)
    grad_normed_one = back_total(
        product_t(grad_query_rows, w_query)
        + product_t(grad_key_rows, w_key)
        + product_t(grad_value_rows, w_value)
    )
    gain_one_term = jnp.sum(grad_normed_one * normal_one, axis=0)
    frames_grad = (
        grad_h_one + norm_back(grad_normed_one, normal_one, inverse_one, gain_one_f)
    ).astype(jnp.bfloat16)
    stamp_partial = exact_t(stamp_key_grad, w_key.astype(jnp.float32)) + exact_t(
        stamp_value_grad, w_value.astype(jnp.float32)
    )
    attn_shares = (
        lax.psum_scatter(query_term, "seq", scatter_dimension=0, tiled=True),
        lax.psum_scatter(key_term, "seq", scatter_dimension=0, tiled=True),
        lax.psum_scatter(value_term, "seq", scatter_dimension=0, tiled=True),
        lax.psum_scatter(out_term, "seq", scatter_dimension=0, tiled=True),
        lax.psum_scatter(cross_query_term, "seq", scatter_dimension=0, tiled=True),
        lax.psum_scatter(cross_key_term, "seq", scatter_dimension=0, tiled=True),
        lax.psum_scatter(cross_value_term, "seq", scatter_dimension=0, tiled=True),
        lax.psum_scatter(cross_out_term, "seq", scatter_dimension=0, tiled=True),
        lax.psum_scatter(gain_one_term, "seq", scatter_dimension=0, tiled=True),
        lax.psum_scatter(gain_two_term, "seq", scatter_dimension=0, tiled=True),
    )
    hidden_width = gate_bias.shape[0]
    stamp_full = lax.dynamic_update_slice_in_dim(
        jnp.zeros((clip_total, stamp_partial.shape[1]), jnp.float32), stamp_partial, base_clip, 0
    )
    bias_full = lax.dynamic_update_slice_in_dim(
        jnp.zeros((2, hidden_width * lax.axis_size("head")), jnp.float32),
        jnp.stack([gate_bias_local, up_bias_local]),
        head_index * hidden_width,
        1,
    )
    stamp_sum, bias_sum = lax.psum((stamp_full, bias_full), ("seq", "head"))
    every_out, every_normal, every_inverse = layer_norm_parts(
        time_token.astype(jnp.float32), gain_one_f
    )
    time_grad = norm_back(stamp_sum, every_normal, every_inverse, gain_one_f)
    gain_rows = norm1_gain.shape[0]
    time_gain = lax.dynamic_slice_in_dim(
        jnp.sum(stamp_sum * every_normal, axis=0), seq_index * gain_rows, gain_rows
    )
    own_bias = lax.dynamic_slice_in_dim(bias_sum, head_index * hidden_width, hidden_width, 1)
    return (
        result,
        frames_grad,
        time_grad,
        attn_shares[8] + time_gain,
        attn_shares[9],
        lax.psum_scatter(glu_terms[3], "seq", scatter_dimension=0, tiled=True),
        attn_shares[0],
        attn_shares[1],
        attn_shares[2],
        attn_shares[3],
        attn_shares[4],
        attn_shares[5],
        attn_shares[6],
        attn_shares[7],
        lax.psum_scatter(glu_terms[0], "seq", scatter_dimension=0, tiled=True),
        lax.psum_scatter(glu_terms[1], "seq", scatter_dimension=0, tiled=True),
        lax.psum_scatter(glu_terms[2], "seq", scatter_dimension=0, tiled=True),
        own_bias[0],
        own_bias[1],
        lax.psum_scatter(glu_terms[4], "seq", scatter_dimension=0, tiled=True),
    )


def solution(mesh):
    in_specs = (
        P("seq", None),
        P(),
        P(),
        P(),
        P("seq"),
        P("seq"),
        P("seq"),
        P("seq", "head"),
        P("seq", "head"),
        P("seq", "head"),
        P("seq", "head"),
        P("seq", "head"),
        P("seq", "head"),
        P("seq", "head"),
        P("seq", "head"),
        P("seq", "head"),
        P("seq", "head"),
        P("seq", "head"),
        P("head"),
        P("head"),
        P("seq"),
        P("seq", None),
    )
    out_specs = (
        P("seq", None),
        P("seq", None),
        P(),
        P("seq"),
        P("seq"),
        P("seq"),
        P("seq", "head"),
        P("seq", "head"),
        P("seq", "head"),
        P("seq", "head"),
        P("seq", "head"),
        P("seq", "head"),
        P("seq", "head"),
        P("seq", "head"),
        P("seq", "head"),
        P("seq", "head"),
        P("seq", "head"),
        P("head"),
        P("head"),
        P("seq"),
    )
    return jax.shard_map(
        per_device, mesh=mesh, in_specs=in_specs, out_specs=out_specs, check_vma=False
    )
```

profile of v0, /device:TPU:0, one launch (start us, length us, event | category | flops | bytes accessed | tf_op | source)
XLA Modules:
  0.0 2313.0 jit_solution(17041787698826603360)
XLA Ops:
  19.5 63.2 %all-reduce.13 = (bf16[1536]{0:T(1024)(128)(2,1)}, bf16[1536]{0:T(1024)(128)(2,1)S(1)}, bf16[1536]{0:T(1024)(128)(2,1)}, bf16[1536]{0:T(1024)(128)(2,1)}) all-reduce(bf16[1536]{0:T(1024)(128)(2,1)S(1)} %dynamic-update-slice.1, bf16[1536]{0:T(1024)(128)(2,1)S(1)} %dynamic-update-slice, ...), channel_id=1, replica_groups=mesh['seq'=16,'head'=2] {'seq'}, use_global_device_ids=true, to_apply=%add.4 | all-reduce | flops 6144 | bytes 24576
  87.0 3.2 fusion.110
  91.3 8.9 all-gather.16.cloned.1.call-done
  100.2 3.3 fusion.107
  106.0 38.2 %all-gather.14.cloned.1.call-done = bf16[1536,768]{1,0:T(8,128)(2,1)} async-done(((bf16[96,768]{1,0:T(8,128)(2,1)}), bf16[1536,768]{1,0:T(8,128)(2,1)}) %all-gather.14.cloned.1.call-update) | async-done | bytes 2359312 | tf_op jit(solution)/shard_map/all_gather | solution.py:259
  149.1 3.2 collective-permute-start
  168.2 4.6 fusion.117
  172.9 3.9 fusion
  182.1 8.5 fusion.53
  190.9 3.9 convolution_convert_fusion.3
  197.8 32.9 %all-gather.24.cloned.1.call-done = bf16[768,768]{1,0:T(8,128)(2,1)} async-done(((bf16[48,768]{1,0:T(8,128)(2,1)}), bf16[768,768]{1,0:T(8,128)(2,1)}) %all-gather.24.cloned.1.call-update) | async-done | bytes 1179664 | tf_op jit(solution)/shard_map/all_gather | solution.py:262
  232.6 38.1 %all-gather.20.cloned.1.call-done = bf16[768,768]{1,0:T(8,128)(2,1)} async-done(((bf16[48,768]{1,0:T(8,128)(2,1)}), bf16[768,768]{1,0:T(8,128)(2,1)}) %all-gather.20.cloned.1.call-update) | async-done | bytes 1179664 | tf_op jit(solution)/shard_map/all_gather | solution.py:263
  273.4 42.1 %all-reduce.22.cloned.1.call-done = bf16[384,1536]{1,0:T(8,128)(2,1)} async-done(((bf16[384,1536]{1,0:T(8,128)(2,1)}), bf16[384,1536]{1,0:T(8,128)(2,1)}) %all-reduce.22.cloned.1.call-update) | async-done | bytes 1179664 | tf_op jit(solution)/shard_map/psum | solution.py:232
  317.8 43.1 %all-gather.22.cloned.1.call-done = bf16[1536,768]{1,0:T(8,128)(2,1)} async-done(((bf16[96,768]{1,0:T(8,128)(2,1)}), bf16[1536,768]{1,0:T(8,128)(2,1)}) %all-gather.22.cloned.1.call-update) | async-done | bytes 2359312 | tf_op jit(solution)/shard_map/all_gather | solution.py:261
  361.0 3.8 convolution_convert_fusion.6
  371.0 34.1 %all-gather.26.cloned.1.call-done = bf16[1536,768]{1,0:T(8,128)(2,1)} async-done(((bf16[96,768]{1,0:T(8,128)(2,1)}), bf16[1536,768]{1,0:T(8,128)(2,1)}) %all-gather.26.cloned.1.call-update) | async-done | bytes 2359312 | tf_op jit(solution)/shard_map/all_gather | solution.py:264
  405.1 4.1 convolution_convert_fusion.2
  414.7 36.4 %all-reduce.24.cloned.1.call-done = bf16[384,1536]{1,0:T(8,128)(2,1)} async-done(((bf16[384,1536]{1,0:T(8,128)(2,1)}), bf16[384,1536]{1,0:T(8,128)(2,1)}) %all-reduce.24.cloned.1.call-update) | async-done | bytes 1179664 | tf_op jit(solution)/shard_map/psum | solution.py:232
  455.2 80.2 %all-gather.30.cloned.1.call-done = bf16[1536,3072]{1,0:T(8,128)(2,1)} async-done(((bf16[96,3072]{1,0:T(8,128)(2,1)}), bf16[1536,3072]{1,0:T(8,128)(2,1)}) %all-gather.30.cloned.1.call-update) | async-done | bytes 9437200 | tf_op jit(solution)/shard_map/all_gather | solution.py:266
  535.4 9.1 fusion.120
  544.5 73.2 %all-gather.32.cloned.1.call-done = bf16[1536,3072]{1,0:T(8,128)(2,1)} async-done(((bf16[96,3072]{1,0:T(8,128)(2,1)}), bf16[1536,3072]{1,0:T(8,128)(2,1)}) %all-gather.32.cloned.1.call-update) | async-done | bytes 9437200 | tf_op jit(solution)/shard_map/all_gather | solution.py:267
  617.7 10.1 fusion.121
  627.8 72.4 %all-gather.28.cloned.1.call-done = bf16[1536,3072]{1,0:T(8,128)(2,1)} async-done(((bf16[96,3072]{1,0:T(8,128)(2,1)}), bf16[1536,3072]{1,0:T(8,128)(2,1)}) %all-gather.28.cloned.1.call-update) | async-done | bytes 9437200 | tf_op jit(solution)/shard_map/all_gather | solution.py:265
  700.2 13.7 convert_reduce_fusion
  713.9 4.0 fusion.122
  717.9 7.9 fusion.22
  729.3 37.7 %all-reduce.26.cloned.1.call-done = bf16[384,1536]{1,0:T(8,128)(2,1)} async-done(((bf16[384,1536]{1,0:T(8,128)(2,1)}), bf16[384,1536]{1,0:T(8,128)(2,1)}) %all-reduce.26.cloned.1.call-update) | async-done | bytes 1179664 | tf_op jit(solution)/shard_map/psum | solution.py:235
  767.0 3.6 fusion.33
  770.7 3.6 convert_reduce_fusion.3
  779.0 3.6 multiply_reduce_fusion.1
  789.7 9.3 convolution_convert_fusion.1
  799.0 33.5 %all-reduce.28.cloned.1.call-done = bf16[384,1536]{1,0:T(8,128)(2,1)} async-done(((bf16[384,1536]{1,0:T(8,128)(2,1)}), bf16[384,1536]{1,0:T(8,128)(2,1)}) %all-reduce.28.cloned.1.call-update) | async-done | bytes 1179664 | tf_op jit(solution)/shard_map/psum | solution.py:235
  832.5 3.2 fusion.38
  841.6 7.6 fusion.2
  849.2 11.9 multiply_reduce_fusion
  861.7 11.8 multiply_convert_fusion
  884.7 6.6 fusion.50
  894.3 3.7 fusion.124
  898.0 3.2 convolution_add_fusion.6
  915.1 3.4 fusion.41
  926.7 5.0 fusion.67
  932.8 5.2 fusion.64
  939.1 5.3 fusion.61
  948.1 4.4 convolution_add_fusion.1
  954.2 4.5 convolution_add_fusion.2
  959.7 3.8 fusion.105
  964.8 10.8 fusion.127
  975.6 10.8 fusion.128
  987.7 11.0 convolution_bitcast_fusion
  998.7 18.7 copy.122
  1019.6 6.5 all-reduce.30.cloned.1.call-done
  1030.3 68.4 %all-reduce.32.cloned.1.call-done = (bf16[384,1536]{1,0:T(8,128)(2,1)}, bf16[384,1536]{1,0:T(8,128)(2,1)}) async-done(((bf16[384,1536]{1,0:T(8,128)(2,1)}, bf16[384,1536]{1,0:T(8,128)(2,1)}), (bf16[384,1536]{1,0:T(8,128)(2,1)}, bf16[384,1536]{1,0:T(8,128)(2,1)})) %all-reduce.32.cloned.1.call-update) | async-done | bytes 2359312 | tf_op jit(solution)/shard_map/psum | solution.py:232
  1101.1 61.6 %all-reduce.12 = (f32[1536]{0:T(1024)S(1)}, f32[1536]{0:T(1024)S(1)}, f32[1536]{0:T(1024)S(1)}, f32[1536]{0:T(1024)S(1)}) all-reduce(f32[1536]{0:T(1024)S(1)} %get-tuple-element.219, f32[1536]{0:T(1024)S(1)} %copy-done.95, f32[1536]{0:T(1024)S(1)} %copy-done.94, ...), channel_id=2, replica_groups=mesh['seq'=16,'head'=2] {'seq'}, use_global_device_ids=true, to_apply=%region_35.36.clone | all-reduce | flops 6144 | bytes 49152
  1165.1 3.2 add_convert_fusion
  1170.2 62.6 %reduce-scatter.24.cloned.1.call-done = f32[48,768]{1,0:T(8,128)} async-done(((f32[768,768]{1,0:T(8,128)}), f32[48,768]{1,0:T(8,128)}) %reduce-scatter.24.cloned.1.call-update) | async-done | bytes 147472 | tf_op jit(solution)/shard_map/reduce_scatter | solution.py:470
  1232.9 79.4 %reduce-scatter.22.cloned.1.call-done = f32[96,768]{1,0:T(8,128)} async-done(((f32[1536,768]{1,0:T(8,128)}), f32[96,768]{1,0:T(8,128)}) %reduce-scatter.22.cloned.1.call-update) | async-done | bytes 294928 | tf_op jit(solution)/shard_map/reduce_scatter | solution.py:469
  1312.3 79.1 %reduce-scatter.28.cloned.1.call-done = f32[96,768]{1,0:T(8,128)} async-done(((f32[1536,768]{1,0:T(8,128)}), f32[96,768]{1,0:T(8,128)}) %reduce-scatter.28.cloned.1.call-update) | async-done | bytes 294928 | tf_op jit(solution)/shard_map/reduce_scatter | solution.py:472
  1391.4 79.6 %reduce-scatter.20.cloned.1.call-done = f32[96,768]{1,0:T(8,128)} async-done(((f32[1536,768]{1,0:T(8,128)}), f32[96,768]{1,0:T(8,128)}) %reduce-scatter.20.cloned.1.call-update) | async-done | bytes 294928 | tf_op jit(solution)/shard_map/reduce_scatter | solution.py:468
  1470.9 79.1 %reduce-scatter.18.cloned.1.call-done = f32[96,768]{1,0:T(8,128)} async-done(((f32[1536,768]{1,0:T(8,128)}), f32[96,768]{1,0:T(8,128)}) %reduce-scatter.18.cloned.1.call-update) | async-done | bytes 294928 | tf_op jit(solution)/shard_map/reduce_scatter | solution.py:467
  1550.0 79.4 %reduce-scatter.16.cloned.1.call-done = f32[96,768]{1,0:T(8,128)} async-done(((f32[1536,768]{1,0:T(8,128)}), f32[96,768]{1,0:T(8,128)}) %reduce-scatter.16.cloned.1.call-update) | async-done | bytes 294928 | tf_op jit(solution)/shard_map/reduce_scatter | solution.py:466
  1629.5 79.1 %reduce-scatter.14.cloned.1.call-done = f32[96,768]{1,0:T(8,128)} async-done(((f32[1536,768]{1,0:T(8,128)}), f32[96,768]{1,0:T(8,128)}) %reduce-scatter.14.cloned.1.call-update) | async-done | bytes 294928 | tf_op jit(solution)/shard_map/reduce_scatter | solution.py:465
  1708.5 199.0 %reduce-scatter.30.cloned.1.call-done = f32[96,3072]{1,0:T(8,128)} async-done(((f32[1536,3072]{1,0:T(8,128)}), f32[96,3072]{1,0:T(8,128)}) %reduce-scatter.30.cloned.1.call-update) | async-done | bytes 1179664 | tf_op jit(solution)/shard_map/reduce_scatter | solution.py:511
  1907.5 199.0 %reduce-scatter.32.cloned.1.call-done = f32[96,3072]{1,0:T(8,128)} async-done(((f32[1536,3072]{1,0:T(8,128)}), f32[96,3072]{1,0:T(8,128)}) %reduce-scatter.32.cloned.1.call-update) | async-done | bytes 1179664 | tf_op jit(solution)/shard_map/reduce_scatter | solution.py:512
  2106.5 199.2 %reduce-scatter.34.cloned.1.call-done = f32[96,3072]{1,0:T(8,128)} async-done(((f32[1536,3072]{1,0:T(8,128)}), f32[96,3072]{1,0:T(8,128)}) %reduce-scatter.34.cloned.1.call-update) | async-done | bytes 1179664
  (460 shorter events, 151.2 us)
Async XLA Ops:
  7.2 190.4 %copy-start = (bf16[6,128,768]{2,1,0:T(8,128)(2,1)S(1)}, bf16[6,128,768]{2,1,0:T(8,128)(2,1)}, u32[]{:S(2)}) copy-start(bf16[6,128,768]{2,1,0:T(8,128)(2,1)} %param.24) | copy-start | bytes 3538948
  7.2 10.1 copy-start.111
  7.3 75.4 %copy-start.3 = (bf16[384,1536]{1,0:T(8,128)(2,1)S(1)}, bf16[384,1536]{1,0:T(8,128)(2,1)}, u32[]{:S(2)}) copy-start(bf16[384,1536]{1,0:T(8,128)(2,1)} %param.22) | copy-start | bytes 3538948
  7.3 79.7 %all-gather.12.cloned.1.call-start = ((), (), s32[]{:S(2)}) async-start(), calls=%async_computation.11 | async-start | bytes 2506752 | tf_op jit(solution)/shard_map/all_gather | solution.py:258
  9.2 74.4 %copy-start.61 = (bf16[6,1536]{1,0:T(8,128)(2,1)S(1)}, bf16[6,1536]{1,0:T(8,128)(2,1)}, u32[]{:S(2)}) copy-start(bf16[6,1536]{1,0:T(8,128)(2,1)} %param.23) | copy-start | bytes 55300
  9.2 91.0 %all-gather.16.cloned.1.call-start = ((), (), s32[]{:S(2)}) async-start(), calls=%async_computation.13 | async-start | bytes 2506752 | tf_op jit(solution)/shard_map/all_gather | solution.py:257
  10.9 133.3 %all-gather.14.cloned.1.call-start = ((), (), s32[]{:S(2)}) async-start(), calls=%async_computation.12 | async-start | bytes 2506752 | tf_op jit(solution)/shard_map/all_gather | solution.py:259
  12.6 178.2 %all-gather.18.cloned.1.call-start = ((), (), s32[]{:S(2)}) async-start(), calls=%async_computation.14 | async-start | bytes 2506752 | tf_op jit(solution)/shard_map/all_gather | solution.py:260
  14.4 216.4 %all-gather.24.cloned.1.call-start = ((), (), s32[]{:S(2)}) async-start(), calls=%async_computation.18 | async-start | bytes 1253376 | tf_op jit(solution)/shard_map/all_gather | solution.py:262
  15.1 255.7 %all-gather.20.cloned.1.call-start = ((), (), s32[]{:S(2)}) async-start(), calls=%async_computation.16 | async-start | bytes 1253376 | tf_op jit(solution)/shard_map/all_gather | solution.py:263
  15.8 299.7 %all-reduce.22.cloned.1.call-start = ((), (), s32[]{:S(2)}) async-start(), calls=%async_computation.15 | async-start | bytes 2359296 | tf_op jit(solution)/shard_map/psum | solution.py:232
  17.2 73.0 %copy-start.102 = (s32[384]{0:T(512)}, s32[384]{0:T(512)S(1)}, u32[]{:S(2)}) copy-start(s32[384]{0:T(512)S(1)} %broadcast_subtract_fusion) | copy-start | bytes 4612
  82.7 73.7 %copy-start.37 = (f32[1536]{0:T(1024)}, f32[1536]{0:T(1024)S(1)}, u32[]{:S(2)}) copy-start(f32[1536]{0:T(1024)S(1)} %convert_element_type.279) | copy-start | bytes 18436
  83.0 61.2 %copy-start.74 = (f32[384]{0:T(512)}, f32[384]{0:T(512)S(1)}, u32[]{:S(2)}) copy-start(f32[384]{0:T(512)S(1)} %broadcast_multiply_fusion.8) | copy-start | bytes 4612
  83.4 60.8 %copy-start.76 = (f32[384]{0:T(512)}, f32[384]{0:T(512)S(1)}, u32[]{:S(2)}) copy-start(f32[384]{0:T(512)S(1)} %add_rsqrt_fusion.2) | copy-start | bytes 4612
  103.6 64.6 %copy-start.34 = (bf16[384,12,32]{0,2,1:T(8,128)(2,1)}, bf16[384,12,32]{0,2,1:T(8,128)(2,1)S(1)}, u32[]{:S(2)}) copy-start(bf16[384,12,32]{0,2,1:T(8,128)(2,1)S(1)} %slice.172) | copy-start | bytes 884740
  103.8 64.4 %copy-start.48 = (bf16[384,12,16]{0,2,1:T(8,128)(2,1)}, bf16[384,12,16]{0,2,1:T(8,128)(2,1)S(1)}, u32[]{:S(2)}) copy-start(bf16[384,12,16]{0,2,1:T(8,128)(2,1)S(1)} %get-tuple-element.271) | copy-start | bytes 442372
  103.8 64.4 %copy-start.51 = (bf16[384,12,16]{0,2,1:T(8,128)(2,1)}, bf16[384,12,16]{0,2,1:T(8,128)(2,1)S(1)}, u32[]{:S(2)}) copy-start(bf16[384,12,16]{0,2,1:T(8,128)(2,1)S(1)} %get-tuple-element.272) | copy-start | bytes 442372
  149.1 12.9 collective-permute-start
  152.3 9.8 collective-permute-start.1
  159.9 21.8 copy-start.89
  194.8 166.2 %all-gather.22.cloned.1.call-start = ((), (), s32[]{:S(2)}) async-start(), calls=%async_computation.17 | async-start | bytes 2506752 | tf_op jit(solution)/shard_map/all_gather | solution.py:261
  195.6 209.6 %all-gather.26.cloned.1.call-start = ((), (), s32[]{:S(2)}) async-start(), calls=%async_computation.19 | async-start | bytes 2506752 | tf_op jit(solution)/shard_map/all_gather | solution.py:264
  197.3 253.8 %all-reduce.24.cloned.1.call-start = ((), (), s32[]{:S(2)}) async-start(), calls=%async_computation.20 | async-start | bytes 2359296 | tf_op jit(solution)/shard_map/psum | solution.py:232
  197.7 74.8 %copy-start.22 = (bf16[2,128,768]{2,1,0:T(8,128)(2,1)}, bf16[2,128,768]{2,1,0:T(8,128)(2,1)S(1)}, u32[]{:S(2)}) copy-start(bf16[2,128,768]{2,1,0:T(8,128)(2,1)S(1)} %constant_dynamic-slice_fusion.1) | copy-start | bytes 1179652
  232.6 133.5 %copy-start.32 = (bf16[256,768]{0,1:T(8,128)(2,1)}, bf16[256,768]{0,1:T(8,128)(2,1)S(1)}, u32[]{:S(2)}) copy-start(bf16[256,768]{0,1:T(8,128)(2,1)S(1)} %copy.104) | copy-start | bytes 1179652
  317.3 47.5 %copy-start.83 = (f32[384]{0:T(512)}, f32[384]{0:T(512)S(1)}, u32[]{:S(2)}) copy-start(f32[384]{0:T(512)S(1)} %broadcast_multiply_fusion.7) | copy-start | bytes 4612
  317.8 46.9 %copy-start.87 = (f32[384]{0:T(512)}, f32[384]{0:T(512)S(1)}, u32[]{:S(2)}) copy-start(f32[384]{0:T(512)S(1)} %add_rsqrt_fusion.1) | copy-start | bytes 4612
  409.2 126.2 %all-gather.30.cloned.1.call-start = ((), (), s32[]{:S(2)}) async-start(), calls=%async_computation.22 | async-start | bytes 10027008 | tf_op jit(solution)/shard_map/all_gather | solution.py:266
  410.2 207.5 %all-gather.32.cloned.1.call-start = ((), (), s32[]{:S(2)}) async-start(), calls=%async_computation.23 | async-start | bytes 10027008 | tf_op jit(solution)/shard_map/all_gather | solution.py:267
  412.5 287.7 %all-gather.28.cloned.1.call-start = ((), (), s32[]{:S(2)}) async-start(), calls=%async_computation.21 | async-start | bytes 10027008 | tf_op jit(solution)/shard_map/all_gather | solution.py:265
  413.5 353.5 %all-reduce.26.cloned.1.call-start = ((), (), s32[]{:S(2)}) async-start(), calls=%async_computation.24 | async-start | bytes 2359296 | tf_op jit(solution)/shard_map/psum | solution.py:235
  455.2 245.0 %copy-start.20 = (bf16[384,1536]{1,0:T(8,128)(2,1)}, bf16[384,1536]{1,0:T(8,128)(2,1)S(1)}, u32[]{:S(2)}) copy-start(bf16[384,1536]{1,0:T(8,128)(2,1)S(1)} %multiply_convert_fusion.5) | copy-start | bytes 3538948
  700.2 13.7 copy-start.112
  725.8 44.9 %copy-start.30 = (bf16[384,1536]{1,0:T(8,128)(2,1)S(1)}, bf16[384,1536]{1,0:T(8,128)(2,1)}, u32[]{:S(2)}) copy-start(bf16[384,1536]{1,0:T(8,128)(2,1)} %param.43) | copy-start | bytes 3538948
  725.8 106.7 %all-reduce.28.cloned.1.call-start = ((), (), s32[]{:S(2)}) async-start(), calls=%async_computation.25 | async-start | bytes 2359296 | tf_op jit(solution)/shard_map/psum | solution.py:235
  789.4 236.8 %all-reduce.30.cloned.1.call-start = ((), (), s32[]{:S(2)}) async-start(), calls=%async_computation.37 | async-start | bytes 196608 | tf_op jit(solution)/shard_map/psum | solution.py:486
  789.7 42.8 %copy-start.84 = (f32[384]{0:T(512)S(1)}, f32[384]{0:T(512)}, u32[]{:S(2)}) copy-start(f32[384]{0:T(512)} %copy-done.83) | copy-start | bytes 4612
  789.7 42.8 %copy-start.88 = (f32[384]{0:T(512)S(1)}, f32[384]{0:T(512)}, u32[]{:S(2)}) copy-start(f32[384]{0:T(512)} %copy-done.87) | copy-start | bytes 4612
  849.2 27.7 %copy-start.13 = (f32[12,64,896]{2,1,0:T(8,128)}, f32[12,64,896]{2,1,0:T(8,128)S(1)}, u32[]{:S(2)}) copy-start(f32[12,64,896]{2,1,0:T(8,128)S(1)} %fusion.2) | copy-start | bytes 8257540
  849.2 11.9 copy-start.60
  849.2 11.9 copy-start.90
  861.7 11.8 copy-start.35
  861.7 11.9 copy-start.49
  861.7 11.8 copy-start.52
  879.6 24.0 %collective-permute-start.2 = (bf16[2,256,768]{1,2,0:T(8,128)(2,1)}, bf16[2,256,768]{1,2,0:T(8,128)(2,1)}, u32[]{:S(2)}, u32[]{:S(2)}) collective-permute-start(bf16[2,256,768]{1,2,0:T(8,128)(2,1)} %get-tuple-element.251), channel_id=1, source_target_pairs={{0,2},{2,4},{4,6},{6,8},{8,10},{10,12},{12,14},{14,16},{16,18},{18... | collective-permute-start | bytes 2359304 | tf_op jit(solution)/shard_map/ppermute | solution.py:33
  882.3 21.3 collective-permute-start.3
  903.4 195.3 %all-reduce.32.cloned.1.call-start = ((), (), s32[]{:S(2)}) async-start(), calls=%async_computation.38 | async-start | bytes 4718592 | tf_op jit(solution)/shard_map/psum | solution.py:232
  914.4 255.9 %reduce-scatter.26.cloned.1.call-start = ((), (), s32[]{:S(2)}) async-start(), calls=%async_computation.32 | async-start | bytes 2506752 | tf_op jit(solution)/shard_map/reduce_scatter | solution.py:471
  921.2 311.7 %reduce-scatter.24.cloned.1.call-start = ((), (), s32[]{:S(2)}) async-start(), calls=%async_computation.31 | async-start | bytes 2506752 | tf_op jit(solution)/shard_map/reduce_scatter | solution.py:470
  926.7 385.7 %reduce-scatter.22.cloned.1.call-start = ((), (), s32[]{:S(2)}) async-start(), calls=%async_computation.30 | async-start | bytes 5013504 | tf_op jit(solution)/shard_map/reduce_scatter | solution.py:469
  931.8 459.6 %reduce-scatter.28.cloned.1.call-start = ((), (), s32[]{:S(2)}) async-start(), calls=%async_computation.33 | async-start | bytes 5013504 | tf_op jit(solution)/shard_map/reduce_scatter | solution.py:472
  938.1 532.9 %reduce-scatter.20.cloned.1.call-start = ((), (), s32[]{:S(2)}) async-start(), calls=%async_computation.29 | async-start | bytes 5013504 | tf_op jit(solution)/shard_map/reduce_scatter | solution.py:468
  944.5 605.5 %reduce-scatter.18.cloned.1.call-start = ((), (), s32[]{:S(2)}) async-start(), calls=%async_computation.28 | async-start | bytes 5013504 | tf_op jit(solution)/shard_map/reduce_scatter | solution.py:467
  952.5 676.9 %reduce-scatter.16.cloned.1.call-start = ((), (), s32[]{:S(2)}) async-start(), calls=%async_computation.27 | async-start | bytes 5013504 | tf_op jit(solution)/shard_map/reduce_scatter | solution.py:466
  958.7 749.8 %reduce-scatter.14.cloned.1.call-start = ((), (), s32[]{:S(2)}) async-start(), calls=%async_computation.26 | async-start | bytes 5013504 | tf_op jit(solution)/shard_map/reduce_scatter | solution.py:465
  963.5 944.0 %reduce-scatter.30.cloned.1.call-start = ((), (), s32[]{:S(2)}) async-start(), calls=%async_computation.34 | async-start | bytes 20054016 | tf_op jit(solution)/shard_map/reduce_scatter | solution.py:511
  975.6 1131.0 %reduce-scatter.32.cloned.1.call-start = ((), (), s32[]{:S(2)}) async-start(), calls=%async_computation.35 | async-start | bytes 20054016 | tf_op jit(solution)/shard_map/reduce_scatter | solution.py:512
  986.5 1319.2 %reduce-scatter.34.cloned.1.call-start = ((), (), s32[]{:S(2)}) async-start(), calls=%async_computation.36 | async-start | bytes 20054016
  1017.4 83.7 %copy-start.94 = (f32[1536]{0:T(1024)S(1)}, f32[1536]{0:T(1024)}, u32[]{:S(2)}) copy-start(f32[1536]{0:T(1024)} %get-tuple-element.215) | copy-start | bytes 18436
  1017.4 83.7 %copy-start.95 = (f32[1536]{0:T(1024)S(1)}, f32[1536]{0:T(1024)}, u32[]{:S(2)}) copy-start(f32[1536]{0:T(1024)} %get-tuple-element.217) | copy-start | bytes 18436
  1017.4 83.7 %copy-start.98 = (f32[1536]{0:T(1024)S(1)}, f32[1536]{0:T(1024)}, u32[]{:S(2)}) copy-start(f32[1536]{0:T(1024)} %get-tuple-element.263) | copy-start | bytes 18436
  1098.7 66.4 %copy-start.58 = (bf16[384,1536]{1,0:T(8,128)(2,1)S(1)}, bf16[384,1536]{1,0:T(8,128)(2,1)}, u32[]{:S(2)}) copy-start(bf16[384,1536]{1,0:T(8,128)(2,1)} %get-tuple-element.237) | copy-start | bytes 3538948
  1165.1 1140.6 %copy-start.1 = (bf16[6,128,768]{2,1,0:T(8,128)(2,1)S(1)}, bf16[6,128,768]{2,1,0:T(8,128)(2,1)}, u32[]{:S(2)}) copy-start(bf16[6,128,768]{2,1,0:T(8,128)(2,1)} %param.24) | copy-start | bytes 3538948
  (91 other events, 320.6 us)
Sparse Core Ops, SparseCore 0:
  11.0 45.1 all-gather.11
  59.1 41.0 all-gather.15
  103.1 41.0 all-gather.13
  146.9 43.8 all-gather.17
  193.6 37.1 all-gather.23
  233.4 37.2 all-gather.19
  273.6 41.8 all-reduce.21
  318.6 42.3 all-gather.21
  364.1 40.9 all-gather.25
  409.3 41.6 all-reduce.23
  453.9 81.4 all-gather.29
  538.1 79.5 all-gather.31
  620.6 79.5 all-gather.27
  725.9 41.0 all-reduce.25
  789.5 42.8 all-reduce.27
  903.5 122.6 all-reduce.29
  1029.0 69.6 all-reduce.31
  1103.4 63.2 reduce-scatter.25
  1171.0 61.8 reduce-scatter.23
  1237.7 74.6 reduce-scatter.21
  1316.8 74.5 reduce-scatter.27
  1396.3 74.5 reduce-scatter.19
  1475.4 74.5 reduce-scatter.17
  1554.8 74.6 reduce-scatter.15
  1633.9 74.5 reduce-scatter.13
  1713.6 193.8 reduce-scatter.29
  1912.6 193.8 reduce-scatter.31
  2111.8 193.8 reduce-scatter.33
where the time goes:
time: 2320 us; the launch traced here: 2310 us
  waiting for transfers between devices  1780 us (77%)
  matrix products  228 us (10%)
  blocking collectives  125 us (5%)
  other arithmetic  75.5 us (3%)
  local copies, waits for them, and re-layouts  72.7 us (3%)
    unnamed x29, waiting for transfers between devices  200 us
    reduce_scatter x1, waiting for transfers between devices, per_device(): lax.psum_scatter(glu_terms[0], 'seq', scatter_dimension=0, tiled=True)  199 us
    reduce_scatter x1, waiting for transfers between devices, per_device(): lax.psum_scatter(glu_terms[1], 'seq', scatter_dimension=0, tiled=True)  199 us
    psum x3, waiting for transfers between devices, branch_total(): lax.psum(partial_sum.astype(jnp.bfloat16), 'head').astype(jnp.float32)  147 us
    unnamed x2, blocking collectives  125 us
    all_gather x1, waiting for transfers between devices, per_device(): lax.all_gather(up_weight.astype(jnp.bfloat16), 'seq', axis=0, tiled=True)  80.2 us
    reduce_scatter x1, waiting for transfers between devices, per_device(): lax.psum_scatter(out_term, 'seq', scatter_dimension=0, tiled=True)  79.6 us
    reduce_scatter x1, waiting for transfers between devices, per_device(): lax.psum_scatter(key_term, 'seq', scatter_dimension=0, tiled=True)  79.4 us
  transfers between devices with their start and end apart: 32, of which 26 were waited for; matrix products, arithmetic and copies ran while one was open for 11% of the time, Pallas kernels for 0%

commit v1 on v0

v1 whole, which is shorter than its diff:
```python
from functools import reduce

import jax
import jax.numpy as jnp
from jax import lax
from jax.sharding import PartitionSpec as P

HD = 64
ROT = 32
HALF = 256


EPS = 1e-05
NEG = -1e30


def extended(block, sides, width):
    for axis, dim in sides:
        count = lax.axis_size(axis)
        forward = [(i, i + 1) for i in range(count - 1)]
        backward = [(target, source) for source, target in forward]
        low = lax.ppermute(
            lax.slice_in_dim(block, block.shape[dim] - width, None, axis=dim), axis, forward
        )
        high = lax.ppermute(lax.slice_in_dim(block, 0, width, axis=dim), axis, backward)
        block = jnp.concatenate([low, block, high], axis=dim)
    return block


def passed_along(value, axis, steps):
    count = lax.axis_size(axis)
    first, last = (max(0, -steps), min(count, count - steps))
    return lax.ppermute(value, axis, [(source, source + steps) for source in range(first, last)])


def layer_norm_parts(values, gain):
    average = jnp.mean(values, axis=-1, keepdims=True)
    centered = values - average
    spread = jnp.mean(centered * centered, axis=-1, keepdims=True)
    inverse = lax.rsqrt(spread + EPS)
    normal = centered * inverse
    return (normal * gain, normal, inverse)


def norm_back(grad_out, normal, inverse, gain):
    shaped = grad_out * gain
    return (
        shaped
        - jnp.mean(shaped, axis=-1, keepdims=True)
        - normal * jnp.mean(shaped * normal, axis=-1, keepdims=True)
    ) * inverse


def angles(positions):
    ladder = jnp.arange(ROT // 2, dtype=jnp.float32)
    frequency = 10000.0 ** (-2.0 * ladder / ROT)
    phases = positions.astype(jnp.float32)[:, None] * frequency[None, :]
    return (jnp.cos(phases), jnp.sin(phases))


def rotate(values, cos_table, sin_table):
    shaped = values.reshape(values.shape[0], -1, HD)
    rot_half = ROT // 2
    leading = shaped[:, :, :rot_half]
    trailing = shaped[:, :, rot_half:ROT]
    cos_row = cos_table[:, None, :]
    sin_row = sin_table[:, None, :]
    turned = jnp.concatenate(
        [
            leading * cos_row - trailing * sin_row,
            trailing * cos_row + leading * sin_row,
            shaped[:, :, ROT:],
        ],
        axis=-1,
    )
    return turned.reshape(values.shape)


def product(matrix_a, matrix_b):
    return jnp.dot(matrix_a, matrix_b, preferred_element_type=jnp.float32)


def product_t(matrix_a, matrix_b):
    return lax.dot_general(
        matrix_a, matrix_b, (((1,), (1,)), ((), ())), preferred_element_type=jnp.float32
    )


def product_tn(matrix_a, matrix_b):
    return lax.dot_general(
        matrix_a, matrix_b, (((0,), (0,)), ((), ())), preferred_element_type=jnp.float32
    )


def exact_t(matrix_a, matrix_b):
    return lax.dot_general(
        matrix_a,
        matrix_b,
        (((1,), (1,)), ((), ())),
        precision=lax.Precision.HIGHEST,
        preferred_element_type=jnp.float32,
    )


def exact_tn(matrix_a, matrix_b):
    return lax.dot_general(
        matrix_a,
        matrix_b,
        (((0,), (0,)), ((), ())),
        precision=lax.Precision.HIGHEST,
        preferred_element_type=jnp.float32,
    )


def score_parts(query_h, key_parts, score_scale):
    return [
        jnp.where(
            visible[None],
            jnp.einsum("qhd,khd->hqk", query_h, key_h, preferred_element_type=jnp.float32)
            * score_scale,
            NEG,
        )
        for key_h, value_h, visible in key_parts
    ]


def attend_forward(query_h, key_parts, score_scale):
    scores = score_parts(query_h, key_parts, score_scale)
    row_peak = reduce(jnp.maximum, [jnp.max(score_part, axis=-1) for score_part in scores])
    exp_parts = [jnp.exp(score_part - row_peak[:, :, None]) for score_part in scores]
    row_total = reduce(jnp.add, [jnp.sum(exp_part, axis=-1) for exp_part in exp_parts])
    attn_mixed = reduce(
        jnp.add,
        [
            jnp.einsum(
                "hqk,khd->qhd",
                (exp_part / row_total[:, :, None]).astype(jnp.bfloat16),
                key_part[1],
                preferred_element_type=jnp.float32,
            )
            for exp_part, key_part in zip(exp_parts, key_parts)
        ],
    )
    return (attn_mixed, row_peak + jnp.log(row_total))


def attend_backward(query_h, key_parts, score_scale, log_total, grad_h):
    scores = score_parts(query_h, key_parts, score_scale)
    prob_parts = [jnp.exp(score_part - log_total[:, :, None]) for score_part in scores]
    dprob_parts = [
        jnp.einsum("qhd,khd->hqk", grad_h, key_part[1], preferred_element_type=jnp.float32)
        for key_part in key_parts
    ]
    row_dot = reduce(
        jnp.add,
        [
            jnp.sum(prob_part * dprob_part, axis=-1)
            for prob_part, dprob_part in zip(prob_parts, dprob_parts)
        ],
    )
    dscore_parts = [
        (prob_part * (dprob_part - row_dot[:, :, None])).astype(jnp.bfloat16)
        for prob_part, dprob_part in zip(prob_parts, dprob_parts)
    ]
    grad_query = (
        reduce(
            jnp.add,
            [
                jnp.einsum(
                    "hqk,khd->qhd", dscore_part, key_part[0], preferred_element_type=jnp.float32
                )
                for dscore_part, key_part in zip(dscore_parts, key_parts)
            ],
        )
        * score_scale
    )
    grad_keys = [
        jnp.einsum("hqk,qhd->khd", dscore_part, query_h, preferred_element_type=jnp.float32)
        * score_scale
        for dscore_part in dscore_parts
    ]
    grad_values = [
        jnp.einsum(
            "hqk,qhd->khd",
            prob_part.astype(jnp.bfloat16),
            grad_h,
            preferred_element_type=jnp.float32,
        )
        for prob_part in prob_parts
    ]
    return (grad_query, grad_keys, grad_values)


LANES = 128
RING_LIMIT = 16


def ring_place(chip, chips):
    return jnp.where(chip % 2 == 0, chip // 2, chips - 1 - chip // 2)


def ring_chip(place, chips):
    return jnp.where(2 * place < chips, 2 * place, 2 * (chips - 1 - place) + 1)


def static_chip(place, chips):
    return 2 * place if 2 * place < chips else 2 * (chips - 1 - place) + 1


def ring_pairs(chips, step):
    return [
        (2 * static_chip(place, chips) + core, 2 * static_chip((place + step) % chips, chips) + core)
        for place in range(chips)
        for core in range(2)
    ]


def owner_order(matrix, seq_index, seq_count):
    chips = seq_count // 2
    width = matrix.shape[-1] // seq_count
    core = seq_index % 2
    place = ring_place(seq_index // 2, chips)
    blocks = []
    for which in (core, 1 - core):
        for near in range(chips):
            chip = ring_chip((place + near) % chips, chips)
            blocks.append(
                lax.dynamic_slice_in_dim(matrix, (2 * chip + which) * width, width, axis=-1)
            )
    return jnp.concatenate(blocks, axis=-1)


def over_core(values, seq_count):
    return lax.ppermute(values, "seq", [(index, index ^ 1) for index in range(seq_count)])


def ring_sum(chunks, seq_count):
    chips = seq_count // 2
    far = chips // 2
    half = chunks[0].shape[-1] // 2
    ahead, behind = ring_pairs(chips, 1), ring_pairs(chips, -1)
    onward = lax.ppermute(chunks[far][..., :half], "seq", ahead)
    backward = lax.ppermute(chunks[far][..., half:], "seq", behind)

    def joined(term, arrived, low_side):
        term, arrived = term.astype(jnp.float32), arrived.astype(jnp.float32)
        if arrived.shape != term.shape:
            pads = (0, half) if low_side else (half, 0)
            arrived = jnp.pad(arrived, ((0, 0),) * (term.ndim - 1) + (pads,))
        return (term + arrived).astype(jnp.bfloat16)

    for near in range(1, far):
        onward = lax.ppermute(joined(chunks[far - near], onward, True), "seq", ahead)
        backward = lax.ppermute(joined(chunks[far + near], backward, False), "seq", behind)
    total = chunks[0].astype(jnp.float32)
    return total + onward.astype(jnp.float32) + backward.astype(jnp.float32)


def owned_sum(rows, columns, seq_count):
    chips = seq_count // 2
    if chips > RING_LIMIT:
        return None
    half = rows.shape[-1] // 2
    away = product_tn(rows[:, half:], columns).astype(jnp.bfloat16)
    arrived = over_core(away, seq_count)
    mine = (product_tn(rows[:, :half], columns) + arrived.astype(jnp.float32)).astype(jnp.bfloat16)
    width = half // chips
    return ring_sum(
        [mine[near * width : (near + 1) * width] for near in range(chips)], seq_count
    )


def weight_grad(rows, columns, seq_index, seq_count):
    if seq_count // 2 > RING_LIMIT:
        return lax.psum_scatter(
            product_tn(rows, columns).astype(jnp.bfloat16), "seq", scatter_dimension=0, tiled=True
        ).astype(jnp.float32)
    return owned_sum(owner_order(rows, seq_index, seq_count), columns, seq_count)


def head_total(partial_sum):
    low = lax.optimization_barrier(partial_sum.astype(jnp.bfloat16))
    count = lax.axis_size("head")
    total = low.astype(jnp.float32)
    for step in range(1, count):
        pairs = [(index, (index + step) % count) for index in range(count)]
        total = total + lax.ppermute(low, "head", pairs).astype(jnp.float32)
    return total


def low_gather(block):
    return lax.all_gather(block.astype(jnp.bfloat16), "seq", axis=0, tiled=True)


def per_device(
    frames,
    time_token,
    prompt,
    clip_ids,
    norm1_gain,
    norm2_gain,
    norm3_gain,
    query_weight,
    key_weight,
    value_weight,
    out_weight,
    cross_query,
    cross_key,
    cross_value,
    cross_out,
    gate_weight,
    up_weight,
    down_weight,
    gate_bias,
    up_bias,
    down_bias,
    out_grad,
):
    local_rows, width = frames.shape
    clip_total = time_token.shape[0]
    ctx_tokens = prompt.shape[1]
    slot_count = local_rows // (2 * HALF) + 2
    seq_count = lax.axis_size("seq")
    seq_index = lax.axis_index("seq")
    head_index = lax.axis_index("head")
    first_row = seq_index * local_rows
    score_scale = HD ** (-0.5)
    part = query_weight.shape[1]
    hidden_width = gate_weight.shape[1]
    gain_rows = norm1_gain.shape[0]
    ctx_rows = cross_key.shape[0]
    ctx_width = prompt.shape[2]
    head_count = part // HD

    vectors = jnp.stack([norm1_gain, norm2_gain, norm3_gain, down_bias], axis=1)
    vectors = jnp.pad(vectors, ((0, 0), (0, LANES - 4)))
    ctx_pair = jnp.concatenate([cross_key, cross_value], axis=0)
    attn_local = jnp.concatenate(
        [query_weight, key_weight, value_weight, out_weight, cross_query, cross_out, ctx_pair, vectors],
        axis=1,
    )
    attn_weights = low_gather(attn_local)
    glu_weights = low_gather(jnp.concatenate([gate_weight, up_weight, down_weight], axis=1))
    w_qkv = attn_weights[:, : 3 * part]
    w_out = attn_weights[:, 3 * part : 4 * part]
    c_query = attn_weights[:, 4 * part : 5 * part]
    c_out = attn_weights[:, 5 * part : 6 * part]
    ctx_weights = attn_weights[:, 6 * part : 7 * part].reshape(seq_count, 2, ctx_rows, part)
    c_key = ctx_weights[:, 0].reshape(ctx_width, part)
    c_value = ctx_weights[:, 1].reshape(ctx_width, part)
    rows_of = attn_weights[:, 7 * part : 7 * part + 8].astype(jnp.float32).T
    gain_one_f, gain_two_f, gain_three_f, bias_f = rows_of[0], rows_of[1], rows_of[2], rows_of[3]
    w_gate_up = glu_weights[:, : 2 * hidden_width]
    w_down = glu_weights[:, 2 * hidden_width :]

    positions = first_row + jnp.arange(local_rows, dtype=jnp.int32)
    cos_table, sin_table = angles(positions)
    padded_ids = jnp.pad(clip_ids, (HALF, HALF), constant_values=-1)
    own_ids = lax.dynamic_slice_in_dim(clip_ids, first_row, local_rows)
    near_ids = lax.dynamic_slice_in_dim(padded_ids, first_row, local_rows + 2 * HALF)
    base_clip = jnp.minimum(own_ids[0], clip_total - slot_count)
    own_slot = own_ids - base_clip
    slot_range = jnp.arange(slot_count, dtype=jnp.int32)
    pad_rows = -slot_count % 16
    stamp_end = local_rows + slot_count

    stamp_rows = lax.dynamic_slice_in_dim(time_token, base_clip, slot_count, 0)
    source = jnp.concatenate(
        [frames, jnp.pad(stamp_rows, ((0, pad_rows), (0, 0)))], axis=0
    ).astype(jnp.float32)
    normed_out, normal_one, inverse_one = layer_norm_parts(source, gain_one_f)
    normed_one = normed_out.astype(jnp.bfloat16)
    frames_f = source[:local_rows]
    qkv = product(normed_one, w_qkv)
    query_rows = rotate(qkv[:local_rows, :part], cos_table, sin_table).astype(jnp.bfloat16)
    key_rows = rotate(qkv[:local_rows, part : 2 * part], cos_table, sin_table).astype(jnp.bfloat16)
    value_rows = qkv[:local_rows, 2 * part :].astype(jnp.bfloat16)
    near = extended(jnp.stack([key_rows, value_rows]), (("seq", 1),), HALF)
    window = local_rows + 2 * HALF
    near_key_h = near[0].reshape(window, head_count, HD)
    near_value_h = near[1].reshape(window, head_count, HD)
    query_h = query_rows.reshape(local_rows, head_count, HD)
    stamps = qkv[local_rows:stamp_end].astype(jnp.bfloat16)
    stamp_key_h = stamps[:, part : 2 * part].reshape(slot_count, head_count, HD)
    stamp_value_h = stamps[:, 2 * part :].reshape(slot_count, head_count, HD)

    query_pos = jnp.arange(local_rows, dtype=jnp.int32)
    key_pos = jnp.arange(window, dtype=jnp.int32) - HALF
    visible = (own_ids[:, None] == near_ids[None, :]) & (
        jnp.abs(query_pos[:, None] - key_pos[None, :]) <= HALF
    )
    own_stamp = own_slot[:, None] == slot_range[None, :]
    self_keys = [(near_key_h, near_value_h, visible), (stamp_key_h, stamp_value_h, own_stamp)]
    attn_mix_h, self_logs = attend_forward(query_h, self_keys, score_scale)
    attn_mixed = attn_mix_h.reshape(local_rows, part).astype(jnp.bfloat16)
    h_one = frames_f + head_total(product_t(attn_mixed, w_out))
    middle_out, normal_two, inverse_two = layer_norm_parts(h_one, gain_two_f)
    normed_two = middle_out.astype(jnp.bfloat16)
    cross_h = product(normed_two, c_query).astype(jnp.bfloat16).reshape(local_rows, head_count, HD)
    context_rows = lax.dynamic_slice_in_dim(prompt, base_clip, slot_count, 0).reshape(
        slot_count * ctx_tokens, ctx_width
    )
    ctx_key_h = product(context_rows, c_key).astype(jnp.bfloat16)
    ctx_key_h = ctx_key_h.reshape(slot_count * ctx_tokens, head_count, HD)
    ctx_value_h = product(context_rows, c_value).astype(jnp.bfloat16)
    ctx_value_h = ctx_value_h.reshape(slot_count * ctx_tokens, head_count, HD)
    key_slot = jnp.arange(slot_count * ctx_tokens, dtype=jnp.int32) // ctx_tokens
    cross_keys = [(ctx_key_h, ctx_value_h, own_slot[:, None] == key_slot[None, :])]
    cross_mix_h, cross_logs = attend_forward(cross_h, cross_keys, score_scale)
    cross_mixed = cross_mix_h.reshape(local_rows, part).astype(jnp.bfloat16)
    h_two = h_one + head_total(product_t(cross_mixed, c_out))
    third_out, normal_three, inverse_three = layer_norm_parts(h_two, gain_three_f)
    normed_three = third_out.astype(jnp.bfloat16)

    gate_up = product(normed_three, w_gate_up)
    gate_pre = gate_up[:, :hidden_width] + gate_bias
    up_pre = gate_up[:, hidden_width:] + up_bias
    sigmoid_gate = jax.nn.sigmoid(gate_pre)
    hidden = (gate_pre * sigmoid_gate * up_pre).astype(jnp.bfloat16)
    result = (h_two + head_total(product_t(hidden, w_down)) + bias_f).astype(jnp.bfloat16)
    grad_top = out_grad.astype(jnp.float32)
    grad_hidden = product(out_grad, w_down)
    grad_up = (grad_hidden * gate_pre * sigmoid_gate).astype(jnp.bfloat16)
    grad_gate = (
        grad_hidden * up_pre * sigmoid_gate * (1.0 + gate_pre * (1.0 - sigmoid_gate))
    ).astype(jnp.bfloat16)
    grad_gate_up = jnp.concatenate([grad_gate, grad_up], axis=1)
    bias_local = jnp.sum(grad_gate_up.astype(jnp.float32), axis=0).reshape(2, hidden_width)
    grad_normed_three = head_total(product_t(grad_gate_up, w_gate_up))
    down_share = weight_grad(out_grad, hidden, seq_index, seq_count)
    gate_up_share = weight_grad(normed_three, grad_gate_up, seq_index, seq_count)
    gain_three_term = jnp.sum(grad_normed_three * normal_three, axis=0)
    down_bias_term = jnp.sum(grad_top, axis=0)

    grad_h_two = grad_top + norm_back(grad_normed_three, normal_three, inverse_three, gain_three_f)
    grad_two_low = grad_h_two.astype(jnp.bfloat16)
    grad_cross_h = product(grad_two_low, c_out).astype(jnp.bfloat16)
    grad_cross_h = grad_cross_h.reshape(local_rows, head_count, HD)
    cross_out_share = weight_grad(grad_two_low, cross_mixed, seq_index, seq_count)
    grad_cross_q, ctx_key_grads, ctx_value_grads = attend_backward(
        cross_h, cross_keys, score_scale, cross_logs, grad_cross_h
    )
    grad_cross_query = grad_cross_q.reshape(local_rows, part).astype(jnp.bfloat16)
    ctx_grads = jnp.concatenate(
        [ctx_key_grads[0].reshape(-1, part), ctx_value_grads[0].reshape(-1, part)], axis=1
    ).astype(jnp.bfloat16)
    grad_normed_two = head_total(product_t(grad_cross_query, c_query))
    ctx_share = weight_grad(context_rows, ctx_grads, seq_index, seq_count)
    cross_query_share = weight_grad(normed_two, grad_cross_query, seq_index, seq_count)
    gain_two_term = jnp.sum(grad_normed_two * normal_two, axis=0)
    grad_h_one = grad_h_two + norm_back(grad_normed_two, normal_two, inverse_two, gain_two_f)
    grad_one_low = grad_h_one.astype(jnp.bfloat16)
    grad_attn_h = product(grad_one_low, w_out).astype(jnp.bfloat16)
    grad_attn_h = grad_attn_h.reshape(local_rows, head_count, HD)
    out_share = weight_grad(grad_one_low, attn_mixed, seq_index, seq_count)

    grad_query, grad_keys, grad_values = attend_backward(
        query_h, self_keys, score_scale, self_logs, grad_attn_h
    )
    near_grads = jnp.stack([grad_keys[0], grad_values[0]]).reshape(2, window, part)
    from_above = passed_along(near_grads[:, :HALF].astype(jnp.bfloat16), "seq", -1).astype(
        jnp.float32
    )
    from_below = passed_along(
        near_grads[:, HALF + local_rows :].astype(jnp.bfloat16), "seq", 1
    ).astype(jnp.float32)
    own_grads = (
        near_grads[:, HALF : HALF + local_rows]
        + jnp.pad(from_below, ((0, 0), (0, local_rows - HALF), (0, 0)))
        + jnp.pad(from_above, ((0, 0), (local_rows - HALF, 0), (0, 0)))
    )
    grad_query_rows = rotate(grad_query.reshape(local_rows, part), cos_table, -sin_table)
    grad_key_rows = rotate(own_grads[0], cos_table, -sin_table)
    stamp_grads = jnp.concatenate(
        [
            jnp.zeros((slot_count, part), jnp.float32),
            grad_keys[1].reshape(slot_count, part),
            grad_values[1].reshape(slot_count, part),
        ],
        axis=1,
    )
    frame_grads = jnp.concatenate([grad_query_rows, grad_key_rows, own_grads[1]], axis=1)
    grad_qkv = jnp.concatenate(
        [
            frame_grads.astype(jnp.bfloat16),
            jnp.pad(stamp_grads, ((0, pad_rows), (0, 0))).astype(jnp.bfloat16),
        ],
        axis=0,
    )
    grad_normed_all = product_t(grad_qkv, w_qkv)
    grad_normed_one = head_total(grad_normed_all[:local_rows])
    qkv_share = weight_grad(normed_one, grad_qkv, seq_index, seq_count)
    gain_one_term = jnp.sum(grad_normed_one * normal_one[:local_rows], axis=0)
    frames_grad = (
        grad_h_one
        + norm_back(grad_normed_one, normal_one[:local_rows], inverse_one[:local_rows], gain_one_f)
    ).astype(jnp.bfloat16)

    stamp_full = lax.dynamic_update_slice_in_dim(
        jnp.zeros((clip_total, width), jnp.float32), grad_normed_all[local_rows:stamp_end], base_clip, 0
    )
    bias_full = lax.dynamic_update_slice_in_dim(
        jnp.zeros((2, hidden_width * lax.axis_size("head")), jnp.float32),
        bias_local,
        head_index * hidden_width,
        1,
    )
    share = 1.0 / lax.axis_size("head")
    gains_full = share * jnp.stack(
        [gain_one_term, gain_two_term, gain_three_term, down_bias_term]
    )
    stamp_sum, bias_sum, gains_sum = lax.psum((stamp_full, bias_full, gains_full), ("seq", "head"))
    every_out, every_normal, every_inverse = layer_norm_parts(
        time_token.astype(jnp.float32), gain_one_f
    )
    time_grad = norm_back(stamp_sum, every_normal, every_inverse, gain_one_f)
    time_gain = jnp.sum(stamp_sum * every_normal, axis=0)
    gains_own = lax.dynamic_slice_in_dim(
        gains_sum.at[0].add(time_gain), seq_index * gain_rows, gain_rows, 1
    )
    own_bias = lax.dynamic_slice_in_dim(bias_sum, head_index * hidden_width, hidden_width, 1)
    return (
        result,
        frames_grad,
        time_grad,
        gains_own[0],
        gains_own[1],
        gains_own[2],
        qkv_share[:, :part],
        qkv_share[:, part : 2 * part],
        qkv_share[:, 2 * part :],
        out_share,
        cross_query_share,
        ctx_share[:, :part],
        ctx_share[:, part:],
        cross_out_share,
        gate_up_share[:, :hidden_width],
        gate_up_share[:, hidden_width:],
        down_share,
        own_bias[0],
        own_bias[1],
        gains_own[3],
    )


def solution(mesh):
    in_specs = (
        P("seq", None),
        P(),
        P(),
        P(),
        P("seq"),
        P("seq"),
        P("seq"),
        P("seq", "head"),
        P("seq", "head"),
        P("seq", "head"),
        P("seq", "head"),
        P("seq", "head"),
        P("seq", "head"),
        P("seq", "head"),
        P("seq", "head"),
        P("seq", "head"),
        P("seq", "head"),
        P("seq", "head"),
        P("head"),
        P("head"),
        P("seq"),
        P("seq", None),
    )
    out_specs = (
        P("seq", None),
        P("seq", None),
        P(),
        P("seq"),
        P("seq"),
        P("seq"),
        P("seq", "head"),
        P("seq", "head"),
        P("seq", "head"),
        P("seq", "head"),
        P("seq", "head"),
        P("seq", "head"),
        P("seq", "head"),
        P("seq", "head"),
        P("seq", "head"),
        P("seq", "head"),
        P("seq", "head"),
        P("head"),
        P("head"),
        P("seq"),
    )
    return jax.shard_map(
        per_device, mesh=mesh, in_specs=in_specs, out_specs=out_specs, check_vma=False
    )
```

time: 2320 us -> 1050 us (0.45)
  waiting for transfers between devices: 1780 us -> 505 us
  blocking collectives: 125 us -> 0 us
  starting transfers between devices: 11.4 us -> 102 us
  other arithmetic: 75.5 us -> 119 us
  local copies, waits for them, and re-layouts: 72.7 us -> 114 us
  matrix products: 228 us -> 187 us
    reduce_scatter x10 -> x0, waiting for transfers between devices: 936 us -> none  [the longest x1 199 us: per_device(): lax.psum_scatter(glu_terms[0], 'seq', scatter_dimension=0, tiled=True)]
    all_gather x11 -> x2, waiting for transfers between devices: 421 us -> 96 us  [low_gather(): return lax.all_gather(block.astype(jnp.bfloat16), 'seq', axis=0, tiled=True)]
    ppermute x0 -> x69, waiting for transfers between devices: none -> 292 us  [the longest x21 146 us: ring_sum(): lax.ppermute(joined(chunks[far + near], backward, False), 'seq', behind)]
    unnamed x29 -> x3, waiting for transfers between devices: 200 us -> 0.05 us
    unnamed x2 -> x0, blocking collectives: 125 us -> none
    psum x6 -> x1, waiting for transfers between devices: 225 us -> 117 us  [per_device(): lax.psum((stamp_full, bias_full, gains_full), ('seq', 'head'))]
    ppermute x0 -> x69, starting transfers between devices: none -> 93.7 us  [the longest x21 31.9 us: ring_sum(): lax.ppermute(joined(chunks[far - near], onward, True), 'seq', ahead)]
    concatenate x0 -> x16, local copies, waits for them, and re-layouts: none -> 28.3 us  [the longest x14 27.7 us: owner_order(): return jnp.concatenate(blocks, axis=-1)]
  transfers between devices with their start and end apart: 32 -> 76, of which waited for: 26 -> 42; matrix products, arithmetic and copies ran while one was open for 11% -> 34% of each run, Pallas kernels for 0% -> 0%
where the time goes in v1:
time: 1050 us; the launch traced here: 1040 us
  waiting for transfers between devices  505 us (48%)
  matrix products  187 us (18%)
  other arithmetic  119 us (11%)
  local copies, waits for them, and re-layouts  114 us (11%)
  starting transfers between devices  102 us (10%)
  between operations  17.4 us (2%)
    ppermute x21, waiting for transfers between devices, ring_sum(): lax.ppermute(joined(chunks[far + near], backward, False), 'seq', behind)  146 us
    psum x1, waiting for transfers between devices, per_device(): lax.psum((stamp_full, bias_full, gains_full), ('seq', 'head'))  117 us
    all_gather x2, waiting for transfers between devices, low_gather(): return lax.all_gather(block.astype(jnp.bfloat16), 'seq', axis=0, tiled=True)  96 us
    ppermute x21, waiting for transfers between devices, ring_sum(): lax.ppermute(joined(chunks[far - near], onward, True), 'seq', ahead)  68.5 us
    dot_general x14, matrix products, product_tn(): lax.dot_general(matrix_a, matrix_b, (((0,), (0,)), ((), ())), preferred_e...  58.9 us
    dot_general x6, matrix products, product_t(): lax.dot_general(matrix_a, matrix_b, (((1,), (1,)), ((), ())), preferred_e...  42.5 us
    ppermute x6, waiting for transfers between devices, head_total(): total = total + lax.ppermute(low, 'head', pairs).astype(jnp.float32)  40.2 us
    dot_general x8, matrix products, product(): return jnp.dot(matrix_a, matrix_b, preferred_element_type=jnp.float32)  37.4 us
  transfers between devices with their start and end apart: 76, of which 42 were waited for; matrix products, arithmetic and copies ran while one was open for 34% of the time, Pallas kernels for 0%

profile of v1, /device:TPU:0, one launch (start us, length us, event | category | flops | bytes accessed | tf_op | source)
XLA Modules:
  0.0 1044.4 jit_solution(2110183681542790097)
XLA Ops:
  34.7 77.1 %all-gather.3.cloned.1.call-done = bf16[1536,5504]{1,0:T(8,128)(2,1)} async-done(((bf16[96,5504]{1,0:T(8,128)(2,1)}), bf16[1536,5504]{1,0:T(8,128)(2,1)}) %all-gather.3.cloned.1.call-update) | async-done | bytes 16908304 | tf_op jit(solution)/shard_map/all_gather | solution.py:292
  114.7 7.5 fusion.137
  134.8 4.1 collective-permute-start
  157.1 4.6 fusion.138
  161.9 3.9 fusion.4
  168.0 5.3 fusion.61
  173.4 4.3 convolution_convert_fusion.6
  186.3 7.8 collective-permute-done.2
  198.1 4.0 fusion.66
  209.7 4.0 convolution_convert_fusion.5
  250.5 18.9 %all-gather.5.cloned.1.call-done = bf16[1536,9216]{1,0:T(8,128)(2,1)} async-done(((bf16[96,9216]{1,0:T(8,128)(2,1)}), bf16[1536,9216]{1,0:T(8,128)(2,1)}) %all-gather.5.cloned.1.call-update) | async-done | bytes 28311568 | tf_op jit(solution)/shard_map/all_gather | solution.py:292
  269.5 11.1 %fusion.2 = f32[384,6144]{1,0:T(8,128)S(1)} fusion(bf16[384,1536]{1,0:T(8,128)(2,1)} %copy-done.30, bf16[1536,9216]{1,0:T(8,128)(2,1)} %all-gather.5.cloned.1.call-done), kind=kOutput, calls=%fused_computation.3 | convolution fusion | flops 7247757312 | bytes 29491200 | tf_op jit(solution)/shard_map/dot_general | solution.py:80
  280.7 9.1 fusion.21
  293.4 13.7 %fusion.30 = bf16[384,1536]{1,0:T(8,128)(2,1)} fusion(bf16[1536,9216]{1,0:T(8,128)(2,1)} %all-gather.5.cloned.1.call-done, bf16[384,3072]{1,0:T(8,128)(2,1)} %copy-done.18, bf16[384,3072]{1,0:T(8,128)(2,1)} %copy-done.16), kind=kOutput, calls=%fused_computation.59 | convolution fusion | flops 7257784320 | bytes 24772608 | tf_op jit(solution)/shard_map/dot_general | solution.py:84
  308.9 9.3 fusion.27
  319.8 10.1 convolution_convert_fusion
  330.0 4.4 collective-permute-start.55
  334.4 4.4 convolution_convert_fusion.1
  338.9 3.4 multiply_reduce_fusion.3
  342.3 15.7 %collective-permute-done.4 = bf16[384,1536]{1,0:T(8,128)(2,1)} collective-permute-done((bf16[384,1536]{1,0:T(8,128)(2,1)}, bf16[384,1536]{1,0:T(8,128)(2,1)}, u32[]{:S(2)}, u32[]{:S(2)}) %collective-permute-start.4) | collective-permute-done | bytes 1179680 | tf_op jit(solution)/shard_map/ppermute | solution.py:287
  358.0 6.0 fusion.118
  368.4 3.5 multiply_reduce_fusion.1
  375.1 4.0 convolution_convert_fusion.4
  398.1 8.5 collective-permute-done.6
  411.7 4.2 fusion.117
  421.0 10.9 %multiply_reduce_fusion = (f32[12,384]{1,0:T(8,128)S(1)}, f32[12,384,896]{2,1,0:T(8,128)}) fusion(f32[12,384,896]{2,1,0:T(8,128)} %copy-done.2, f32[12,384]{1,0:T(8,128)S(1)} %copy-done.70, bf16[384,12,64]{0,2,1:T(8,128)(2,1)S(1)} %bitcast.150, bf16[896,12,64]{0,2,1:T(8,128)(2,1)S(1)} %bitcast.161), kind=kOutput, calls=%fused_computation.6 | convolution fusion | flops 540864000 | bytes 35033088 | tf_op jit(solution)/shard_map/qhd,khd->hqk/dot_general | solution.py:151
  432.0 9.1 fusion.10
  441.7 11.6 %multiply_convert_fusion = bf16[12,384,896]{2,1,0:T(8,128)(2,1)S(1)} fusion(f32[12,384,896]{2,1,0:T(8,128)} %get-tuple-element.259, f32[12,384,896]{2,1,0:T(8,128)} %copy-done.2, f32[12,384]{1,0:T(8,128)S(1)} %add.1188, f32[12,384]{1,0:T(8,128)S(1)} %copy-done.70), kind=kLoop, calls=%fused_computation.5 | loop fusion | flops 16515072 | bytes 41324544 | tf_op jit(solution)/shard_map/convert_element_type | solution.py:162
  491.9 10.5 %collective-permute-start.47 = (bf16[96,384]{1,0:T(8,128)(2,1)}, bf16[96,384]{1,0:T(8,128)(2,1)S(1)}, u32[]{:S(2)}, u32[]{:S(2)}) collective-permute-start(bf16[96,384]{1,0:T(8,128)(2,1)} %get-tuple-element.149), channel_id=1, source_target_pairs={{0,8},{2,10},{8,16},{10,18},{16,24},{18,26},{24,28},{26,30},{28,20... | collective-permute-start | bytes 221192 | tf_op jit(solution)/shard_map/ppermute | solution.py:242
  512.2 3.4 collective-permute-done.30
  515.6 3.2 collective-permute-start.48
  518.9 3.4 collective-permute-done.48
  539.4 4.3 collective-permute-done.43
  545.5 4.3 collective-permute-done.34
  552.3 3.4 collective-permute-done.52
  557.4 9.4 collective-permute-done.35
  567.6 5.2 collective-permute-done.53
  574.2 3.7 collective-permute-done.44
  584.4 7.2 fusion.14
  595.3 6.0 convolution_convert_fusion.2
  615.9 3.8 collective-permute-done.36
  629.5 3.9 collective-permute-done.25
  634.7 3.9 collective-permute-done.26
  640.2 8.1 collective-permute-done.9
  651.9 3.8 add_convert_fusion.13
  657.4 116.8 %all-reduce.23.cloned.1.call-done = (f32[6,1536]{1,0:T(8,128)}, f32[4,1536]{1,0:T(4,128)}, f32[2,6144]{1,0:T(2,128)}) async-done(((f32[6,1536]{1,0:T(8,128)}, f32[4,1536]{1,0:T(4,128)}, f32[2,6144]{1,0:T(2,128)}), (f32[6,1536]{1,0:T(8,128)}, f32[4,1536]{1,0:T(4,128)}, f32[2,6144]{1,0:T(2,128)})) %all-reduce.23.cloned.1.call-update) | async-done | bytes 110608 | tf_op jit(solution)/shard_map/psum | solution.py:512
  780.2 5.9 add_convert_fusion.1
  789.9 5.9 collective-permute-done.65
  797.5 6.8 add_convert_fusion.2
  806.7 10.4 add_convert_fusion
  822.4 12.4 %collective-permute-done.56 = bf16[96,3072]{1,0:T(8,128)(2,1)S(1)} collective-permute-done((bf16[96,3072]{1,0:T(8,128)(2,1)S(1)}, bf16[96,3072]{1,0:T(8,128)(2,1)S(1)}, u32[]{:S(2)}, u32[]{:S(2)}) %collective-permute-start.56) | collective-permute-done | bytes 589856 | tf_op jit(solution)/shard_map/ppermute | solution.py:242
  840.8 3.5 collective-permute-done.12
  846.9 22.7 %collective-permute-done.57 = bf16[96,6144]{1,0:T(8,128)(2,1)S(1)} collective-permute-done((bf16[96,6144]{1,0:T(8,128)(2,1)S(1)}, bf16[96,6144]{1,0:T(8,128)(2,1)S(1)}, u32[]{:S(2)}, u32[]{:S(2)}) %collective-permute-start.57) | collective-permute-done | bytes 1179680 | tf_op jit(solution)/shard_map/ppermute | solution.py:253
  871.1 11.1 %collective-permute-done.67 = bf16[96,3072]{1,0:T(8,128)(2,1)S(1)} collective-permute-done((bf16[96,3072]{1,0:T(8,128)(2,1)S(1)}, bf16[96,3072]{1,0:T(8,128)(2,1)S(1)}, u32[]{:S(2)}, u32[]{:S(2)}) %collective-permute-start.67) | collective-permute-done | bytes 589856 | tf_op jit(solution)/shard_map/ppermute | solution.py:253
  887.5 4.3 collective-permute-done.13
  893.5 17.1 %collective-permute-done.60 = bf16[96,3072]{1,0:T(8,128)(2,1)S(1)} collective-permute-done((bf16[96,3072]{1,0:T(8,128)(2,1)S(1)}, bf16[96,3072]{1,0:T(8,128)(2,1)S(1)}, u32[]{:S(2)}, u32[]{:S(2)}) %collective-permute-start.60) | collective-permute-done | bytes 589856 | tf_op jit(solution)/shard_map/ppermute | solution.py:243
  910.6 6.5 collective-permute-done.58
  923.1 23.5 %collective-permute-done.61 = bf16[96,6144]{1,0:T(8,128)(2,1)S(1)} collective-permute-done((bf16[96,6144]{1,0:T(8,128)(2,1)S(1)}, bf16[96,6144]{1,0:T(8,128)(2,1)S(1)}, u32[]{:S(2)}, u32[]{:S(2)}) %collective-permute-start.61) | collective-permute-done | bytes 1179680 | tf_op jit(solution)/shard_map/ppermute | solution.py:254
  948.4 10.8 %collective-permute-done.71 = bf16[96,3072]{1,0:T(8,128)(2,1)S(1)} collective-permute-done((bf16[96,3072]{1,0:T(8,128)(2,1)S(1)}, bf16[96,3072]{1,0:T(8,128)(2,1)S(1)}, u32[]{:S(2)}, u32[]{:S(2)}) %collective-permute-start.71) | collective-permute-done | bytes 589856 | tf_op jit(solution)/shard_map/ppermute | solution.py:254
  962.5 6.2 collective-permute-done.17
  970.4 23.6 %collective-permute-done.62 = bf16[96,6144]{1,0:T(8,128)(2,1)S(1)} collective-permute-done((bf16[96,6144]{1,0:T(8,128)(2,1)S(1)}, bf16[96,6144]{1,0:T(8,128)(2,1)S(1)}, u32[]{:S(2)}, u32[]{:S(2)}) %collective-permute-start.62) | collective-permute-done | bytes 1179680 | tf_op jit(solution)/shard_map/ppermute | solution.py:254
  996.4 10.3 collective-permute-done.72
  1008.9 7.2 collective-permute-done.18
  1017.2 18.2 %collective-permute-done.63 = bf16[96,6144]{1,0:T(8,128)(2,1)S(1)} collective-permute-done((bf16[96,6144]{1,0:T(8,128)(2,1)S(1)}, bf16[96,6144]{1,0:T(8,128)(2,1)S(1)}, u32[]{:S(2)}, u32[]{:S(2)}) %collective-permute-start.63) | collective-permute-done | bytes 1179680 | tf_op jit(solution)/shard_map/ppermute | solution.py:254
  (645 shorter events, 335.5 us)
Async XLA Ops:
  7.2 104.5 %all-gather.3.cloned.1.call-start = ((), (), s32[]{:S(2)}) async-start(), calls=%async_computation | async-start | bytes 17965056 | tf_op jit(solution)/shard_map/all_gather | solution.py:292
  19.2 250.3 %all-gather.5.cloned.1.call-start = ((), (), s32[]{:S(2)}) async-start(), calls=%async_computation.1 | async-start | bytes 30081024 | tf_op jit(solution)/shard_map/all_gather | solution.py:292
  22.3 751.9 %all-reduce.23.cloned.1.call-start = ((), (), s32[]{:S(2)}) async-start(), calls=%async_computation.2 | async-start | bytes 245760 | tf_op jit(solution)/shard_map/psum | solution.py:512
  133.5 15.0 %collective-permute-start.1 = (bf16[2,256,768]{2,1,0:T(8,128)(2,1)}, bf16[2,256,768]{2,1,0:T(8,128)(2,1)}, u32[]{:S(2)}, u32[]{:S(2)}) collective-permute-start(bf16[2,256,768]{2,1,0:T(8,128)(2,1)} %get-tuple-element.213), channel_id=1, source_target_pairs={{2,0},{4,2},{6,4},{8,6},{10,8},{12,10},{14,12},{16,14},{18,16},{20... | collective-permute-start | bytes 2359304 | tf_op jit(solution)/shard_map/ppermute | solution.py:25
  134.8 13.7 %collective-permute-start = (bf16[2,256,768]{2,1,0:T(8,128)(2,1)}, bf16[2,256,768]{2,1,0:T(8,128)(2,1)}, u32[]{:S(2)}, u32[]{:S(2)}) collective-permute-start(bf16[2,256,768]{2,1,0:T(8,128)(2,1)} %get-tuple-element.212), channel_id=1, source_target_pairs={{0,2},{2,4},{4,6},{6,8},{8,10},{10,12},{12,14},{14,16},{16,18},{18... | collective-permute-start | bytes 2359304 | tf_op jit(solution)/shard_map/ppermute | solution.py:22
  177.6 16.5 %collective-permute-start.2 = (bf16[384,1536]{1,0:T(8,128)(2,1)}, bf16[384,1536]{1,0:T(8,128)(2,1)}, u32[]{:S(2)}, u32[]{:S(2)}) collective-permute-start(bf16[384,1536]{1,0:T(8,128)(2,1)} %convolution_convert_fusion.6), channel_id=1, source_target_pairs={{0,1},{1,0},{2,3},{3,2},{4,5},{5,4},{6,7},{7,6},{8,9},{9,8},{10,11... | collective-permute-start | bytes 3538952 | tf_op jit(solution)/shard_map/ppermute | solution.py:287
  213.8 27.1 %collective-permute-start.3 = (bf16[384,1536]{1,0:T(8,128)(2,1)}, bf16[384,1536]{1,0:T(8,128)(2,1)}, u32[]{:S(2)}, u32[]{:S(2)}) collective-permute-start(bf16[384,1536]{1,0:T(8,128)(2,1)} %convolution_convert_fusion.5), channel_id=1, source_target_pairs={{0,1},{1,0},{2,3},{3,2},{4,5},{5,4},{6,7},{7,6},{8,9},{9,8},{10,11... | collective-permute-start | bytes 3538952 | tf_op jit(solution)/shard_map/ppermute | solution.py:287
  307.1 31.8 %collective-permute-start.5 = (bf16[384,1536]{1,0:T(8,128)(2,1)}, bf16[384,1536]{1,0:T(8,128)(2,1)}, u32[]{:S(2)}, u32[]{:S(2)}) collective-permute-start(bf16[384,1536]{1,0:T(8,128)(2,1)} %fusion.30), channel_id=1, source_target_pairs={{0,1},{1,0},{2,3},{3,2},{4,5},{5,4},{6,7},{7,6},{8,9},{9,8},{10,11... | collective-permute-start | bytes 3538952 | tf_op jit(solution)/shard_map/ppermute | solution.py:287
  318.1 39.9 %collective-permute-start.4 = (bf16[384,1536]{1,0:T(8,128)(2,1)}, bf16[384,1536]{1,0:T(8,128)(2,1)}, u32[]{:S(2)}, u32[]{:S(2)}) collective-permute-start(bf16[384,1536]{1,0:T(8,128)(2,1)} %fusion.27), channel_id=1, source_target_pairs={{0,1},{1,0},{2,3},{3,2},{4,5},{5,4},{6,7},{7,6},{8,9},{9,8},{10,11... | collective-permute-start | bytes 3538952 | tf_op jit(solution)/shard_map/ppermute | solution.py:287
  330.0 476.7 %collective-permute-start.55 = (bf16[768,6144]{1,0:T(8,128)(2,1)}, bf16[768,6144]{1,0:T(8,128)(2,1)}, u32[]{:S(2)}, u32[]{:S(2)}) collective-permute-start(bf16[768,6144]{1,0:T(8,128)(2,1)} %convolution_convert_fusion), channel_id=1, source_target_pairs={{0,2},{2,0},{4,6},{6,4},{8,10},{10,8},{12,14},{14,12},{16,18},{18,... | collective-permute-start | bytes 28311560 | tf_op jit(solution)/shard_map/ppermute | solution.py:234
  338.7 441.5 %collective-permute-start.64 = (bf16[768,3072]{1,0:T(8,128)(2,1)}, bf16[768,3072]{1,0:T(8,128)(2,1)}, u32[]{:S(2)}, u32[]{:S(2)}) collective-permute-start(bf16[768,3072]{1,0:T(8,128)(2,1)} %convolution_convert_fusion.1), channel_id=1, source_target_pairs={{0,2},{2,0},{4,6},{6,4},{8,10},{10,8},{12,14},{14,12},{16,18},{18,... | collective-permute-start | bytes 14155784 | tf_op jit(solution)/shard_map/ppermute | solution.py:234
  379.1 27.6 %collective-permute-start.6 = (bf16[384,1536]{1,0:T(8,128)(2,1)}, bf16[384,1536]{1,0:T(8,128)(2,1)}, u32[]{:S(2)}, u32[]{:S(2)}) collective-permute-start(bf16[384,1536]{1,0:T(8,128)(2,1)} %convolution_convert_fusion.4), channel_id=1, source_target_pairs={{0,1},{1,0},{2,3},{3,2},{4,5},{5,4},{6,7},{7,6},{8,9},{9,8},{10,11... | collective-permute-start | bytes 3538952 | tf_op jit(solution)/shard_map/ppermute | solution.py:287
  384.6 83.2 %collective-permute-start.28 = (bf16[768,768]{1,0:T(8,128)(2,1)}, bf16[768,768]{1,0:T(8,128)(2,1)}, u32[]{:S(2)}, u32[]{:S(2)}) collective-permute-start(bf16[768,768]{1,0:T(8,128)(2,1)} %convolution_convert_fusion.8), channel_id=1, source_target_pairs={{0,2},{2,0},{4,6},{6,4},{8,10},{10,8},{12,14},{14,12},{16,18},{18,... | collective-permute-start | bytes 3538952 | tf_op jit(solution)/shard_map/ppermute | solution.py:234
  389.4 82.9 %collective-permute-start.37 = (bf16[384,1536]{1,0:T(8,128)(2,1)}, bf16[384,1536]{1,0:T(8,128)(2,1)}, u32[]{:S(2)}, u32[]{:S(2)}) collective-permute-start(bf16[384,1536]{1,0:T(8,128)(2,1)} %convolution_convert_fusion.3), channel_id=1, source_target_pairs={{0,2},{2,0},{4,6},{6,4},{8,10},{10,8},{12,14},{14,12},{16,18},{18,... | collective-permute-start | bytes 3538952 | tf_op jit(solution)/shard_map/ppermute | solution.py:234
  406.6 72.8 %collective-permute-start.46 = (bf16[768,768]{1,0:T(8,128)(2,1)}, bf16[768,768]{1,0:T(8,128)(2,1)}, u32[]{:S(2)}, u32[]{:S(2)}) collective-permute-start(bf16[768,768]{1,0:T(8,128)(2,1)} %convolution_convert_fusion.7), channel_id=1, source_target_pairs={{0,2},{2,0},{4,6},{6,4},{8,10},{10,8},{12,14},{14,12},{16,18},{18,... | collective-permute-start | bytes 3538952 | tf_op jit(solution)/shard_map/ppermute | solution.py:234
  467.7 110.8 %collective-permute-start.8 = (bf16[2,256,768]{1,2,0:T(8,128)(2,1)}, bf16[2,256,768]{1,2,0:T(8,128)(2,1)}, u32[]{:S(2)}, u32[]{:S(2)}) collective-permute-start(bf16[2,256,768]{1,2,0:T(8,128)(2,1)} %get-tuple-element.79), channel_id=1, source_target_pairs={{2,0},{4,2},{6,4},{8,6},{10,8},{12,10},{14,12},{16,14},{18,16},{20... | collective-permute-start | bytes 2359304 | tf_op jit(solution)/shard_map/ppermute | solution.py:33
  472.3 19.6 %collective-permute-start.29 = (bf16[96,384]{1,0:T(8,128)(2,1)}, bf16[96,384]{1,0:T(8,128)(2,1)}, u32[]{:S(2)}, u32[]{:S(2)}) collective-permute-start(bf16[96,384]{1,0:T(8,128)(2,1)} %get-tuple-element.173), channel_id=1, source_target_pairs={{0,8},{2,10},{8,16},{10,18},{16,24},{18,26},{24,28},{26,30},{28,20... | collective-permute-start | bytes 221192 | tf_op jit(solution)/shard_map/ppermute | solution.py:242
  479.4 9.6 collective-permute-start.38
  489.0 35.8 %collective-permute-start.42 = (bf16[48,768]{1,0:T(8,128)(2,1)}, bf16[48,768]{1,0:T(8,128)(2,1)S(1)}, u32[]{:S(2)}, u32[]{:S(2)}) collective-permute-start(bf16[48,768]{1,0:T(8,128)(2,1)} %get-tuple-element.170), channel_id=1, source_target_pairs={{0,4},{2,6},{8,0},{10,2},{16,8},{18,10},{24,16},{26,18},{28,24},{3... | collective-permute-start | bytes 221192 | tf_op jit(solution)/shard_map/ppermute | solution.py:243
  491.9 12.8 %collective-permute-start.47 = (bf16[96,384]{1,0:T(8,128)(2,1)}, bf16[96,384]{1,0:T(8,128)(2,1)S(1)}, u32[]{:S(2)}, u32[]{:S(2)}) collective-permute-start(bf16[96,384]{1,0:T(8,128)(2,1)} %get-tuple-element.149), channel_id=1, source_target_pairs={{0,8},{2,10},{8,16},{10,18},{16,24},{18,26},{24,28},{26,30},{28,20... | collective-permute-start | bytes 221192 | tf_op jit(solution)/shard_map/ppermute | solution.py:242
  509.8 5.8 collective-permute-start.30
  515.6 6.6 collective-permute-start.48
  522.3 5.7 collective-permute-start.40
  524.8 5.8 collective-permute-start.33
  535.7 43.1 %collective-permute-start.7 = (bf16[2,256,768]{1,2,0:T(8,128)(2,1)S(1)}, bf16[2,256,768]{1,2,0:T(8,128)(2,1)S(1)}, u32[]{:S(2)}, u32[]{:S(2)}) collective-permute-start(bf16[2,256,768]{1,2,0:T(8,128)(2,1)S(1)} %copy-done.80), channel_id=1, source_target_pairs={{0,2},{2,4},{4,6},{6,8},{8,10},{10,12},{12,14},{14,16},{16,18},{18... | collective-permute-start | bytes 2359304 | tf_op jit(solution)/shard_map/ppermute | solution.py:33
  543.7 6.1 collective-permute-start.34
  549.8 5.9 collective-permute-start.52
  555.7 11.1 %collective-permute-start.35 = (bf16[96,768]{1,0:T(8,128)(2,1)S(1)}, bf16[96,768]{1,0:T(8,128)(2,1)S(1)}, u32[]{:S(2)}, u32[]{:S(2)}) collective-permute-start(bf16[96,768]{1,0:T(8,128)(2,1)S(1)} %add_convert_fusion.40), channel_id=1, source_target_pairs={{0,4},{2,6},{8,0},{10,2},{16,8},{18,10},{24,16},{26,18},{28,24},{3... | collective-permute-start | bytes 442376 | tf_op jit(solution)/shard_map/ppermute | solution.py:254
  566.8 5.9 collective-permute-start.53
  577.9 13.8 %collective-permute-start.19 = (bf16[768,768]{1,0:T(8,128)(2,1)S(1)}, bf16[768,768]{1,0:T(8,128)(2,1)S(1)}, u32[]{:S(2)}, u32[]{:S(2)}) collective-permute-start(bf16[768,768]{1,0:T(8,128)(2,1)S(1)} %copy-done.74), channel_id=1, source_target_pairs={{0,2},{2,0},{4,6},{6,4},{8,10},{10,8},{12,14},{14,12},{16,18},{18,... | collective-permute-start | bytes 3538952 | tf_op jit(solution)/shard_map/ppermute | solution.py:234
  578.6 37.0 %collective-permute-start.32 = (bf16[96,768]{1,0:T(8,128)(2,1)}, bf16[96,768]{1,0:T(8,128)(2,1)}, u32[]{:S(2)}, u32[]{:S(2)}) collective-permute-start(bf16[96,768]{1,0:T(8,128)(2,1)} %get-tuple-element.171), channel_id=1, source_target_pairs={{0,8},{2,10},{8,16},{10,18},{16,24},{18,26},{24,28},{26,30},{28,20... | collective-permute-start | bytes 442376 | tf_op jit(solution)/shard_map/ppermute | solution.py:253
  578.8 25.8 %collective-permute-start.41 = (bf16[48,1536]{1,0:T(8,128)(2,1)}, bf16[48,1536]{1,0:T(8,128)(2,1)}, u32[]{:S(2)}, u32[]{:S(2)}) collective-permute-start(bf16[48,1536]{1,0:T(8,128)(2,1)} %get-tuple-element.167), channel_id=1, source_target_pairs={{0,8},{2,10},{8,16},{10,18},{16,24},{18,26},{24,28},{26,30},{28,20... | collective-permute-start | bytes 442376 | tf_op jit(solution)/shard_map/ppermute | solution.py:253
  593.2 10.3 collective-permute-start.20
  603.5 5.7 collective-permute-start.45
  604.7 21.7 %collective-permute-start.50 = (bf16[96,768]{1,0:T(8,128)(2,1)}, bf16[96,768]{1,0:T(8,128)(2,1)S(1)}, u32[]{:S(2)}, u32[]{:S(2)}) collective-permute-start(bf16[96,768]{1,0:T(8,128)(2,1)} %get-tuple-element.147), channel_id=1, source_target_pairs={{0,8},{2,10},{8,16},{10,18},{16,24},{18,26},{24,28},{26,30},{28,20... | collective-permute-start | bytes 442376 | tf_op jit(solution)/shard_map/ppermute | solution.py:253
  615.6 7.3 collective-permute-start.24
  624.8 23.5 %collective-permute-start.9 = (bf16[384,1536]{1,0:T(8,128)(2,1)S(1)}, bf16[384,1536]{1,0:T(8,128)(2,1)S(1)}, u32[]{:S(2)}, u32[]{:S(2)}) collective-permute-start(bf16[384,1536]{1,0:T(8,128)(2,1)S(1)} %slice.846), channel_id=1, source_target_pairs={{0,1},{1,0},{2,3},{3,2},{4,5},{5,4},{6,7},{7,6},{8,9},{9,8},{10,11... | collective-permute-start | bytes 3538952 | tf_op jit(solution)/shard_map/ppermute | solution.py:287
  626.3 171.1 %collective-permute-start.10 = (bf16[768,2304]{1,0:T(8,128)(2,1)}, bf16[768,2304]{1,0:T(8,128)(2,1)}, u32[]{:S(2)}, u32[]{:S(2)}) collective-permute-start(bf16[768,2304]{1,0:T(8,128)(2,1)} %convolution_convert_fusion.2), channel_id=1, source_target_pairs={{0,2},{2,0},{4,6},{6,4},{8,10},{10,8},{12,14},{14,12},{16,18},{18,... | collective-permute-start | bytes 10616840 | tf_op jit(solution)/shard_map/ppermute | solution.py:234
  638.7 17.0 %collective-permute-start.23 = (bf16[96,768]{1,0:T(8,128)(2,1)}, bf16[96,768]{1,0:T(8,128)(2,1)}, u32[]{:S(2)}, u32[]{:S(2)}) collective-permute-start(bf16[96,768]{1,0:T(8,128)(2,1)} %get-tuple-element.191), channel_id=1, source_target_pairs={{0,8},{2,10},{8,16},{10,18},{16,24},{18,26},{24,28},{26,30},{28,20... | collective-permute-start | bytes 442376 | tf_op jit(solution)/shard_map/ppermute | solution.py:253
  648.3 7.3 collective-permute-start.27
  787.0 8.9 collective-permute-start.65
  789.9 81.2 %collective-permute-start.69 = (bf16[96,1536]{1,0:T(8,128)(2,1)}, bf16[96,1536]{1,0:T(8,128)(2,1)}, u32[]{:S(2)}, u32[]{:S(2)}) collective-permute-start(bf16[96,1536]{1,0:T(8,128)(2,1)} %get-tuple-element.71), channel_id=1, source_target_pairs={{0,4},{2,6},{8,0},{10,2},{16,8},{18,10},{24,16},{26,18},{28,24},{3... | collective-permute-start | bytes 884744 | tf_op jit(solution)/shard_map/ppermute | solution.py:243
  796.8 40.7 %collective-permute-start.66 = (bf16[96,3072]{1,0:T(8,128)(2,1)}, bf16[96,3072]{1,0:T(8,128)(2,1)S(1)}, u32[]{:S(2)}, u32[]{:S(2)}) collective-permute-start(bf16[96,3072]{1,0:T(8,128)(2,1)} %add_convert_fusion.20), channel_id=1, source_target_pairs={{0,8},{2,10},{8,16},{10,18},{16,24},{18,26},{24,28},{26,30},{28,20... | collective-permute-start | bytes 1769480 | tf_op jit(solution)/shard_map/ppermute | solution.py:253
  806.1 13.6 %collective-permute-start.11 = (bf16[96,1152]{1,0:T(8,128)(2,1)}, bf16[96,1152]{1,0:T(8,128)(2,1)}, u32[]{:S(2)}, u32[]{:S(2)}) collective-permute-start(bf16[96,1152]{1,0:T(8,128)(2,1)} %get-tuple-element.76), channel_id=1, source_target_pairs={{0,8},{2,10},{8,16},{10,18},{16,24},{18,26},{24,28},{26,30},{28,20... | collective-permute-start | bytes 663560 | tf_op jit(solution)/shard_map/ppermute | solution.py:242
  818.5 16.3 %collective-permute-start.56 = (bf16[96,3072]{1,0:T(8,128)(2,1)S(1)}, bf16[96,3072]{1,0:T(8,128)(2,1)S(1)}, u32[]{:S(2)}, u32[]{:S(2)}) collective-permute-start(bf16[96,3072]{1,0:T(8,128)(2,1)S(1)} %get-tuple-element.66), channel_id=1, source_target_pairs={{0,8},{2,10},{8,16},{10,18},{16,24},{18,26},{24,28},{26,30},{28,20... | collective-permute-start | bytes 1769480 | tf_op jit(solution)/shard_map/ppermute | solution.py:242
  821.2 23.1 %collective-permute-start.12 = (bf16[96,2304]{1,0:T(8,128)(2,1)S(1)}, bf16[96,2304]{1,0:T(8,128)(2,1)S(1)}, u32[]{:S(2)}, u32[]{:S(2)}) collective-permute-start(bf16[96,2304]{1,0:T(8,128)(2,1)S(1)} %add_convert_fusion.26), channel_id=1, source_target_pairs={{0,8},{2,10},{8,16},{10,18},{16,24},{18,26},{24,28},{26,30},{28,20... | collective-permute-start | bytes 1327112 | tf_op jit(solution)/shard_map/ppermute | solution.py:253
  836.3 33.3 %collective-permute-start.57 = (bf16[96,6144]{1,0:T(8,128)(2,1)S(1)}, bf16[96,6144]{1,0:T(8,128)(2,1)S(1)}, u32[]{:S(2)}, u32[]{:S(2)}) collective-permute-start(bf16[96,6144]{1,0:T(8,128)(2,1)S(1)} %add_convert_fusion.8), channel_id=1, source_target_pairs={{0,8},{2,10},{8,16},{10,18},{16,24},{18,26},{24,28},{26,30},{28,20... | collective-permute-start | bytes 3538952 | tf_op jit(solution)/shard_map/ppermute | solution.py:253
  838.7 43.5 %collective-permute-start.67 = (bf16[96,3072]{1,0:T(8,128)(2,1)S(1)}, bf16[96,3072]{1,0:T(8,128)(2,1)S(1)}, u32[]{:S(2)}, u32[]{:S(2)}) collective-permute-start(bf16[96,3072]{1,0:T(8,128)(2,1)S(1)} %add_convert_fusion.19), channel_id=1, source_target_pairs={{0,8},{2,10},{8,16},{10,18},{16,24},{18,26},{24,28},{26,30},{28,20... | collective-permute-start | bytes 1769480 | tf_op jit(solution)/shard_map/ppermute | solution.py:253
  840.2 45.7 %collective-permute-start.15 = (bf16[96,1152]{1,0:T(8,128)(2,1)S(1)}, bf16[96,1152]{1,0:T(8,128)(2,1)S(1)}, u32[]{:S(2)}, u32[]{:S(2)}) collective-permute-start(bf16[96,1152]{1,0:T(8,128)(2,1)S(1)} %get-tuple-element.77), channel_id=1, source_target_pairs={{0,4},{2,6},{8,0},{10,2},{16,8},{18,10},{24,16},{26,18},{28,24},{3... | collective-permute-start | bytes 663560 | tf_op jit(solution)/shard_map/ppermute | solution.py:243
  845.5 46.3 %collective-permute-start.13 = (bf16[96,2304]{1,0:T(8,128)(2,1)S(1)}, bf16[96,2304]{1,0:T(8,128)(2,1)S(1)}, u32[]{:S(2)}, u32[]{:S(2)}) collective-permute-start(bf16[96,2304]{1,0:T(8,128)(2,1)S(1)} %add_convert_fusion.25), channel_id=1, source_target_pairs={{0,8},{2,10},{8,16},{10,18},{16,24},{18,26},{24,28},{26,30},{28,20... | collective-permute-start | bytes 1327112 | tf_op jit(solution)/shard_map/ppermute | solution.py:253
  869.9 47.1 %collective-permute-start.58 = (bf16[96,6144]{1,0:T(8,128)(2,1)S(1)}, bf16[96,6144]{1,0:T(8,128)(2,1)S(1)}, u32[]{:S(2)}, u32[]{:S(2)}) collective-permute-start(bf16[96,6144]{1,0:T(8,128)(2,1)S(1)} %add_convert_fusion.7), channel_id=1, source_target_pairs={{0,8},{2,10},{8,16},{10,18},{16,24},{18,26},{24,28},{26,30},{28,20... | collective-permute-start | bytes 3538952 | tf_op jit(solution)/shard_map/ppermute | solution.py:253
  883.9 35.3 %collective-permute-start.70 = (bf16[96,3072]{1,0:T(8,128)(2,1)S(1)}, bf16[96,3072]{1,0:T(8,128)(2,1)S(1)}, u32[]{:S(2)}, u32[]{:S(2)}) collective-permute-start(bf16[96,3072]{1,0:T(8,128)(2,1)S(1)} %get-tuple-element.69), channel_id=1, source_target_pairs={{0,4},{2,6},{8,0},{10,2},{16,8},{18,10},{24,16},{26,18},{28,24},{3... | collective-permute-start | bytes 1769480 | tf_op jit(solution)/shard_map/ppermute | solution.py:254
  885.4 110.0 %collective-permute-start.68 = (bf16[96,3072]{1,0:T(8,128)(2,1)S(1)}, bf16[96,3072]{1,0:T(8,128)(2,1)S(1)}, u32[]{:S(2)}, u32[]{:S(2)}) collective-permute-start(bf16[96,3072]{1,0:T(8,128)(2,1)S(1)} %get-tuple-element.68), channel_id=1, source_target_pairs={{0,8},{2,10},{8,16},{10,18},{16,24},{18,26},{24,28},{26,30},{28,20... | collective-permute-start | bytes 1769480 | tf_op jit(solution)/shard_map/ppermute | solution.py:253
  885.9 24.6 %collective-permute-start.60 = (bf16[96,3072]{1,0:T(8,128)(2,1)S(1)}, bf16[96,3072]{1,0:T(8,128)(2,1)S(1)}, u32[]{:S(2)}, u32[]{:S(2)}) collective-permute-start(bf16[96,3072]{1,0:T(8,128)(2,1)S(1)} %get-tuple-element.67), channel_id=1, source_target_pairs={{0,4},{2,6},{8,0},{10,2},{16,8},{18,10},{24,16},{26,18},{28,24},{3... | collective-permute-start | bytes 1769480 | tf_op jit(solution)/shard_map/ppermute | solution.py:243
  891.9 29.9 %collective-permute-start.16 = (bf16[96,2304]{1,0:T(8,128)(2,1)S(1)}, bf16[96,2304]{1,0:T(8,128)(2,1)S(1)}, u32[]{:S(2)}, u32[]{:S(2)}) collective-permute-start(bf16[96,2304]{1,0:T(8,128)(2,1)S(1)} %get-tuple-element.75), channel_id=1, source_target_pairs={{0,4},{2,6},{8,0},{10,2},{16,8},{18,10},{24,16},{26,18},{28,24},{3... | collective-permute-start | bytes 1327112 | tf_op jit(solution)/shard_map/ppermute | solution.py:254
  917.6 29.0 %collective-permute-start.61 = (bf16[96,6144]{1,0:T(8,128)(2,1)S(1)}, bf16[96,6144]{1,0:T(8,128)(2,1)S(1)}, u32[]{:S(2)}, u32[]{:S(2)}) collective-permute-start(bf16[96,6144]{1,0:T(8,128)(2,1)S(1)} %get-tuple-element.65), channel_id=1, source_target_pairs={{0,4},{2,6},{8,0},{10,2},{16,8},{18,10},{24,16},{26,18},{28,24},{3... | collective-permute-start | bytes 3538952 | tf_op jit(solution)/shard_map/ppermute | solution.py:254
  920.4 38.8 %collective-permute-start.71 = (bf16[96,3072]{1,0:T(8,128)(2,1)S(1)}, bf16[96,3072]{1,0:T(8,128)(2,1)S(1)}, u32[]{:S(2)}, u32[]{:S(2)}) collective-permute-start(bf16[96,3072]{1,0:T(8,128)(2,1)S(1)} %add_convert_fusion.16), channel_id=1, source_target_pairs={{0,4},{2,6},{8,0},{10,2},{16,8},{18,10},{24,16},{26,18},{28,24},{3... | collective-permute-start | bytes 1769480 | tf_op jit(solution)/shard_map/ppermute | solution.py:254
  921.9 46.8 %collective-permute-start.17 = (bf16[96,2304]{1,0:T(8,128)(2,1)S(1)}, bf16[96,2304]{1,0:T(8,128)(2,1)S(1)}, u32[]{:S(2)}, u32[]{:S(2)}) collective-permute-start(bf16[96,2304]{1,0:T(8,128)(2,1)S(1)} %add_convert_fusion.22), channel_id=1, source_target_pairs={{0,4},{2,6},{8,0},{10,2},{16,8},{18,10},{24,16},{26,18},{28,24},{3... | collective-permute-start | bytes 1327112 | tf_op jit(solution)/shard_map/ppermute | solution.py:254
  946.9 47.1 %collective-permute-start.62 = (bf16[96,6144]{1,0:T(8,128)(2,1)S(1)}, bf16[96,6144]{1,0:T(8,128)(2,1)S(1)}, u32[]{:S(2)}, u32[]{:S(2)}) collective-permute-start(bf16[96,6144]{1,0:T(8,128)(2,1)S(1)} %add_convert_fusion.4), channel_id=1, source_target_pairs={{0,4},{2,6},{8,0},{10,2},{16,8},{18,10},{24,16},{26,18},{28,24},{3... | collective-permute-start | bytes 3538952 | tf_op jit(solution)/shard_map/ppermute | solution.py:254
  960.4 46.2 %collective-permute-start.72 = (bf16[96,3072]{1,0:T(8,128)(2,1)S(1)}, bf16[96,3072]{1,0:T(8,128)(2,1)S(1)}, u32[]{:S(2)}, u32[]{:S(2)}) collective-permute-start(bf16[96,3072]{1,0:T(8,128)(2,1)S(1)} %add_convert_fusion.15), channel_id=1, source_target_pairs={{0,4},{2,6},{8,0},{10,2},{16,8},{18,10},{24,16},{26,18},{28,24},{3... | collective-permute-start | bytes 1769480 | tf_op jit(solution)/shard_map/ppermute | solution.py:254
  962.0 46.9 %collective-permute-start.14 = (bf16[96,2304]{1,0:T(8,128)(2,1)S(1)}, bf16[96,2304]{1,0:T(8,128)(2,1)S(1)}, u32[]{:S(2)}, u32[]{:S(2)}) collective-permute-start(bf16[96,2304]{1,0:T(8,128)(2,1)S(1)} %get-tuple-element.74), channel_id=1, source_target_pairs={{0,8},{2,10},{8,16},{10,18},{16,24},{18,26},{24,28},{26,30},{28,20... | collective-permute-start | bytes 1327112 | tf_op jit(solution)/shard_map/ppermute | solution.py:253
  968.8 47.3 %collective-permute-start.18 = (bf16[96,2304]{1,0:T(8,128)(2,1)S(1)}, bf16[96,2304]{1,0:T(8,128)(2,1)S(1)}, u32[]{:S(2)}, u32[]{:S(2)}) collective-permute-start(bf16[96,2304]{1,0:T(8,128)(2,1)S(1)} %add_convert_fusion.21), channel_id=1, source_target_pairs={{0,4},{2,6},{8,0},{10,2},{16,8},{18,10},{24,16},{26,18},{28,24},{3... | collective-permute-start | bytes 1327112 | tf_op jit(solution)/shard_map/ppermute | solution.py:254
  994.0 23.2 %collective-permute-start.59 = (bf16[96,6144]{1,0:T(8,128)(2,1)S(1)}, bf16[96,6144]{1,0:T(8,128)(2,1)S(1)}, u32[]{:S(2)}, u32[]{:S(2)}) collective-permute-start(bf16[96,6144]{1,0:T(8,128)(2,1)S(1)} %get-tuple-element.64), channel_id=1, source_target_pairs={{0,8},{2,10},{8,16},{10,18},{16,24},{18,26},{24,28},{26,30},{28,20... | collective-permute-start | bytes 3538952 | tf_op jit(solution)/shard_map/ppermute | solution.py:253
  995.4 39.9 %collective-permute-start.63 = (bf16[96,6144]{1,0:T(8,128)(2,1)S(1)}, bf16[96,6144]{1,0:T(8,128)(2,1)S(1)}, u32[]{:S(2)}, u32[]{:S(2)}) collective-permute-start(bf16[96,6144]{1,0:T(8,128)(2,1)S(1)} %add_convert_fusion.3), channel_id=1, source_target_pairs={{0,4},{2,6},{8,0},{10,2},{16,8},{18,10},{24,16},{26,18},{28,24},{3... | collective-permute-start | bytes 3538952 | tf_op jit(solution)/shard_map/ppermute | solution.py:254
  (159 other events, 1996.9 us)
Sparse Core Ops, SparseCore 0:
  19.3 92.3 all-gather.2
  113.4 156.0 all-gather.4
  651.3 122.9 all-reduce.22

commit v2 on v1

--- a/solution.py
+++ b/solution.py
@@ -1,8 +1,11 @@
+import functools
 from functools import reduce
 
 import jax
 import jax.numpy as jnp
 from jax import lax
+from jax.experimental import pallas as pl
+from jax.experimental.pallas import tpu as pltpu
 from jax.sharding import PartitionSpec as P
 
 HD = 64
@@ -192,7 +195,9 @@
 
 
 LANES = 128
-RING_LIMIT = 16
+BLOCK = 256
+VMEM_BYTES = 60 * 1024 * 1024
+MESH = pl.DeviceIdType.MESH
 
 
 def ring_place(chip, chips):
@@ -215,71 +220,263 @@
     ]
 
 
-def owner_order(matrix, seq_index, seq_count):
+def owner_matrix(width, seq_index, seq_count):
     chips = seq_count // 2
-    width = matrix.shape[-1] // seq_count
+    seg = width // seq_count
     core = seq_index % 2
     place = ring_place(seq_index // 2, chips)
-    blocks = []
-    for which in (core, 1 - core):
-        for near in range(chips):
-            chip = ring_chip((place + near) % chips, chips)
-            blocks.append(
-                lax.dynamic_slice_in_dim(matrix, (2 * chip + which) * width, width, axis=-1)
-            )
-    return jnp.concatenate(blocks, axis=-1)
+    row = jnp.arange(width, dtype=jnp.int32)
+    which = row // (width // 2)
+    near = row % (width // 2) // seg
+    chip = ring_chip((place + near) % chips, chips)
+    source = (2 * chip + jnp.where(which == 0, core, 1 - core)) * seg + row % seg
+    return (source[:, None] == row[None, :]).astype(jnp.bfloat16)
 
 
 def over_core(values, seq_count):
     return lax.ppermute(values, "seq", [(index, index ^ 1) for index in range(seq_count)])
 
 
-def ring_sum(chunks, seq_count):
-    chips = seq_count // 2
-    far = chips // 2
-    half = chunks[0].shape[-1] // 2
-    ahead, behind = ring_pairs(chips, 1), ring_pairs(chips, -1)
-    onward = lax.ppermute(chunks[far][..., :half], "seq", ahead)
-    backward = lax.ppermute(chunks[far][..., half:], "seq", behind)
-
-    def joined(term, arrived, low_side):
-        term, arrived = term.astype(jnp.float32), arrived.astype(jnp.float32)
+class Ring:
+    def __init__(self, term, seq_count):
+        self.term = term
+        self.chips = seq_count // 2
+        self.far = self.chips // 2
+        self.near = self.far
+        self.ahead, self.behind = ring_pairs(self.chips, 1), ring_pairs(self.chips, -1)
+        first = term(self.far)
+        self.half = first.shape[-1] // 2
+        self.send(first[..., : self.half], first[..., self.half :])
+
+    def send(self, onward, backward):
+        self.onward = lax.ppermute(onward.astype(jnp.bfloat16), "seq", self.ahead)
+        self.backward = lax.ppermute(backward.astype(jnp.bfloat16), "seq", self.behind)
+
+    def joined(self, near, arrived, low_side):
+        term = self.term(near).astype(jnp.float32)
+        arrived = arrived.astype(jnp.float32)
         if arrived.shape != term.shape:
-            pads = (0, half) if low_side else (half, 0)
+            pads = (0, self.half) if low_side else (self.half, 0)
             arrived = jnp.pad(arrived, ((0, 0),) * (term.ndim - 1) + (pads,))
-        return (term + arrived).astype(jnp.bfloat16)
-
-    for near in range(1, far):
-        onward = lax.ppermute(joined(chunks[far - near], onward, True), "seq", ahead)
-        backward = lax.ppermute(joined(chunks[far + near], backward, False), "seq", behind)
-    total = chunks[0].astype(jnp.float32)
-    return total + onward.astype(jnp.float32) + backward.astype(jnp.float32)
-
-
-def owned_sum(rows, columns, seq_count):
-    chips = seq_count // 2
-    if chips > RING_LIMIT:
-        return None
-    half = rows.shape[-1] // 2
-    away = product_tn(rows[:, half:], columns).astype(jnp.bfloat16)
+        return term + arrived
+
+    def step(self):
+        if self.near == 1:
+            return
+        self.near -= 1
+        self.send(
+            self.joined(self.near, self.onward, True),
+            self.joined(2 * self.far - self.near, self.backward, False),
+        )
+
+    def after(self, value):
+        value, self.onward, self.backward = lax.optimization_barrier(
+            (value, self.onward, self.backward)
+        )
+        return value
+
+    def finish(self):
+        while self.near > 1:
+            self.step()
+        return (
+            self.term(0).astype(jnp.float32)
+            + self.onward.astype(jnp.float32)
+            + self.backward.astype(jnp.float32)
+        )
+
+
+def core_sum(rows_t, columns, seq_count):
+    half = rows_t.shape[0] // 2
+    away = product(rows_t[half:], columns).astype(jnp.bfloat16)
     arrived = over_core(away, seq_count)
-    mine = (product_tn(rows[:, :half], columns) + arrived.astype(jnp.float32)).astype(jnp.bfloat16)
-    width = half // chips
-    return ring_sum(
-        [mine[near * width : (near + 1) * width] for near in range(chips)], seq_count
-    )
-
-
-def weight_grad(rows, columns, seq_index, seq_count):
-    if seq_count // 2 > RING_LIMIT:
-        return lax.psum_scatter(
-            product_tn(rows, columns).astype(jnp.bfloat16), "seq", scatter_dimension=0, tiled=True
-        ).astype(jnp.float32)
-    return owned_sum(owner_order(rows, seq_index, seq_count), columns, seq_count)
+    return (product(rows_t[:half], columns) + arrived.astype(jnp.float32)).astype(jnp.bfloat16)
+
+
+def block_of(matrix, near, chips):
+    width = matrix.shape[0] // chips
+    return matrix[near * width : (near + 1) * width]
+
+
+def side_by_side(matrices, chips):
+    return lambda near: jnp.concatenate([block_of(each, near, chips) for each in matrices], axis=-1)
+
+
+def all_sum(values, axes):
+    for axis in axes:
+        count = lax.axis_size(axis)
+        bit = 1
+        while bit < count:
+            values = values + lax.ppermute(
+                values, axis, [(index, index ^ bit) for index in range(count)]
+            )
+            bit *= 2
+    return values
+
+
+def glu_kernel(
+    blocks,
+    normed,
+    normed_t,
+    top,
+    top_t,
+    w_gate,
+    w_up,
+    w_down,
+    b_gate,
+    b_up,
+    out,
+    grad_normed,
+    sums,
+    bias_grads,
+    out_acc,
+    grad_acc,
+    mine,
+    away,
+    arrived,
+    send_sem,
+    recv_sem,
+):
+    index = pl.program_id(0)
+    seq_index = lax.axis_index("seq")
+    partner = seq_index + 1 - 2 * (seq_index % 2)
+    half = normed_t.shape[0] // 2
+
+    def crossing(block):
+        return pltpu.make_async_remote_copy(
+            src_ref=away.at[block % 2],
+            dst_ref=arrived.at[block],
+            send_sem=send_sem.at[block % 2],
+            recv_sem=recv_sem.at[block],
+            device_id={"seq": partner},
+            device_id_type=MESH,
+        )
+
+    @pl.when(index == 0)
+    def _():
+        barrier = pltpu.get_barrier_semaphore()
+        pl.semaphore_signal(barrier, inc=1, device_id={"seq": partner}, device_id_type=MESH)
+        pl.semaphore_wait(barrier, 1)
+        out_acc[...] = jnp.zeros_like(out_acc)
+        grad_acc[...] = jnp.zeros_like(grad_acc)
+
+    @pl.when(index < blocks)
+    def _():
+        gate_pre = product(normed[...], w_gate[...]) + b_gate[...]
+        up_pre = product(normed[...], w_up[...]) + b_up[...]
+        grad_hidden = product(top[...], w_down[...])
+        sigmoid_gate = jax.nn.sigmoid(gate_pre)
+        silu_gate = gate_pre * sigmoid_gate
+        hidden = (silu_gate * up_pre).astype(jnp.bfloat16)
+        grad_up = (grad_hidden * silu_gate).astype(jnp.bfloat16)
+        grad_gate = (
+            grad_hidden * up_pre * sigmoid_gate * (1.0 + gate_pre * (1.0 - sigmoid_gate))
+        ).astype(jnp.bfloat16)
+        bias_grads[0:1, :] = jnp.sum(grad_gate.astype(jnp.float32), axis=0, keepdims=True)
+        bias_grads[1:2, :] = jnp.sum(grad_up.astype(jnp.float32), axis=0, keepdims=True)
+        out_acc[...] += product_t(hidden, w_down[...])
+        grad_acc[...] += product_t(grad_gate, w_gate[...]) + product_t(grad_up, w_up[...])
+
+        @pl.when(index >= 2)
+        def _():
+            crossing(index - 2).wait_send()
+
+        slot = index % 2
+        away[slot, 0] = product(normed_t[half:, :], grad_gate).astype(jnp.bfloat16)
+        away[slot, 1] = product(normed_t[half:, :], grad_up).astype(jnp.bfloat16)
+        away[slot, 2] = product(top_t[half:, :], hidden).astype(jnp.bfloat16)
+        crossing(index).start()
+        mine[slot, 0] = product(normed_t[:half, :], grad_gate)
+        mine[slot, 1] = product(normed_t[:half, :], grad_up)
+        mine[slot, 2] = product(top_t[:half, :], hidden)
+
+    @pl.when(index >= 1)
+    def _():
+        crossing(index - 1).wait_recv()
+        prior = index - 1
+        sums[...] = (mine[prior % 2] + arrived[prior].astype(jnp.float32)).astype(jnp.bfloat16)
+
+    @pl.when(index == blocks)
+    def _():
+        crossing(blocks - 2).wait_send()
+        crossing(blocks - 1).wait_send()
+        out[...] = out_acc[...].astype(jnp.bfloat16)
+        grad_normed[...] = grad_acc[...].astype(jnp.bfloat16)
+
+
+def glu_layer(normed, normed_t, top, top_t, weights, gate_bias, up_bias):
+    rows, width = normed.shape
+    hidden_width = gate_bias.shape[0]
+    blocks = hidden_width // BLOCK
+    half = width // 2
+    whole = pl.BlockSpec((rows, width), lambda i: (0, 0))
+    whole_t = pl.BlockSpec((width, rows), lambda i: (0, 0))
+
+    def weight_spec(which):
+        return pl.BlockSpec(
+            (width, BLOCK), lambda i: (0, which * blocks + jnp.minimum(i, blocks - 1))
+        )
+
+    bias_spec = pl.BlockSpec((1, BLOCK), lambda i: (0, jnp.minimum(i, blocks - 1)))
+    work = rows * width * hidden_width
+    return pl.pallas_call(
+        functools.partial(glu_kernel, blocks),
+        grid=(blocks + 1,),
+        in_specs=[
+            whole,
+            whole_t,
+            whole,
+            whole_t,
+            weight_spec(0),
+            weight_spec(1),
+            weight_spec(2),
+            bias_spec,
+            bias_spec,
+        ],
+        out_specs=[
+            whole,
+            whole,
+            pl.BlockSpec((3, half, BLOCK), lambda i: (0, 0, jnp.maximum(i - 1, 0))),
+            pl.BlockSpec((2, BLOCK), lambda i: (0, jnp.minimum(i, blocks - 1))),
+        ],
+        out_shape=[
+            jax.ShapeDtypeStruct((rows, width), jnp.bfloat16),
+            jax.ShapeDtypeStruct((rows, width), jnp.bfloat16),
+            jax.ShapeDtypeStruct((3, half, hidden_width), jnp.bfloat16),
+            jax.ShapeDtypeStruct((2, hidden_width), jnp.float32),
+        ],
+        scratch_shapes=[
+            pltpu.VMEM((rows, width), jnp.float32),
+            pltpu.VMEM((rows, width), jnp.float32),
+            pltpu.VMEM((2, 3, half, BLOCK), jnp.float32),
+            pltpu.VMEM((2, 3, half, BLOCK), jnp.bfloat16),
+            pltpu.VMEM((blocks, 3, half, BLOCK), jnp.bfloat16),
+            pltpu.SemaphoreType.DMA((2,)),
+            pltpu.SemaphoreType.DMA((blocks,)),
+        ],
+        compiler_params=pltpu.CompilerParams(
+            collective_id=1, has_side_effects=True, vmem_limit_bytes=VMEM_BYTES
+        ),
+        cost_estimate=pl.CostEstimate(
+            flops=18 * work, bytes_accessed=12 * width * hidden_width, transcendentals=rows * hidden_width
+        ),
+        name="glu_layer",
+    )(
+        normed,
+        normed_t,
+        top,
+        top_t,
+        weights,
+        weights,
+        weights,
+        gate_bias[None],
+        up_bias[None],
+    )
 
 
 def head_total(partial_sum):
-    low = lax.optimization_barrier(partial_sum.astype(jnp.bfloat16))
+    low = partial_sum
+    if low.dtype != jnp.bfloat16:
+        low = lax.optimization_barrier(partial_sum.astype(jnp.bfloat16))
     count = lax.axis_size("head")
     total = low.astype(jnp.float32)
     for step in range(1, count):
@@ -331,6 +528,11 @@
     ctx_rows = cross_key.shape[0]
     ctx_width = prompt.shape[2]
     head_count = part // HD
+    chips = seq_count // 2
+    order = owner_matrix(width, seq_index, seq_count)
+
+    def ordered(matrix, by=order):
+        return product_t(by, matrix).astype(jnp.bfloat16)
 
     vectors = jnp.stack([norm1_gain, norm2_gain, norm3_gain, down_bias], axis=1)
     vectors = jnp.pad(vectors, ((0, 0), (0, LANES - 4)))
@@ -350,8 +552,6 @@
     c_value = ctx_weights[:, 1].reshape(ctx_width, part)
     rows_of = attn_weights[:, 7 * part : 7 * part + 8].astype(jnp.float32).T
     gain_one_f, gain_two_f, gain_three_f, bias_f = rows_of[0], rows_of[1], rows_of[2], rows_of[3]
-    w_gate_up = glu_weights[:, : 2 * hidden_width]
-    w_down = glu_weights[:, 2 * hidden_width :]
 
     positions = first_row + jnp.arange(local_rows, dtype=jnp.int32)
     cos_table, sin_table = angles(positions)
@@ -412,23 +612,21 @@
     third_out, normal_three, inverse_three = layer_norm_parts(h_two, gain_three_f)
     normed_three = third_out.astype(jnp.bfloat16)
 
-    gate_up = product(normed_three, w_gate_up)
-    gate_pre = gate_up[:, :hidden_width] + gate_bias
-    up_pre = gate_up[:, hidden_width:] + up_bias
-    sigmoid_gate = jax.nn.sigmoid(gate_pre)
-    hidden = (gate_pre * sigmoid_gate * up_pre).astype(jnp.bfloat16)
-    result = (h_two + head_total(product_t(hidden, w_down)) + bias_f).astype(jnp.bfloat16)
+    glu_out, grad_normed_low, glu_sums, bias_local = glu_layer(
+        normed_three,
+        ordered(normed_three),
+        out_grad,
+        ordered(out_grad),
+        glu_weights,
+        gate_bias,
+        up_bias,
+    )
+    grad_normed_three = head_total(grad_normed_low)
+    result = (h_two + head_total(glu_out) + bias_f).astype(jnp.bfloat16)
+    glu_ring = Ring(
+        lambda near: glu_sums[:, near * gain_rows : (near + 1) * gain_rows], seq_count
+    )
     grad_top = out_grad.astype(jnp.float32)
-    grad_hidden = product(out_grad, w_down)
-    grad_up = (grad_hidden * gate_pre * sigmoid_gate).astype(jnp.bfloat16)
-    grad_gate = (
-        grad_hidden * up_pre * sigmoid_gate * (1.0 + gate_pre * (1.0 - sigmoid_gate))
-    ).astype(jnp.bfloat16)
-    grad_gate_up = jnp.concatenate([grad_gate, grad_up], axis=1)
-    bias_local = jnp.sum(grad_gate_up.astype(jnp.float32), axis=0).reshape(2, hidden_width)
-    grad_normed_three = head_total(product_t(grad_gate_up, w_gate_up))
-    down_share = weight_grad(out_grad, hidden, seq_index, seq_count)
-    gate_up_share = weight_grad(normed_three, grad_gate_up, seq_index, seq_count)
     gain_three_term = jnp.sum(grad_normed_three * normal_three, axis=0)
     down_bias_term = jnp.sum(grad_top, axis=0)
 
@@ -436,7 +634,9 @@
     grad_two_low = grad_h_two.astype(jnp.bfloat16)
     grad_cross_h = product(grad_two_low, c_out).astype(jnp.bfloat16)
     grad_cross_h = grad_cross_h.reshape(local_rows, head_count, HD)
-    cross_out_share = weight_grad(grad_two_low, cross_mixed, seq_index, seq_count)
+    cross_out_sum = core_sum(ordered(grad_two_low), cross_mixed, seq_count)
+    grad_cross_h = glu_ring.after(grad_cross_h)
+    glu_ring.step()
     grad_cross_q, ctx_key_grads, ctx_value_grads = attend_backward(
         cross_h, cross_keys, score_scale, cross_logs, grad_cross_h
     )
@@ -445,19 +645,35 @@
         [ctx_key_grads[0].reshape(-1, part), ctx_value_grads[0].reshape(-1, part)], axis=1
     ).astype(jnp.bfloat16)
     grad_normed_two = head_total(product_t(grad_cross_query, c_query))
-    ctx_share = weight_grad(context_rows, ctx_grads, seq_index, seq_count)
-    cross_query_share = weight_grad(normed_two, grad_cross_query, seq_index, seq_count)
+    grad_normed_two = glu_ring.after(grad_normed_two)
+    glu_ring.step()
+    cross_query_sum = core_sum(ordered(normed_two), grad_cross_query, seq_count)
+    ctx_order = owner_matrix(ctx_width, seq_index, seq_count)
+    ctx_sum = core_sum(ordered(context_rows, ctx_order), ctx_grads, seq_count)
     gain_two_term = jnp.sum(grad_normed_two * normal_two, axis=0)
     grad_h_one = grad_h_two + norm_back(grad_normed_two, normal_two, inverse_two, gain_two_f)
     grad_one_low = grad_h_one.astype(jnp.bfloat16)
     grad_attn_h = product(grad_one_low, w_out).astype(jnp.bfloat16)
     grad_attn_h = grad_attn_h.reshape(local_rows, head_count, HD)
-    out_share = weight_grad(grad_one_low, attn_mixed, seq_index, seq_count)
+    out_sum = core_sum(ordered(grad_one_low), attn_mixed, seq_count)
+    joined_sums = side_by_side([cross_out_sum, cross_query_sum, out_sum], chips)
+
+    def cross_term(near):
+        ctx_block = block_of(ctx_sum, near, chips)
+        ctx_block = jnp.concatenate([ctx_block[:, :part], ctx_block[:, part:]], axis=0)
+        return jnp.concatenate([joined_sums(near), ctx_block], axis=1)
+
+    grad_attn_h = glu_ring.after(grad_attn_h)
+    glu_ring.step()
 
     grad_query, grad_keys, grad_values = attend_backward(
         query_h, self_keys, score_scale, self_logs, grad_attn_h
     )
     near_grads = jnp.stack([grad_keys[0], grad_values[0]]).reshape(2, window, part)
+    near_grads = glu_ring.after(near_grads)
+    glu_share = glu_ring.finish()
+    cross_ring = Ring(cross_term, seq_count)
+    cross_share = cross_ring.finish()
     from_above = passed_along(near_grads[:, :HALF].astype(jnp.bfloat16), "seq", -1).astype(
         jnp.float32
     )
@@ -489,8 +705,15 @@
     )
     grad_normed_all = product_t(grad_qkv, w_qkv)
     grad_normed_one = head_total(grad_normed_all[:local_rows])
-    qkv_share = weight_grad(normed_one, grad_qkv, seq_index, seq_count)
-    gain_one_term = jnp.sum(grad_normed_one * normal_one[:local_rows], axis=0)
+    qkv_ring = Ring(
+        side_by_side([core_sum(ordered(normed_one), grad_qkv, seq_count)], chips), seq_count
+    )
+    qkv_share = qkv_ring.finish()
+    cross_out_share = cross_share[:, :part]
+    cross_query_share = cross_share[:, part : 2 * part]
+    out_share = cross_share[:, 2 * part : 3 * part]
+    ctx_share = cross_share[:, 3 * part :]
+    gain_one_term = jnp.sum(grad_normed_all[:local_rows] * normal_one[:local_rows], axis=0)
     frames_grad = (
         grad_h_one
         + norm_back(grad_normed_one, normal_one[:local_rows], inverse_one[:local_rows], gain_one_f)
@@ -499,26 +722,30 @@
     stamp_full = lax.dynamic_update_slice_in_dim(
         jnp.zeros((clip_total, width), jnp.float32), grad_normed_all[local_rows:stamp_end], base_clip, 0
     )
-    bias_full = lax.dynamic_update_slice_in_dim(
-        jnp.zeros((2, hidden_width * lax.axis_size("head")), jnp.float32),
-        bias_local,
-        head_index * hidden_width,
-        1,
-    )
-    share = 1.0 / lax.axis_size("head")
-    gains_full = share * jnp.stack(
-        [gain_one_term, gain_two_term, gain_three_term, down_bias_term]
-    )
-    stamp_sum, bias_sum, gains_sum = lax.psum((stamp_full, bias_full, gains_full), ("seq", "head"))
+    late = all_sum(jnp.concatenate([stamp_full, gain_one_term[None]], axis=0), ("seq", "head"))
+    stamp_sum = late[:clip_total]
+    early = all_sum(
+        jnp.concatenate(
+            [
+                bias_local.reshape(-1, width),
+                jnp.stack([gain_two_term, gain_three_term, down_bias_term]),
+            ],
+            axis=0,
+        ),
+        ("seq",),
+    )
+    own_bias = early[:-3].reshape(2, hidden_width)
     every_out, every_normal, every_inverse = layer_norm_parts(
         time_token.astype(jnp.float32), gain_one_f
     )
     time_grad = norm_back(stamp_sum, every_normal, every_inverse, gain_one_f)
     time_gain = jnp.sum(stamp_sum * every_normal, axis=0)
     gains_own = lax.dynamic_slice_in_dim(
-        gains_sum.at[0].add(time_gain), seq_index * gain_rows, gain_rows, 1
-    )
-    own_bias = lax.dynamic_slice_in_dim(bias_sum, head_index * hidden_width, hidden_width, 1)
+        jnp.concatenate([late[clip_total:] + time_gain[None], early[-3:]], axis=0),
+        seq_index * gain_rows,
+        gain_rows,
+        1,
+    )
     return (
         result,
         frames_grad,
@@ -531,12 +758,12 @@
         qkv_share[:, 2 * part :],
         out_share,
         cross_query_share,
-        ctx_share[:, :part],
-        ctx_share[:, part:],
+        ctx_share[:ctx_rows],
+        ctx_share[ctx_rows:],
         cross_out_share,
-        gate_up_share[:, :hidden_width],
-        gate_up_share[:, hidden_width:],
-        down_share,
+        glu_share[0],
+        glu_share[1],
+        glu_share[2],
         own_bias[0],
         own_bias[1],
         gains_own[3],

time: 1050 us -> 753 us (0.72)
  waiting for transfers between devices: 505 us -> 306 us
  matrix products: 187 us -> 126 us
  Pallas kernels: 0 us -> 59.8 us
  local copies, waits for them, and re-layouts: 114 us -> 54.7 us
  starting transfers between devices: 102 us -> 77.8 us
  other arithmetic: 119 us -> 102 us
    ppermute x56 -> x33, waiting for transfers between devices: 251 us -> 106 us  [the longest x9 44.8 us: all_sum(): lax.ppermute(values, axis, [(index, index ^ bit) for index in range(count)])]
    psum x1 -> x0, waiting for transfers between devices: 117 us -> none  [per_device(): lax.psum((stamp_full, bias_full, gains_full), ('seq', 'head'))]
    pallas_call x0 -> x1, Pallas kernels: none -> 59.8 us  [glu_layer(): pl.pallas_call(functools.partial(glu_kernel, blocks), grid=(blocks + 1,),...]
    dot_general x14 -> x0, matrix products: 58.9 us -> none  [product_tn(): lax.dot_general(matrix_a, matrix_b, (((0,), (0,)), ((), ())), preferred_e...]
    ppermute x6, waiting for transfers between devices: 40.2 us -> 96.2 us  [head_total(): total = total + lax.ppermute(low, 'head', pairs).astype(jnp.float32)]
    ppermute x56 -> x33, starting transfers between devices: 76.7 us -> 46.8 us  [the longest x12 28.1 us: send(): lax.ppermute(backward.astype(jnp.bfloat16), 'seq', self.behind)]
    concatenate x14 -> x0, local copies, waits for them, and re-layouts: 27.7 us -> none  [owner_order(): return jnp.concatenate(blocks, axis=-1)]
    dynamic_slice x8 -> x0, local copies, waits for them, and re-layouts: 13.4 us -> none  [the longest x7 12.6 us: owner_order(): lax.dynamic_slice_in_dim(matrix, (2 * chip + which) * width, width, axis=-1)]
  transfers between devices with their start and end apart: 76 -> 50, of which waited for: 42 -> 24; matrix products, arithmetic and copies ran while one was open for 34% -> 34% of each run, Pallas kernels for 0% -> 0%
where the time goes in v2:
time: 753 us; the launch traced here: 744 us
  waiting for transfers between devices  306 us (41%)
  matrix products  126 us (17%)
  other arithmetic  102 us (14%)
  starting transfers between devices  77.8 us (10%)
  Pallas kernels  59.8 us (8%)
  local copies, waits for them, and re-layouts  54.7 us (7%)
  between operations  17.6 us (2%)
    all_gather x2, waiting for transfers between devices, low_gather(): return lax.all_gather(block.astype(jnp.bfloat16), 'seq', axis=0, tiled=True)  104 us
    ppermute x6, waiting for transfers between devices, head_total(): total = total + lax.ppermute(low, 'head', pairs).astype(jnp.float32)  96.2 us
    pallas_call x1, Pallas kernels, glu_layer(): pl.pallas_call(functools.partial(glu_kernel, blocks), grid=(blocks + 1,),...  59.8 us
    ppermute x9, waiting for transfers between devices, all_sum(): lax.ppermute(values, axis, [(index, index ^ bit) for index in range(count)])  44.8 us
    dot_general x11, matrix products, product_t(): lax.dot_general(matrix_a, matrix_b, (((1,), (1,)), ((), ())), preferred_e...  39.1 us
    dot_general x16, matrix products, product(): return jnp.dot(matrix_a, matrix_b, preferred_element_type=jnp.float32)  36.8 us
    ppermute x12, waiting for transfers between devices, send(): lax.ppermute(backward.astype(jnp.bfloat16), 'seq', self.behind)  35.3 us
    ppermute x12, starting transfers between devices, send(): lax.ppermute(backward.astype(jnp.bfloat16), 'seq', self.behind)  28.1 us
  transfers between devices with their start and end apart: 50, of which 24 were waited for; matrix products, arithmetic and copies ran while one was open for 34% of the time, Pallas kernels for 0%

profile of v2, /device:TPU:0, one launch (start us, length us, event | category | flops | bytes accessed | tf_op | source)
XLA Modules:
  0.0 743.6 jit_solution(15020267621676543603)
XLA Ops:
  30.3 3.7 fusion.27.top_t
  34.0 74.4 %all-gather.3.cloned.1.call-done = bf16[1536,5504]{1,0:T(8,128)(2,1)} async-done(((bf16[96,5504]{1,0:T(8,128)(2,1)}), bf16[1536,5504]{1,0:T(8,128)(2,1)}) %all-gather.3.cloned.1.call-update) | async-done | bytes 16908304 | tf_op jit(solution)/shard_map/all_gather | solution.py:489
  111.4 7.5 %fusion.186 = (bf16[400,2304]{1,0:T(8,128)(2,1)}, f32[400,2304]{1,0:T(8,128)S(1)}) fusion(bf16[1536,5504]{1,0:T(8,128)(2,1)} %all-gather.3.cloned.1.call-done, f32[1536]{0:T(1024)S(1)} %get-tuple-element.64, f32[400]{0:T(512)S(1)} %add_rsqrt_fusion.2, f32[400]{0:T(512)S(1)} %broadcast_multiply_fusion.8, ...), kind=kOutput, calls=%fused_computation.381 | convolution fusion | flops 2838220800 | bytes 13802624 | tf_op jit(solution)/shard_map/dot_general | solution.py:83
  127.7 3.0 collective-permute-start
  140.0 2.6 copy.79
  142.6 2.5 copy.77
  145.1 4.6 fusion.187
  149.8 3.9 fusion
  155.9 5.1 fusion.54
  161.1 4.1 convolution_convert_fusion.4
  173.9 7.8 %collective-permute-done.2 = bf16[384,1536]{1,0:T(8,128)(2,1)} collective-permute-done((bf16[384,1536]{1,0:T(8,128)(2,1)}, bf16[384,1536]{1,0:T(8,128)(2,1)}, u32[]{:S(2)}, u32[]{:S(2)}) %collective-permute-start.2) | collective-permute-done | bytes 1179680 | tf_op jit(solution)/shard_map/ppermute | solution.py:484
  181.7 2.9 fusion.170
  186.0 2.9 fusion.59
  193.3 3.2 convolution_convert_fusion.3
  200.4 3.8 fusion.25
  204.2 17.9 %collective-permute-done.3 = bf16[384,1536]{1,0:T(8,128)(2,1)S(1)} collective-permute-done((bf16[384,1536]{1,0:T(8,128)(2,1)S(1)}, bf16[384,1536]{1,0:T(8,128)(2,1)S(1)}, u32[]{:S(2)}, u32[]{:S(2)}) %collective-permute-start.3) | collective-permute-done | bytes 1179680 | tf_op jit(solution)/shard_map/ppermute | solution.py:484
  223.3 8.8 %multiply_convert_fusion.3.normed = bf16[384,1536]{1,0:T(8,128)(2,1)S(1)} fusion(f32[384,1536]{1,0:T(8,128)S(1)} %get-tuple-element.71, f32[1536]{0:T(1024)S(1)} %copy-done.100, f32[384]{0:T(512)S(1)} %add_rsqrt_fusion, f32[384]{0:T(512)S(1)} %broadcast_multiply_fusion.6), kind=kLoop, calls=%fused_computation.87 | loop fusion | flops 2359296 | bytes 3548160 | tf_op jit(solution)/shard_map/convert_element_type | solution.py:613
  233.1 3.7 fusion.26.normed_t
  236.8 29.4 %all-gather.5.cloned.1.call-done.w_gate.w_up.w_down = bf16[1536,9216]{1,0:T(8,128)(2,1)} async-done(((bf16[96,9216]{1,0:T(8,128)(2,1)}), bf16[1536,9216]{1,0:T(8,128)(2,1)}) %all-gather.5.cloned.1.call-update) | async-done | bytes 28311568 | tf_op jit(solution)/shard_map/all_gather | solution.py:489
  266.1 59.8 %glu_layer.1 = (bf16[384,1536]{1,0:T(8,128)(2,1)}, bf16[384,1536]{1,0:T(8,128)(2,1)}, bf16[3,768,3072]{2,1,0:T(8,128)(2,1)}, f32[2,3072]{1,0:T(2,128)}) custom-call(bf16[384,1536]{1,0:T(8,128)(2,1)} %copy-done.41, bf16[1536,384]{1,0:T(8,128)(2,1)} %fusion.26.normed_t, bf16[384,1536]{1,0:T(8,128)(2,1)} %top.1, bf16[1536,384]{1,0:T(8,128)(2,1)} %fusion.27.top_t, ...), custom_call_target="tpu_custom_call" | custom-call | flops 32614907904 | bytes 56623104 | tf_op jit(solution)/shard_map/glu_layer/pallas_call | solution.py:421
  328.4 5.5 fusion.29
  334.2 2.8 fusion.171
  337.0 7.3 collective-permute-start.7
  344.9 10.3 %collective-permute-done.5 = bf16[384,1536]{1,0:T(8,128)(2,1)} collective-permute-done((bf16[384,1536]{1,0:T(8,128)(2,1)}, bf16[384,1536]{1,0:T(8,128)(2,1)}, u32[]{:S(2)}, u32[]{:S(2)}) %collective-permute-start.5) | collective-permute-done | bytes 1179680 | tf_op jit(solution)/shard_map/ppermute | solution.py:484
  355.2 2.6 multiply_reduce_fusion.3
  357.8 21.7 %collective-permute-done.4 = bf16[384,1536]{1,0:T(8,128)(2,1)} collective-permute-done((bf16[384,1536]{1,0:T(8,128)(2,1)}, bf16[384,1536]{1,0:T(8,128)(2,1)}, u32[]{:S(2)}, u32[]{:S(2)}) %collective-permute-start.4) | collective-permute-done | bytes 1179680 | tf_op jit(solution)/shard_map/ppermute | solution.py:484
  379.5 4.7 convert_add_fusion.1
  385.7 2.8 fusion.62
  388.8 4.4 fusion.28
  393.2 3.4 add_convert_fusion.5
  396.6 7.3 collective-permute-start.10
  406.4 2.9 convolution_convert_fusion.2
  421.8 14.3 %collective-permute-done.8 = bf16[384,1536]{1,0:T(8,128)(2,1)S(1)} collective-permute-done((bf16[384,1536]{1,0:T(8,128)(2,1)S(1)}, bf16[384,1536]{1,0:T(8,128)(2,1)S(1)}, u32[]{:S(2)}, u32[]{:S(2)}) %collective-permute-start.8) | collective-permute-done | bytes 1179680 | tf_op jit(solution)/shard_map/ppermute | solution.py:484
  436.5 4.6 collective-permute-done.10
  441.1 4.4 collective-permute-done.9
  447.7 2.7 fusion.30
  454.7 5.1 add_convert_fusion.3
  466.7 36.9 %collective-permute-done.26 = f32[7,1536]{1,0:T(8,128)} collective-permute-done((f32[7,1536]{1,0:T(8,128)S(1)}, f32[7,1536]{1,0:T(8,128)}, u32[]{:S(2)}, u32[]{:S(2)}) %collective-permute-start.26) | collective-permute-done | bytes 43040 | tf_op jit(solution)/shard_map/ppermute | solution.py:309
  514.3 2.8 collective-permute-done.44
  520.2 15.6 %multiply_reduce_fusion = (f32[12,384]{1,0:T(8,128)S(1)}, f32[12,384,896]{2,1,0:T(8,128)}) fusion(f32[12,384,896]{2,1,0:T(8,128)} %copy-done.2, f32[12,384]{1,0:T(8,128)S(1)} %copy-done.35, bf16[384,12,64]{0,2,1:T(8,128)(2,1)S(1)} %bitcast.119, bf16[896,12,64]{0,2,1:T(8,128)(2,1)} %bitcast.131), kind=kOutput, calls=%fused_computation.1 | convolution fusion | flops 540864000 | bytes 35033088 | tf_op jit(solution)/shard_map/qhd,khd->hqk/dot_general | solution.py:154
  538.1 6.0 add_convert_fusion.1
  546.2 10.1 %multiply_convert_fusion = bf16[12,384,896]{2,1,0:T(8,128)(2,1)} fusion(f32[12,384,896]{2,1,0:T(8,128)} %get-tuple-element.184, f32[12,384,896]{2,1,0:T(8,128)S(1)} %bitcast.115, f32[12,384]{1,0:T(8,128)S(1)} %add.507, f32[12,384]{1,0:T(8,128)S(1)} %copy-done.35), kind=kLoop, calls=%fused_computation | loop fusion | flops 16515072 | bytes 41324544 | tf_op jit(solution)/shard_map/convert_element_type | solution.py:165
  556.3 4.1 fusion.8
  564.1 6.4 fusion.51
  571.7 5.0 convolution_multiply_fusion
  579.8 6.2 collective-permute-done.13
  590.6 3.7 collective-permute-done.42
  597.3 3.2 collective-permute-start.47
  602.5 6.0 convolution_convert_fusion
  608.5 14.0 %collective-permute-start.27 = (bf16[768,2304]{1,0:T(8,128)(2,1)}, bf16[768,2304]{1,0:T(8,128)(2,1)}, u32[]{:S(2)}, u32[]{:S(2)}) collective-permute-start(bf16[768,2304]{1,0:T(8,128)(2,1)} %convolution_convert_fusion), channel_id=1, source_target_pairs={{0,2},{2,0},{4,6},{6,4},{8,10},{10,8},{12,14},{14,12},{16,18},{18,... | collective-permute-start | bytes 10616840 | tf_op jit(solution)/shard_map/ppermute | solution.py:237
  622.5 3.9 fusion.12
  630.4 24.2 %collective-permute-done.17 = bf16[384,1536]{1,0:T(8,128)(2,1)S(1)} collective-permute-done((bf16[384,1536]{1,0:T(8,128)(2,1)S(1)}, bf16[384,1536]{1,0:T(8,128)(2,1)S(1)}, u32[]{:S(2)}, u32[]{:S(2)}) %collective-permute-start.17) | collective-permute-done | bytes 1179680 | tf_op jit(solution)/shard_map/ppermute | solution.py:484
  654.6 3.2 multiply_reduce_fusion.5
  657.9 3.6 convert_add_fusion
  661.5 2.9 collective-permute-start.19
  664.5 6.4 add_convert_fusion
  673.3 5.5 collective-permute-done.28
  679.7 3.0 collective-permute-start.21
  682.7 6.9 collective-permute-done.21
  691.2 3.9 collective-permute-start.32
  698.5 5.9 collective-permute-done.30
  706.1 9.0 %collective-permute-done.33 = bf16[96,2304]{1,0:T(8,128)(2,1)S(1)} collective-permute-done((bf16[96,2304]{1,0:T(8,128)(2,1)S(1)}, bf16[96,2304]{1,0:T(8,128)(2,1)S(1)}, u32[]{:S(2)}, u32[]{:S(2)}) %collective-permute-start.33) | collective-permute-done | bytes 442400 | tf_op jit(solution)/shard_map/ppermute | solution.py:253
  717.8 8.9 %collective-permute-done.34 = bf16[96,2304]{1,0:T(8,128)(2,1)S(1)} collective-permute-done((bf16[96,2304]{1,0:T(8,128)(2,1)S(1)}, bf16[96,2304]{1,0:T(8,128)(2,1)S(1)}, u32[]{:S(2)}, u32[]{:S(2)}) %collective-permute-start.34) | collective-permute-done | bytes 442400 | tf_op jit(solution)/shard_map/ppermute | solution.py:253
  728.3 6.9 collective-permute-done.35
  (565 shorter events, 153.5 us)
Async XLA Ops:
  7.2 101.2 %all-gather.3.cloned.1.call-start = ((), (), s32[]{:S(2)}) async-start(), calls=%async_computation | async-start | bytes 17965056 | tf_op jit(solution)/shard_map/all_gather | solution.py:489
  15.9 250.2 %all-gather.5.cloned.1.call-start = ((), (), s32[]{:S(2)}) async-start(), calls=%async_computation.1 | async-start | bytes 30081024 | tf_op jit(solution)/shard_map/all_gather | solution.py:489
  27.1 84.3 %copy-start.119 = (f32[400]{0:T(512)}, f32[400]{0:T(512)S(1)}, u32[]{:S(2)}) copy-start(f32[400]{0:T(512)S(1)} %broadcast_multiply_fusion.8) | copy-start | bytes 4804
  27.6 83.8 %copy-start.114 = (f32[400]{0:T(512)}, f32[400]{0:T(512)S(1)}, u32[]{:S(2)}) copy-start(f32[400]{0:T(512)S(1)} %add_rsqrt_fusion.2) | copy-start | bytes 4804
  111.4 89.0 %copy-start.97 = (f32[1536]{0:T(1024)}, f32[1536]{0:T(1024)S(1)}, u32[]{:S(2)}) copy-start(f32[1536]{0:T(1024)S(1)} %get-tuple-element.64) | copy-start | bytes 18436
  127.7 9.0 %collective-permute-start = (bf16[2,256,768]{2,1,0:T(8,128)(2,1)}, bf16[2,256,768]{2,1,0:T(8,128)(2,1)}, u32[]{:S(2)}, u32[]{:S(2)}) collective-permute-start(bf16[2,256,768]{2,1,0:T(8,128)(2,1)} %get-tuple-element.155), channel_id=1, source_target_pairs={{0,2},{2,4},{4,6},{6,8},{8,10},{10,12},{12,14},{14,16},{16,18},{18... | collective-permute-start | bytes 2359304 | tf_op jit(solution)/shard_map/ppermute | solution.py:25
  130.7 6.0 collective-permute-start.1
  165.2 16.5 %collective-permute-start.2 = (bf16[384,1536]{1,0:T(8,128)(2,1)}, bf16[384,1536]{1,0:T(8,128)(2,1)}, u32[]{:S(2)}, u32[]{:S(2)}) collective-permute-start(bf16[384,1536]{1,0:T(8,128)(2,1)} %convolution_convert_fusion.4), channel_id=1, source_target_pairs={{0,1},{1,0},{2,3},{3,2},{4,5},{5,4},{6,7},{7,6},{8,9},{9,8},{10,11... | collective-permute-start | bytes 3538952 | tf_op jit(solution)/shard_map/ppermute | solution.py:484
  184.6 143.8 %copy-start.107 = (f32[384]{0:T(512)}, f32[384]{0:T(512)S(1)}, u32[]{:S(2)}) copy-start(f32[384]{0:T(512)S(1)} %broadcast_multiply_fusion.7) | copy-start | bytes 4612
  185.0 143.4 %copy-start.117 = (f32[384]{0:T(512)}, f32[384]{0:T(512)S(1)}, u32[]{:S(2)}) copy-start(f32[384]{0:T(512)S(1)} %add_rsqrt_fusion.1) | copy-start | bytes 4612
  196.6 25.5 %collective-permute-start.3 = (bf16[384,1536]{1,0:T(8,128)(2,1)S(1)}, bf16[384,1536]{1,0:T(8,128)(2,1)S(1)}, u32[]{:S(2)}, u32[]{:S(2)}) collective-permute-start(bf16[384,1536]{1,0:T(8,128)(2,1)S(1)} %convolution_convert_fusion.3), channel_id=1, source_target_pairs={{0,1},{1,0},{2,3},{3,2},{4,5},{5,4},{6,7},{7,6},{8,9},{9,8},{10,11... | collective-permute-start | bytes 3538952 | tf_op jit(solution)/shard_map/ppermute | solution.py:484
  326.0 29.2 %collective-permute-start.5 = (bf16[384,1536]{1,0:T(8,128)(2,1)}, bf16[384,1536]{1,0:T(8,128)(2,1)}, u32[]{:S(2)}, u32[]{:S(2)}) collective-permute-start(bf16[384,1536]{1,0:T(8,128)(2,1)} %get-tuple-element.37), channel_id=1, source_target_pairs={{0,1},{1,0},{2,3},{3,2},{4,5},{5,4},{6,7},{7,6},{8,9},{9,8},{10,11... | collective-permute-start | bytes 3538952 | tf_op jit(solution)/shard_map/ppermute | solution.py:484
  333.9 45.6 %collective-permute-start.4 = (bf16[384,1536]{1,0:T(8,128)(2,1)}, bf16[384,1536]{1,0:T(8,128)(2,1)}, u32[]{:S(2)}, u32[]{:S(2)}) collective-permute-start(bf16[384,1536]{1,0:T(8,128)(2,1)} %get-tuple-element.36), channel_id=1, source_target_pairs={{0,1},{1,0},{2,3},{3,2},{4,5},{5,4},{6,7},{7,6},{8,9},{9,8},{10,11... | collective-permute-start | bytes 3538952 | tf_op jit(solution)/shard_map/ppermute | solution.py:484
  337.0 56.2 %collective-permute-start.6 = (bf16[3,96,1536]{2,1,0:T(8,128)(2,1)}, bf16[3,96,1536]{2,1,0:T(8,128)(2,1)}, u32[]{:S(2)}, u32[]{:S(2)}) collective-permute-start(bf16[3,96,1536]{2,1,0:T(8,128)(2,1)} %get-tuple-element.81), channel_id=1, source_target_pairs={{0,8},{2,10},{8,16},{10,18},{16,24},{18,26},{24,28},{26,30},{28,20... | collective-permute-start | bytes 2654216 | tf_op jit(solution)/shard_map/ppermute | solution.py:252
  337.0 56.2 %collective-permute-start.7 = (bf16[3,96,1536]{2,1,0:T(8,128)(2,1)}, bf16[3,96,1536]{2,1,0:T(8,128)(2,1)}, u32[]{:S(2)}, u32[]{:S(2)}) collective-permute-start(bf16[3,96,1536]{2,1,0:T(8,128)(2,1)} %get-tuple-element.80), channel_id=1, source_target_pairs={{0,4},{2,6},{8,0},{10,2},{16,8},{18,10},{24,16},{26,18},{28,24},{3... | collective-permute-start | bytes 2654216 | tf_op jit(solution)/shard_map/ppermute | solution.py:253
  344.9 34.6 %copy-start.17 = (bf16[384,1536]{1,0:T(8,128)(2,1)S(1)}, bf16[384,1536]{1,0:T(8,128)(2,1)}, u32[]{:S(2)}) copy-start(bf16[384,1536]{1,0:T(8,128)(2,1)} %get-tuple-element.37) | copy-start | bytes 3538948
  344.9 34.6 %copy-start.37 = (bf16[384,1536]{1,0:T(8,128)(2,1)S(1)}, bf16[384,1536]{1,0:T(8,128)(2,1)}, u32[]{:S(2)}) copy-start(bf16[384,1536]{1,0:T(8,128)(2,1)} %top.1) | copy-start | bytes 3538948
  344.9 34.6 %copy-start.109 = (f32[1536]{0:T(1024)S(1)}, f32[1536]{0:T(1024)}, u32[]{:S(2)}) copy-start(f32[1536]{0:T(1024)} %get-tuple-element.61) | copy-start | bytes 18436
  396.6 44.5 %collective-permute-start.10 = (bf16[3,96,3072]{2,1,0:T(8,128)(2,1)S(1)}, bf16[3,96,3072]{2,1,0:T(8,128)(2,1)S(1)}, u32[]{:S(2)}, u32[]{:S(2)}) collective-permute-start(bf16[3,96,3072]{2,1,0:T(8,128)(2,1)S(1)} %get-tuple-element.78), channel_id=1, source_target_pairs={{0,4},{2,6},{8,0},{10,2},{16,8},{18,10},{24,16},{26,18},{28,24},{3... | collective-permute-start | bytes 5308424 | tf_op jit(solution)/shard_map/ppermute | solution.py:253
  403.9 41.5 %collective-permute-start.9 = (bf16[3,96,3072]{2,1,0:T(8,128)(2,1)S(1)}, bf16[3,96,3072]{2,1,0:T(8,128)(2,1)S(1)}, u32[]{:S(2)}, u32[]{:S(2)}) collective-permute-start(bf16[3,96,3072]{2,1,0:T(8,128)(2,1)S(1)} %get-tuple-element.79), channel_id=1, source_target_pairs={{0,8},{2,10},{8,16},{10,18},{16,24},{18,26},{24,28},{26,30},{28,20... | collective-permute-start | bytes 5308424 | tf_op jit(solution)/shard_map/ppermute | solution.py:252
  409.3 26.8 %collective-permute-start.8 = (bf16[384,1536]{1,0:T(8,128)(2,1)S(1)}, bf16[384,1536]{1,0:T(8,128)(2,1)S(1)}, u32[]{:S(2)}, u32[]{:S(2)}) collective-permute-start(bf16[384,1536]{1,0:T(8,128)(2,1)S(1)} %convolution_convert_fusion.2), channel_id=1, source_target_pairs={{0,1},{1,0},{2,3},{3,2},{4,5},{5,4},{6,7},{7,6},{8,9},{9,8},{10,11... | collective-permute-start | bytes 3538952 | tf_op jit(solution)/shard_map/ppermute | solution.py:484
  411.7 3.8 collective-permute-start.36
  412.6 3.9 collective-permute-start.37
  415.6 4.7 collective-permute-start.39
  419.9 91.1 %collective-permute-start.40 = (bf16[96,1536]{1,0:T(8,128)(2,1)}, bf16[96,1536]{1,0:T(8,128)(2,1)}, u32[]{:S(2)}, u32[]{:S(2)}) collective-permute-start(bf16[96,1536]{1,0:T(8,128)(2,1)} %pad_maximum_fusion.13), channel_id=1, source_target_pairs={{0,8},{2,10},{8,16},{10,18},{16,24},{18,26},{24,28},{26,30},{28,20... | collective-permute-start | bytes 884744 | tf_op jit(solution)/shard_map/ppermute | solution.py:252
  446.6 3.8 collective-permute-start.23
  450.5 4.2 collective-permute-start.24
  453.2 53.8 %collective-permute-start.38 = (bf16[768,768]{1,0:T(8,128)(2,1)}, bf16[768,768]{1,0:T(8,128)(2,1)}, u32[]{:S(2)}, u32[]{:S(2)}) collective-permute-start(bf16[768,768]{1,0:T(8,128)(2,1)} %convolution_convert_fusion.5), channel_id=1, source_target_pairs={{0,2},{2,0},{4,6},{6,4},{8,10},{10,8},{12,14},{14,12},{16,18},{18,... | collective-permute-start | bytes 3538952 | tf_op jit(solution)/shard_map/ppermute | solution.py:237
  454.7 7.2 collective-permute-start.25
  459.9 59.0 %collective-permute-start.11 = (bf16[3,96,3072]{2,1,0:T(8,128)(2,1)}, bf16[3,96,3072]{2,1,0:T(8,128)(2,1)S(1)}, u32[]{:S(2)}, u32[]{:S(2)}) collective-permute-start(bf16[3,96,3072]{2,1,0:T(8,128)(2,1)} %get-tuple-element.77), channel_id=1, source_target_pairs={{0,8},{2,10},{8,16},{10,18},{16,24},{18,26},{24,28},{26,30},{28,20... | collective-permute-start | bytes 5308424 | tf_op jit(solution)/shard_map/ppermute | solution.py:252
  461.9 57.0 %collective-permute-start.12 = (bf16[3,96,3072]{2,1,0:T(8,128)(2,1)}, bf16[3,96,3072]{2,1,0:T(8,128)(2,1)}, u32[]{:S(2)}, u32[]{:S(2)}) collective-permute-start(bf16[3,96,3072]{2,1,0:T(8,128)(2,1)} %get-tuple-element.76), channel_id=1, source_target_pairs={{0,4},{2,6},{8,0},{10,2},{16,8},{18,10},{24,16},{26,18},{28,24},{3... | collective-permute-start | bytes 5308424 | tf_op jit(solution)/shard_map/ppermute | solution.py:253
  461.9 41.7 %collective-permute-start.26 = (f32[7,1536]{1,0:T(8,128)S(1)}, f32[7,1536]{1,0:T(8,128)}, u32[]{:S(2)}, u32[]{:S(2)}) collective-permute-start(f32[7,1536]{1,0:T(8,128)S(1)} %add.526), channel_id=1, source_target_pairs={{0,16},{2,18},{4,20},{6,22},{8,24},{10,26},{12,28},{14,30},{16,0},... | collective-permute-start | bytes 129032 | tf_op jit(solution)/shard_map/ppermute | solution.py:309
  510.3 6.8 collective-permute-start.44
  512.8 47.6 %collective-permute-start.41 = (bf16[96,3072]{1,0:T(8,128)(2,1)}, bf16[96,3072]{1,0:T(8,128)(2,1)}, u32[]{:S(2)}, u32[]{:S(2)}) collective-permute-start(bf16[96,3072]{1,0:T(8,128)(2,1)} %add_convert_fusion.18), channel_id=1, source_target_pairs={{0,8},{2,10},{8,16},{10,18},{16,24},{18,26},{24,28},{26,30},{28,20... | collective-permute-start | bytes 1769480 | tf_op jit(solution)/shard_map/ppermute | solution.py:252
  518.0 59.1 %collective-permute-start.45 = (bf16[96,3072]{1,0:T(8,128)(2,1)}, bf16[96,3072]{1,0:T(8,128)(2,1)}, u32[]{:S(2)}, u32[]{:S(2)}) collective-permute-start(bf16[96,3072]{1,0:T(8,128)(2,1)} %add_convert_fusion.15), channel_id=1, source_target_pairs={{0,4},{2,6},{8,0},{10,2},{16,8},{18,10},{24,16},{26,18},{28,24},{3... | collective-permute-start | bytes 1769480 | tf_op jit(solution)/shard_map/ppermute | solution.py:253
  520.2 26.0 %slice-start = ((s8[16515072]{0:T(1024)(128)(4,1)}), s8[4194304]{0:T(1024)(128)(4,1)S(1)}, s32[]{:S(2)}) async-start(s8[16515072]{0:T(1024)(128)(4,1)} %bitcast.114), calls=%async_computation.2 | async-start | bytes 8388608
  520.2 26.0 %slice-start.1 = ((s8[16515072]{0:T(1024)(128)(4,1)}), s8[4194304]{0:T(1024)(128)(4,1)S(1)}, s32[]{:S(2)}) async-start(s8[16515072]{0:T(1024)(128)(4,1)} %bitcast.114), calls=%async_computation.3 | async-start | bytes 8388608
  520.2 26.0 %slice-start.2 = ((s8[16515072]{0:T(1024)(128)(4,1)}), s8[3932160]{0:T(1024)(128)(4,1)S(1)}, s32[]{:S(2)}) async-start(s8[16515072]{0:T(1024)(128)(4,1)} %bitcast.114), calls=%async_computation.4 | async-start | bytes 7864320
  544.1 41.9 %collective-permute-start.13 = (bf16[3,96,3072]{2,1,0:T(8,128)(2,1)}, bf16[3,96,3072]{2,1,0:T(8,128)(2,1)}, u32[]{:S(2)}, u32[]{:S(2)}) collective-permute-start(bf16[3,96,3072]{2,1,0:T(8,128)(2,1)} %get-tuple-element.75), channel_id=1, source_target_pairs={{0,8},{2,10},{8,16},{10,18},{16,24},{18,26},{24,28},{26,30},{28,20... | collective-permute-start | bytes 5308424 | tf_op jit(solution)/shard_map/ppermute | solution.py:252
  545.4 41.8 %collective-permute-start.14 = (bf16[3,96,3072]{2,1,0:T(8,128)(2,1)}, bf16[3,96,3072]{2,1,0:T(8,128)(2,1)}, u32[]{:S(2)}, u32[]{:S(2)}) collective-permute-start(bf16[3,96,3072]{2,1,0:T(8,128)(2,1)} %get-tuple-element.74), channel_id=1, source_target_pairs={{0,4},{2,6},{8,0},{10,2},{16,8},{18,10},{24,16},{26,18},{28,24},{3... | collective-permute-start | bytes 5308424 | tf_op jit(solution)/shard_map/ppermute | solution.py:253
  562.6 31.8 %collective-permute-start.42 = (bf16[96,3072]{1,0:T(8,128)(2,1)}, bf16[96,3072]{1,0:T(8,128)(2,1)}, u32[]{:S(2)}, u32[]{:S(2)}) collective-permute-start(bf16[96,3072]{1,0:T(8,128)(2,1)} %add_convert_fusion.17), channel_id=1, source_target_pairs={{0,8},{2,10},{8,16},{10,18},{16,24},{18,26},{24,28},{26,30},{28,20... | collective-permute-start | bytes 1769480 | tf_op jit(solution)/shard_map/ppermute | solution.py:252
  579.0 18.1 %collective-permute-start.46 = (bf16[96,3072]{1,0:T(8,128)(2,1)S(1)}, bf16[96,3072]{1,0:T(8,128)(2,1)S(1)}, u32[]{:S(2)}, u32[]{:S(2)}) collective-permute-start(bf16[96,3072]{1,0:T(8,128)(2,1)S(1)} %add_convert_fusion.14), channel_id=1, source_target_pairs={{0,4},{2,6},{8,0},{10,2},{16,8},{18,10},{24,16},{26,18},{28,24},{3... | collective-permute-start | bytes 1769480 | tf_op jit(solution)/shard_map/ppermute | solution.py:253
  587.6 34.9 %slice-start.11 = ((s8[16908288]{0:T(1024)(128)(4,1)}), s8[4194304]{0:T(1024)(128)(4,1)S(1)}, s32[]{:S(2)}) async-start(s8[16908288]{0:T(1024)(128)(4,1)} %bitcast.128), calls=%async_computation.13 | async-start | bytes 8388608
  587.7 12.9 %collective-permute-start.15 = (bf16[2,256,768]{1,2,0:T(8,128)(2,1)S(1)}, bf16[2,256,768]{1,2,0:T(8,128)(2,1)S(1)}, u32[]{:S(2)}, u32[]{:S(2)}) collective-permute-start(bf16[2,256,768]{1,2,0:T(8,128)(2,1)S(1)} %get-tuple-element.91), channel_id=1, source_target_pairs={{0,2},{2,4},{4,6},{6,8},{8,10},{10,12},{12,14},{14,16},{16,18},{18... | collective-permute-start | bytes 2359304 | tf_op jit(solution)/shard_map/ppermute | solution.py:36
  589.3 11.2 %collective-permute-start.16 = (bf16[2,256,768]{1,2,0:T(8,128)(2,1)S(1)}, bf16[2,256,768]{1,2,0:T(8,128)(2,1)S(1)}, u32[]{:S(2)}, u32[]{:S(2)}) collective-permute-start(bf16[2,256,768]{1,2,0:T(8,128)(2,1)S(1)} %get-tuple-element.92), channel_id=1, source_target_pairs={{2,0},{4,2},{6,4},{8,6},{10,8},{12,10},{14,12},{16,14},{18,16},{20... | collective-permute-start | bytes 2359304 | tf_op jit(solution)/shard_map/ppermute | solution.py:36
  595.6 32.6 %collective-permute-start.43 = (bf16[96,3072]{1,0:T(8,128)(2,1)S(1)}, bf16[96,3072]{1,0:T(8,128)(2,1)S(1)}, u32[]{:S(2)}, u32[]{:S(2)}) collective-permute-start(bf16[96,3072]{1,0:T(8,128)(2,1)S(1)} %add_convert_fusion.16), channel_id=1, source_target_pairs={{0,8},{2,10},{8,16},{10,18},{16,24},{18,26},{24,28},{26,30},{28,20... | collective-permute-start | bytes 1769480 | tf_op jit(solution)/shard_map/ppermute | solution.py:252
  597.3 25.1 %slice-start.12 = ((s8[16908288]{0:T(1024)(128)(4,1)}), s8[4194304]{0:T(1024)(128)(4,1)S(1)}, s32[]{:S(2)}) async-start(s8[16908288]{0:T(1024)(128)(4,1)} %bitcast.128), calls=%async_computation.14 | async-start | bytes 8388608
  597.3 30.9 %collective-permute-start.47 = (bf16[96,3072]{1,0:T(8,128)(2,1)S(1)}, bf16[96,3072]{1,0:T(8,128)(2,1)S(1)}, u32[]{:S(2)}, u32[]{:S(2)}) collective-permute-start(bf16[96,3072]{1,0:T(8,128)(2,1)S(1)} %add_convert_fusion.13), channel_id=1, source_target_pairs={{0,4},{2,6},{8,0},{10,2},{16,8},{18,10},{24,16},{26,18},{28,24},{3... | collective-permute-start | bytes 1769480 | tf_op jit(solution)/shard_map/ppermute | solution.py:253
  608.5 56.0 %collective-permute-start.27 = (bf16[768,2304]{1,0:T(8,128)(2,1)}, bf16[768,2304]{1,0:T(8,128)(2,1)}, u32[]{:S(2)}, u32[]{:S(2)}) collective-permute-start(bf16[768,2304]{1,0:T(8,128)(2,1)} %convolution_convert_fusion), channel_id=1, source_target_pairs={{0,2},{2,0},{4,6},{6,4},{8,10},{10,8},{12,14},{14,12},{16,18},{18,... | collective-permute-start | bytes 10616840 | tf_op jit(solution)/shard_map/ppermute | solution.py:237
  626.6 28.0 %collective-permute-start.17 = (bf16[384,1536]{1,0:T(8,128)(2,1)S(1)}, bf16[384,1536]{1,0:T(8,128)(2,1)S(1)}, u32[]{:S(2)}, u32[]{:S(2)}) collective-permute-start(bf16[384,1536]{1,0:T(8,128)(2,1)S(1)} %slice.823), channel_id=1, source_target_pairs={{0,1},{1,0},{2,3},{3,2},{4,5},{5,4},{6,7},{7,6},{8,9},{9,8},{10,11... | collective-permute-start | bytes 3538952 | tf_op jit(solution)/shard_map/ppermute | solution.py:484
  628.2 26.3 %copy-start.98 = (f32[1536]{0:T(1024)S(1)}, f32[1536]{0:T(1024)}, u32[]{:S(2)}) copy-start(f32[1536]{0:T(1024)} %copy-done.97) | copy-start | bytes 18436
  657.9 3.7 collective-permute-start.18
  661.5 11.7 %collective-permute-start.19 = (f32[7,1536]{1,0:T(8,128)S(1)}, f32[7,1536]{1,0:T(8,128)S(1)}, u32[]{:S(2)}, u32[]{:S(2)}) collective-permute-start(f32[7,1536]{1,0:T(8,128)S(1)} %fusion.228), channel_id=1, source_target_pairs={{0,4},{2,6},{4,0},{6,2},{8,12},{10,14},{12,8},{14,10},{16,20},{18,... | collective-permute-start | bytes 129032 | tf_op jit(solution)/shard_map/ppermute | solution.py:309
  671.0 7.9 %collective-permute-start.28 = (bf16[96,1152]{1,0:T(8,128)(2,1)S(1)}, bf16[96,1152]{1,0:T(8,128)(2,1)S(1)}, u32[]{:S(2)}, u32[]{:S(2)}) collective-permute-start(bf16[96,1152]{1,0:T(8,128)(2,1)S(1)} %get-tuple-element.89), channel_id=1, source_target_pairs={{0,8},{2,10},{8,16},{10,18},{16,24},{18,26},{24,28},{26,30},{28,20... | collective-permute-start | bytes 663560 | tf_op jit(solution)/shard_map/ppermute | solution.py:252
  673.2 6.4 collective-permute-start.20
  678.9 16.1 %collective-permute-start.29 = (bf16[96,2304]{1,0:T(8,128)(2,1)S(1)}, bf16[96,2304]{1,0:T(8,128)(2,1)S(1)}, u32[]{:S(2)}, u32[]{:S(2)}) collective-permute-start(bf16[96,2304]{1,0:T(8,128)(2,1)S(1)} %add_convert_fusion.24), channel_id=1, source_target_pairs={{0,8},{2,10},{8,16},{10,18},{16,24},{18,26},{24,28},{26,30},{28,20... | collective-permute-start | bytes 1327112 | tf_op jit(solution)/shard_map/ppermute | solution.py:252
  679.7 10.0 %collective-permute-start.21 = (f32[7,1536]{1,0:T(8,128)S(1)}, f32[7,1536]{1,0:T(8,128)S(1)}, u32[]{:S(2)}, u32[]{:S(2)}) collective-permute-start(f32[7,1536]{1,0:T(8,128)S(1)} %add.519), channel_id=1, source_target_pairs={{0,16},{2,18},{4,20},{6,22},{8,24},{10,26},{12,28},{14,30},{16,0},... | collective-permute-start | bytes 129032 | tf_op jit(solution)/shard_map/ppermute | solution.py:309
  689.6 7.5 %collective-permute-start.22 = (f32[7,1536]{1,0:T(8,128)S(1)}, f32[7,1536]{1,0:T(8,128)S(1)}, u32[]{:S(2)}, u32[]{:S(2)}) collective-permute-start(f32[7,1536]{1,0:T(8,128)S(1)} %add.520), channel_id=1, source_target_pairs={{0,1},{1,0},{2,3},{3,2},{4,5},{5,4},{6,7},{7,6},{8,9},{9,8},{10,11... | collective-permute-start | bytes 129032 | tf_op jit(solution)/shard_map/ppermute | solution.py:309
  691.2 7.4 collective-permute-start.32
  695.2 9.3 %collective-permute-start.30 = (bf16[96,2304]{1,0:T(8,128)(2,1)S(1)}, bf16[96,2304]{1,0:T(8,128)(2,1)S(1)}, u32[]{:S(2)}, u32[]{:S(2)}) collective-permute-start(bf16[96,2304]{1,0:T(8,128)(2,1)S(1)} %add_convert_fusion.23), channel_id=1, source_target_pairs={{0,8},{2,10},{8,16},{10,18},{16,24},{18,26},{24,28},{26,30},{28,20... | collective-permute-start | bytes 1327112 | tf_op jit(solution)/shard_map/ppermute | solution.py:252
  704.6 10.5 %collective-permute-start.33 = (bf16[96,2304]{1,0:T(8,128)(2,1)S(1)}, bf16[96,2304]{1,0:T(8,128)(2,1)S(1)}, u32[]{:S(2)}, u32[]{:S(2)}) collective-permute-start(bf16[96,2304]{1,0:T(8,128)(2,1)S(1)} %get-tuple-element.88), channel_id=1, source_target_pairs={{0,4},{2,6},{8,0},{10,2},{16,8},{18,10},{24,16},{26,18},{28,24},{3... | collective-permute-start | bytes 1327112 | tf_op jit(solution)/shard_map/ppermute | solution.py:253
  715.2 11.5 %collective-permute-start.34 = (bf16[96,2304]{1,0:T(8,128)(2,1)S(1)}, bf16[96,2304]{1,0:T(8,128)(2,1)S(1)}, u32[]{:S(2)}, u32[]{:S(2)}) collective-permute-start(bf16[96,2304]{1,0:T(8,128)(2,1)S(1)} %add_convert_fusion.20), channel_id=1, source_target_pairs={{0,4},{2,6},{8,0},{10,2},{16,8},{18,10},{24,16},{26,18},{28,24},{3... | collective-permute-start | bytes 1327112 | tf_op jit(solution)/shard_map/ppermute | solution.py:253
  716.8 11.5 %collective-permute-start.31 = (bf16[96,2304]{1,0:T(8,128)(2,1)S(1)}, bf16[96,2304]{1,0:T(8,128)(2,1)S(1)}, u32[]{:S(2)}, u32[]{:S(2)}) collective-permute-start(bf16[96,2304]{1,0:T(8,128)(2,1)S(1)} %get-tuple-element.87), channel_id=1, source_target_pairs={{0,8},{2,10},{8,16},{10,18},{16,24},{18,26},{24,28},{26,30},{28,20... | collective-permute-start | bytes 1327112 | tf_op jit(solution)/shard_map/ppermute | solution.py:252
  726.9 8.4 %collective-permute-start.35 = (bf16[96,2304]{1,0:T(8,128)(2,1)S(1)}, bf16[96,2304]{1,0:T(8,128)(2,1)S(1)}, u32[]{:S(2)}, u32[]{:S(2)}) collective-permute-start(bf16[96,2304]{1,0:T(8,128)(2,1)S(1)} %add_convert_fusion.19), channel_id=1, source_target_pairs={{0,4},{2,6},{8,0},{10,2},{16,8},{18,10},{24,16},{26,18},{28,24},{3... | collective-permute-start | bytes 1327112 | tf_op jit(solution)/shard_map/ppermute | solution.py:253
  (135 other events, 1077.3 us)
Sparse Core Ops, SparseCore 0:
  16.0 92.3 all-gather.2
  110.0 156.0 all-gather.4

commit v3 on v2

--- a/solution.py
+++ b/solution.py
@@ -196,6 +196,9 @@
 
 LANES = 128
 BLOCK = 256
+TAIL_WIDTH = 768
+SELF_PIECES = 3
+QUERY_BLOCK = 128
 VMEM_BYTES = 60 * 1024 * 1024
 MESH = pl.DeviceIdType.MESH
 
@@ -473,6 +476,499 @@
     )
 
 
+def xor_place(index, bit):
+    return index + bit * (1 - 2 * (index // bit % 2))
+
+
+def ring_neighbours(seq_index, seq_count):
+    chips = seq_count // 2
+    chip, core = seq_index // 2, seq_index % 2
+    odd = chip % 2
+    place = (1 - odd) * (chip // 2) + odd * (chips - 1 - chip // 2)
+    found = []
+    for step in (1, chips - 1):
+        there = (place + step) % chips
+        upper = there // (chips // 2)
+        found.append(2 * ((1 - upper) * 2 * there + upper * (2 * (chips - 1 - there) + 1)) + core)
+    return found
+
+
+class ChipRing:
+    def __init__(self, seq_count, pieces, sends, lands, send_sem, recv_sem):
+        self.chips = seq_count // 2
+        self.far = self.chips // 2
+        self.pieces = pieces
+        self.sends, self.lands = sends, lands
+        self.send_sem, self.recv_sem = send_sem, recv_sem
+        self.sides = ring_neighbours(lax.axis_index("seq"), seq_count)
+        self.greeted = [{"seq": side} for side in self.sides]
+        half, width = pieces[0].shape
+        self.seg = half // self.chips
+        self.width, self.mid = width, width // 2
+
+    def copy(self, piece, side, hop):
+        mid, seg = self.mid, self.seg
+        if hop == 0:
+            source = self.pieces[piece].at[pl.ds(self.far * seg, seg), pl.ds(side * mid, mid)]
+            target = self.lands.at[piece, side, 0, :, pl.ds(0, mid)]
+        else:
+            source = self.sends.at[piece, side, hop - 1]
+            target = self.lands.at[piece, side, hop]
+        return pltpu.make_async_remote_copy(
+            src_ref=source,
+            dst_ref=target,
+            send_sem=self.send_sem.at[piece, side, hop],
+            recv_sem=self.recv_sem.at[piece, side, hop],
+            device_id={"seq": self.sides[side]},
+            device_id_type=MESH,
+        )
+
+    def start(self, piece):
+        for side in range(2):
+            self.copy(piece, side, 0).start()
+
+    def advance(self, piece, hop):
+        mid, seg = self.mid, self.seg
+        for side in range(2):
+            near = self.far - hop if side == 0 else self.far + hop
+            term = self.pieces[piece][near * seg : (near + 1) * seg, :].astype(jnp.float32)
+            self.copy(piece, side, hop - 1).wait_recv()
+            if hop == 1:
+                land = self.lands[piece, side, 0, :, :mid].astype(jnp.float32)
+                low = term[:, :mid] + land if side == 0 else term[:, :mid]
+                high = term[:, mid:] if side == 0 else term[:, mid:] + land
+                self.sends[piece, side, 0, :, :mid] = low.astype(jnp.bfloat16)
+                self.sends[piece, side, 0, :, mid:] = high.astype(jnp.bfloat16)
+            else:
+                land = self.lands[piece, side, hop - 1].astype(jnp.float32)
+                self.sends[piece, side, hop - 1] = (term + land).astype(jnp.bfloat16)
+            self.copy(piece, side, hop).start()
+
+    def total(self, piece):
+        total = self.pieces[piece][: self.seg, :].astype(jnp.float32)
+        for side in range(2):
+            self.copy(piece, side, self.far - 1).wait_recv()
+            total = total + self.lands[piece, side, self.far - 1].astype(jnp.float32)
+        return total
+
+    def close(self):
+        for piece in range(len(self.pieces)):
+            for side in range(2):
+                for hop in range(self.far):
+                    self.copy(piece, side, hop).wait_send()
+
+
+def ring_scratch(seq_count, pieces, seg, width):
+    far = seq_count // 4
+    return [
+        pltpu.VMEM((pieces, 2, far - 1, seg, width), jnp.bfloat16),
+        pltpu.VMEM((pieces, 2, far, seg, width), jnp.bfloat16),
+        pltpu.SemaphoreType.DMA((pieces, 2, far)),
+        pltpu.SemaphoreType.DMA((pieces, 2, far)),
+    ]
+
+
+def greet(devices):
+    barrier = pltpu.get_barrier_semaphore()
+    for device in devices:
+        pl.semaphore_signal(barrier, inc=1, device_id=device, device_id_type=MESH)
+    pl.semaphore_wait(barrier, len(devices))
+
+
+def tail_kernel(seq_count, head_count, ready_count, made_count, *refs):
+    ready = refs[:ready_count]
+    rows_t, columns, small, out, small_out = refs[ready_count : ready_count + 5]
+    (
+        mine,
+        away,
+        arrived,
+        small_send,
+        small_land,
+        core_send,
+        core_recv,
+        step_send,
+        step_recv,
+        *ring_refs,
+    ) = refs[ready_count + 5 :]
+    half = rows_t.shape[0] // 2
+    width = columns.shape[1] // made_count
+    pieces = [*ready, *(mine.at[made] for made in range(made_count))]
+    ring = ChipRing(seq_count, pieces, *ring_refs)
+    seq_index = lax.axis_index("seq")
+    head_index = lax.axis_index("head")
+    partners = []
+    bit = 1
+    while bit < seq_count:
+        partners.append({"seq": xor_place(seq_index, bit)})
+        bit *= 2
+    seq_steps = len(partners)
+    bit = 1
+    while bit < head_count:
+        partners.append({"head": xor_place(head_index, bit)})
+        bit *= 2
+    greet(ring.greeted + partners)
+
+    def core_copy(made):
+        return pltpu.make_async_remote_copy(
+            src_ref=away.at[made],
+            dst_ref=arrived.at[made],
+            send_sem=core_send.at[made],
+            recv_sem=core_recv.at[made],
+            device_id=partners[0],
+            device_id_type=MESH,
+        )
+
+    def step_copy(step):
+        rows = small.shape[0] if step < seq_steps else small.shape[0] // 2
+        return pltpu.make_async_remote_copy(
+            src_ref=small_send.at[step, pl.ds(0, rows)],
+            dst_ref=small_land.at[step, pl.ds(0, rows)],
+            send_sem=step_send.at[step],
+            recv_sem=step_recv.at[step],
+            device_id=partners[step],
+            device_id_type=MESH,
+        )
+
+    def step_on(step):
+        late = small.shape[0] // 2
+        if step == 0:
+            small_send[0] = small[...]
+        else:
+            step_copy(step - 1).wait_recv()
+            if step <= seq_steps:
+                total = small_send[step - 1] + small_land[step - 1]
+                if step == seq_steps:
+                    small_out[late:, :] = total[late:]
+                if step < len(partners):
+                    small_send[step] = total
+                else:
+                    small_out[:late, :] = total[:late]
+            else:
+                total = small_send[step - 1, :late] + small_land[step - 1, :late]
+                if step < len(partners):
+                    small_send[step, :late] = total
+                else:
+                    small_out[:late, :] = total
+        if step < len(partners):
+            step_copy(step).start()
+
+    for piece in range(ready_count):
+        ring.start(piece)
+    step_on(0)
+    for made in range(made_count):
+        cols = slice(made * width, (made + 1) * width)
+        away[made] = product(rows_t[half:, :], columns[:, cols]).astype(jnp.bfloat16)
+        core_copy(made).start()
+    for made in range(made_count):
+        cols = slice(made * width, (made + 1) * width)
+        term = product(rows_t[:half, :], columns[:, cols])
+        core_copy(made).wait_recv()
+        mine[made] = (term + arrived[made].astype(jnp.float32)).astype(jnp.bfloat16)
+        ring.start(ready_count + made)
+    done = 1
+    for hop in range(1, ring.far):
+        for piece in range(len(pieces)):
+            ring.advance(piece, hop)
+        while done <= len(partners) * hop // (ring.far - 1):
+            step_on(done)
+            done += 1
+    for piece in range(len(pieces)):
+        out[:, piece * width : (piece + 1) * width] = ring.total(piece)
+    for made in range(made_count):
+        core_copy(made).wait_send()
+    ring.close()
+    for step in range(len(partners)):
+        step_copy(step).wait_send()
+
+
+def tail_sums(ready, rows_t, columns, small, seq_count):
+    head_count = lax.axis_size("head")
+    chips = seq_count // 2
+    half = rows_t.shape[0] // 2
+    seg = half // chips
+    width = TAIL_WIDTH
+    made_count = columns.shape[1] // width
+    pieces = len(ready) + made_count
+    steps = (seq_count - 1).bit_length() + (head_count - 1).bit_length()
+    bf = jnp.bfloat16
+    return pl.pallas_call(
+        functools.partial(tail_kernel, seq_count, head_count, len(ready), made_count),
+        in_specs=[pl.BlockSpec(memory_space=pltpu.VMEM)] * (len(ready) + 3),
+        out_specs=[pl.BlockSpec(memory_space=pltpu.VMEM)] * 2,
+        out_shape=[
+            jax.ShapeDtypeStruct((seg, pieces * width), jnp.float32),
+            jax.ShapeDtypeStruct(small.shape, jnp.float32),
+        ],
+        scratch_shapes=[
+            pltpu.VMEM((made_count, half, width), bf),
+            pltpu.VMEM((made_count, half, width), bf),
+            pltpu.VMEM((made_count, half, width), bf),
+            pltpu.VMEM((steps, *small.shape), jnp.float32),
+            pltpu.VMEM((steps, *small.shape), jnp.float32),
+            pltpu.SemaphoreType.DMA((made_count,)),
+            pltpu.SemaphoreType.DMA((made_count,)),
+            pltpu.SemaphoreType.DMA((steps,)),
+            pltpu.SemaphoreType.DMA((steps,)),
+            *ring_scratch(seq_count, pieces, seg, width),
+        ],
+        compiler_params=pltpu.CompilerParams(
+            collective_id=2, has_side_effects=True, vmem_limit_bytes=VMEM_BYTES
+        ),
+        cost_estimate=pl.CostEstimate(
+            flops=2 * rows_t.shape[0] * rows_t.shape[1] * columns.shape[1],
+            bytes_accessed=16 * pieces * half * width,
+            transcendentals=0,
+        ),
+        name="tail_sums",
+    )(*ready, rows_t, columns, small)
+
+
+def turned_back(values, tables):
+    shift = ROT // 2
+    return (
+        values * tables[0]
+        + pltpu.roll(values, LANES - shift, 1) * tables[1]
+        - pltpu.roll(values, shift, 1) * tables[2]
+    )
+
+
+def self_back_kernel(seq_count, pairs, score_scale, ready_count, *refs):
+    (
+        query,
+        keys,
+        values,
+        stamp_key,
+        stamp_value,
+        grad_out,
+        logs,
+        key_ids,
+        query_ids,
+        query_slots,
+        tables,
+    ) = refs[:11]
+    ready = refs[11 : 11 + ready_count]
+    out, shares = refs[11 + ready_count : 13 + ready_count]
+    (
+        bias,
+        acc,
+        own,
+        halo,
+        halo_land,
+        halo_send_sem,
+        halo_recv_sem,
+        *ring_refs,
+    ) = refs[13 + ready_count :]
+    pair = pl.program_id(0)
+    rows = query.shape[0]
+    slots = stamp_key.shape[0]
+    span = QUERY_BLOCK + 2 * HALF
+    seq_index = lax.axis_index("seq")
+    before = (seq_index + seq_count - 1) % seq_count
+    behind = (seq_index + 1) % seq_count
+    ring = ChipRing(seq_count, list(ready), *ring_refs) if ready else None
+    hops = ring.far if ready else 1
+
+    def halo_copy(which, side):
+        return pltpu.make_async_remote_copy(
+            src_ref=halo.at[which, side],
+            dst_ref=halo_land.at[which, side],
+            send_sem=halo_send_sem.at[which, side],
+            recv_sem=halo_recv_sem.at[which, side],
+            device_id={"seq": before if side == 0 else behind},
+            device_id_type=MESH,
+        )
+
+    @pl.when(pair == 0)
+    def _():
+        greet((ring.greeted if ready else []) + [{"seq": before}, {"seq": behind}])
+        for piece in range(ready_count):
+            ring.start(piece)
+        for block in range(rows // QUERY_BLOCK):
+            start = block * QUERY_BLOCK
+            asked = query_ids[:, start : start + QUERY_BLOCK]
+            key_row = lax.broadcasted_iota(jnp.int32, (span, QUERY_BLOCK), 0)
+            query_row = lax.broadcasted_iota(jnp.int32, (span, QUERY_BLOCK), 1)
+            away = key_row - HALF - query_row
+            seen = (key_ids[start : start + span, :] == asked) & (jnp.abs(away) <= HALF)
+            bias[block, :span, :] = jnp.where(seen, 0.0, NEG)
+            slot_row = lax.broadcasted_iota(jnp.int32, (slots, QUERY_BLOCK), 0)
+            bias[block, span:, :] = jnp.where(
+                slot_row == query_slots[:, start : start + QUERY_BLOCK], 0.0, NEG
+            )
+
+    for hop in range(1, hops):
+
+        @pl.when(pair == hop)
+        def _():
+            for piece in range(ready_count):
+                ring.advance(piece, hop)
+
+    @pl.when(pair < pairs)
+    def _():
+        acc[...] = jnp.zeros_like(acc)
+        lane = lax.broadcasted_iota(jnp.int32, (1, LANES), 1)
+        stamp_k, stamp_v = stamp_key[...], stamp_value[...]
+        grad_queries = []
+        for block in range(rows // QUERY_BLOCK):
+            start = block * QUERY_BLOCK
+            near_k = jnp.concatenate([keys[0, start : start + span, :], stamp_k], axis=0)
+            near_v = jnp.concatenate([values[0, start : start + span, :], stamp_v], axis=0)
+            block_q = query[start : start + QUERY_BLOCK, :]
+            block_g = grad_out[start : start + QUERY_BLOCK, :]
+            grad_q = jnp.zeros((QUERY_BLOCK, LANES), jnp.float32)
+            grad_k = jnp.zeros((span + slots, LANES), jnp.float32)
+            grad_v = jnp.zeros((span + slots, LANES), jnp.float32)
+            for head in range(LANES // HD):
+                here = lane // HD == head
+                head_q = jnp.where(here, block_q, jnp.zeros_like(block_q))
+                head_g = jnp.where(here, block_g, jnp.zeros_like(block_g))
+                head_k = jnp.where(here, near_k, jnp.zeros_like(near_k))
+                scores = product_t(near_k, head_q) * score_scale + bias[block]
+                probs = jnp.exp(scores - logs[0, head : head + 1, start : start + QUERY_BLOCK])
+                grad_p = product_t(near_v, head_g)
+                dot = jnp.sum(probs * grad_p, axis=0, keepdims=True)
+                grad_s = (probs * (grad_p - dot)).astype(jnp.bfloat16)
+                grad_k = grad_k + product(grad_s, head_q)
+                grad_v = grad_v + product(probs.astype(jnp.bfloat16), head_g)
+                grad_q = grad_q + product_tn(grad_s, head_k)
+            grad_queries.append(grad_q)
+            acc[0, start : start + span, :] += grad_k[:span]
+            acc[1, start : start + span, :] += grad_v[:span]
+            acc[0, 2 * HALF + rows :, :] += grad_k[span:]
+            acc[1, 2 * HALF + rows :, :] += grad_v[span:]
+        column = pl.multiple_of(pair * LANES, LANES)
+        grad_q = jnp.concatenate(grad_queries, axis=0) * score_scale
+        out[:rows, pl.ds(column, LANES)] = turned_back(grad_q, tables).astype(jnp.bfloat16)
+        out[rows:, pl.ds(column, LANES)] = jnp.zeros((slots, LANES), jnp.bfloat16)
+        for which in range(2):
+            scale = score_scale if which == 0 else 1.0
+            shift = (which + 1) * pairs * LANES
+            halo[pair, 0, which] = (acc[which, :HALF, :] * scale).astype(jnp.bfloat16)
+            halo[pair, 1, which] = (acc[which, HALF + rows : 2 * HALF + rows, :] * scale).astype(
+                jnp.bfloat16
+            )
+            own[pair, which] = acc[which, HALF : HALF + rows, :] * scale
+            out[rows:, pl.ds(column + shift, LANES)] = (
+                acc[which, 2 * HALF + rows :, :] * scale
+            ).astype(jnp.bfloat16)
+        halo_copy(pair, 0).start()
+        halo_copy(pair, 1).start()
+
+    @pl.when(pair == pairs)
+    def _():
+        for which in range(pairs):
+            halo_copy(which, 0).wait_recv()
+            halo_copy(which, 1).wait_recv()
+            own[which, :, rows - HALF :, :] += halo_land[which, 0].astype(jnp.float32)
+            own[which, :, :HALF, :] += halo_land[which, 1].astype(jnp.float32)
+            column = (pairs + which) * LANES
+            out[:rows, column : column + LANES] = turned_back(own[which, 0], tables).astype(
+                jnp.bfloat16
+            )
+            column = (2 * pairs + which) * LANES
+            out[:rows, column : column + LANES] = own[which, 1].astype(jnp.bfloat16)
+        if not ready:
+            shares[...] = jnp.zeros_like(shares)
+        for piece in range(ready_count):
+            shares[:, piece * ring.width : (piece + 1) * ring.width] = ring.total(piece)
+        if ready:
+            ring.close()
+        for which in range(pairs):
+            halo_copy(which, 0).wait_send()
+            halo_copy(which, 1).wait_send()
+
+
+def self_back(
+    query, near, stamps, grad_out, logs, key_ids, query_ids, query_slots, tables, ready, score_scale, seq_count
+):
+    rows, part = query.shape
+    slots = stamps.shape[0]
+    pairs = part // LANES
+    window = near.shape[1]
+    half, width = ready[0].shape if ready else (8 * seq_count // 2, LANES)
+    seg = half // (seq_count // 2)
+    share_width = max(len(ready), 1) * width
+    span = QUERY_BLOCK + 2 * HALF
+    blocks = rows // QUERY_BLOCK
+    last = pairs - 1
+
+    def at(first, shape, lead=()):
+        return pl.BlockSpec(shape, lambda i: (*lead, 0, first + jnp.minimum(i, last)))
+
+    def whole(shape):
+        return pl.BlockSpec(shape, lambda i: (0,) * len(shape), pipeline_mode=pl.Buffered(1))
+
+    return pl.pallas_call(
+        functools.partial(self_back_kernel, seq_count, pairs, score_scale, len(ready)),
+        grid=(pairs + 1,),
+        in_specs=[
+            at(0, (rows, LANES)),
+            at(0, (1, window, LANES), (0,)),
+            at(0, (1, window, LANES), (1,)),
+            at(pairs, (slots, LANES)),
+            at(2 * pairs, (slots, LANES)),
+            at(0, (rows, LANES)),
+            pl.BlockSpec((1, LANES // HD, rows), lambda i: (jnp.minimum(i, last), 0, 0)),
+            whole((window, 1)),
+            whole((1, rows)),
+            whole((1, rows)),
+            whole((3, rows, LANES)),
+            *(whole((half, width)) for _ in ready),
+        ],
+        out_specs=[
+            pl.BlockSpec((rows + slots, 3 * part), lambda i: (0, 0)),
+            pl.BlockSpec((seg, share_width), lambda i: (0, 0)),
+        ],
+        out_shape=[
+            jax.ShapeDtypeStruct((rows + slots, 3 * part), jnp.bfloat16),
+            jax.ShapeDtypeStruct((seg, share_width), jnp.float32),
+        ],
+        scratch_shapes=[
+            pltpu.VMEM((blocks, span + slots, QUERY_BLOCK), jnp.float32),
+            pltpu.VMEM((2, window + slots, LANES), jnp.float32),
+            pltpu.VMEM((pairs, 2, rows, LANES), jnp.float32),
+            pltpu.VMEM((pairs, 2, 2, HALF, LANES), jnp.bfloat16),
+            pltpu.VMEM((pairs, 2, 2, HALF, LANES), jnp.bfloat16),
+            pltpu.SemaphoreType.DMA((pairs, 2)),
+            pltpu.SemaphoreType.DMA((pairs, 2)),
+            *(ring_scratch(seq_count, len(ready), seg, width) if ready else []),
+        ],
+        compiler_params=pltpu.CompilerParams(
+            collective_id=3, has_side_effects=True, vmem_limit_bytes=VMEM_BYTES
+        ),
+        cost_estimate=pl.CostEstimate(
+            flops=10 * rows * window * part,
+            bytes_accessed=16 * len(ready) * half * width,
+            transcendentals=rows * window * part // HD,
+        ),
+        name="self_back",
+    )(
+        query,
+        near,
+        near,
+        stamps,
+        stamps,
+        grad_out,
+        logs.reshape(pairs, LANES // HD, rows),
+        key_ids[:, None],
+        query_ids[None],
+        query_slots[None],
+        tables,
+        *ready,
+    )
+
+
+def tail_or_rings(ready, rows_t, columns, small, seq_count):
+    if rows_t.shape[0] // seq_count % 16 == 0:
+        return tail_sums(ready, rows_t, columns, small, seq_count)
+    made = core_sum(rows_t, columns, seq_count)
+    ring = Ring(side_by_side([*ready, made], seq_count // 2), seq_count)
+    late = small.shape[0] // 2
+    small = all_sum(small, ("seq",))
+    small = jnp.concatenate([all_sum(small[:late], ("head",)), small[late:]], axis=0)
+    return ring.finish(), small
+
+
 def head_total(partial_sum):
     low = partial_sum
     if low.dtype != jnp.bfloat16:
@@ -529,6 +1025,8 @@
     ctx_width = prompt.shape[2]
     head_count = part // HD
     chips = seq_count // 2
+    bias_rows = 2 * hidden_width // width
+    small_rows = -(-max(clip_total + 1, bias_rows + 3) // 8) * 8
     order = owner_matrix(width, seq_index, seq_count)
 
     def ordered(matrix, by=order):
@@ -580,9 +1078,9 @@
     near_key_h = near[0].reshape(window, head_count, HD)
     near_value_h = near[1].reshape(window, head_count, HD)
     query_h = query_rows.reshape(local_rows, head_count, HD)
-    stamps = qkv[local_rows:stamp_end].astype(jnp.bfloat16)
-    stamp_key_h = stamps[:, part : 2 * part].reshape(slot_count, head_count, HD)
-    stamp_value_h = stamps[:, 2 * part :].reshape(slot_count, head_count, HD)
+    stamps = qkv[local_rows:].astype(jnp.bfloat16)
+    stamp_key_h = stamps[:slot_count, part : 2 * part].reshape(slot_count, head_count, HD)
+    stamp_value_h = stamps[:slot_count, 2 * part :].reshape(slot_count, head_count, HD)
 
     query_pos = jnp.arange(local_rows, dtype=jnp.int32)
     key_pos = jnp.arange(window, dtype=jnp.int32) - HALF
@@ -622,10 +1120,13 @@
         up_bias,
     )
     grad_normed_three = head_total(grad_normed_low)
+    grad_normed_three, glu_out = lax.optimization_barrier((grad_normed_three, glu_out))
     result = (h_two + head_total(glu_out) + bias_f).astype(jnp.bfloat16)
     glu_ring = Ring(
         lambda near: glu_sums[:, near * gain_rows : (near + 1) * gain_rows], seq_count
     )
+    grad_normed_three = glu_ring.after(grad_normed_three)
+    glu_ring.step()
     grad_top = out_grad.astype(jnp.float32)
     gain_three_term = jnp.sum(grad_normed_three * normal_three, axis=0)
     down_bias_term = jnp.sum(grad_top, axis=0)
@@ -635,8 +1136,6 @@
     grad_cross_h = product(grad_two_low, c_out).astype(jnp.bfloat16)
     grad_cross_h = grad_cross_h.reshape(local_rows, head_count, HD)
     cross_out_sum = core_sum(ordered(grad_two_low), cross_mixed, seq_count)
-    grad_cross_h = glu_ring.after(grad_cross_h)
-    glu_ring.step()
     grad_cross_q, ctx_key_grads, ctx_value_grads = attend_backward(
         cross_h, cross_keys, score_scale, cross_logs, grad_cross_h
     )
@@ -644,75 +1143,54 @@
     ctx_grads = jnp.concatenate(
         [ctx_key_grads[0].reshape(-1, part), ctx_value_grads[0].reshape(-1, part)], axis=1
     ).astype(jnp.bfloat16)
+    grad_cross_query = glu_ring.after(grad_cross_query)
+    glu_ring.step()
     grad_normed_two = head_total(product_t(grad_cross_query, c_query))
-    grad_normed_two = glu_ring.after(grad_normed_two)
-    glu_ring.step()
     cross_query_sum = core_sum(ordered(normed_two), grad_cross_query, seq_count)
     ctx_order = owner_matrix(ctx_width, seq_index, seq_count)
     ctx_sum = core_sum(ordered(context_rows, ctx_order), ctx_grads, seq_count)
     gain_two_term = jnp.sum(grad_normed_two * normal_two, axis=0)
     grad_h_one = grad_h_two + norm_back(grad_normed_two, normal_two, inverse_two, gain_two_f)
     grad_one_low = grad_h_one.astype(jnp.bfloat16)
-    grad_attn_h = product(grad_one_low, w_out).astype(jnp.bfloat16)
-    grad_attn_h = grad_attn_h.reshape(local_rows, head_count, HD)
+    grad_attn = product(grad_one_low, w_out).astype(jnp.bfloat16)
     out_sum = core_sum(ordered(grad_one_low), attn_mixed, seq_count)
-    joined_sums = side_by_side([cross_out_sum, cross_query_sum, out_sum], chips)
-
-    def cross_term(near):
-        ctx_block = block_of(ctx_sum, near, chips)
-        ctx_block = jnp.concatenate([ctx_block[:, :part], ctx_block[:, part:]], axis=0)
-        return jnp.concatenate([joined_sums(near), ctx_block], axis=1)
-
-    grad_attn_h = glu_ring.after(grad_attn_h)
+    ctx_sum = jnp.transpose(ctx_sum.reshape(chips, ctx_rows, 2, part), (0, 2, 1, 3))
+    ready_sums = [cross_out_sum, cross_query_sum, out_sum, ctx_sum.reshape(width // 2, part)]
+
+    grad_attn = glu_ring.after(grad_attn)
     glu_ring.step()
-
-    grad_query, grad_keys, grad_values = attend_backward(
-        query_h, self_keys, score_scale, self_logs, grad_attn_h
-    )
-    near_grads = jnp.stack([grad_keys[0], grad_values[0]]).reshape(2, window, part)
-    near_grads = glu_ring.after(near_grads)
+    if gain_rows % 16 == 0:
+        early_sums, ready_sums = ready_sums[:SELF_PIECES], ready_sums[SELF_PIECES:]
+    else:
+        early_sums = []
+    ones = jnp.ones((local_rows, HD - ROT), jnp.float32)
+    flat = jnp.zeros((local_rows, ROT // 2), jnp.float32)
+    low_side = [sin_table, flat, 0 * ones]
+    high_side = [flat, sin_table, 0 * ones]
+    tables = jnp.stack(
+        [
+            jnp.tile(jnp.concatenate(each, axis=1), (1, LANES // HD))
+            for each in ([cos_table, cos_table, ones], low_side, high_side)
+        ]
+    )
+    grad_qkv, early_share = self_back(
+        query_rows,
+        near,
+        stamps,
+        grad_attn,
+        self_logs,
+        near_ids,
+        own_ids,
+        own_slot,
+        tables,
+        early_sums,
+        score_scale,
+        seq_count,
+    )
+    grad_qkv = glu_ring.after(grad_qkv)
     glu_share = glu_ring.finish()
-    cross_ring = Ring(cross_term, seq_count)
-    cross_share = cross_ring.finish()
-    from_above = passed_along(near_grads[:, :HALF].astype(jnp.bfloat16), "seq", -1).astype(
-        jnp.float32
-    )
-    from_below = passed_along(
-        near_grads[:, HALF + local_rows :].astype(jnp.bfloat16), "seq", 1
-    ).astype(jnp.float32)
-    own_grads = (
-        near_grads[:, HALF : HALF + local_rows]
-        + jnp.pad(from_below, ((0, 0), (0, local_rows - HALF), (0, 0)))
-        + jnp.pad(from_above, ((0, 0), (local_rows - HALF, 0), (0, 0)))
-    )
-    grad_query_rows = rotate(grad_query.reshape(local_rows, part), cos_table, -sin_table)
-    grad_key_rows = rotate(own_grads[0], cos_table, -sin_table)
-    stamp_grads = jnp.concatenate(
-        [
-            jnp.zeros((slot_count, part), jnp.float32),
-            grad_keys[1].reshape(slot_count, part),
-            grad_values[1].reshape(slot_count, part),
-        ],
-        axis=1,
-    )
-    frame_grads = jnp.concatenate([grad_query_rows, grad_key_rows, own_grads[1]], axis=1)
-    grad_qkv = jnp.concatenate(
-        [
-            frame_grads.astype(jnp.bfloat16),
-            jnp.pad(stamp_grads, ((0, pad_rows), (0, 0))).astype(jnp.bfloat16),
-        ],
-        axis=0,
-    )
     grad_normed_all = product_t(grad_qkv, w_qkv)
     grad_normed_one = head_total(grad_normed_all[:local_rows])
-    qkv_ring = Ring(
-        side_by_side([core_sum(ordered(normed_one), grad_qkv, seq_count)], chips), seq_count
-    )
-    qkv_share = qkv_ring.finish()
-    cross_out_share = cross_share[:, :part]
-    cross_query_share = cross_share[:, part : 2 * part]
-    out_share = cross_share[:, 2 * part : 3 * part]
-    ctx_share = cross_share[:, 3 * part :]
     gain_one_term = jnp.sum(grad_normed_all[:local_rows] * normal_one[:local_rows], axis=0)
     frames_grad = (
         grad_h_one
@@ -722,18 +1200,36 @@
     stamp_full = lax.dynamic_update_slice_in_dim(
         jnp.zeros((clip_total, width), jnp.float32), grad_normed_all[local_rows:stamp_end], base_clip, 0
     )
-    late = all_sum(jnp.concatenate([stamp_full, gain_one_term[None]], axis=0), ("seq", "head"))
+    small = jnp.concatenate(
+        [
+            jnp.pad(
+                jnp.concatenate([stamp_full, gain_one_term[None]], axis=0),
+                ((0, small_rows - clip_total - 1), (0, 0)),
+            ),
+            jnp.pad(
+                jnp.concatenate(
+                    [
+                        bias_local.reshape(-1, width),
+                        jnp.stack([gain_two_term, gain_three_term, down_bias_term]),
+                    ],
+                    axis=0,
+                ),
+                ((0, small_rows - bias_rows - 3), (0, 0)),
+            ),
+        ],
+        axis=0,
+    )
+    shares, small = tail_or_rings(ready_sums, ordered(normed_one), grad_qkv, small, seq_count)
+    if gain_rows % 16 == 0:
+        shares = jnp.concatenate([early_share, shares], axis=1)
+    cross_out_share = shares[:, :part]
+    cross_query_share = shares[:, part : 2 * part]
+    out_share = shares[:, 2 * part : 3 * part]
+    ctx_share = shares[:, 3 * part : 4 * part]
+    qkv_share = shares[:, 4 * part :]
+    late = small[: clip_total + 1]
+    early = small[small_rows : small_rows + bias_rows + 3]
     stamp_sum = late[:clip_total]
-    early = all_sum(
-        jnp.concatenate(
-            [
-                bias_local.reshape(-1, width),
-                jnp.stack([gain_two_term, gain_three_term, down_bias_term]),
-            ],
-            axis=0,
-        ),
-        ("seq",),
-    )
     own_bias = early[:-3].reshape(2, hidden_width)
     every_out, every_normal, every_inverse = layer_norm_parts(
         time_token.astype(jnp.float32), gain_one_f

time: 753 us -> 678 us (0.900)
  Pallas kernels: 59.8 us -> 197 us
  waiting for transfers between devices: 306 us -> 195 us
  starting transfers between devices: 77.8 us -> 31.2 us
  matrix products: 126 us -> 95.8 us
  other arithmetic: 102 us -> 72.2 us
    pallas_call x0 -> x2, Pallas kernels: none -> 137 us  [the longest x1 75.1 us: self_back(): pl.pallas_call(functools.partial(self_back_kernel, seq_count, pairs, scor...]
    ppermute x11 -> x0, waiting for transfers between devices: 44.8 us -> none  [the longest x9 44.8 us: all_sum(): lax.ppermute(values, axis, [(index, index ^ bit) for index in range(count)])]
    ppermute x12 -> x4, waiting for transfers between devices: 35.3 us -> 0.01 us  [send(): lax.ppermute(backward.astype(jnp.bfloat16), 'seq', self.behind)]
    ppermute x6, waiting for transfers between devices: 96.2 us -> 67.2 us  [head_total(): total = total + lax.ppermute(low, 'head', pairs).astype(jnp.float32)]
    ppermute x12 -> x4, starting transfers between devices: 28.1 us -> 9 us  [send(): lax.ppermute(backward.astype(jnp.bfloat16), 'seq', self.behind)]
    ppermute x5 -> x4, starting transfers between devices: 15.2 us -> 0.58 us  [over_core(): lax.ppermute(values, 'seq', [(index, index ^ 1) for index in range(seq_co...]
    ppermute x12 -> x4, waiting for transfers between devices: 25.8 us -> 11.7 us  [send(): self.onward = lax.ppermute(onward.astype(jnp.bfloat16), 'seq', self.ahead)]
    dot_general x3 -> x1, matrix products: 16.8 us -> 3.47 us  [attend_backward(): jnp.einsum('qhd,khd->hqk', grad_h, key_part[1], preferred_element_type=jn...]
  transfers between devices with their start and end apart: 50 -> 22, of which waited for: 24 -> 10; matrix products, arithmetic and copies ran while one was open for 34% -> 29% of each run, Pallas kernels for 0% -> 11%
where the time goes in v3:
time: 678 us; the launch traced here: 668 us
  Pallas kernels  197 us (29%)
  waiting for transfers between devices  195 us (29%)
  matrix products  95.8 us (14%)
  other arithmetic  72.2 us (11%)
  local copies, waits for them, and re-layouts  60.9 us (9%)
  starting transfers between devices  31.2 us (5%)
  between operations  16.5 us (2%)
    all_gather x2, waiting for transfers between devices, low_gather(): return lax.all_gather(block.astype(jnp.bfloat16), 'seq', axis=0, tiled=True)  116 us
    pallas_call x1, Pallas kernels, self_back(): pl.pallas_call(functools.partial(self_back_kernel, seq_count, pairs, scor...  75.1 us
    ppermute x6, waiting for transfers between devices, head_total(): total = total + lax.ppermute(low, 'head', pairs).astype(jnp.float32)  67.2 us
    pallas_call x1, Pallas kernels, tail_sums(): pl.pallas_call(functools.partial(tail_kernel, seq_count, head_count, len(...  61.9 us
    pallas_call x1, Pallas kernels, glu_layer(): pl.pallas_call(functools.partial(glu_kernel, blocks), grid=(blocks + 1,),...  59.9 us
    dot_general x11, matrix products, product_t(): lax.dot_general(matrix_a, matrix_b, (((1,), (1,)), ((), ())), preferred_e...  39.8 us
    dot_general x14, matrix products, product(): return jnp.dot(matrix_a, matrix_b, preferred_element_type=jnp.float32)  37.2 us
  transfers between devices with their start and end apart: 22, of which 10 were waited for; matrix products, arithmetic and copies ran while one was open for 29% of the time, Pallas kernels for 11%

profile of v3, /device:TPU:0, one launch (start us, length us, event | category | flops | bytes accessed | tf_op | source)
XLA Modules:
  0.0 668.0 jit_solution(2744454107199478928)
XLA Ops:
  27.2 3.7 fusion.23.top_t
  30.9 77.5 %all-gather.3.cloned.1.call-done = bf16[1536,5504]{1,0:T(8,128)(2,1)} async-done(((bf16[96,5504]{1,0:T(8,128)(2,1)}), bf16[1536,5504]{1,0:T(8,128)(2,1)}) %all-gather.3.cloned.1.call-update) | async-done | bytes 16908304 | tf_op jit(solution)/shard_map/all_gather | solution.py:985
  109.5 1.9 slice_reduce_fusion
  111.4 7.4 %fusion.153 = (bf16[400,2304]{1,0:T(8,128)(2,1)}, f32[400,2304]{1,0:T(8,128)S(1)}) fusion(bf16[1536,5504]{1,0:T(8,128)(2,1)} %all-gather.3.cloned.1.call-done, f32[1536]{0:T(1024)S(1)} %get-tuple-element.76, f32[400]{0:T(512)S(1)} %add_rsqrt_fusion.2, f32[400]{0:T(512)S(1)} %broadcast_multiply_fusion.8, ...), kind=kOutput, calls=%fused_computation.322 | convolution fusion | flops 2838220800 | bytes 13802624 | tf_op jit(solution)/shard_map/dot_general | solution.py:83
  124.0 3.1 collective-permute-start
  128.8 2.8 copy.100
  136.8 1.9 fusion.146
  139.3 2.6 copy.101
  141.9 2.5 copy.99
  144.4 4.5 fusion
  149.0 4.5 fusion.1
  154.5 6.1 fusion.47
  160.6 4.3 convolution_convert_fusion.3
  167.1 1.8 fusion.141
  174.0 2.4 convolution_convert_fusion.8
  177.6 3.9 collective-permute-done.2
  181.4 2.9 fusion.143
  185.8 3.7 fusion.52
  195.2 4.1 convolution_convert_fusion.2
  204.8 1.8 subtract_multiply_fusion
  209.2 3.7 fusion.21
  213.0 2.9 copy.118.refs_1_
  216.5 2.9 collective-permute-done.3
  219.4 2.8 fusion.142
  224.4 3.7 fusion.22.normed_t
  228.1 38.1 %all-gather.5.cloned.1.call-done.w_gate.w_up.w_down = bf16[1536,9216]{1,0:T(8,128)(2,1)} async-done(((bf16[96,9216]{1,0:T(8,128)(2,1)}), bf16[1536,9216]{1,0:T(8,128)(2,1)}) %all-gather.5.cloned.1.call-update) | async-done | bytes 28311568 | tf_op jit(solution)/shard_map/all_gather | solution.py:985
  266.2 59.9 %glu_layer.1 = (bf16[384,1536]{1,0:T(8,128)(2,1)}, bf16[384,1536]{1,0:T(8,128)(2,1)}, bf16[3,768,3072]{2,1,0:T(8,128)(2,1)}, f32[2,3072]{1,0:T(2,128)}) custom-call(bf16[384,1536]{1,0:T(8,128)(2,1)} %copy-done.29, bf16[1536,384]{1,0:T(8,128)(2,1)} %fusion.22.normed_t, bf16[384,1536]{1,0:T(8,128)(2,1)} %top.1, bf16[1536,384]{1,0:T(8,128)(2,1)} %fusion.23.top_t, ...), custom_call_target="tpu_custom_call" | custom-call | flops 32614907904 | bytes 56623104 | tf_op jit(solution)/shard_map/glu_layer/pallas_call | solution.py:424
  326.1 1.8 collective-permute-start.4
  327.9 2.8 fusion.144
  330.7 4.5 collective-permute-start.7
  335.2 3.8 fusion.25
  340.3 14.1 %collective-permute-done.4 = bf16[384,1536]{1,0:T(8,128)(2,1)} collective-permute-done((bf16[384,1536]{1,0:T(8,128)(2,1)}, bf16[384,1536]{1,0:T(8,128)(2,1)}, u32[]{:S(2)}, u32[]{:S(2)}) %collective-permute-start.4) | collective-permute-done | bytes 1179680 | tf_op jit(solution)/shard_map/ppermute | solution.py:980
  354.4 2.0 convert_add_fusion.3
  358.2 5.3 add_convert_fusion.4
  365.0 3.3 collective-permute-start.9
  370.0 13.5 %collective-permute-done.5 = bf16[384,1536]{1,0:T(8,128)(2,1)S(1)} collective-permute-done((bf16[384,1536]{1,0:T(8,128)(2,1)S(1)}, bf16[384,1536]{1,0:T(8,128)(2,1)S(1)}, u32[]{:S(2)}, u32[]{:S(2)}) %collective-permute-start.5) | collective-permute-done | bytes 1179680 | tf_op jit(solution)/shard_map/ppermute | solution.py:980
  383.5 3.0 convert_add_fusion.1
  386.5 3.7 fusion.24
  392.7 2.9 convolution_convert_fusion.6
  396.2 3.5 multiply_reduce_fusion
  404.5 2.0 collective-permute-done.8
  406.5 2.8 convolution_convert_fusion.1
  409.7 3.4 add_convert_fusion.2
  413.2 3.9 collective-permute-start.11
  417.9 1.8 convolution_convert_fusion.5
  419.8 16.0 %collective-permute-done.10 = bf16[384,1536]{1,0:T(8,128)(2,1)S(1)} collective-permute-done((bf16[384,1536]{1,0:T(8,128)(2,1)S(1)}, bf16[384,1536]{1,0:T(8,128)(2,1)S(1)}, u32[]{:S(2)}, u32[]{:S(2)}) %collective-permute-start.10) | collective-permute-done | bytes 1179680 | tf_op jit(solution)/shard_map/ppermute | solution.py:980
  438.0 4.4 fusion.49.refs_5_
  442.4 2.7 fusion.26
  445.2 1.9 convolution_convert_fusion.4
  447.0 9.6 %collective-permute-done.11 = bf16[3,96,3072]{2,1,0:T(8,128)(2,1)S(1)} collective-permute-done((bf16[3,96,3072]{2,1,0:T(8,128)(2,1)S(1)}, bf16[3,96,3072]{2,1,0:T(8,128)(2,1)S(1)}, u32[]{:S(2)}, u32[]{:S(2)}) %collective-permute-start.11) | collective-permute-done | bytes 1769504 | tf_op jit(solution)/shard_map/ppermute | solution.py:255
  456.7 3.1 add_convert_fusion
  459.8 3.8 collective-permute-start.16
  466.7 3.1 add_convert_fusion.10.refs_11_
  469.9 3.2 add_convert_fusion.9.refs_12_
  473.1 3.1 add_convert_fusion.8.refs_13_
  476.2 75.1 %self_back.1 = (bf16[400,2304]{1,0:T(8,128)(2,1)}, f32[96,2304]{1,0:T(8,128)}) custom-call(bf16[384,768]{1,0:T(8,128)(2,1)} %copy.113.refs_0_, bf16[2,896,768]{2,1,0:T(8,128)(2,1)} %copy-done.6, bf16[2,896,768]{2,1,0:T(8,128)(2,1)} %copy-done.6, bf16[16,2304]{1,0:T(8,128)(2,1)} %slice.341.refs_3_.refs_4_, bf16[16,2304]{1,0:T(8,128)(2,1)} %slice.341.refs_3_.refs_4_, ...), custom_call_target="tpu_custom_call" | custom-call | flops 2642411520 | bytes 28311552 | tf_op jit(solution)/shard_map/self_back/pallas_call | solution.py:901
  551.3 2.1 fusion.151
  553.4 5.9 fusion.9
  560.1 5.3 convert_add_fusion
  565.8 4.0 slice_bitcast_fusion
  569.8 16.8 %collective-permute-done.18 = bf16[384,1536]{1,0:T(8,128)(2,1)S(1)} collective-permute-done((bf16[384,1536]{1,0:T(8,128)(2,1)S(1)}, bf16[384,1536]{1,0:T(8,128)(2,1)S(1)}, u32[]{:S(2)}, u32[]{:S(2)}) %collective-permute-start.18) | collective-permute-done | bytes 1179680 | tf_op jit(solution)/shard_map/ppermute | solution.py:980
  588.1 61.9 %tail_sums.1 = (f32[96,3072]{1,0:T(8,128)}, f32[16,1536]{1,0:T(8,128)}) custom-call(bf16[768,768]{1,0:T(8,128)(2,1)} %bitcast.131, bf16[1536,400]{1,0:T(8,128)(2,1)} %copy.118.refs_1_, bf16[400,2304]{1,0:T(8,128)(2,1)} %get-tuple-element.57.refs_2_, f32[16,1536]{1,0:T(8,128)} %pad_maximum_fusion.10.refs_3_), custom_call_target="tpu_custom_call" | custom-call | flops 2831155200 | bytes 37748736 | tf_op jit(solution)/shard_map/tail_sums/pallas_call | solution.py:694
  650.1 2.1 fusion.150
  656.8 4.2 add_convert_fusion.7
  (380 shorter events, 87.5 us)
Async XLA Ops:
  7.2 14.0 %copy-start = (bf16[6,128,768]{2,1,0:T(8,128)(2,1)S(1)}, bf16[6,128,768]{2,1,0:T(8,128)(2,1)}, u32[]{:S(2)}) copy-start(bf16[6,128,768]{2,1,0:T(8,128)(2,1)} %param.24) | copy-start | bytes 3538948
  7.2 8.7 %copy-start.26 = (f32[96,3072]{1,0:T(8,128)S(1)}, f32[96,3072]{1,0:T(8,128)}, u32[]{:S(2)}) copy-start(f32[96,3072]{1,0:T(8,128)} %param.39) | copy-start | bytes 3538948
  7.2 101.2 %all-gather.3.cloned.1.call-start = ((), (), s32[]{:S(2)}) async-start(), calls=%async_computation | async-start | bytes 17965056 | tf_op jit(solution)/shard_map/all_gather | solution.py:985
  15.9 250.3 %all-gather.5.cloned.1.call-start = ((), (), s32[]{:S(2)}) async-start(), calls=%async_computation.1 | async-start | bytes 30081024 | tf_op jit(solution)/shard_map/all_gather | solution.py:985
  19.1 8.0 %copy-start.80 = (s32[384]{0:T(512)}, s32[384]{0:T(512)S(1)}, u32[]{:S(2)}) copy-start(s32[384]{0:T(512)S(1)} %dynamic_slice.15) | copy-start | bytes 4612
  20.9 6.3 copy-start.67
  21.0 6.2 copy-start.62
  22.3 89.1 %copy-start.78 = (f32[400]{0:T(512)}, f32[400]{0:T(512)S(1)}, u32[]{:S(2)}) copy-start(f32[400]{0:T(512)S(1)} %broadcast_multiply_fusion.8) | copy-start | bytes 4804
  22.8 88.6 %copy-start.73 = (f32[400]{0:T(512)}, f32[400]{0:T(512)S(1)}, u32[]{:S(2)}) copy-start(f32[400]{0:T(512)S(1)} %add_rsqrt_fusion.2) | copy-start | bytes 4804
  23.0 7.9 %copy-start.41 = (f32[384,16]{0,1:T(8,128)}, f32[384,16]{0,1:T(8,128)S(1)}, u32[]{:S(2)}) copy-start(f32[384,16]{0,1:T(8,128)S(1)} %get-tuple-element.126) | copy-start | bytes 73732
  23.0 7.9 %copy-start.43 = (f32[384,16]{0,1:T(8,128)}, f32[384,16]{0,1:T(8,128)S(1)}, u32[]{:S(2)}) copy-start(f32[384,16]{0,1:T(8,128)S(1)} %get-tuple-element.127) | copy-start | bytes 73732
  122.7 10.9 %copy-start.42 = (f32[384,16]{0,1:T(8,128)S(1)}, f32[384,16]{0,1:T(8,128)}, u32[]{:S(2)}) copy-start(f32[384,16]{0,1:T(8,128)} %copy-done.41) | copy-start | bytes 73732
  122.7 10.9 %copy-start.44 = (f32[384,16]{0,1:T(8,128)S(1)}, f32[384,16]{0,1:T(8,128)}, u32[]{:S(2)}) copy-start(f32[384,16]{0,1:T(8,128)} %copy-done.43) | copy-start | bytes 73732
  124.0 11.3 %collective-permute-start = (bf16[2,256,768]{2,1,0:T(8,128)(2,1)}, bf16[2,256,768]{2,1,0:T(8,128)(2,1)}, u32[]{:S(2)}, u32[]{:S(2)}) collective-permute-start(bf16[2,256,768]{2,1,0:T(8,128)(2,1)} %get-tuple-element.117), channel_id=1, source_target_pairs={{0,2},{2,4},{4,6},{6,8},{8,10},{10,12},{12,14},{14,16},{16,18},{18... | collective-permute-start | bytes 2359304 | tf_op jit(solution)/shard_map/ppermute | solution.py:25
  127.0 8.2 %collective-permute-start.1 = (bf16[2,256,768]{2,1,0:T(8,128)(2,1)}, bf16[2,256,768]{2,1,0:T(8,128)(2,1)}, u32[]{:S(2)}, u32[]{:S(2)}) collective-permute-start(bf16[2,256,768]{2,1,0:T(8,128)(2,1)} %get-tuple-element.118), channel_id=1, source_target_pairs={{2,0},{4,2},{6,4},{8,6},{10,8},{12,10},{14,12},{16,14},{18,16},{20... | collective-permute-start | bytes 2359304 | tf_op jit(solution)/shard_map/ppermute | solution.py:28
  164.9 16.5 %collective-permute-start.2 = (bf16[384,1536]{1,0:T(8,128)(2,1)}, bf16[384,1536]{1,0:T(8,128)(2,1)}, u32[]{:S(2)}, u32[]{:S(2)}) collective-permute-start(bf16[384,1536]{1,0:T(8,128)(2,1)} %convolution_convert_fusion.3), channel_id=1, source_target_pairs={{0,1},{1,0},{2,3},{3,2},{4,5},{5,4},{6,7},{7,6},{8,9},{9,8},{10,11... | collective-permute-start | bytes 3538952 | tf_op jit(solution)/shard_map/ppermute | solution.py:980
  174.0 17.0 %copy-start.14 = (bf16[256,768]{0,1:T(8,128)(2,1)}, bf16[256,768]{0,1:T(8,128)(2,1)S(1)}, u32[]{:S(2)}) copy-start(bf16[256,768]{0,1:T(8,128)(2,1)S(1)} %copy.106) | copy-start | bytes 1179652
  177.6 15.0 %copy-start.19 = (bf16[256,768]{0,1:T(8,128)(2,1)}, bf16[256,768]{0,1:T(8,128)(2,1)S(1)}, u32[]{:S(2)}) copy-start(bf16[256,768]{0,1:T(8,128)(2,1)S(1)} %copy.104) | copy-start | bytes 1179652
  184.3 150.9 %copy-start.65 = (f32[384]{0:T(512)}, f32[384]{0:T(512)S(1)}, u32[]{:S(2)}) copy-start(f32[384]{0:T(512)S(1)} %broadcast_multiply_fusion.7) | copy-start | bytes 4612
  184.7 150.5 %copy-start.76 = (f32[384]{0:T(512)}, f32[384]{0:T(512)S(1)}, u32[]{:S(2)}) copy-start(f32[384]{0:T(512)S(1)} %add_rsqrt_fusion.1) | copy-start | bytes 4612
  195.1 6.8 %copy-start.81 = (s32[384]{0:T(512)S(1)}, s32[384]{0:T(512)}, u32[]{:S(2)}) copy-start(s32[384]{0:T(512)} %copy-done.80) | copy-start | bytes 4612
  195.1 7.3 %copy-start.63 = (s32[896]{0:T(1024)S(1)}, s32[896]{0:T(1024)}, u32[]{:S(2)}) copy-start(s32[896]{0:T(1024)} %copy-done.62) | copy-start | bytes 10756
  195.2 8.3 %copy-start.40 = (f32[384,64]{0,1:T(8,128)S(1)}, f32[384,64]{0,1:T(8,128)}, u32[]{:S(2)}) copy-start(f32[384,64]{0,1:T(8,128)} %get-tuple-element.146) | copy-start | bytes 294916
  195.2 8.4 %copy-start.39 = (f32[384,64]{0,1:T(8,128)S(1)}, f32[384,64]{0,1:T(8,128)}, u32[]{:S(2)}) copy-start(f32[384,64]{0,1:T(8,128)} %get-tuple-element.124) | copy-start | bytes 294916
  195.2 8.6 %copy-start.38 = (f32[384,64]{0,1:T(8,128)S(1)}, f32[384,64]{0,1:T(8,128)}, u32[]{:S(2)}) copy-start(f32[384,64]{0,1:T(8,128)} %get-tuple-element.125) | copy-start | bytes 294916
  199.3 20.1 %collective-permute-start.3 = (bf16[384,1536]{1,0:T(8,128)(2,1)}, bf16[384,1536]{1,0:T(8,128)(2,1)}, u32[]{:S(2)}, u32[]{:S(2)}) collective-permute-start(bf16[384,1536]{1,0:T(8,128)(2,1)} %convolution_convert_fusion.2), channel_id=1, source_target_pairs={{0,1},{1,0},{2,3},{3,2},{4,5},{5,4},{6,7},{7,6},{8,9},{9,8},{10,11... | collective-permute-start | bytes 3538952 | tf_op jit(solution)/shard_map/ppermute | solution.py:980
  326.1 9.1 %copy-start.4 = (f32[384,1536]{1,0:T(8,128)S(1)}, f32[384,1536]{1,0:T(8,128)}, u32[]{:S(2)}) copy-start(f32[384,1536]{1,0:T(8,128)} %copy-done.3) | copy-start | bytes 7077892
  326.1 28.3 %collective-permute-start.4 = (bf16[384,1536]{1,0:T(8,128)(2,1)}, bf16[384,1536]{1,0:T(8,128)(2,1)}, u32[]{:S(2)}, u32[]{:S(2)}) collective-permute-start(bf16[384,1536]{1,0:T(8,128)(2,1)} %get-tuple-element.42), channel_id=1, source_target_pairs={{0,1},{1,0},{2,3},{3,2},{4,5},{5,4},{6,7},{7,6},{8,9},{9,8},{10,11... | collective-permute-start | bytes 3538952 | tf_op jit(solution)/shard_map/ppermute | solution.py:980
  330.7 25.6 %collective-permute-start.6 = (bf16[3,96,1536]{2,1,0:T(8,128)(2,1)}, bf16[3,96,1536]{2,1,0:T(8,128)(2,1)}, u32[]{:S(2)}, u32[]{:S(2)}) collective-permute-start(bf16[3,96,1536]{2,1,0:T(8,128)(2,1)} %get-tuple-element.93), channel_id=1, source_target_pairs={{0,8},{2,10},{8,16},{10,18},{16,24},{18,26},{24,28},{26,30},{28,20... | collective-permute-start | bytes 2654216 | tf_op jit(solution)/shard_map/ppermute | solution.py:255
  330.7 8.9 %copy-start.72 = (f32[2,3072]{1,0:T(2,128)S(1)}, f32[2,3072]{1,0:T(2,128)}, u32[]{:S(2)}) copy-start(f32[2,3072]{1,0:T(2,128)} %get-tuple-element.58) | copy-start | bytes 73732
  330.7 25.6 %collective-permute-start.7 = (bf16[3,96,1536]{2,1,0:T(8,128)(2,1)}, bf16[3,96,1536]{2,1,0:T(8,128)(2,1)}, u32[]{:S(2)}, u32[]{:S(2)}) collective-permute-start(bf16[3,96,1536]{2,1,0:T(8,128)(2,1)} %get-tuple-element.92), channel_id=1, source_target_pairs={{0,4},{2,6},{8,0},{10,2},{16,8},{18,10},{24,16},{26,18},{28,24},{3... | collective-permute-start | bytes 2654216 | tf_op jit(solution)/shard_map/ppermute | solution.py:256
  340.3 16.1 %copy-start.25 = (bf16[384,1536]{1,0:T(8,128)(2,1)S(1)}, bf16[384,1536]{1,0:T(8,128)(2,1)}, u32[]{:S(2)}) copy-start(bf16[384,1536]{1,0:T(8,128)(2,1)} %get-tuple-element.44) | copy-start | bytes 3538948
  356.4 27.1 %collective-permute-start.5 = (bf16[384,1536]{1,0:T(8,128)(2,1)S(1)}, bf16[384,1536]{1,0:T(8,128)(2,1)S(1)}, u32[]{:S(2)}, u32[]{:S(2)}) collective-permute-start(bf16[384,1536]{1,0:T(8,128)(2,1)S(1)} %copy-done.25), channel_id=1, source_target_pairs={{0,1},{1,0},{2,3},{3,2},{4,5},{5,4},{6,7},{7,6},{8,9},{9,8},{10,11... | collective-permute-start | bytes 3538952 | tf_op jit(solution)/shard_map/ppermute | solution.py:980
  358.2 32.1 %slice-start.6 = ((s8[16908288]{0:T(1024)(128)(4,1)}), s8[131072]{0:T(1024)(128)(4,1)S(1)}, s32[]{:S(2)}) async-start(s8[16908288]{0:T(1024)(128)(4,1)} %bitcast.100), calls=%async_computation.8 | async-start | bytes 262144
  358.2 32.1 %slice-start.7 = ((s8[16908288]{0:T(1024)(128)(4,1)}), s8[4194304]{0:T(1024)(128)(4,1)S(1)}, s32[]{:S(2)}) async-start(s8[16908288]{0:T(1024)(128)(4,1)} %bitcast.100), calls=%async_computation.9 | async-start | bytes 8388608
  363.5 43.0 %collective-permute-start.8 = (bf16[3,96,3072]{2,1,0:T(8,128)(2,1)}, bf16[3,96,3072]{2,1,0:T(8,128)(2,1)}, u32[]{:S(2)}, u32[]{:S(2)}) collective-permute-start(bf16[3,96,3072]{2,1,0:T(8,128)(2,1)} %get-tuple-element.91), channel_id=1, source_target_pairs={{0,8},{2,10},{8,16},{10,18},{16,24},{18,26},{24,28},{26,30},{28,20... | collective-permute-start | bytes 5308424 | tf_op jit(solution)/shard_map/ppermute | solution.py:255
  365.0 18.5 %copy-start.24 = (bf16[384,1536]{1,0:T(8,128)(2,1)S(1)}, bf16[384,1536]{1,0:T(8,128)(2,1)}, u32[]{:S(2)}) copy-start(bf16[384,1536]{1,0:T(8,128)(2,1)} %top.1) | copy-start | bytes 3538948
  365.0 18.5 %copy-start.69 = (f32[1536]{0:T(1024)S(1)}, f32[1536]{0:T(1024)}, u32[]{:S(2)}) copy-start(f32[1536]{0:T(1024)} %get-tuple-element.73) | copy-start | bytes 18436
  365.0 41.5 %collective-permute-start.9 = (bf16[3,96,3072]{2,1,0:T(8,128)(2,1)}, bf16[3,96,3072]{2,1,0:T(8,128)(2,1)}, u32[]{:S(2)}, u32[]{:S(2)}) collective-permute-start(bf16[3,96,3072]{2,1,0:T(8,128)(2,1)} %get-tuple-element.90), channel_id=1, source_target_pairs={{0,4},{2,6},{8,0},{10,2},{16,8},{18,10},{24,16},{26,18},{28,24},{3... | collective-permute-start | bytes 5308424 | tf_op jit(solution)/shard_map/ppermute | solution.py:256
  383.5 6.8 %slice-start.8 = ((s8[16908288]{0:T(1024)(128)(4,1)}), s8[4194304]{0:T(1024)(128)(4,1)S(1)}, s32[]{:S(2)}) async-start(s8[16908288]{0:T(1024)(128)(4,1)} %bitcast.100), calls=%async_computation.10 | async-start | bytes 8388608
  395.6 70.5 %collective-permute-start.13 = (bf16[768,768]{1,0:T(8,128)(2,1)}, bf16[768,768]{1,0:T(8,128)(2,1)}, u32[]{:S(2)}, u32[]{:S(2)}) collective-permute-start(bf16[768,768]{1,0:T(8,128)(2,1)} %convolution_convert_fusion.6), channel_id=1, source_target_pairs={{0,2},{2,0},{4,6},{6,4},{8,10},{10,8},{12,14},{14,12},{16,18},{18,... | collective-permute-start | bytes 3538952 | tf_op jit(solution)/shard_map/ppermute | solution.py:240
  399.9 9.8 %slice-start.2 = ((s8[14155776]{0:T(1024)(128)(4,1)}), s8[1572864]{0:T(1024)(128)(4,1)S(1)}, s32[]{:S(2)}) async-start(s8[14155776]{0:T(1024)(128)(4,1)} %bitcast.98), calls=%async_computation.4 | async-start | bytes 3145728
  399.9 9.8 %slice-start.3 = ((s8[14155776]{0:T(1024)(128)(4,1)}), s8[4194304]{0:T(1024)(128)(4,1)S(1)}, s32[]{:S(2)}) async-start(s8[14155776]{0:T(1024)(128)(4,1)} %bitcast.98), calls=%async_computation.5 | async-start | bytes 8388608
  401.8 7.9 %slice-start.4 = ((s8[14155776]{0:T(1024)(128)(4,1)}), s8[4194304]{0:T(1024)(128)(4,1)S(1)}, s32[]{:S(2)}) async-start(s8[14155776]{0:T(1024)(128)(4,1)} %bitcast.98), calls=%async_computation.6 | async-start | bytes 8388608
  403.3 6.4 slice-start.5
  403.3 60.4 %collective-permute-start.19 = (bf16[384,1536]{1,0:T(8,128)(2,1)S(1)}, bf16[384,1536]{1,0:T(8,128)(2,1)S(1)}, u32[]{:S(2)}, u32[]{:S(2)}) collective-permute-start(bf16[384,1536]{1,0:T(8,128)(2,1)S(1)} %convolution_convert_fusion), channel_id=1, source_target_pairs={{0,2},{2,0},{4,6},{6,4},{8,10},{10,8},{12,14},{14,12},{16,18},{18,... | collective-permute-start | bytes 3538952 | tf_op jit(solution)/shard_map/ppermute | solution.py:240
  409.3 8.7 %copy-start.48 = (bf16[1536,384]{1,0:T(8,128)(2,1)S(1)}, bf16[1536,384]{1,0:T(8,128)(2,1)}, u32[]{:S(2)}) copy-start(bf16[1536,384]{1,0:T(8,128)(2,1)} %fusion.25) | copy-start | bytes 3538948
  409.3 26.5 %collective-permute-start.10 = (bf16[384,1536]{1,0:T(8,128)(2,1)S(1)}, bf16[384,1536]{1,0:T(8,128)(2,1)S(1)}, u32[]{:S(2)}, u32[]{:S(2)}) collective-permute-start(bf16[384,1536]{1,0:T(8,128)(2,1)S(1)} %convolution_convert_fusion.1), channel_id=1, source_target_pairs={{0,1},{1,0},{2,3},{3,2},{4,5},{5,4},{6,7},{7,6},{8,9},{9,8},{10,11... | collective-permute-start | bytes 3538952 | tf_op jit(solution)/shard_map/ppermute | solution.py:980
  413.2 22.6 %copy-start.5 = (f32[384,1536]{1,0:T(8,128)S(1)}, f32[384,1536]{1,0:T(8,128)}, u32[]{:S(2)}) copy-start(f32[384,1536]{1,0:T(8,128)} %copy-done.3) | copy-start | bytes 7077892
  413.2 22.6 %copy-start.61 = (f32[1536]{0:T(1024)S(1)}, f32[1536]{0:T(1024)}, u32[]{:S(2)}) copy-start(f32[1536]{0:T(1024)} %get-tuple-element.75) | copy-start | bytes 18436
  413.2 22.6 %copy-start.66 = (f32[384]{0:T(512)S(1)}, f32[384]{0:T(512)}, u32[]{:S(2)}) copy-start(f32[384]{0:T(512)} %copy-done.65) | copy-start | bytes 4612
  413.2 22.6 %copy-start.77 = (f32[384]{0:T(512)S(1)}, f32[384]{0:T(512)}, u32[]{:S(2)}) copy-start(f32[384]{0:T(512)} %copy-done.76) | copy-start | bytes 4612
  413.2 43.5 %collective-permute-start.11 = (bf16[3,96,3072]{2,1,0:T(8,128)(2,1)S(1)}, bf16[3,96,3072]{2,1,0:T(8,128)(2,1)S(1)}, u32[]{:S(2)}, u32[]{:S(2)}) collective-permute-start(bf16[3,96,3072]{2,1,0:T(8,128)(2,1)S(1)} %get-tuple-element.89), channel_id=1, source_target_pairs={{0,8},{2,10},{8,16},{10,18},{16,24},{18,26},{24,28},{26,30},{28,20... | collective-permute-start | bytes 5308424 | tf_op jit(solution)/shard_map/ppermute | solution.py:255
  417.1 39.6 %collective-permute-start.12 = (bf16[3,96,3072]{2,1,0:T(8,128)(2,1)S(1)}, bf16[3,96,3072]{2,1,0:T(8,128)(2,1)S(1)}, u32[]{:S(2)}, u32[]{:S(2)}) collective-permute-start(bf16[3,96,3072]{2,1,0:T(8,128)(2,1)S(1)} %get-tuple-element.88), channel_id=1, source_target_pairs={{0,4},{2,6},{8,0},{10,2},{16,8},{18,10},{24,16},{26,18},{28,24},{3... | collective-permute-start | bytes 5308424 | tf_op jit(solution)/shard_map/ppermute | solution.py:256
  419.8 17.1 %copy-start.11 = (f32[384,1536]{1,0:T(8,128)S(1)}, f32[384,1536]{1,0:T(8,128)}, u32[]{:S(2)}) copy-start(f32[384,1536]{1,0:T(8,128)} %copy-done.10) | copy-start | bytes 7077892
  435.8 34.2 %collective-permute-start.14 = (bf16[768,768]{1,0:T(8,128)(2,1)}, bf16[768,768]{1,0:T(8,128)(2,1)}, u32[]{:S(2)}, u32[]{:S(2)}) collective-permute-start(bf16[768,768]{1,0:T(8,128)(2,1)} %convolution_convert_fusion.5), channel_id=1, source_target_pairs={{0,2},{2,0},{4,6},{6,4},{8,10},{10,8},{12,14},{14,12},{16,18},{18,... | collective-permute-start | bytes 3538952 | tf_op jit(solution)/shard_map/ppermute | solution.py:240
  445.1 11.5 %copy-start.51 = (bf16[1536,384]{1,0:T(8,128)(2,1)}, bf16[1536,384]{1,0:T(8,128)(2,1)S(1)}, u32[]{:S(2)}) copy-start(bf16[1536,384]{1,0:T(8,128)(2,1)S(1)} %fusion.26) | copy-start | bytes 3538948
  456.7 16.4 %collective-permute-start.15 = (bf16[768,768]{1,0:T(8,128)(2,1)}, bf16[768,768]{1,0:T(8,128)(2,1)}, u32[]{:S(2)}, u32[]{:S(2)}) collective-permute-start(bf16[768,768]{1,0:T(8,128)(2,1)} %convolution_convert_fusion.4), channel_id=1, source_target_pairs={{0,2},{2,0},{4,6},{6,4},{8,10},{10,8},{12,14},{14,12},{16,18},{18,... | collective-permute-start | bytes 3538952 | tf_op jit(solution)/shard_map/ppermute | solution.py:240
  459.8 93.6 %collective-permute-start.16 = (bf16[3,96,3072]{2,1,0:T(8,128)(2,1)}, bf16[3,96,3072]{2,1,0:T(8,128)(2,1)}, u32[]{:S(2)}, u32[]{:S(2)}) collective-permute-start(bf16[3,96,3072]{2,1,0:T(8,128)(2,1)} %get-tuple-element.87), channel_id=1, source_target_pairs={{0,8},{2,10},{8,16},{10,18},{16,24},{18,26},{24,28},{26,30},{28,20... | collective-permute-start | bytes 5308424 | tf_op jit(solution)/shard_map/ppermute | solution.py:255
  463.6 89.8 %collective-permute-start.17 = (bf16[3,96,3072]{2,1,0:T(8,128)(2,1)}, bf16[3,96,3072]{2,1,0:T(8,128)(2,1)}, u32[]{:S(2)}, u32[]{:S(2)}) collective-permute-start(bf16[3,96,3072]{2,1,0:T(8,128)(2,1)} %get-tuple-element.86), channel_id=1, source_target_pairs={{0,4},{2,6},{8,0},{10,2},{16,8},{18,10},{24,16},{26,18},{28,24},{3... | collective-permute-start | bytes 5308424 | tf_op jit(solution)/shard_map/ppermute | solution.py:256
  559.5 27.2 %collective-permute-start.18 = (bf16[384,1536]{1,0:T(8,128)(2,1)S(1)}, bf16[384,1536]{1,0:T(8,128)(2,1)S(1)}, u32[]{:S(2)}, u32[]{:S(2)}) collective-permute-start(bf16[384,1536]{1,0:T(8,128)(2,1)S(1)} %slice.448), channel_id=1, source_target_pairs={{0,1},{1,0},{2,3},{3,2},{4,5},{5,4},{6,7},{7,6},{8,9},{9,8},{10,11... | collective-permute-start | bytes 3538952 | tf_op jit(solution)/shard_map/ppermute | solution.py:980
  565.8 20.8 %copy-start.7 = (f32[400,1536]{1,0:T(8,128)S(1)}, f32[400,1536]{1,0:T(8,128)}, u32[]{:S(2)}) copy-start(f32[400,1536]{1,0:T(8,128)} %subtract_multiply_fusion) | copy-start | bytes 7372804
  565.8 20.8 %copy-start.13 = (f32[400,1536]{1,0:T(8,128)S(1)}, f32[400,1536]{1,0:T(8,128)}, u32[]{:S(2)}) copy-start(f32[400,1536]{1,0:T(8,128)} %copy-done.12) | copy-start | bytes 7372804
  650.1 6.7 %copy-start.75 = (f32[400]{0:T(512)S(1)}, f32[400]{0:T(512)}, u32[]{:S(2)}) copy-start(f32[400]{0:T(512)} %copy-done.73) | copy-start | bytes 4804
  (60 other events, 217.5 us)
Sparse Core Ops, SparseCore 0:
  16.0 92.3 all-gather.2
  110.0 156.1 all-gather.4

commit v4 on v3

--- a/solution.py
+++ b/solution.py
@@ -197,7 +197,7 @@
 LANES = 128
 BLOCK = 256
 TAIL_WIDTH = 768
-SELF_PIECES = 3
+SELF_PIECES = 4
 QUERY_BLOCK = 128
 VMEM_BYTES = 60 * 1024 * 1024
 MESH = pl.DeviceIdType.MESH
@@ -241,12 +241,16 @@
 
 
 class Ring:
-    def __init__(self, term, seq_count):
+    def __init__(self, term, seq_count, moving=None):
         self.term = term
         self.chips = seq_count // 2
         self.far = self.chips // 2
         self.near = self.far
         self.ahead, self.behind = ring_pairs(self.chips, 1), ring_pairs(self.chips, -1)
+        if moving is not None:
+            self.near = self.far - 2
+            self.send(moving[0], moving[1])
+            return
         first = term(self.far)
         self.half = first.shape[-1] // 2
         self.send(first[..., : self.half], first[..., self.half :])
@@ -278,14 +282,13 @@
         )
         return value
 
-    def finish(self):
+    def last_terms(self):
         while self.near > 1:
             self.step()
-        return (
-            self.term(0).astype(jnp.float32)
-            + self.onward.astype(jnp.float32)
-            + self.backward.astype(jnp.float32)
-        )
+        return [self.term(0), self.onward, self.backward]
+
+    def finish(self):
+        return sum(each.astype(jnp.float32) for each in self.last_terms())
 
 
 def core_sum(rows_t, columns, seq_count):
@@ -316,8 +319,141 @@
     return values
 
 
+def xor_place(index, bit):
+    return index + bit * (1 - 2 * (index // bit % 2))
+
+
+def chip_near(seq_index, seq_count, step):
+    chips = seq_count // 2
+    chip = seq_index // 2
+    odd = chip % 2
+    place = (1 - odd) * (chip // 2) + odd * (chips - 1 - chip // 2)
+    there = (place + chips + step) % chips
+    upper = there // (chips // 2)
+    return (1 - upper) * 2 * there + upper * (2 * (chips - 1 - there) + 1)
+
+
+def ring_neighbours(seq_index, seq_count):
+    return [2 * chip_near(seq_index, seq_count, step) + seq_index % 2 for step in (1, -1)]
+
+
+def gather_kernel(
+    seq_count, bounds, local, out, token, own_sem, ring_send, ring_recv, core_send, core_recv
+):
+    token[...] = jnp.zeros_like(token)
+    far = seq_count // 4
+    seq_index = lax.axis_index("seq")
+    core = seq_index % 2
+    partner = {"seq": xor_place(seq_index, 1)}
+    sides = ring_neighbours(seq_index, seq_count)
+    greet([partner] + [{"seq": side} for side in sides])
+
+    def columns_of(piece, side, hop):
+        low, high = bounds[piece], bounds[piece + 1]
+        if hop == far - 1:
+            mid = low + (high - low) // (2 * LANES) * LANES
+            low, high = (low, mid) if side == 0 else (mid, high)
+        return pl.ds(low, high - low)
+
+    def ring_copy(piece, side, hop):
+        columns = columns_of(piece, side, hop)
+        target = out.at[
+            chip_near(seq_index, seq_count, -hop if side == 0 else hop), core, :, columns
+        ]
+        return pltpu.make_async_remote_copy(
+            src_ref=local.at[:, columns] if hop == 0 else target,
+            dst_ref=target,
+            send_sem=ring_send.at[piece, side, hop],
+            recv_sem=ring_recv.at[piece, side, hop],
+            device_id={"seq": sides[side]},
+            device_id_type=MESH,
+        )
+
+    def core_copy(piece, side, hop):
+        if hop < 0:
+            columns = pl.ds(bounds[piece], bounds[piece + 1] - bounds[piece])
+            target = out.at[seq_index // 2, core, :, columns]
+            source = local.at[:, columns]
+        else:
+            chip = chip_near(seq_index, seq_count, -1 - hop if side == 0 else 1 + hop)
+            target = out.at[chip, core, :, columns_of(piece, side, hop)]
+            source = target
+        return pltpu.make_async_remote_copy(
+            src_ref=source,
+            dst_ref=target,
+            send_sem=core_send.at[piece, side, hop + 1],
+            recv_sem=core_recv.at[piece, side, hop + 1],
+            device_id=partner,
+            device_id_type=MESH,
+        )
+
+    pieces = range(len(bounds) - 1)
+    arrivals = [(piece, side, hop) for hop in range(far) for piece in pieces for side in range(2)]
+    own_copy = pltpu.make_async_copy(local, out.at[seq_index // 2, core], own_sem)
+    for piece in pieces:
+        for side in range(2):
+            ring_copy(piece, side, 0).start()
+    own_copy.start()
+    for piece in pieces:
+        core_copy(piece, 0, -1).start()
+    for piece, side, hop in arrivals:
+        ring_copy(piece, side, hop).wait_recv()
+        if hop + 1 < far:
+            ring_copy(piece, side, hop + 1).start()
+        core_copy(piece, side, hop).start()
+    crossed = [(piece, 0, -1) for piece in pieces] + arrivals
+    for piece, side, hop in crossed:
+        core_copy(piece, side, hop).wait_recv()
+    own_copy.wait()
+    for piece, side, hop in crossed:
+        core_copy(piece, side, hop).wait_send()
+    for piece, side, hop in arrivals:
+        ring_copy(piece, side, hop).wait_send()
+
+
+def ring_gather(local, bounds, seq_count, collective_id):
+    rows, width = local.shape
+    local = local.astype(jnp.bfloat16)
+    if rows % 16:
+        return lax.all_gather(local, "seq", axis=0, tiled=True), jnp.zeros((8, LANES), jnp.float32)
+    pieces, far = len(bounds) - 1, seq_count // 4
+    gathered, token = pl.pallas_call(
+        functools.partial(gather_kernel, seq_count, bounds),
+        in_specs=[pl.BlockSpec(memory_space=pl.ANY)],
+        out_specs=[
+            pl.BlockSpec(memory_space=pl.ANY),
+            pl.BlockSpec(memory_space=pltpu.VMEM),
+        ],
+        out_shape=[
+            jax.ShapeDtypeStruct((seq_count // 2, 2, rows, width), jnp.bfloat16),
+            jax.ShapeDtypeStruct((8, LANES), jnp.float32),
+        ],
+        scratch_shapes=[
+            pltpu.SemaphoreType.DMA,
+            pltpu.SemaphoreType.DMA((pieces, 2, far)),
+            pltpu.SemaphoreType.DMA((pieces, 2, far)),
+            pltpu.SemaphoreType.DMA((pieces, 2, far + 1)),
+            pltpu.SemaphoreType.DMA((pieces, 2, far + 1)),
+        ],
+        compiler_params=pltpu.CompilerParams(collective_id=collective_id, has_side_effects=True),
+        cost_estimate=pl.CostEstimate(
+            flops=0, bytes_accessed=32 * rows * seq_count * width, transcendentals=0
+        ),
+        name="ring_gather",
+    )(local)
+    return gathered.reshape(seq_count * rows, width), token
+
+
+def kept_places(seq_count):
+    chips = seq_count // 2
+    far = chips // 2
+    return [*range(far - 2), *range(far + 3, chips)]
+
+
 def glu_kernel(
     blocks,
+    seq_count,
+    ringed,
     normed,
     normed_t,
     top,
@@ -329,20 +465,23 @@
     b_up,
     out,
     grad_normed,
-    sums,
     bias_grads,
-    out_acc,
-    grad_acc,
-    mine,
-    away,
-    arrived,
-    send_sem,
-    recv_sem,
+    kept,
+    *refs,
 ):
     index = pl.program_id(0)
     seq_index = lax.axis_index("seq")
-    partner = seq_index + 1 - 2 * (seq_index % 2)
+    partner = {"seq": xor_place(seq_index, 1)}
     half = normed_t.shape[0] // 2
+    chips = seq_count // 2
+    far, seg = chips // 2, half // chips
+    mid = BLOCK // 2
+    if ringed:
+        moving, *refs = refs
+    out_acc, grad_acc, mine, away, arrived, send_sem, recv_sem, *refs = refs
+    sides = ring_neighbours(seq_index, seq_count)
+    if ringed:
+        sums, first_send, first_land, second_send, second_land, *ring_sems = refs
 
     def crossing(block):
         return pltpu.make_async_remote_copy(
@@ -350,15 +489,24 @@
             dst_ref=arrived.at[block],
             send_sem=send_sem.at[block % 2],
             recv_sem=recv_sem.at[block],
-            device_id={"seq": partner},
+            device_id=partner,
             device_id_type=MESH,
         )
 
+    def hop(block, side, which):
+        source, target = (first_send, first_land) if which == 0 else (second_send, second_land)
+        return pltpu.make_async_remote_copy(
+            src_ref=source.at[block, side],
+            dst_ref=target.at[block, side],
+            send_sem=ring_sems[2 * which].at[block, side],
+            recv_sem=ring_sems[2 * which + 1].at[block, side],
+            device_id={"seq": sides[side]},
+            device_id_type=MESH,
+        )
+
     @pl.when(index == 0)
     def _():
-        barrier = pltpu.get_barrier_semaphore()
-        pl.semaphore_signal(barrier, inc=1, device_id={"seq": partner}, device_id_type=MESH)
-        pl.semaphore_wait(barrier, 1)
+        greet([partner] + ([{"seq": side} for side in sides] if ringed else []))
         out_acc[...] = jnp.zeros_like(out_acc)
         grad_acc[...] = jnp.zeros_like(grad_acc)
 
@@ -388,15 +536,54 @@
         away[slot, 1] = product(normed_t[half:, :], grad_up).astype(jnp.bfloat16)
         away[slot, 2] = product(top_t[half:, :], hidden).astype(jnp.bfloat16)
         crossing(index).start()
-        mine[slot, 0] = product(normed_t[:half, :], grad_gate)
-        mine[slot, 1] = product(normed_t[:half, :], grad_up)
-        mine[slot, 2] = product(top_t[:half, :], hidden)
-
-    @pl.when(index >= 1)
+        mine[slot, 0] = product(normed_t[:half, :], grad_gate).astype(jnp.bfloat16)
+        mine[slot, 1] = product(normed_t[:half, :], grad_up).astype(jnp.bfloat16)
+        mine[slot, 2] = product(top_t[:half, :], hidden).astype(jnp.bfloat16)
+
+    def chunk(block, near):
+        return sums[block % 3, :, near * seg : (near + 1) * seg, :].astype(jnp.float32)
+
+    @pl.when((index >= 1) & (index <= blocks))
     def _():
-        crossing(index - 1).wait_recv()
-        prior = index - 1
-        sums[...] = (mine[prior % 2] + arrived[prior].astype(jnp.float32)).astype(jnp.bfloat16)
+        block = index - 1
+        crossing(block).wait_recv()
+        total = mine[block % 2].astype(jnp.float32) + arrived[block].astype(jnp.float32)
+        total = total.astype(jnp.bfloat16)
+        if ringed:
+            sums[block % 3] = total
+            for side in range(2):
+                first_send[block, side] = total[
+                    :, far * seg : (far + 1) * seg, side * mid : (side + 1) * mid
+                ]
+                hop(block, side, 0).start()
+            for at, near in enumerate(kept_places(seq_count)):
+                kept[at] = total[:, near * seg : (near + 1) * seg, :]
+        else:
+            kept[...] = total
+
+    if ringed:
+
+        @pl.when((index >= 2) & (index <= blocks + 1))
+        def _():
+            block = index - 2
+            for side in range(2):
+                term = chunk(block, far - 1 if side == 0 else far + 1)
+                hop(block, side, 0).wait_recv()
+                land = first_land[block, side].astype(jnp.float32)
+                low = term[:, :, :mid] + land if side == 0 else term[:, :, :mid]
+                high = term[:, :, mid:] if side == 0 else term[:, :, mid:] + land
+                second_send[block, side, :, :, :mid] = low.astype(jnp.bfloat16)
+                second_send[block, side, :, :, mid:] = high.astype(jnp.bfloat16)
+                hop(block, side, 1).start()
+
+        @pl.when(index >= 3)
+        def _():
+            block = index - 3
+            for side in range(2):
+                term = chunk(block, far - 2 if side == 0 else far + 2)
+                hop(block, side, 1).wait_recv()
+                land = second_land[block, side].astype(jnp.float32)
+                moving[side] = (term + land).astype(jnp.bfloat16)
 
     @pl.when(index == blocks)
     def _():
@@ -405,30 +592,66 @@
         out[...] = out_acc[...].astype(jnp.bfloat16)
         grad_normed[...] = grad_acc[...].astype(jnp.bfloat16)
 
-
-def glu_layer(normed, normed_t, top, top_t, weights, gate_bias, up_bias):
+    if ringed:
+
+        @pl.when(index == blocks + 2)
+        def _():
+            for block in range(blocks):
+                for side in range(2):
+                    hop(block, side, 0).wait_send()
+                    hop(block, side, 1).wait_send()
+
+
+def glu_layer(normed, normed_t, top, top_t, weights, gate_bias, up_bias, seq_count):
     rows, width = normed.shape
     hidden_width = gate_bias.shape[0]
     blocks = hidden_width // BLOCK
     half = width // 2
-    whole = pl.BlockSpec((rows, width), lambda i: (0, 0))
-    whole_t = pl.BlockSpec((width, rows), lambda i: (0, 0))
+    seg = width // seq_count
+    ringed = seg % 16 == 0
+    kept = len(kept_places(seq_count))
+    bf = jnp.bfloat16
+
+    def whole(shape):
+        return pl.BlockSpec(shape, lambda i: (0, 0), pipeline_mode=pl.Buffered(1))
+
+    def at(lag):
+        return lambda i: jnp.clip(i - lag, 0, blocks - 1)
 
     def weight_spec(which):
-        return pl.BlockSpec(
-            (width, BLOCK), lambda i: (0, which * blocks + jnp.minimum(i, blocks - 1))
-        )
-
-    bias_spec = pl.BlockSpec((1, BLOCK), lambda i: (0, jnp.minimum(i, blocks - 1)))
+        return pl.BlockSpec((width, BLOCK), lambda i: (0, which * blocks + at(0)(i)))
+
+    bias_spec = pl.BlockSpec((1, BLOCK), lambda i: (0, at(0)(i)))
     work = rows * width * hidden_width
+    if ringed:
+        term_specs = [
+            pl.BlockSpec((kept, 3, seg, BLOCK), lambda i: (0, 0, 0, at(1)(i))),
+            pl.BlockSpec((2, 3, seg, BLOCK), lambda i: (0, 0, 0, at(3)(i))),
+        ]
+        term_shapes = [
+            jax.ShapeDtypeStruct((kept, 3, seg, hidden_width), bf),
+            jax.ShapeDtypeStruct((2, 3, seg, hidden_width), bf),
+        ]
+        ring_scratches = [
+            pltpu.VMEM((3, 3, half, BLOCK), bf),
+            pltpu.VMEM((blocks, 2, 3, seg, BLOCK // 2), bf),
+            pltpu.VMEM((blocks, 2, 3, seg, BLOCK // 2), bf),
+            pltpu.VMEM((blocks, 2, 3, seg, BLOCK), bf),
+            pltpu.VMEM((blocks, 2, 3, seg, BLOCK), bf),
+            *(pltpu.SemaphoreType.DMA((blocks, 2)) for _ in range(4)),
+        ]
+    else:
+        term_specs = [pl.BlockSpec((3, half, BLOCK), lambda i: (0, 0, at(1)(i)))]
+        term_shapes = [jax.ShapeDtypeStruct((3, half, hidden_width), bf)]
+        ring_scratches = []
     return pl.pallas_call(
-        functools.partial(glu_kernel, blocks),
-        grid=(blocks + 1,),
+        functools.partial(glu_kernel, blocks, seq_count, ringed),
+        grid=(blocks + (3 if ringed else 1),),
         in_specs=[
-            whole,
-            whole_t,
-            whole,
-            whole_t,
+            whole((rows, width)),
+            whole((width, rows)),
+            whole((rows, width)),
+            whole((width, rows)),
             weight_spec(0),
             weight_spec(1),
             weight_spec(2),
@@ -436,25 +659,26 @@
             bias_spec,
         ],
         out_specs=[
-            whole,
-            whole,
-            pl.BlockSpec((3, half, BLOCK), lambda i: (0, 0, jnp.maximum(i - 1, 0))),
-            pl.BlockSpec((2, BLOCK), lambda i: (0, jnp.minimum(i, blocks - 1))),
+            pl.BlockSpec((rows, width), lambda i: (0, 0)),
+            pl.BlockSpec((rows, width), lambda i: (0, 0)),
+            pl.BlockSpec((2, BLOCK), lambda i: (0, at(0)(i))),
+            *term_specs,
         ],
         out_shape=[
-            jax.ShapeDtypeStruct((rows, width), jnp.bfloat16),
-            jax.ShapeDtypeStruct((rows, width), jnp.bfloat16),
-            jax.ShapeDtypeStruct((3, half, hidden_width), jnp.bfloat16),
+            jax.ShapeDtypeStruct((rows, width), bf),
+            jax.ShapeDtypeStruct((rows, width), bf),
             jax.ShapeDtypeStruct((2, hidden_width), jnp.float32),
+            *term_shapes,
         ],
         scratch_shapes=[
             pltpu.VMEM((rows, width), jnp.float32),
             pltpu.VMEM((rows, width), jnp.float32),
-            pltpu.VMEM((2, 3, half, BLOCK), jnp.float32),
-            pltpu.VMEM((2, 3, half, BLOCK), jnp.bfloat16),
-            pltpu.VMEM((blocks, 3, half, BLOCK), jnp.bfloat16),
+            pltpu.VMEM((2, 3, half, BLOCK), bf),
+            pltpu.VMEM((2, 3, half, BLOCK), bf),
+            pltpu.VMEM((blocks, 3, half, BLOCK), bf),
             pltpu.SemaphoreType.DMA((2,)),
             pltpu.SemaphoreType.DMA((blocks,)),
+            *ring_scratches,
         ],
         compiler_params=pltpu.CompilerParams(
             collective_id=1, has_side_effects=True, vmem_limit_bytes=VMEM_BYTES
@@ -476,23 +700,6 @@
     )
 
 
-def xor_place(index, bit):
-    return index + bit * (1 - 2 * (index // bit % 2))
-
-
-def ring_neighbours(seq_index, seq_count):
-    chips = seq_count // 2
-    chip, core = seq_index // 2, seq_index % 2
-    odd = chip % 2
-    place = (1 - odd) * (chip // 2) + odd * (chips - 1 - chip // 2)
-    found = []
-    for step in (1, chips - 1):
-        there = (place + step) % chips
-        upper = there // (chips // 2)
-        found.append(2 * ((1 - upper) * 2 * there + upper * (2 * (chips - 1 - there) + 1)) + core)
-    return found
-
-
 class ChipRing:
     def __init__(self, seq_count, pieces, sends, lands, send_sem, recv_sem):
         self.chips = seq_count // 2
@@ -577,7 +784,9 @@
 
 def tail_kernel(seq_count, head_count, ready_count, made_count, *refs):
     ready = refs[:ready_count]
-    rows_t, columns, small, out, small_out = refs[ready_count : ready_count + 5]
+    rows_t, columns, small, split, *refs = refs[ready_count:]
+    last_terms, refs = refs[:3], refs[3:]
+    out, small_out, joint, last_out, *refs = refs
     (
         mine,
         away,
@@ -588,8 +797,11 @@
         core_recv,
         step_send,
         step_recv,
+        split_land,
+        split_send,
+        split_recv,
         *ring_refs,
-    ) = refs[ready_count + 5 :]
+    ) = refs
     half = rows_t.shape[0] // 2
     width = columns.shape[1] // made_count
     pieces = [*ready, *(mine.at[made] for made in range(made_count))]
@@ -652,6 +864,18 @@
         if step < len(partners):
             step_copy(step).start()
 
+    def split_copy(step):
+        return pltpu.make_async_remote_copy(
+            src_ref=split,
+            dst_ref=split_land.at[step],
+            send_sem=split_send.at[step],
+            recv_sem=split_recv.at[step],
+            device_id={"head": (head_index + 1 + step) % head_count},
+            device_id_type=MESH,
+        )
+
+    for step in range(head_count - 1):
+        split_copy(step).start()
     for piece in range(ready_count):
         ring.start(piece)
     step_on(0)
@@ -665,6 +889,10 @@
         core_copy(made).wait_recv()
         mine[made] = (term + arrived[made].astype(jnp.float32)).astype(jnp.bfloat16)
         ring.start(ready_count + made)
+    last_total = last_terms[0][...].astype(jnp.float32)
+    for term in last_terms[1:]:
+        last_total = last_total + term[...].astype(jnp.float32)
+    last_out[...] = last_total
     done = 1
     for hop in range(1, ring.far):
         for piece in range(len(pieces)):
@@ -672,8 +900,15 @@
         while done <= len(partners) * hop // (ring.far - 1):
             step_on(done)
             done += 1
+    total = split[...].astype(jnp.float32)
+    for step in range(head_count - 1):
+        split_copy(step).wait_recv()
+        total = total + split_land[step].astype(jnp.float32)
+    joint[...] = total
     for piece in range(len(pieces)):
         out[:, piece * width : (piece + 1) * width] = ring.total(piece)
+    for step in range(head_count - 1):
+        split_copy(step).wait_send()
     for made in range(made_count):
         core_copy(made).wait_send()
     ring.close()
@@ -681,7 +916,7 @@
         step_copy(step).wait_send()
 
 
-def tail_sums(ready, rows_t, columns, small, seq_count):
+def tail_sums(ready, rows_t, columns, small, split, last_terms, seq_count):
     head_count = lax.axis_size("head")
     chips = seq_count // 2
     half = rows_t.shape[0] // 2
@@ -693,11 +928,13 @@
     bf = jnp.bfloat16
     return pl.pallas_call(
         functools.partial(tail_kernel, seq_count, head_count, len(ready), made_count),
-        in_specs=[pl.BlockSpec(memory_space=pltpu.VMEM)] * (len(ready) + 3),
-        out_specs=[pl.BlockSpec(memory_space=pltpu.VMEM)] * 2,
+        in_specs=[pl.BlockSpec(memory_space=pltpu.VMEM)] * (len(ready) + 7),
+        out_specs=[pl.BlockSpec(memory_space=pltpu.VMEM)] * 4,
         out_shape=[
             jax.ShapeDtypeStruct((seg, pieces * width), jnp.float32),
             jax.ShapeDtypeStruct(small.shape, jnp.float32),
+            jax.ShapeDtypeStruct(split.shape, jnp.float32),
+            jax.ShapeDtypeStruct(last_terms[0].shape, jnp.float32),
         ],
         scratch_shapes=[
             pltpu.VMEM((made_count, half, width), bf),
@@ -709,6 +946,9 @@
             pltpu.SemaphoreType.DMA((made_count,)),
             pltpu.SemaphoreType.DMA((steps,)),
             pltpu.SemaphoreType.DMA((steps,)),
+            pltpu.VMEM((head_count - 1, *split.shape), bf),
+            pltpu.SemaphoreType.DMA((head_count - 1,)),
+            pltpu.SemaphoreType.DMA((head_count - 1,)),
             *ring_scratch(seq_count, pieces, seg, width),
         ],
         compiler_params=pltpu.CompilerParams(
@@ -720,7 +960,7 @@
             transcendentals=0,
         ),
         name="tail_sums",
-    )(*ready, rows_t, columns, small)
+    )(*ready, rows_t, columns, small, split, *last_terms)
 
 
 def turned_back(values, tables):
@@ -958,15 +1198,15 @@
     )
 
 
-def tail_or_rings(ready, rows_t, columns, small, seq_count):
+def tail_or_rings(ready, rows_t, columns, small, split, last_terms, seq_count):
     if rows_t.shape[0] // seq_count % 16 == 0:
-        return tail_sums(ready, rows_t, columns, small, seq_count)
+        return tail_sums(ready, rows_t, columns, small, split, last_terms, seq_count)
     made = core_sum(rows_t, columns, seq_count)
     ring = Ring(side_by_side([*ready, made], seq_count // 2), seq_count)
     late = small.shape[0] // 2
     small = all_sum(small, ("seq",))
     small = jnp.concatenate([all_sum(small[:late], ("head",)), small[late:]], axis=0)
-    return ring.finish(), small
+    return ring.finish(), small, head_total(split), sum(each.astype(jnp.float32) for each in last_terms)
 
 
 def head_total(partial_sum):
@@ -1036,19 +1276,33 @@
     vectors = jnp.pad(vectors, ((0, 0), (0, LANES - 4)))
     ctx_pair = jnp.concatenate([cross_key, cross_value], axis=0)
     attn_local = jnp.concatenate(
-        [query_weight, key_weight, value_weight, out_weight, cross_query, cross_out, ctx_pair, vectors],
+        [
+            vectors,
+            query_weight,
+            key_weight,
+            value_weight,
+            out_weight,
+            cross_query,
+            cross_out,
+            ctx_pair,
+        ],
         axis=1,
     )
-    attn_weights = low_gather(attn_local)
-    glu_weights = low_gather(jnp.concatenate([gate_weight, up_weight, down_weight], axis=1))
-    w_qkv = attn_weights[:, : 3 * part]
-    w_out = attn_weights[:, 3 * part : 4 * part]
-    c_query = attn_weights[:, 4 * part : 5 * part]
-    c_out = attn_weights[:, 5 * part : 6 * part]
-    ctx_weights = attn_weights[:, 6 * part : 7 * part].reshape(seq_count, 2, ctx_rows, part)
+    starts = [LANES + each * part for each in range(8)]
+    attn_weights, token = ring_gather(
+        attn_local, (0, starts[1], *starts[2:]), seq_count, 4
+    )
+    glu_local = jnp.concatenate([gate_weight, up_weight, down_weight], axis=1).astype(jnp.bfloat16)
+    token, glu_local = lax.optimization_barrier((token, glu_local))
+    glu_weights = low_gather(glu_local)
+    w_qkv = attn_weights[:, LANES : starts[3]]
+    w_out = attn_weights[:, starts[3] : starts[4]]
+    c_query = attn_weights[:, starts[4] : starts[5]]
+    c_out = attn_weights[:, starts[5] : starts[6]]
+    ctx_weights = attn_weights[:, starts[6] :].reshape(seq_count, 2, ctx_rows, part)
     c_key = ctx_weights[:, 0].reshape(ctx_width, part)
     c_value = ctx_weights[:, 1].reshape(ctx_width, part)
-    rows_of = attn_weights[:, 7 * part : 7 * part + 8].astype(jnp.float32).T
+    rows_of = attn_weights[:, :8].astype(jnp.float32).T + token[0, 0]
     gain_one_f, gain_two_f, gain_three_f, bias_f = rows_of[0], rows_of[1], rows_of[2], rows_of[3]
 
     positions = first_row + jnp.arange(local_rows, dtype=jnp.int32)
@@ -1110,7 +1364,7 @@
     third_out, normal_three, inverse_three = layer_norm_parts(h_two, gain_three_f)
     normed_three = third_out.astype(jnp.bfloat16)
 
-    glu_out, grad_normed_low, glu_sums, bias_local = glu_layer(
+    glu_out, grad_normed_low, bias_local, glu_left, *moving = glu_layer(
         normed_three,
         ordered(normed_three),
         out_grad,
@@ -1118,15 +1372,16 @@
         glu_weights,
         gate_bias,
         up_bias,
+        seq_count,
     )
     grad_normed_three = head_total(grad_normed_low)
-    grad_normed_three, glu_out = lax.optimization_barrier((grad_normed_three, glu_out))
-    result = (h_two + head_total(glu_out) + bias_f).astype(jnp.bfloat16)
-    glu_ring = Ring(
-        lambda near: glu_sums[:, near * gain_rows : (near + 1) * gain_rows], seq_count
-    )
-    grad_normed_three = glu_ring.after(grad_normed_three)
-    glu_ring.step()
+    if moving:
+        places = kept_places(seq_count)
+        glu_ring = Ring(lambda near: glu_left[places.index(near)], seq_count, moving[0])
+    else:
+        glu_ring = Ring(
+            lambda near: glu_left[:, near * gain_rows : (near + 1) * gain_rows], seq_count
+        )
     grad_top = out_grad.astype(jnp.float32)
     gain_three_term = jnp.sum(grad_normed_three * normal_three, axis=0)
     down_bias_term = jnp.sum(grad_top, axis=0)
@@ -1149,16 +1404,19 @@
     cross_query_sum = core_sum(ordered(normed_two), grad_cross_query, seq_count)
     ctx_order = owner_matrix(ctx_width, seq_index, seq_count)
     ctx_sum = core_sum(ordered(context_rows, ctx_order), ctx_grads, seq_count)
+    ctx_sum = jnp.transpose(ctx_sum.reshape(chips, ctx_rows, 2, part), (0, 2, 1, 3))
+    grad_normed_two, cross_out_sum, cross_query_sum, ctx_sum = lax.optimization_barrier(
+        (grad_normed_two, cross_out_sum, cross_query_sum, ctx_sum.reshape(width // 2, part))
+    )
     gain_two_term = jnp.sum(grad_normed_two * normal_two, axis=0)
     grad_h_one = grad_h_two + norm_back(grad_normed_two, normal_two, inverse_two, gain_two_f)
     grad_one_low = grad_h_one.astype(jnp.bfloat16)
     grad_attn = product(grad_one_low, w_out).astype(jnp.bfloat16)
+    grad_attn, glu_out = lax.optimization_barrier((grad_attn, glu_out))
+    glu_total = head_total(glu_out)
     out_sum = core_sum(ordered(grad_one_low), attn_mixed, seq_count)
-    ctx_sum = jnp.transpose(ctx_sum.reshape(chips, ctx_rows, 2, part), (0, 2, 1, 3))
-    ready_sums = [cross_out_sum, cross_query_sum, out_sum, ctx_sum.reshape(width // 2, part)]
-
-    grad_attn = glu_ring.after(grad_attn)
-    glu_ring.step()
+    ready_sums = [cross_out_sum, cross_query_sum, out_sum, ctx_sum]
+
     if gain_rows % 16 == 0:
         early_sums, ready_sums = ready_sums[:SELF_PIECES], ready_sums[SELF_PIECES:]
     else:
@@ -1187,16 +1445,12 @@
         score_scale,
         seq_count,
     )
+    grad_qkv, glu_total = lax.optimization_barrier((grad_qkv, glu_total))
+    result = (h_two + glu_total + bias_f).astype(jnp.bfloat16)
     grad_qkv = glu_ring.after(grad_qkv)
-    glu_share = glu_ring.finish()
+    glu_terms = glu_ring.last_terms()
     grad_normed_all = product_t(grad_qkv, w_qkv)
-    grad_normed_one = head_total(grad_normed_all[:local_rows])
     gain_one_term = jnp.sum(grad_normed_all[:local_rows] * normal_one[:local_rows], axis=0)
-    frames_grad = (
-        grad_h_one
-        + norm_back(grad_normed_one, normal_one[:local_rows], inverse_one[:local_rows], gain_one_f)
-    ).astype(jnp.bfloat16)
-
     stamp_full = lax.dynamic_update_slice_in_dim(
         jnp.zeros((clip_total, width), jnp.float32), grad_normed_all[local_rows:stamp_end], base_clip, 0
     )
@@ -1219,7 +1473,19 @@
         ],
         axis=0,
     )
-    shares, small = tail_or_rings(ready_sums, ordered(normed_one), grad_qkv, small, seq_count)
+    shares, small, grad_normed_one, glu_share = tail_or_rings(
+        ready_sums,
+        ordered(normed_one),
+        grad_qkv,
+        small,
+        grad_normed_all[:local_rows].astype(jnp.bfloat16),
+        glu_terms,
+        seq_count,
+    )
+    frames_grad = (
+        grad_h_one
+        + norm_back(grad_normed_one, normal_one[:local_rows], inverse_one[:local_rows], gain_one_f)
+    ).astype(jnp.bfloat16)
     if gain_rows % 16 == 0:
         shares = jnp.concatenate([early_share, shares], axis=1)
     cross_out_share = shares[:, :part]

time: 678 us -> 646 us (0.953)
  waiting for transfers between devices: 195 us -> 61.6 us
  Pallas kernels: 197 us -> 296 us
  starting transfers between devices: 31.2 us -> 18.4 us
  local copies, waits for them, and re-layouts: 60.9 us -> 70.5 us
    all_gather x2 -> x1, waiting for transfers between devices: 116 us -> 0.01 us  [low_gather(): return lax.all_gather(block.astype(jnp.bfloat16), 'seq', axis=0, tiled=True)]
    pallas_call x1 -> x2, Pallas kernels: 59.9 us -> 171 us  [the longest x1 89.1 us: ring_gather(): pl.pallas_call(functools.partial(gather_kernel, seq_count, bounds), in_sp...]
    ppermute x4 -> x2, waiting for transfers between devices: 11.7 us -> 0.01 us  [send(): self.onward = lax.ppermute(onward.astype(jnp.bfloat16), 'seq', self.ahead)]
    pallas_call x1, Pallas kernels: 75.1 us -> 66.1 us  [self_back(): pl.pallas_call(functools.partial(self_back_kernel, seq_count, pairs, scor...]
    add x2 -> x1, other arithmetic: 8.27 us -> 0.65 us  [per_device(): rows_of = attn_weights[:, :8].astype(jnp.float32).T + token[0, 0]]
    ppermute x4 -> x2, starting transfers between devices: 9.18 us -> 1.78 us  [send(): self.onward = lax.ppermute(onward.astype(jnp.bfloat16), 'seq', self.ahead)]
    convert_element_type x3 -> x1, other arithmetic: 11.9 us -> 5.1 us  [send(): backward.astype(jnp.bfloat16)]
    ppermute x6 -> x5, waiting for transfers between devices: 67.2 us -> 61.6 us  [head_total(): total = total + lax.ppermute(low, 'head', pairs).astype(jnp.float32)]
  transfers between devices with their start and end apart: 22 -> 16, of which waited for: 10 -> 4; matrix products, arithmetic and copies ran while one was open for 29% -> 31% of each run, Pallas kernels for 11% -> 10%
where the time goes in v4:
time: 646 us; the launch traced here: 639 us
  Pallas kernels  296 us (46%)
  matrix products  101 us (16%)
  other arithmetic  75.3 us (12%)
  local copies, waits for them, and re-layouts  70.5 us (11%)
  waiting for transfers between devices  61.6 us (10%)
  starting transfers between devices  18.4 us (3%)
  between operations  16.6 us (3%)
    pallas_call x1, Pallas kernels, ring_gather(): pl.pallas_call(functools.partial(gather_kernel, seq_count, bounds), in_sp...  89.1 us
    pallas_call x1, Pallas kernels, glu_layer(): pl.pallas_call(functools.partial(glu_kernel, blocks, seq_count, ringed),...  82 us
    pallas_call x1, Pallas kernels, self_back(): pl.pallas_call(functools.partial(self_back_kernel, seq_count, pairs, scor...  66.1 us
    ppermute x5, waiting for transfers between devices, head_total(): total = total + lax.ppermute(low, 'head', pairs).astype(jnp.float32)  61.6 us
    pallas_call x1, Pallas kernels, tail_sums(): pl.pallas_call(functools.partial(tail_kernel, seq_count, head_count, len(...  58.5 us
    dot_general x11, matrix products, product_t(): lax.dot_general(matrix_a, matrix_b, (((1,), (1,)), ((), ())), preferred_e...  41.9 us
    dot_general x14, matrix products, product(): return jnp.dot(matrix_a, matrix_b, preferred_element_type=jnp.float32)  39.6 us
  transfers between devices with their start and end apart: 16, of which 4 were waited for; matrix products, arithmetic and copies ran while one was open for 31% of the time, Pallas kernels for 10%

profile of v4, /device:TPU:0, one launch (start us, length us, event | category | flops | bytes accessed | tf_op | source)
XLA Modules:
  0.0 638.6 jit_solution(1994331068458092904)
XLA Ops:
  11.4 1.6 convert_dynamic-update-slice_fusion.5
  13.0 1.6 convert_dynamic-update-slice_fusion.4
  14.7 1.7 convert_dynamic-update-slice_fusion.3
  16.4 1.6 convert_dynamic-update-slice_fusion.2
  20.1 89.1 %ring_gather.1 = (bf16[8,2,96,5504]{3,2,1,0:T(8,128)(2,1)}, f32[8,128]{1,0:T(8,128)}) custom-call(bf16[96,5504]{1,0:T(8,128)(2,1)} %maximum_dynamic-update-slice_fusion.local), custom_call_target="tpu_custom_call" | custom-call | bytes 270532608 | tf_op jit(solution)/shard_map/ring_gather/pallas_call | solution.py:420
  119.1 7.7 %fusion.153 = (bf16[400,2304]{1,0:T(8,128)(2,1)}, f32[400,2304]{1,0:T(8,128)S(1)}) fusion(bf16[1536,5504]{1,0:T(8,128)(2,1)} %bitcast.154, f32[1536]{0:T(1024)S(1)} %get-tuple-element.92, f32[400]{0:T(512)S(1)} %add_rsqrt_fusion.2, f32[400]{0:T(512)S(1)} %broadcast_multiply_fusion.8, bf16[2,1536]{1,0:T(2,128)(2,1)S(1)} %constant_dynamic-slice_fusion.1, ...), kind=kOutput, calls=%fused_computation.321 | convolution fusion | flops 2838220800 | bytes 13802624 | tf_op jit(solution)/shard_map/dot_general | solution.py:83
  135.8 4.2 collective-permute-start
  140.0 3.4 slice.314
  143.5 2.7 copy.132
  146.1 1.8 slice.309
  165.9 2.6 convolution_convert_fusion.7
  168.6 4.4 fusion.23
  173.0 2.1 pad_maximum_fusion.refs_1_.refs_2_
  175.1 1.9 fusion.146
  177.5 2.6 copy.133
  180.1 2.5 copy.131
  182.6 4.5 fusion
  187.2 4.5 fusion.1
  192.7 5.9 fusion.48
  198.8 4.1 convolution_convert_fusion.3
  202.8 1.6 collective-permute-start.2
  210.1 2.7 copy.150.refs_0_
  216.0 15.1 %collective-permute-done.2 = bf16[384,1536]{1,0:T(8,128)(2,1)} collective-permute-done((bf16[384,1536]{1,0:T(8,128)(2,1)}, bf16[384,1536]{1,0:T(8,128)(2,1)}, u32[]{:S(2)}, u32[]{:S(2)}) %collective-permute-start.2) | collective-permute-done | bytes 1179680 | tf_op jit(solution)/shard_map/ppermute | solution.py:1220
  231.1 2.2 fusion.144
  234.7 2.9 fusion.53
  242.0 3.0 convolution_convert_fusion.2
  245.1 1.7 collective-permute-start.3
  246.8 3.7 fusion.25.top_t
  250.5 1.8 subtract_multiply_fusion
  253.6 20.3 %collective-permute-done.3 = bf16[384,1536]{1,0:T(8,128)(2,1)} collective-permute-done((bf16[384,1536]{1,0:T(8,128)(2,1)S(1)}, bf16[384,1536]{1,0:T(8,128)(2,1)}, u32[]{:S(2)}, u32[]{:S(2)}) %collective-permute-start.3) | collective-permute-done | bytes 1179680 | tf_op jit(solution)/shard_map/ppermute | solution.py:1220
  273.9 2.8 fusion.143
  278.8 3.9 fusion.24.normed_t
  282.7 82.0 %glu_layer.1 = (bf16[384,1536]{1,0:T(8,128)(2,1)}, bf16[384,1536]{1,0:T(8,128)(2,1)}, f32[2,3072]{1,0:T(2,128)}, bf16[3,3,96,3072]{3,2,1,0:T(8,128)(2,1)}, bf16[2,3,96,3072]{3,2,1,0:T(8,128)(2,1)}) custom-call(bf16[384,1536]{1,0:T(8,128)(2,1)} %copy-done.35, bf16[1536,384]{1,0:T(8,128)(2,1)} %fusion.24.normed_t, bf16[384,1536]{1,0:T(8,128)(2,1)} %top.1, ...), custom_call_target="tpu_custom_call" | custom-call | flops 32614907904 | bytes 56623104 | tf_op jit(solution)/shard_map/glu_layer/pallas_call | solution.py:647
  366.2 5.6 fusion.27
  371.8 2.2 slice_bitcast_fusion.1
  376.4 15.4 %collective-permute-done.4 = bf16[384,1536]{1,0:T(8,128)(2,1)S(1)} collective-permute-done((bf16[384,1536]{1,0:T(8,128)(2,1)}, bf16[384,1536]{1,0:T(8,128)(2,1)S(1)}, u32[]{:S(2)}, u32[]{:S(2)}) %collective-permute-start.4) | collective-permute-done | bytes 1179680 | tf_op jit(solution)/shard_map/ppermute | solution.py:1220
  393.3 1.9 convert_reduce_fusion
  395.2 4.4 fusion.56
  399.6 3.7 fusion.26
  404.7 3.1 convolution_convert_fusion.6
  407.9 3.5 multiply_reduce_fusion
  416.0 4.1 convolution_convert_fusion.1
  420.1 1.6 collective-permute-start.7
  421.7 1.8 convolution_convert_fusion.5
  423.6 5.1 fusion.21
  432.4 2.6 copy.144
  435.0 3.1 add_convert_fusion.5.refs_11_
  438.1 10.7 %collective-permute-done.7 = bf16[384,1536]{1,0:T(8,128)(2,1)} collective-permute-done((bf16[384,1536]{1,0:T(8,128)(2,1)}, bf16[384,1536]{1,0:T(8,128)(2,1)}, u32[]{:S(2)}, u32[]{:S(2)}) %collective-permute-start.7) | collective-permute-done | bytes 1179680 | tf_op jit(solution)/shard_map/ppermute | solution.py:1220
  448.8 2.0 convert_add_fusion.4
  450.8 3.2 add_convert_fusion.4.refs_12_
  454.1 1.6 multiply_reduce_fusion.4
  456.6 2.7 fusion.28
  459.3 1.8 convolution_convert_fusion.4
  461.2 3.6 fusion.50.refs_5_
  466.2 2.8 slice_bitcast_fusion.refs_4_
  472.5 3.1 add_convert_fusion.2.refs_13_
  475.6 66.1 %self_back.1 = (bf16[400,2304]{1,0:T(8,128)(2,1)}, f32[96,3072]{1,0:T(8,128)}) custom-call(bf16[384,768]{1,0:T(8,128)(2,1)} %copy.148.refs_0_, bf16[2,896,768]{2,1,0:T(8,128)(2,1)} %copy-done.5, bf16[2,896,768]{2,1,0:T(8,128)(2,1)} %copy-done.5, bf16[16,2304]{1,0:T(8,128)(2,1)} %slice.320.refs_3_.refs_4_, bf16[16,2304]{1,0:T(8,128)(2,1)} %slice.320.refs_3_.refs_4_, ...), custom_call_target="tpu_custom_call" | custom-call | flops 2642411520 | bytes 37748736 | tf_op jit(solution)/shard_map/self_back/pallas_call | solution.py:1141
  541.7 3.5 convert_add_fusion.3
  545.2 5.3 fusion.9
  555.7 58.5 %tail_sums.1 = (f32[96,2304]{1,0:T(8,128)}, f32[16,1536]{1,0:T(8,128)}, f32[384,1536]{1,0:T(8,128)}, f32[3,96,3072]{2,1,0:T(8,128)}) custom-call(bf16[1536,400]{1,0:T(8,128)(2,1)} %copy.150.refs_0_, bf16[400,2304]{1,0:T(8,128)(2,1)} %get-tuple-element.69.refs_1_, f32[16,1536]{1,0:T(8,128)} %pad_maximum_fusion.10.refs_2_, bf16[384,1536]{1,0:T(8,128)(2,1)} %slice.423.refs_3_, ...), custom_call_target="tpu_custom_call" | custom-call | flops 2831155200 | bytes 28311552 | tf_op jit(solution)/shard_map/tail_sums/pallas_call | solution.py:929
  615.9 3.0 multiply_reduce_fusion.10
  620.8 1.9 slice_bitcast_fusion.3
  623.9 3.3 add_convert_fusion.1
  627.9 3.4 add_convert_fusion
  (372 shorter events, 93.1 us)
Async XLA Ops:
  7.2 149.8 %copy-start = (bf16[6,128,768]{2,1,0:T(8,128)(2,1)S(1)}, bf16[6,128,768]{2,1,0:T(8,128)(2,1)}, u32[]{:S(2)}) copy-start(bf16[6,128,768]{2,1,0:T(8,128)(2,1)} %param.24) | copy-start | bytes 3538948
  7.2 102.0 %copy-start.31 = (f32[96,3072]{1,0:T(8,128)S(1)}, f32[96,3072]{1,0:T(8,128)}, u32[]{:S(2)}) copy-start(f32[96,3072]{1,0:T(8,128)} %param.39) | copy-start | bytes 3538948
  7.2 275.5 %all-gather.2.cloned.1.call-start = ((), (), s32[]{:S(2)}) async-start(), calls=%async_computation | async-start | bytes 30081024 | tf_op jit(solution)/shard_map/all_gather | solution.py:1225
  8.9 9.1 %copy-start.52 = (f32[96,768]{1,0:T(8,128)S(1)}, f32[96,768]{1,0:T(8,128)}, u32[]{:S(2)}) copy-start(f32[96,768]{1,0:T(8,128)} %param.33) | copy-start | bytes 884740
  8.9 9.8 %copy-start.53 = (f32[96,768]{1,0:T(8,128)S(1)}, f32[96,768]{1,0:T(8,128)}, u32[]{:S(2)}) copy-start(f32[96,768]{1,0:T(8,128)} %param.36) | copy-start | bytes 884740
  14.7 94.6 %copy-start.32 = (f32[96,3072]{1,0:T(8,128)S(1)}, f32[96,3072]{1,0:T(8,128)}, u32[]{:S(2)}) copy-start(f32[96,3072]{1,0:T(8,128)} %param.38) | copy-start | bytes 3538948
  111.9 5.2 copy-start.8
  118.6 50.0 %copy-start.57 = (f32[1536]{0:T(1024)}, f32[1536]{0:T(1024)S(1)}, u32[]{:S(2)}) copy-start(f32[1536]{0:T(1024)S(1)} %get-tuple-element.92) | copy-start | bytes 18436
  118.6 8.2 %copy-start.80 = (f32[400]{0:T(512)}, f32[400]{0:T(512)S(1)}, u32[]{:S(2)}) copy-start(f32[400]{0:T(512)S(1)} %broadcast_multiply_fusion.8) | copy-start | bytes 4804
  119.1 7.7 %copy-start.76 = (f32[400]{0:T(512)}, f32[400]{0:T(512)S(1)}, u32[]{:S(2)}) copy-start(f32[400]{0:T(512)S(1)} %add_rsqrt_fusion.2) | copy-start | bytes 4804
  134.6 38.4 %collective-permute-start.1 = (bf16[2,256,768]{2,1,0:T(8,128)(2,1)}, bf16[2,256,768]{2,1,0:T(8,128)(2,1)}, u32[]{:S(2)}, u32[]{:S(2)}) collective-permute-start(bf16[2,256,768]{2,1,0:T(8,128)(2,1)} %get-tuple-element.126), channel_id=1, source_target_pairs={{2,0},{4,2},{6,4},{8,6},{10,8},{12,10},{14,12},{16,14},{18,16},{20... | collective-permute-start | bytes 2359304 | tf_op jit(solution)/shard_map/ppermute | solution.py:28
  135.8 37.2 %collective-permute-start = (bf16[2,256,768]{2,1,0:T(8,128)(2,1)}, bf16[2,256,768]{2,1,0:T(8,128)(2,1)}, u32[]{:S(2)}, u32[]{:S(2)}) collective-permute-start(bf16[2,256,768]{2,1,0:T(8,128)(2,1)} %get-tuple-element.125), channel_id=1, source_target_pairs={{0,2},{2,4},{4,6},{6,8},{8,10},{10,12},{12,14},{14,16},{16,18},{18... | collective-permute-start | bytes 2359304 | tf_op jit(solution)/shard_map/ppermute | solution.py:25
  151.8 7.6 %copy-start.44 = (f32[384,16]{0,1:T(8,128)S(1)}, f32[384,16]{0,1:T(8,128)}, u32[]{:S(2)}) copy-start(f32[384,16]{0,1:T(8,128)} %copy-done.43) | copy-start | bytes 73732
  151.8 7.6 %copy-start.46 = (f32[384,16]{0,1:T(8,128)S(1)}, f32[384,16]{0,1:T(8,128)}, u32[]{:S(2)}) copy-start(f32[384,16]{0,1:T(8,128)} %copy-done.45) | copy-start | bytes 73732
  151.8 7.6 %copy-start.94 = (f32[64]{0:T(128)S(1)}, f32[64]{0:T(128)}, u32[]{:S(2)}) copy-start(f32[64]{0:T(128)} %pad.43.clone) | copy-start | bytes 772
  151.8 7.6 %copy-start.95 = (f32[64]{0:T(128)S(1)}, f32[64]{0:T(128)}, u32[]{:S(2)}) copy-start(f32[64]{0:T(128)} %pad.46.clone) | copy-start | bytes 772
  151.8 9.5 %copy-start.89 = (bf16[2,12,64]{2,1,0:T(8,128)(2,1)S(1)}, bf16[2,12,64]{2,1,0:T(8,128)(2,1)}, u32[]{:S(2)}) copy-start(bf16[2,12,64]{2,1,0:T(8,128)(2,1)} %reshape.544) | copy-start | bytes 9220
  151.8 10.3 %copy-start.11 = (bf16[1536,768]{1,0:T(8,128)(2,1)S(1)}, bf16[1536,768]{1,0:T(8,128)(2,1)}, u32[]{:S(2)}) copy-start(bf16[1536,768]{1,0:T(8,128)(2,1)} %slice.314) | copy-start | bytes 7077892
  152.7 9.4 %copy-start.73 = (s32[384]{0:T(512)}, s32[384]{0:T(512)S(1)}, u32[]{:S(2)}) copy-start(s32[384]{0:T(512)S(1)} %broadcast_subtract_fusion) | copy-start | bytes 4612
  153.5 8.6 %copy-start.66 = (s32[896]{0:T(1024)}, s32[896]{0:T(1024)S(1)}, u32[]{:S(2)}) copy-start(s32[896]{0:T(1024)S(1)} %pad_dynamic-slice_fusion) | copy-start | bytes 10756
  157.0 6.3 copy-start.19
  163.3 5.3 copy-start.77
  187.2 5.5 copy-start.27
  198.7 7.3 %copy-start.67 = (s32[896]{0:T(1024)S(1)}, s32[896]{0:T(1024)}, u32[]{:S(2)}) copy-start(s32[896]{0:T(1024)} %copy-done.66) | copy-start | bytes 10756
  198.7 8.2 %copy-start.85 = (s32[384]{0:T(512)S(1)}, s32[384]{0:T(512)}, u32[]{:S(2)}) copy-start(s32[384]{0:T(512)} %copy-done.84) | copy-start | bytes 4612
  198.7 8.8 %copy-start.74 = (s32[384]{0:T(512)S(1)}, s32[384]{0:T(512)}, u32[]{:S(2)}) copy-start(s32[384]{0:T(512)} %copy-done.73) | copy-start | bytes 4612
  198.7 9.4 %copy-start.25 = (bf16[256,768]{1,0:T(8,128)(2,1)S(1)}, bf16[256,768]{1,0:T(8,128)(2,1)}, u32[]{:S(2)}) copy-start(bf16[256,768]{1,0:T(8,128)(2,1)} %convolution_convert_fusion.8) | copy-start | bytes 1179652
  198.7 9.5 %copy-start.26 = (bf16[256,768]{1,0:T(8,128)(2,1)S(1)}, bf16[256,768]{1,0:T(8,128)(2,1)}, u32[]{:S(2)}) copy-start(bf16[256,768]{1,0:T(8,128)(2,1)} %convolution_convert_fusion.7) | copy-start | bytes 1179652
  202.8 28.3 %collective-permute-start.2 = (bf16[384,1536]{1,0:T(8,128)(2,1)}, bf16[384,1536]{1,0:T(8,128)(2,1)}, u32[]{:S(2)}, u32[]{:S(2)}) collective-permute-start(bf16[384,1536]{1,0:T(8,128)(2,1)} %convolution_convert_fusion.3), channel_id=1, source_target_pairs={{0,1},{1,0},{2,3},{3,2},{4,5},{5,4},{6,7},{7,6},{8,9},{9,8},{10,11... | collective-permute-start | bytes 3538952 | tf_op jit(solution)/shard_map/ppermute | solution.py:1220
  204.4 5.5 copy-start.42
  208.3 31.2 %copy-start.23 = (bf16[256,768]{0,1:T(8,128)(2,1)}, bf16[256,768]{0,1:T(8,128)(2,1)S(1)}, u32[]{:S(2)}) copy-start(bf16[256,768]{0,1:T(8,128)(2,1)S(1)} %copy.136) | copy-start | bytes 1179652
  208.5 29.4 %copy-start.15 = (bf16[256,768]{0,1:T(8,128)(2,1)}, bf16[256,768]{0,1:T(8,128)(2,1)S(1)}, u32[]{:S(2)}) copy-start(bf16[256,768]{0,1:T(8,128)(2,1)S(1)} %copy.138) | copy-start | bytes 1179652
  242.0 4.8 copy-start.28
  245.0 5.5 copy-start.34
  245.0 5.5 copy-start.78
  245.1 5.4 copy-start.81
  245.1 28.8 %collective-permute-start.3 = (bf16[384,1536]{1,0:T(8,128)(2,1)S(1)}, bf16[384,1536]{1,0:T(8,128)(2,1)}, u32[]{:S(2)}, u32[]{:S(2)}) collective-permute-start(bf16[384,1536]{1,0:T(8,128)(2,1)S(1)} %convolution_convert_fusion.2), channel_id=1, source_target_pairs={{0,1},{1,0},{2,3},{3,2},{4,5},{5,4},{6,7},{7,6},{8,9},{9,8},{10,11... | collective-permute-start | bytes 3538952 | tf_op jit(solution)/shard_map/ppermute | solution.py:1220
  282.7 83.4 %copy-start.69 = (f32[384]{0:T(512)S(1)}, f32[384]{0:T(512)}, u32[]{:S(2)}) copy-start(f32[384]{0:T(512)} %copy-done.68) | copy-start | bytes 4612
  282.7 83.5 %copy-start.83 = (f32[384]{0:T(512)S(1)}, f32[384]{0:T(512)}, u32[]{:S(2)}) copy-start(f32[384]{0:T(512)} %copy-done.82) | copy-start | bytes 4612
  364.7 27.1 %collective-permute-start.4 = (bf16[384,1536]{1,0:T(8,128)(2,1)}, bf16[384,1536]{1,0:T(8,128)(2,1)S(1)}, u32[]{:S(2)}, u32[]{:S(2)}) collective-permute-start(bf16[384,1536]{1,0:T(8,128)(2,1)} %get-tuple-element.53), channel_id=1, source_target_pairs={{0,1},{1,0},{2,3},{3,2},{4,5},{5,4},{6,7},{7,6},{8,9},{9,8},{10,11... | collective-permute-start | bytes 3538952 | tf_op jit(solution)/shard_map/ppermute | solution.py:1220
  366.2 5.7 copy-start.18
  371.8 20.0 %copy-start.14 = (bf16[384,1536]{1,0:T(8,128)(2,1)S(1)}, bf16[384,1536]{1,0:T(8,128)(2,1)}, u32[]{:S(2)}) copy-start(bf16[384,1536]{1,0:T(8,128)(2,1)} %get-tuple-element.53) | copy-start | bytes 3538948
  374.0 42.0 %collective-permute-start.5 = (bf16[3,96,3072]{2,1,0:T(8,128)(2,1)}, bf16[3,96,3072]{2,1,0:T(8,128)(2,1)}, u32[]{:S(2)}, u32[]{:S(2)}) collective-permute-start(bf16[3,96,3072]{2,1,0:T(8,128)(2,1)} %get-tuple-element.107), channel_id=1, source_target_pairs={{0,8},{2,10},{8,16},{10,18},{16,24},{18,26},{24,28},{26,30},{28,20... | collective-permute-start | bytes 5308424 | tf_op jit(solution)/shard_map/ppermute | solution.py:259
  374.9 18.4 %copy-start.29 = (bf16[384,1536]{1,0:T(8,128)(2,1)S(1)}, bf16[384,1536]{1,0:T(8,128)(2,1)}, u32[]{:S(2)}) copy-start(bf16[384,1536]{1,0:T(8,128)(2,1)} %top.1) | copy-start | bytes 3538948
  374.9 41.0 %collective-permute-start.6 = (bf16[3,96,3072]{2,1,0:T(8,128)(2,1)}, bf16[3,96,3072]{2,1,0:T(8,128)(2,1)}, u32[]{:S(2)}, u32[]{:S(2)}) collective-permute-start(bf16[3,96,3072]{2,1,0:T(8,128)(2,1)} %get-tuple-element.106), channel_id=1, source_target_pairs={{0,4},{2,6},{8,0},{10,2},{16,8},{18,10},{24,16},{26,18},{28,24},{3... | collective-permute-start | bytes 5308424 | tf_op jit(solution)/shard_map/ppermute | solution.py:260
  407.8 27.1 %collective-permute-start.8 = (bf16[768,768]{1,0:T(8,128)(2,1)}, bf16[768,768]{1,0:T(8,128)(2,1)}, u32[]{:S(2)}, u32[]{:S(2)}) collective-permute-start(bf16[768,768]{1,0:T(8,128)(2,1)} %convolution_convert_fusion.6), channel_id=1, source_target_pairs={{0,2},{2,0},{4,6},{6,4},{8,10},{10,8},{12,14},{14,12},{16,18},{18,... | collective-permute-start | bytes 3538952 | tf_op jit(solution)/shard_map/ppermute | solution.py:240
  414.9 14.6 %collective-permute-start.10 = (bf16[384,1536]{1,0:T(8,128)(2,1)S(1)}, bf16[384,1536]{1,0:T(8,128)(2,1)S(1)}, u32[]{:S(2)}, u32[]{:S(2)}) collective-permute-start(bf16[384,1536]{1,0:T(8,128)(2,1)S(1)} %convolution_convert_fusion), channel_id=1, source_target_pairs={{0,2},{2,0},{4,6},{6,4},{8,10},{10,8},{12,14},{14,12},{16,18},{18,... | collective-permute-start | bytes 3538952 | tf_op jit(solution)/shard_map/ppermute | solution.py:240
  416.0 5.7 copy-start.21
  416.0 7.6 %slice-start.2 = ((s8[5308416]{0:T(1024)(128)(4,1)}), s8[4194304]{0:T(1024)(128)(4,1)S(1)}, s32[]{:S(2)}) async-start(s8[5308416]{0:T(1024)(128)(4,1)} %bitcast.119), calls=%async_computation.3 | async-start | bytes 8388608
  416.0 5.7 copy-start.48
  416.0 7.6 %slice-start.3 = ((s8[5308416]{0:T(1024)(128)(4,1)}), s8[1114112]{0:T(1024)(128)(4,1)S(1)}, s32[]{:S(2)}) async-start(s8[5308416]{0:T(1024)(128)(4,1)} %bitcast.119), calls=%async_computation.4 | async-start | bytes 2228224
  420.1 28.7 %collective-permute-start.7 = (bf16[384,1536]{1,0:T(8,128)(2,1)}, bf16[384,1536]{1,0:T(8,128)(2,1)}, u32[]{:S(2)}, u32[]{:S(2)}) collective-permute-start(bf16[384,1536]{1,0:T(8,128)(2,1)} %convolution_convert_fusion.1), channel_id=1, source_target_pairs={{0,1},{1,0},{2,3},{3,2},{4,5},{5,4},{6,7},{7,6},{8,9},{9,8},{10,11... | collective-permute-start | bytes 3538952 | tf_op jit(solution)/shard_map/ppermute | solution.py:1220
  423.5 27.2 %collective-permute-start.9 = (bf16[768,768]{1,0:T(8,128)(2,1)}, bf16[768,768]{1,0:T(8,128)(2,1)}, u32[]{:S(2)}, u32[]{:S(2)}) collective-permute-start(bf16[768,768]{1,0:T(8,128)(2,1)} %convolution_convert_fusion.5), channel_id=1, source_target_pairs={{0,2},{2,0},{4,6},{6,4},{8,10},{10,8},{12,14},{14,12},{16,18},{18,... | collective-permute-start | bytes 3538952 | tf_op jit(solution)/shard_map/ppermute | solution.py:240
  428.7 116.5 %collective-permute-start.13 = (bf16[3,96,3072]{2,1,0:T(8,128)(2,1)}, bf16[3,96,3072]{2,1,0:T(8,128)(2,1)}, u32[]{:S(2)}, u32[]{:S(2)}) collective-permute-start(bf16[3,96,3072]{2,1,0:T(8,128)(2,1)} %get-tuple-element.100), channel_id=1, source_target_pairs={{0,8},{2,10},{8,16},{10,18},{16,24},{18,26},{24,28},{26,30},{28,20... | collective-permute-start | bytes 5308424 | tf_op jit(solution)/shard_map/ppermute | solution.py:259
  429.5 115.7 %collective-permute-start.14 = (bf16[3,96,3072]{2,1,0:T(8,128)(2,1)}, bf16[3,96,3072]{2,1,0:T(8,128)(2,1)}, u32[]{:S(2)}, u32[]{:S(2)}) collective-permute-start(bf16[3,96,3072]{2,1,0:T(8,128)(2,1)} %get-tuple-element.99), channel_id=1, source_target_pairs={{0,4},{2,6},{8,0},{10,2},{16,8},{18,10},{24,16},{26,18},{28,24},{3... | collective-permute-start | bytes 5308424 | tf_op jit(solution)/shard_map/ppermute | solution.py:260
  438.1 12.7 %copy-start.22 = (bf16[12,64,384]{2,1,0:T(8,128)(2,1)S(1)}, bf16[12,64,384]{2,1,0:T(8,128)(2,1)}, u32[]{:S(2)}) copy-start(bf16[12,64,384]{2,1,0:T(8,128)(2,1)} %copy-done.21) | copy-start | bytes 1769476
  438.1 12.7 %copy-start.49 = (bf16[1536,384]{1,0:T(8,128)(2,1)S(1)}, bf16[1536,384]{1,0:T(8,128)(2,1)}, u32[]{:S(2)}) copy-start(bf16[1536,384]{1,0:T(8,128)(2,1)} %fusion.27) | copy-start | bytes 3538948
  459.3 5.4 copy-start.51
  461.2 11.4 %collective-permute-start.11 = (bf16[768,768]{1,0:T(8,128)(2,1)}, bf16[768,768]{1,0:T(8,128)(2,1)S(1)}, u32[]{:S(2)}, u32[]{:S(2)}) collective-permute-start(bf16[768,768]{1,0:T(8,128)(2,1)} %convolution_convert_fusion.4), channel_id=1, source_target_pairs={{0,2},{2,0},{4,6},{6,4},{8,10},{10,8},{12,14},{14,12},{16,18},{18,... | collective-permute-start | bytes 3538952 | tf_op jit(solution)/shard_map/ppermute | solution.py:240
  464.8 5.6 copy-start.72
  464.8 5.6 copy-start.71
  464.8 76.9 %collective-permute-start.12 = (bf16[384,1536]{1,0:T(8,128)(2,1)}, bf16[384,1536]{1,0:T(8,128)(2,1)}, u32[]{:S(2)}, u32[]{:S(2)}) collective-permute-start(bf16[384,1536]{1,0:T(8,128)(2,1)} %get-tuple-element.63), channel_id=1, source_target_pairs={{0,1},{1,0},{2,3},{3,2},{4,5},{5,4},{6,7},{7,6},{8,9},{9,8},{10,11... | collective-permute-start | bytes 3538952 | tf_op jit(solution)/shard_map/ppermute | solution.py:1220
  555.7 60.2 %copy-start.58 = (f32[1536]{0:T(1024)S(1)}, f32[1536]{0:T(1024)}, u32[]{:S(2)}) copy-start(f32[1536]{0:T(1024)} %copy-done.57) | copy-start | bytes 18436
  615.9 4.9 copy-start.17
  (54 other events, 148.7 us)
Sparse Core Ops, SparseCore 0:
  112.0 156.3 all-gather.1

commit v5 on v4

--- a/solution.py
+++ b/solution.py
@@ -194,129 +194,341 @@
     return (grad_query, grad_keys, grad_values)
 
 
+def per_device_plain(
+    frames,
+    time_token,
+    prompt,
+    clip_ids,
+    norm1_gain,
+    norm2_gain,
+    norm3_gain,
+    query_weight,
+    key_weight,
+    value_weight,
+    out_weight,
+    cross_query,
+    cross_key,
+    cross_value,
+    cross_out,
+    gate_weight,
+    up_weight,
+    down_weight,
+    gate_bias,
+    up_bias,
+    down_bias,
+    out_grad,
+):
+    local_rows = frames.shape[0]
+    clip_total = time_token.shape[0]
+    ctx_tokens = prompt.shape[1]
+    slot_count = local_rows // (2 * HALF) + 2
+    seq_index = lax.axis_index("seq")
+    head_index = lax.axis_index("head")
+    first_row = seq_index * local_rows
+    score_scale = HD ** (-0.5)
+    block_rows = min(local_rows, 2 * HALF)
+    block_count = local_rows // block_rows
+    window = block_rows + 2 * HALF
+    block_indices = jnp.arange(block_count, dtype=jnp.int32)
+
+    def branch_total(partial_sum):
+        return lax.psum(partial_sum.astype(jnp.bfloat16), "head").astype(jnp.float32)
+
+    def back_total(partial_sum):
+        return lax.psum(partial_sum.astype(jnp.bfloat16), "head").astype(jnp.float32)
+
+    (
+        gain_one,
+        gain_two,
+        gain_three,
+        w_query,
+        w_key,
+        w_value,
+        w_out,
+        c_query,
+        c_key,
+        c_value,
+        c_out,
+        w_gate,
+        w_up,
+        w_down,
+        b_down,
+    ) = (
+        lax.all_gather(norm1_gain.astype(jnp.bfloat16), "seq", axis=0, tiled=True),
+        lax.all_gather(norm2_gain.astype(jnp.bfloat16), "seq", axis=0, tiled=True),
+        lax.all_gather(norm3_gain.astype(jnp.bfloat16), "seq", axis=0, tiled=True),
+        lax.all_gather(query_weight.astype(jnp.bfloat16), "seq", axis=0, tiled=True),
+        lax.all_gather(key_weight.astype(jnp.bfloat16), "seq", axis=0, tiled=True),
+        lax.all_gather(value_weight.astype(jnp.bfloat16), "seq", axis=0, tiled=True),
+        lax.all_gather(out_weight.astype(jnp.bfloat16), "seq", axis=0, tiled=True),
+        lax.all_gather(cross_query.astype(jnp.bfloat16), "seq", axis=0, tiled=True),
+        lax.all_gather(cross_key.astype(jnp.bfloat16), "seq", axis=0, tiled=True),
+        lax.all_gather(cross_value.astype(jnp.bfloat16), "seq", axis=0, tiled=True),
+        lax.all_gather(cross_out.astype(jnp.bfloat16), "seq", axis=0, tiled=True),
+        lax.all_gather(gate_weight.astype(jnp.bfloat16), "seq", axis=0, tiled=True),
+        lax.all_gather(up_weight.astype(jnp.bfloat16), "seq", axis=0, tiled=True),
+        lax.all_gather(down_weight.astype(jnp.bfloat16), "seq", axis=0, tiled=True),
+        lax.all_gather(down_bias.astype(jnp.bfloat16), "seq", axis=0, tiled=True),
+    )
+    gain_one_f = gain_one.astype(jnp.float32)
+    gain_two_f = gain_two.astype(jnp.float32)
+    positions = first_row + jnp.arange(local_rows, dtype=jnp.int32)
+    cos_table, sin_table = angles(positions)
+    padded_ids = jnp.pad(clip_ids, (HALF, HALF), constant_values=-1)
+    own_ids = lax.dynamic_slice_in_dim(clip_ids, first_row, local_rows)
+    near_ids = lax.dynamic_slice_in_dim(padded_ids, first_row, local_rows + 2 * HALF)
+    base_clip = jnp.minimum(own_ids[0], clip_total - slot_count)
+    own_slot = own_ids - base_clip
+    slot_range = jnp.arange(slot_count, dtype=jnp.int32)
+    frames_f = frames.astype(jnp.float32)
+    normed_out, normal_one, inverse_one = layer_norm_parts(frames_f, gain_one_f)
+    normed_one = normed_out.astype(jnp.bfloat16)
+    query_rows = rotate(product(normed_one, w_query), cos_table, sin_table).astype(jnp.bfloat16)
+    key_rows = rotate(product(normed_one, w_key), cos_table, sin_table).astype(jnp.bfloat16)
+    value_rows = product(normed_one, w_value).astype(jnp.bfloat16)
+    local_width = query_rows.shape[1]
+    head_count = local_width // HD
+    near = extended(jnp.stack([key_rows, value_rows]), (("seq", 1),), HALF)
+    near_key_h = near[0].reshape(local_rows + 2 * HALF, head_count, HD)
+    near_value_h = near[1].reshape(local_rows + 2 * HALF, head_count, HD)
+    query_all_h = query_rows.reshape(local_rows, head_count, HD)
+    stamp_rows = lax.dynamic_slice_in_dim(time_token, base_clip, slot_count, 0).astype(jnp.float32)
+    stamp_out, stamp_normal, stamp_inverse = layer_norm_parts(stamp_rows, gain_one_f)
+    stamp_normed = stamp_out.astype(jnp.bfloat16)
+    stamp_key_h = (
+        product(stamp_normed, w_key).astype(jnp.bfloat16).reshape(slot_count, head_count, HD)
+    )
+    stamp_value_h = (
+        product(stamp_normed, w_value).astype(jnp.bfloat16).reshape(slot_count, head_count, HD)
+    )
+
+    def self_parts(block_index):
+        row_start = block_index * block_rows
+        query_pos = row_start + jnp.arange(block_rows, dtype=jnp.int32)
+        key_pos = row_start - HALF + jnp.arange(window, dtype=jnp.int32)
+        visible = (own_ids[:, None] == near_ids[None, :]) & (
+            jnp.abs(query_pos[:, None] - key_pos[None, :]) <= HALF
+        )
+        own_stamp = own_slot[:, None] == slot_range[None, :]
+        return (
+            query_all_h,
+            [(near_key_h, near_value_h, visible), (stamp_key_h, stamp_value_h, own_stamp)],
+        )
+
+    def self_forward(block_index):
+        query_h, key_parts = self_parts(block_index)
+        attn_mixed, log_total = attend_forward(query_h, key_parts, score_scale)
+        return (attn_mixed.reshape(block_rows, local_width).astype(jnp.bfloat16), log_total)
+
+    attn_blocks, self_logs = lax.map(self_forward, block_indices)
+    attn_mixed = attn_blocks.reshape(local_rows, local_width)
+    h_one = frames_f + branch_total(product_t(attn_mixed, w_out))
+    middle_out, normal_two, inverse_two = layer_norm_parts(h_one, gain_two_f)
+    normed_two = middle_out.astype(jnp.bfloat16)
+    cross_rows = product(normed_two, c_query).astype(jnp.bfloat16)
+    cross_all_h = cross_rows.reshape(local_rows, head_count, HD)
+    context_rows = lax.dynamic_slice_in_dim(prompt, base_clip, slot_count, 0).reshape(
+        slot_count * ctx_tokens, prompt.shape[2]
+    )
+    ctx_key_h = (
+        product(context_rows, c_key)
+        .astype(jnp.bfloat16)
+        .reshape(slot_count * ctx_tokens, head_count, HD)
+    )
+    ctx_value_h = (
+        product(context_rows, c_value)
+        .astype(jnp.bfloat16)
+        .reshape(slot_count * ctx_tokens, head_count, HD)
+    )
+    key_slot = jnp.arange(slot_count * ctx_tokens, dtype=jnp.int32) // ctx_tokens
+
+    def cross_parts(block_index):
+        row_start = block_index * block_rows
+        visible = own_slot[:, None] == key_slot[None, :]
+        return (cross_all_h, [(ctx_key_h, ctx_value_h, visible)])
+
+    def cross_forward(block_index):
+        query_h, key_parts = cross_parts(block_index)
+        cross_mix, log_total = attend_forward(query_h, key_parts, score_scale)
+        return (cross_mix.reshape(block_rows, local_width).astype(jnp.bfloat16), log_total)
+
+    cross_blocks, cross_logs = lax.map(cross_forward, block_indices)
+    cross_mixed = cross_blocks.reshape(local_rows, local_width)
+    h_two = h_one + branch_total(product_t(cross_mixed, c_out))
+    gain_three_f = gain_three.astype(jnp.float32)
+    third_out, normal_three, inverse_three = layer_norm_parts(h_two, gain_three_f)
+    normed_three = third_out.astype(jnp.bfloat16)
+    gate_pre = product(normed_three, w_gate) + gate_bias
+    up_pre = product(normed_three, w_up) + up_bias
+    hidden = (jax.nn.silu(gate_pre) * up_pre).astype(jnp.bfloat16)
+    result = (h_two + branch_total(product_t(hidden, w_down)) + b_down.astype(jnp.float32)).astype(
+        jnp.bfloat16
+    )
+    grad_top = out_grad.astype(jnp.float32)
+    grad_hidden = product(out_grad, w_down)
+    sigmoid_gate = jax.nn.sigmoid(gate_pre)
+    grad_up = (grad_hidden * gate_pre * sigmoid_gate).astype(jnp.bfloat16)
+    grad_gate = (
+        grad_hidden * up_pre * sigmoid_gate * (1.0 + gate_pre * (1.0 - sigmoid_gate))
+    ).astype(jnp.bfloat16)
+    gate_bias_local = jnp.sum(grad_gate.astype(jnp.float32), axis=0)
+    up_bias_local = jnp.sum(grad_up.astype(jnp.float32), axis=0)
+    grad_normed_three = back_total(product_t(grad_gate, w_gate) + product_t(grad_up, w_up))
+    glu_terms = (
+        product_tn(normed_three, grad_gate),
+        product_tn(normed_three, grad_up),
+        product_tn(out_grad, hidden),
+        jnp.sum(grad_normed_three * normal_three, axis=0),
+        jnp.sum(grad_top, axis=0),
+    )
+    grad_h_two = grad_top + norm_back(grad_normed_three, normal_three, inverse_three, gain_three_f)
+    grad_two_low = grad_h_two.astype(jnp.bfloat16)
+    grad_cross_mixed = product(grad_two_low, c_out).astype(jnp.bfloat16)
+    cross_out_term = product_tn(grad_two_low, cross_mixed)
+    grad_cross_h = grad_cross_mixed.reshape(local_rows, head_count, HD)
+
+    def cross_step(ctx_grads, block_index):
+        query_h, key_parts = cross_parts(block_index)
+        grad_query, grad_keys, grad_values = attend_backward(
+            query_h, key_parts, score_scale, cross_logs[block_index], grad_cross_h
+        )
+        return (ctx_grads + jnp.stack([grad_keys[0], grad_values[0]]), grad_query)
+
+    ctx_grads, grad_cross_q = lax.scan(
+        cross_step,
+        jnp.zeros((2, slot_count * ctx_tokens, head_count, HD), jnp.float32),
+        block_indices,
+    )
+    grad_cross_query = grad_cross_q.reshape(local_rows, local_width).astype(jnp.bfloat16)
+    context_float = context_rows.astype(jnp.float32)
+    cross_key_term = exact_tn(context_float, ctx_grads[0].reshape(-1, local_width))
+    cross_value_term = exact_tn(context_float, ctx_grads[1].reshape(-1, local_width))
+    cross_query_term = product_tn(normed_two, grad_cross_query)
+    grad_normed_two = back_total(product_t(grad_cross_query, c_query))
+    gain_two_term = jnp.sum(grad_normed_two * normal_two, axis=0)
+    grad_h_one = grad_h_two + norm_back(grad_normed_two, normal_two, inverse_two, gain_two_f)
+    grad_one_low = grad_h_one.astype(jnp.bfloat16)
+    grad_attn = product(grad_one_low, w_out).astype(jnp.bfloat16)
+    out_term = product_tn(grad_one_low, attn_mixed)
+    grad_attn_h = grad_attn.reshape(local_rows, head_count, HD)
+
+    def self_step(grad_state, block_index):
+        near_grads, stamp_grads = grad_state
+        query_h, key_parts = self_parts(block_index)
+        row_start = block_index * block_rows
+        grad_query, grad_keys, grad_values = attend_backward(
+            query_h, key_parts, score_scale, self_logs[block_index], grad_attn_h
+        )
+        prior = near_grads
+        near_grads = prior + jnp.stack([grad_keys[0], grad_values[0]])
+        stamp_grads = stamp_grads + jnp.stack([grad_keys[1], grad_values[1]])
+        return ((near_grads, stamp_grads), grad_query)
+
+    start_state = (
+        jnp.zeros((2, local_rows + 2 * HALF, head_count, HD), jnp.float32),
+        jnp.zeros((2, slot_count, head_count, HD), jnp.float32),
+    )
+    (near_grads, stamp_grads), grad_query_blocks = lax.scan(self_step, start_state, block_indices)
+    near_grads = near_grads.reshape(2, local_rows + 2 * HALF, local_width)
+    from_above = passed_along(near_grads[:, :HALF].astype(jnp.bfloat16), "seq", -1).astype(
+        jnp.float32
+    )
+    from_below = passed_along(
+        near_grads[:, HALF + local_rows :].astype(jnp.bfloat16), "seq", 1
+    ).astype(jnp.float32)
+    own_grads = (
+        near_grads[:, HALF : HALF + local_rows]
+        + jnp.pad(from_below, ((0, 0), (0, local_rows - HALF), (0, 0)))
+        + jnp.pad(from_above, ((0, 0), (local_rows - HALF, 0), (0, 0)))
+    )
+    grad_query_rows = rotate(
+        grad_query_blocks.reshape(local_rows, local_width), cos_table, -sin_table
+    ).astype(jnp.bfloat16)
+    grad_key_rows = rotate(own_grads[0], cos_table, -sin_table).astype(jnp.bfloat16)
+    grad_value_rows = own_grads[1].astype(jnp.bfloat16)
+    stamp_key_grad = stamp_grads[0].reshape(slot_count, local_width)
+    stamp_value_grad = stamp_grads[1].reshape(slot_count, local_width)
+    stamp_float = stamp_normed.astype(jnp.float32)
+    query_term = product_tn(normed_one, grad_query_rows)
+    key_term = product_tn(normed_one, grad_key_rows) + exact_tn(stamp_float, stamp_key_grad)
+    value_term = product_tn(normed_one, grad_value_rows) + exact_tn(stamp_float, stamp_value_grad)
+    grad_normed_one = back_total(
+        product_t(grad_query_rows, w_query)
+        + product_t(grad_key_rows, w_key)
+        + product_t(grad_value_rows, w_value)
+    )
+    gain_one_term = jnp.sum(grad_normed_one * normal_one, axis=0)
+    frames_grad = (
+        grad_h_one + norm_back(grad_normed_one, normal_one, inverse_one, gain_one_f)
+    ).astype(jnp.bfloat16)
+    stamp_partial = exact_t(stamp_key_grad, w_key.astype(jnp.float32)) + exact_t(
+        stamp_value_grad, w_value.astype(jnp.float32)
+    )
+    attn_shares = (
+        lax.psum_scatter(query_term, "seq", scatter_dimension=0, tiled=True),
+        lax.psum_scatter(key_term, "seq", scatter_dimension=0, tiled=True),
+        lax.psum_scatter(value_term, "seq", scatter_dimension=0, tiled=True),
+        lax.psum_scatter(out_term, "seq", scatter_dimension=0, tiled=True),
+        lax.psum_scatter(cross_query_term, "seq", scatter_dimension=0, tiled=True),
+        lax.psum_scatter(cross_key_term, "seq", scatter_dimension=0, tiled=True),
+        lax.psum_scatter(cross_value_term, "seq", scatter_dimension=0, tiled=True),
+        lax.psum_scatter(cross_out_term, "seq", scatter_dimension=0, tiled=True),
+        lax.psum_scatter(gain_one_term, "seq", scatter_dimension=0, tiled=True),
+        lax.psum_scatter(gain_two_term, "seq", scatter_dimension=0, tiled=True),
+    )
+    hidden_width = gate_bias.shape[0]
+    stamp_full = lax.dynamic_update_slice_in_dim(
+        jnp.zeros((clip_total, stamp_partial.shape[1]), jnp.float32), stamp_partial, base_clip, 0
+    )
+    bias_full = lax.dynamic_update_slice_in_dim(
+        jnp.zeros((2, hidden_width * lax.axis_size("head")), jnp.float32),
+        jnp.stack([gate_bias_local, up_bias_local]),
+        head_index * hidden_width,
+        1,
+    )
+    stamp_sum, bias_sum = lax.psum((stamp_full, bias_full), ("seq", "head"))
+    every_out, every_normal, every_inverse = layer_norm_parts(
+        time_token.astype(jnp.float32), gain_one_f
+    )
+    time_grad = norm_back(stamp_sum, every_normal, every_inverse, gain_one_f)
+    gain_rows = norm1_gain.shape[0]
+    time_gain = lax.dynamic_slice_in_dim(
+        jnp.sum(stamp_sum * every_normal, axis=0), seq_index * gain_rows, gain_rows
+    )
+    own_bias = lax.dynamic_slice_in_dim(bias_sum, head_index * hidden_width, hidden_width, 1)
+    return (
+        result,
+        frames_grad,
+        time_grad,
+        attn_shares[8] + time_gain,
+        attn_shares[9],
+        lax.psum_scatter(glu_terms[3], "seq", scatter_dimension=0, tiled=True),
+        attn_shares[0],
+        attn_shares[1],
+        attn_shares[2],
+        attn_shares[3],
+        attn_shares[4],
+        attn_shares[5],
+        attn_shares[6],
+        attn_shares[7],
+        lax.psum_scatter(glu_terms[0], "seq", scatter_dimension=0, tiled=True),
+        lax.psum_scatter(glu_terms[1], "seq", scatter_dimension=0, tiled=True),
+        lax.psum_scatter(glu_terms[2], "seq", scatter_dimension=0, tiled=True),
+        own_bias[0],
+        own_bias[1],
+        lax.psum_scatter(glu_terms[4], "seq", scatter_dimension=0, tiled=True),
+    )
+
+
 LANES = 128
+FAST_SEQ = 16
 BLOCK = 256
 TAIL_WIDTH = 768
-SELF_PIECES = 4
 QUERY_BLOCK = 128
+HOP_PAIR = 3
+MADE_AT = 1
 VMEM_BYTES = 60 * 1024 * 1024
 MESH = pl.DeviceIdType.MESH
-
-
-def ring_place(chip, chips):
-    return jnp.where(chip % 2 == 0, chip // 2, chips - 1 - chip // 2)
-
-
-def ring_chip(place, chips):
-    return jnp.where(2 * place < chips, 2 * place, 2 * (chips - 1 - place) + 1)
-
-
-def static_chip(place, chips):
-    return 2 * place if 2 * place < chips else 2 * (chips - 1 - place) + 1
-
-
-def ring_pairs(chips, step):
-    return [
-        (2 * static_chip(place, chips) + core, 2 * static_chip((place + step) % chips, chips) + core)
-        for place in range(chips)
-        for core in range(2)
-    ]
-
-
-def owner_matrix(width, seq_index, seq_count):
-    chips = seq_count // 2
-    seg = width // seq_count
-    core = seq_index % 2
-    place = ring_place(seq_index // 2, chips)
-    row = jnp.arange(width, dtype=jnp.int32)
-    which = row // (width // 2)
-    near = row % (width // 2) // seg
-    chip = ring_chip((place + near) % chips, chips)
-    source = (2 * chip + jnp.where(which == 0, core, 1 - core)) * seg + row % seg
-    return (source[:, None] == row[None, :]).astype(jnp.bfloat16)
-
-
-def over_core(values, seq_count):
-    return lax.ppermute(values, "seq", [(index, index ^ 1) for index in range(seq_count)])
-
-
-class Ring:
-    def __init__(self, term, seq_count, moving=None):
-        self.term = term
-        self.chips = seq_count // 2
-        self.far = self.chips // 2
-        self.near = self.far
-        self.ahead, self.behind = ring_pairs(self.chips, 1), ring_pairs(self.chips, -1)
-        if moving is not None:
-            self.near = self.far - 2
-            self.send(moving[0], moving[1])
-            return
-        first = term(self.far)
-        self.half = first.shape[-1] // 2
-        self.send(first[..., : self.half], first[..., self.half :])
-
-    def send(self, onward, backward):
-        self.onward = lax.ppermute(onward.astype(jnp.bfloat16), "seq", self.ahead)
-        self.backward = lax.ppermute(backward.astype(jnp.bfloat16), "seq", self.behind)
-
-    def joined(self, near, arrived, low_side):
-        term = self.term(near).astype(jnp.float32)
-        arrived = arrived.astype(jnp.float32)
-        if arrived.shape != term.shape:
-            pads = (0, self.half) if low_side else (self.half, 0)
-            arrived = jnp.pad(arrived, ((0, 0),) * (term.ndim - 1) + (pads,))
-        return term + arrived
-
-    def step(self):
-        if self.near == 1:
-            return
-        self.near -= 1
-        self.send(
-            self.joined(self.near, self.onward, True),
-            self.joined(2 * self.far - self.near, self.backward, False),
-        )
-
-    def after(self, value):
-        value, self.onward, self.backward = lax.optimization_barrier(
-            (value, self.onward, self.backward)
-        )
-        return value
-
-    def last_terms(self):
-        while self.near > 1:
-            self.step()
-        return [self.term(0), self.onward, self.backward]
-
-    def finish(self):
-        return sum(each.astype(jnp.float32) for each in self.last_terms())
-
-
-def core_sum(rows_t, columns, seq_count):
-    half = rows_t.shape[0] // 2
-    away = product(rows_t[half:], columns).astype(jnp.bfloat16)
-    arrived = over_core(away, seq_count)
-    return (product(rows_t[:half], columns) + arrived.astype(jnp.float32)).astype(jnp.bfloat16)
-
-
-def block_of(matrix, near, chips):
-    width = matrix.shape[0] // chips
-    return matrix[near * width : (near + 1) * width]
-
-
-def side_by_side(matrices, chips):
-    return lambda near: jnp.concatenate([block_of(each, near, chips) for each in matrices], axis=-1)
-
-
-def all_sum(values, axes):
-    for axis in axes:
-        count = lax.axis_size(axis)
-        bit = 1
-        while bit < count:
-            values = values + lax.ppermute(
-                values, axis, [(index, index ^ bit) for index in range(count)]
-            )
-            bit *= 2
-    return values
 
 
 def xor_place(index, bit):
@@ -414,8 +626,6 @@
 def ring_gather(local, bounds, seq_count, collective_id):
     rows, width = local.shape
     local = local.astype(jnp.bfloat16)
-    if rows % 16:
-        return lax.all_gather(local, "seq", axis=0, tiled=True), jnp.zeros((8, LANES), jnp.float32)
     pieces, far = len(bounds) - 1, seq_count // 4
     gathered, token = pl.pallas_call(
         functools.partial(gather_kernel, seq_count, bounds),
@@ -453,7 +663,6 @@
 def glu_kernel(
     blocks,
     seq_count,
-    ringed,
     normed,
     normed_t,
     top,
@@ -472,20 +681,17 @@
     index = pl.program_id(0)
     seq_index = lax.axis_index("seq")
     partner = {"seq": xor_place(seq_index, 1)}
-    half = normed_t.shape[0] // 2
+    core = seq_index % 2
     chips = seq_count // 2
-    far, seg = chips // 2, half // chips
+    far = chips // 2
     mid = BLOCK // 2
-    if ringed:
-        moving, *refs = refs
-    out_acc, grad_acc, mine, away, arrived, send_sem, recv_sem, *refs = refs
+    moving, out_acc, grad_acc, terms, arrived, send_sem, recv_sem, *refs = refs
     sides = ring_neighbours(seq_index, seq_count)
-    if ringed:
-        sums, first_send, first_land, second_send, second_land, *ring_sems = refs
+    sums, first_send, first_land, second_send, second_land, *ring_sems = refs
 
     def crossing(block):
         return pltpu.make_async_remote_copy(
-            src_ref=away.at[block % 2],
+            src_ref=terms.at[block % 2, :, :, 1 - core],
             dst_ref=arrived.at[block],
             send_sem=send_sem.at[block % 2],
             recv_sem=recv_sem.at[block],
@@ -506,7 +712,7 @@
 
     @pl.when(index == 0)
     def _():
-        greet([partner] + ([{"seq": side} for side in sides] if ringed else []))
+        greet([partner] + [{"seq": side} for side in sides])
         out_acc[...] = jnp.zeros_like(out_acc)
         grad_acc[...] = jnp.zeros_like(grad_acc)
 
@@ -532,58 +738,52 @@
             crossing(index - 2).wait_send()
 
         slot = index % 2
-        away[slot, 0] = product(normed_t[half:, :], grad_gate).astype(jnp.bfloat16)
-        away[slot, 1] = product(normed_t[half:, :], grad_up).astype(jnp.bfloat16)
-        away[slot, 2] = product(top_t[half:, :], hidden).astype(jnp.bfloat16)
+        for which, (rows_t, columns) in enumerate(
+            ((normed_t, grad_gate), (normed_t, grad_up), (top_t, hidden))
+        ):
+            term = product(rows_t[...], columns).astype(jnp.bfloat16)
+            terms[slot, which] = term.reshape(terms.shape[2:])
         crossing(index).start()
-        mine[slot, 0] = product(normed_t[:half, :], grad_gate).astype(jnp.bfloat16)
-        mine[slot, 1] = product(normed_t[:half, :], grad_up).astype(jnp.bfloat16)
-        mine[slot, 2] = product(top_t[:half, :], hidden).astype(jnp.bfloat16)
 
     def chunk(block, near):
-        return sums[block % 3, :, near * seg : (near + 1) * seg, :].astype(jnp.float32)
+        return sums[block % 3, :, chip_near(seq_index, seq_count, near)]
 
     @pl.when((index >= 1) & (index <= blocks))
     def _():
         block = index - 1
         crossing(block).wait_recv()
-        total = mine[block % 2].astype(jnp.float32) + arrived[block].astype(jnp.float32)
-        total = total.astype(jnp.bfloat16)
-        if ringed:
-            sums[block % 3] = total
-            for side in range(2):
-                first_send[block, side] = total[
-                    :, far * seg : (far + 1) * seg, side * mid : (side + 1) * mid
-                ]
-                hop(block, side, 0).start()
-            for at, near in enumerate(kept_places(seq_count)):
-                kept[at] = total[:, near * seg : (near + 1) * seg, :]
-        else:
-            kept[...] = total
-
-    if ringed:
-
-        @pl.when((index >= 2) & (index <= blocks + 1))
-        def _():
-            block = index - 2
-            for side in range(2):
-                term = chunk(block, far - 1 if side == 0 else far + 1)
-                hop(block, side, 0).wait_recv()
-                land = first_land[block, side].astype(jnp.float32)
-                low = term[:, :, :mid] + land if side == 0 else term[:, :, :mid]
-                high = term[:, :, mid:] if side == 0 else term[:, :, mid:] + land
-                second_send[block, side, :, :, :mid] = low.astype(jnp.bfloat16)
-                second_send[block, side, :, :, mid:] = high.astype(jnp.bfloat16)
-                hop(block, side, 1).start()
-
-        @pl.when(index >= 3)
-        def _():
-            block = index - 3
-            for side in range(2):
-                term = chunk(block, far - 2 if side == 0 else far + 2)
-                hop(block, side, 1).wait_recv()
-                land = second_land[block, side].astype(jnp.float32)
-                moving[side] = (term + land).astype(jnp.bfloat16)
+        total = terms[block % 2, :, :, core].astype(jnp.float32) + arrived[block].astype(
+            jnp.float32
+        )
+        sums[block % 3] = total.astype(jnp.bfloat16)
+        opposite = chunk(block, far)
+        for side in range(2):
+            first_send[block, side] = opposite[:, :, side * mid : (side + 1) * mid]
+            hop(block, side, 0).start()
+        for at, near in enumerate(kept_places(seq_count)):
+            kept[at] = chunk(block, near)
+
+    @pl.when((index >= 2) & (index <= blocks + 1))
+    def _():
+        block = index - 2
+        for side in range(2):
+            term = chunk(block, far - 1 if side == 0 else far + 1).astype(jnp.float32)
+            hop(block, side, 0).wait_recv()
+            land = first_land[block, side].astype(jnp.float32)
+            low = term[:, :, :mid] + land if side == 0 else term[:, :, :mid]
+            high = term[:, :, mid:] if side == 0 else term[:, :, mid:] + land
+            second_send[block, side, :, :, :mid] = low.astype(jnp.bfloat16)
+            second_send[block, side, :, :, mid:] = high.astype(jnp.bfloat16)
+            hop(block, side, 1).start()
+
+    @pl.when(index >= 3)
+    def _():
+        block = index - 3
+        for side in range(2):
+            term = chunk(block, far - 2 if side == 0 else far + 2).astype(jnp.float32)
+            hop(block, side, 1).wait_recv()
+            land = second_land[block, side].astype(jnp.float32)
+            moving[side] = (term + land).astype(jnp.bfloat16)
 
     @pl.when(index == blocks)
     def _():
@@ -592,23 +792,20 @@
         out[...] = out_acc[...].astype(jnp.bfloat16)
         grad_normed[...] = grad_acc[...].astype(jnp.bfloat16)
 
-    if ringed:
-
-        @pl.when(index == blocks + 2)
-        def _():
-            for block in range(blocks):
-                for side in range(2):
-                    hop(block, side, 0).wait_send()
-                    hop(block, side, 1).wait_send()
+    @pl.when(index == blocks + 2)
+    def _():
+        for block in range(blocks):
+            for side in range(2):
+                hop(block, side, 0).wait_send()
+                hop(block, side, 1).wait_send()
 
 
 def glu_layer(normed, normed_t, top, top_t, weights, gate_bias, up_bias, seq_count):
     rows, width = normed.shape
     hidden_width = gate_bias.shape[0]
     blocks = hidden_width // BLOCK
-    half = width // 2
+    chips = seq_count // 2
     seg = width // seq_count
-    ringed = seg % 16 == 0
     kept = len(kept_places(seq_count))
     bf = jnp.bfloat16
 
@@ -623,30 +820,17 @@
 
     bias_spec = pl.BlockSpec((1, BLOCK), lambda i: (0, at(0)(i)))
     work = rows * width * hidden_width
-    if ringed:
-        term_specs = [
-            pl.BlockSpec((kept, 3, seg, BLOCK), lambda i: (0, 0, 0, at(1)(i))),
-            pl.BlockSpec((2, 3, seg, BLOCK), lambda i: (0, 0, 0, at(3)(i))),
-        ]
-        term_shapes = [
-            jax.ShapeDtypeStruct((kept, 3, seg, hidden_width), bf),
-            jax.ShapeDtypeStruct((2, 3, seg, hidden_width), bf),
-        ]
-        ring_scratches = [
-            pltpu.VMEM((3, 3, half, BLOCK), bf),
-            pltpu.VMEM((blocks, 2, 3, seg, BLOCK // 2), bf),
-            pltpu.VMEM((blocks, 2, 3, seg, BLOCK // 2), bf),
-            pltpu.VMEM((blocks, 2, 3, seg, BLOCK), bf),
-            pltpu.VMEM((blocks, 2, 3, seg, BLOCK), bf),
-            *(pltpu.SemaphoreType.DMA((blocks, 2)) for _ in range(4)),
-        ]
-    else:
-        term_specs = [pl.BlockSpec((3, half, BLOCK), lambda i: (0, 0, at(1)(i)))]
-        term_shapes = [jax.ShapeDtypeStruct((3, half, hidden_width), bf)]
-        ring_scratches = []
+    term_specs = [
+        pl.BlockSpec((kept, 3, seg, BLOCK), lambda i: (0, 0, 0, at(1)(i))),
+        pl.BlockSpec((2, 3, seg, BLOCK), lambda i: (0, 0, 0, at(3)(i))),
+    ]
+    term_shapes = [
+        jax.ShapeDtypeStruct((kept, 3, seg, hidden_width), bf),
+        jax.ShapeDtypeStruct((2, 3, seg, hidden_width), bf),
+    ]
     return pl.pallas_call(
-        functools.partial(glu_kernel, blocks, seq_count, ringed),
-        grid=(blocks + (3 if ringed else 1),),
+        functools.partial(glu_kernel, blocks, seq_count),
+        grid=(blocks + 3,),
         in_specs=[
             whole((rows, width)),
             whole((width, rows)),
@@ -673,12 +857,16 @@
         scratch_shapes=[
             pltpu.VMEM((rows, width), jnp.float32),
             pltpu.VMEM((rows, width), jnp.float32),
-            pltpu.VMEM((2, 3, half, BLOCK), bf),
-            pltpu.VMEM((2, 3, half, BLOCK), bf),
-            pltpu.VMEM((blocks, 3, half, BLOCK), bf),
+            pltpu.VMEM((2, 3, chips, 2, seg, BLOCK), bf),
+            pltpu.VMEM((blocks, 3, chips, seg, BLOCK), bf),
             pltpu.SemaphoreType.DMA((2,)),
             pltpu.SemaphoreType.DMA((blocks,)),
-            *ring_scratches,
+            pltpu.VMEM((3, 3, chips, seg, BLOCK), bf),
+            pltpu.VMEM((blocks, 2, 3, seg, BLOCK // 2), bf),
+            pltpu.VMEM((blocks, 2, 3, seg, BLOCK // 2), bf),
+            pltpu.VMEM((blocks, 2, 3, seg, BLOCK), bf),
+            pltpu.VMEM((blocks, 2, 3, seg, BLOCK), bf),
+            *(pltpu.SemaphoreType.DMA((blocks, 2)) for _ in range(4)),
         ],
         compiler_params=pltpu.CompilerParams(
             collective_id=1, has_side_effects=True, vmem_limit_bytes=VMEM_BYTES
@@ -709,14 +897,16 @@
         self.send_sem, self.recv_sem = send_sem, recv_sem
         self.sides = ring_neighbours(lax.axis_index("seq"), seq_count)
         self.greeted = [{"seq": side} for side in self.sides]
-        half, width = pieces[0].shape
-        self.seg = half // self.chips
+        width = pieces[0].shape[2]
+        self.near = [
+            chip_near(lax.axis_index("seq"), seq_count, step) for step in range(self.chips)
+        ]
         self.width, self.mid = width, width // 2
 
     def copy(self, piece, side, hop):
-        mid, seg = self.mid, self.seg
+        mid = self.mid
         if hop == 0:
-            source = self.pieces[piece].at[pl.ds(self.far * seg, seg), pl.ds(side * mid, mid)]
+            source = self.pieces[piece].at[self.near[self.far], :, pl.ds(side * mid, mid)]
             target = self.lands.at[piece, side, 0, :, pl.ds(0, mid)]
         else:
             source = self.sends.at[piece, side, hop - 1]
@@ -735,10 +925,10 @@
             self.copy(piece, side, 0).start()
 
     def advance(self, piece, hop):
-        mid, seg = self.mid, self.seg
+        mid = self.mid
         for side in range(2):
             near = self.far - hop if side == 0 else self.far + hop
-            term = self.pieces[piece][near * seg : (near + 1) * seg, :].astype(jnp.float32)
+            term = self.pieces[piece][self.near[near]].astype(jnp.float32)
             self.copy(piece, side, hop - 1).wait_recv()
             if hop == 1:
                 land = self.lands[piece, side, 0, :, :mid].astype(jnp.float32)
@@ -752,7 +942,7 @@
             self.copy(piece, side, hop).start()
 
     def total(self, piece):
-        total = self.pieces[piece][: self.seg, :].astype(jnp.float32)
+        total = self.pieces[piece][self.near[0]].astype(jnp.float32)
         for side in range(2):
             self.copy(piece, side, self.far - 1).wait_recv()
             total = total + self.lands[piece, side, self.far - 1].astype(jnp.float32)
@@ -782,30 +972,90 @@
     pl.semaphore_wait(barrier, len(devices))
 
 
-def tail_kernel(seq_count, head_count, ready_count, made_count, *refs):
-    ready = refs[:ready_count]
-    rows_t, columns, small, split, *refs = refs[ready_count:]
-    last_terms, refs = refs[:3], refs[3:]
-    out, small_out, joint, last_out, *refs = refs
+class CoreSum:
+    def __init__(self, partner, terms, arrived, send_sem, recv_sem):
+        self.core = lax.axis_index("seq") % 2
+        self.partner = partner
+        self.terms, self.arrived = terms, arrived
+        self.send_sem, self.recv_sem = send_sem, recv_sem
+
+    def copy(self, piece):
+        return pltpu.make_async_remote_copy(
+            src_ref=self.terms.at[piece % self.terms.shape[0], :, 1 - self.core],
+            dst_ref=self.arrived.at[piece],
+            send_sem=self.send_sem.at[piece],
+            recv_sem=self.recv_sem.at[piece],
+            device_id=self.partner,
+            device_id_type=MESH,
+        )
+
+    def start(self, piece, term):
+        slot = piece % self.terms.shape[0]
+        self.terms[slot] = term.astype(jnp.bfloat16).reshape(self.terms.shape[1:])
+        self.copy(piece).start()
+
+    def finish(self, piece):
+        self.copy(piece).wait_recv()
+        total = self.terms[piece % self.terms.shape[0], :, self.core].astype(jnp.float32)
+        return (total + self.arrived[piece].astype(jnp.float32)).astype(jnp.bfloat16)
+
+    def close(self, piece):
+        self.copy(piece).wait_send()
+
+
+def core_scratch(pieces, chips, seg, width, slots):
+    return [
+        pltpu.VMEM((slots, chips, 2, seg, width), jnp.bfloat16),
+        pltpu.VMEM((pieces, chips, seg, width), jnp.bfloat16),
+        pltpu.SemaphoreType.DMA((pieces,)),
+        pltpu.SemaphoreType.DMA((pieces,)),
+    ]
+
+
+def through_norm(total, normal, inverse, gain):
+    shaped = total * gain
+    return (
+        shaped
+        - jnp.mean(shaped, axis=-1, keepdims=True)
+        - normal * jnp.mean(shaped * normal, axis=-1, keepdims=True)
+    ) * inverse
+
+
+def tail_kernel(seq_count, head_count, made_count, clip_total, *refs):
     (
+        rows_t,
+        columns,
+        weights,
+        normal,
+        inverse,
+        gain,
+        grad_h_one,
+        placing,
+        early,
+        h_two,
+        glu_own,
+        glu_other,
+        down_bias,
+        out,
+        small_out,
+        frames_grad,
+        result,
         mine,
-        away,
-        arrived,
         small_send,
         small_land,
-        core_send,
-        core_recv,
         step_send,
         step_recv,
+        split,
         split_land,
         split_send,
         split_recv,
-        *ring_refs,
+        *refs,
     ) = refs
-    half = rows_t.shape[0] // 2
+    core_refs, ring_refs = refs[:4], refs[4:]
     width = columns.shape[1] // made_count
-    pieces = [*ready, *(mine.at[made] for made in range(made_count))]
-    ring = ChipRing(seq_count, pieces, *ring_refs)
+    rows = grad_h_one.shape[0]
+    late = placing.shape[0]
+    ring = ChipRing(seq_count, [mine.at[made] for made in range(made_count)], *ring_refs)
     seq_index = lax.axis_index("seq")
     head_index = lax.axis_index("head")
     partners = []
@@ -819,22 +1069,13 @@
         partners.append({"head": xor_place(head_index, bit)})
         bit *= 2
     greet(ring.greeted + partners)
-
-    def core_copy(made):
+    cores = CoreSum(partners[0], *core_refs)
+
+    def step_copy(step):
+        count = small_out.shape[0] if step < seq_steps else late
         return pltpu.make_async_remote_copy(
-            src_ref=away.at[made],
-            dst_ref=arrived.at[made],
-            send_sem=core_send.at[made],
-            recv_sem=core_recv.at[made],
-            device_id=partners[0],
-            device_id_type=MESH,
-        )
-
-    def step_copy(step):
-        rows = small.shape[0] if step < seq_steps else small.shape[0] // 2
-        return pltpu.make_async_remote_copy(
-            src_ref=small_send.at[step, pl.ds(0, rows)],
-            dst_ref=small_land.at[step, pl.ds(0, rows)],
+            src_ref=small_send.at[step, pl.ds(0, count)],
+            dst_ref=small_land.at[step, pl.ds(0, count)],
             send_sem=step_send.at[step],
             recv_sem=step_recv.at[step],
             device_id=partners[step],
@@ -842,10 +1083,7 @@
         )
 
     def step_on(step):
-        late = small.shape[0] // 2
-        if step == 0:
-            small_send[0] = small[...]
-        else:
+        if step > 0:
             step_copy(step - 1).wait_recv()
             if step <= seq_steps:
                 total = small_send[step - 1] + small_land[step - 1]
@@ -864,103 +1102,121 @@
         if step < len(partners):
             step_copy(step).start()
 
-    def split_copy(step):
+    def split_copy():
         return pltpu.make_async_remote_copy(
             src_ref=split,
-            dst_ref=split_land.at[step],
-            send_sem=split_send.at[step],
-            recv_sem=split_recv.at[step],
-            device_id={"head": (head_index + 1 + step) % head_count},
+            dst_ref=split_land,
+            send_sem=split_send,
+            recv_sem=split_recv,
+            device_id=partners[seq_steps],
             device_id_type=MESH,
         )
 
-    for step in range(head_count - 1):
-        split_copy(step).start()
-    for piece in range(ready_count):
-        ring.start(piece)
+    for made in range(made_count):
+        cores.start(made, product(rows_t[...], columns[:, made * width : (made + 1) * width]))
+    grad_normed = product_t(columns[...], weights[...])
+    split[...] = grad_normed[:rows].astype(jnp.bfloat16)
+    split_copy().start()
+    row = lax.broadcasted_iota(jnp.int32, (late, 1), 0)
+    gain_term = jnp.sum(grad_normed[:rows] * normal[...], axis=0, keepdims=True)
+    first = jnp.where(row == clip_total, gain_term, 0.0)
+    for slot in range(placing.shape[1]):
+        first = first + placing[:, slot : slot + 1] * grad_normed[rows + slot : rows + slot + 1]
+    small_send[0, :late, :] = first
+    small_send[0, late:, :] = early[...]
     step_on(0)
     for made in range(made_count):
-        cols = slice(made * width, (made + 1) * width)
-        away[made] = product(rows_t[half:, :], columns[:, cols]).astype(jnp.bfloat16)
-        core_copy(made).start()
-    for made in range(made_count):
-        cols = slice(made * width, (made + 1) * width)
-        term = product(rows_t[:half, :], columns[:, cols])
-        core_copy(made).wait_recv()
-        mine[made] = (term + arrived[made].astype(jnp.float32)).astype(jnp.bfloat16)
-        ring.start(ready_count + made)
-    last_total = last_terms[0][...].astype(jnp.float32)
-    for term in last_terms[1:]:
-        last_total = last_total + term[...].astype(jnp.float32)
-    last_out[...] = last_total
+        mine[made] = cores.finish(made)
+        ring.start(made)
+    result[...] = (
+        h_two[...]
+        + (glu_own[...].astype(jnp.float32) + glu_other[...].astype(jnp.float32))
+        + down_bias[...]
+    ).astype(jnp.bfloat16)
     done = 1
     for hop in range(1, ring.far):
-        for piece in range(len(pieces)):
-            ring.advance(piece, hop)
+        for made in range(made_count):
+            ring.advance(made, hop)
         while done <= len(partners) * hop // (ring.far - 1):
             step_on(done)
             done += 1
-    total = split[...].astype(jnp.float32)
-    for step in range(head_count - 1):
-        split_copy(step).wait_recv()
-        total = total + split_land[step].astype(jnp.float32)
-    joint[...] = total
-    for piece in range(len(pieces)):
-        out[:, piece * width : (piece + 1) * width] = ring.total(piece)
-    for step in range(head_count - 1):
-        split_copy(step).wait_send()
+    split_copy().wait_recv()
+    total = split[...].astype(jnp.float32) + split_land[...].astype(jnp.float32)
+    back = through_norm(total, normal[...], inverse[...], gain[...])
+    frames_grad[...] = (grad_h_one[...] + back).astype(jnp.bfloat16)
     for made in range(made_count):
-        core_copy(made).wait_send()
+        out[made] = ring.total(made)
+    split_copy().wait_send()
+    for made in range(made_count):
+        cores.close(made)
     ring.close()
     for step in range(len(partners)):
         step_copy(step).wait_send()
 
 
-def tail_sums(ready, rows_t, columns, small, split, last_terms, seq_count):
+def tail_sums(
+    rows_t, columns, weights, norm, grad_h_one, placing, early, h_two, glu_terms, down_bias, clip_total, seq_count
+):
     head_count = lax.axis_size("head")
     chips = seq_count // 2
-    half = rows_t.shape[0] // 2
-    seg = half // chips
+    rows, wide = grad_h_one.shape
+    seg = rows_t.shape[0] // seq_count
     width = TAIL_WIDTH
     made_count = columns.shape[1] // width
-    pieces = len(ready) + made_count
     steps = (seq_count - 1).bit_length() + (head_count - 1).bit_length()
     bf = jnp.bfloat16
+    vmem = pl.BlockSpec(memory_space=pltpu.VMEM)
+    small = (placing.shape[0] + early.shape[0], wide)
     return pl.pallas_call(
-        functools.partial(tail_kernel, seq_count, head_count, len(ready), made_count),
-        in_specs=[pl.BlockSpec(memory_space=pltpu.VMEM)] * (len(ready) + 7),
-        out_specs=[pl.BlockSpec(memory_space=pltpu.VMEM)] * 4,
+        functools.partial(tail_kernel, seq_count, head_count, made_count, clip_total),
+        grid=(1,),
+        in_specs=[
+            vmem,
+            vmem,
+            pl.BlockSpec((wide, made_count * width), lambda i: (0, 0), pipeline_mode=pl.Buffered(1)),
+            *[vmem] * 10,
+        ],
+        out_specs=[vmem] * 4,
         out_shape=[
-            jax.ShapeDtypeStruct((seg, pieces * width), jnp.float32),
-            jax.ShapeDtypeStruct(small.shape, jnp.float32),
-            jax.ShapeDtypeStruct(split.shape, jnp.float32),
-            jax.ShapeDtypeStruct(last_terms[0].shape, jnp.float32),
+            jax.ShapeDtypeStruct((made_count, seg, width), jnp.float32),
+            jax.ShapeDtypeStruct(small, jnp.float32),
+            jax.ShapeDtypeStruct((rows, wide), bf),
+            jax.ShapeDtypeStruct((rows, wide), bf),
         ],
         scratch_shapes=[
-            pltpu.VMEM((made_count, half, width), bf),
-            pltpu.VMEM((made_count, half, width), bf),
-            pltpu.VMEM((made_count, half, width), bf),
-            pltpu.VMEM((steps, *small.shape), jnp.float32),
-            pltpu.VMEM((steps, *small.shape), jnp.float32),
-            pltpu.SemaphoreType.DMA((made_count,)),
-            pltpu.SemaphoreType.DMA((made_count,)),
+            pltpu.VMEM((made_count, chips, seg, width), bf),
+            pltpu.VMEM((steps, *small), jnp.float32),
+            pltpu.VMEM((steps, *small), jnp.float32),
             pltpu.SemaphoreType.DMA((steps,)),
             pltpu.SemaphoreType.DMA((steps,)),
-            pltpu.VMEM((head_count - 1, *split.shape), bf),
-            pltpu.SemaphoreType.DMA((head_count - 1,)),
-            pltpu.SemaphoreType.DMA((head_count - 1,)),
-            *ring_scratch(seq_count, pieces, seg, width),
+            pltpu.VMEM((rows, wide), bf),
+            pltpu.VMEM((rows, wide), bf),
+            pltpu.SemaphoreType.DMA,
+            pltpu.SemaphoreType.DMA,
+            *core_scratch(made_count, chips, seg, width, made_count),
+            *ring_scratch(seq_count, made_count, seg, width),
         ],
         compiler_params=pltpu.CompilerParams(
             collective_id=2, has_side_effects=True, vmem_limit_bytes=VMEM_BYTES
         ),
         cost_estimate=pl.CostEstimate(
-            flops=2 * rows_t.shape[0] * rows_t.shape[1] * columns.shape[1],
-            bytes_accessed=16 * pieces * half * width,
+            flops=4 * rows_t.shape[0] * rows_t.shape[1] * columns.shape[1],
+            bytes_accessed=32 * made_count * chips * seg * width,
             transcendentals=0,
         ),
         name="tail_sums",
-    )(*ready, rows_t, columns, small, split, *last_terms)
+    )(
+        rows_t,
+        columns,
+        weights,
+        *norm,
+        grad_h_one,
+        placing,
+        early,
+        h_two,
+        *glu_terms,
+        down_bias,
+    )
 
 
 def turned_back(values, tables):
@@ -972,7 +1228,7 @@
     )
 
 
-def self_back_kernel(seq_count, pairs, score_scale, ready_count, *refs):
+def self_back_kernel(seq_count, pairs, score_scale, *refs):
     (
         query,
         keys,
@@ -985,10 +1241,12 @@
         query_ids,
         query_slots,
         tables,
-    ) = refs[:11]
-    ready = refs[11 : 11 + ready_count]
-    out, shares = refs[11 + ready_count : 13 + ready_count]
-    (
+        ready,
+        made_rows,
+        made_columns,
+        out,
+        shares,
+        mine,
         bias,
         acc,
         own,
@@ -996,8 +1254,10 @@
         halo_land,
         halo_send_sem,
         halo_recv_sem,
-        *ring_refs,
-    ) = refs[13 + ready_count :]
+        *refs,
+    ) = refs
+    core_refs, ring_refs = refs[:4], refs[4:]
+    ready_count = ready.shape[0]
     pair = pl.program_id(0)
     rows = query.shape[0]
     slots = stamp_key.shape[0]
@@ -1005,8 +1265,10 @@
     seq_index = lax.axis_index("seq")
     before = (seq_index + seq_count - 1) % seq_count
     behind = (seq_index + 1) % seq_count
-    ring = ChipRing(seq_count, list(ready), *ring_refs) if ready else None
-    hops = ring.far if ready else 1
+    pieces = [*(ready.at[piece] for piece in range(ready_count)), mine]
+    ring = ChipRing(seq_count, pieces, *ring_refs)
+    partner = {"seq": xor_place(seq_index, 1)}
+    cores = CoreSum(partner, *core_refs)
 
     def halo_copy(which, side):
         return pltpu.make_async_remote_copy(
@@ -1020,9 +1282,10 @@
 
     @pl.when(pair == 0)
     def _():
-        greet((ring.greeted if ready else []) + [{"seq": before}, {"seq": behind}])
+        greet(ring.greeted + [partner, {"seq": before}, {"seq": behind}])
         for piece in range(ready_count):
             ring.start(piece)
+        cores.start(0, product_tn(made_rows[...], made_columns[...]))
         for block in range(rows // QUERY_BLOCK):
             start = block * QUERY_BLOCK
             asked = query_ids[:, start : start + QUERY_BLOCK]
@@ -1036,12 +1299,22 @@
                 slot_row == query_slots[:, start : start + QUERY_BLOCK], 0.0, NEG
             )
 
-    for hop in range(1, hops):
-
-        @pl.when(pair == hop)
+    blocks = rows // QUERY_BLOCK
+    order = [(piece, hop) for hop in range(1, ring.far) for piece in range(len(pieces))]
+    due = [1 + at * (pairs * blocks - 1) // len(order) for at in range(len(order))]
+
+    def ring_work(block):
+        @pl.when(pair * blocks + block == MADE_AT)
         def _():
-            for piece in range(ready_count):
-                ring.advance(piece, hop)
+            mine[...] = cores.finish(0)
+            ring.start(ready_count)
+
+        for moment, (piece, hop) in zip(due, order):
+            if moment % blocks == block:
+
+                @pl.when(pair == moment // blocks)
+                def _():
+                    ring.advance(piece, hop)
 
     @pl.when(pair < pairs)
     def _():
@@ -1072,6 +1345,7 @@
                 grad_v = grad_v + product(probs.astype(jnp.bfloat16), head_g)
                 grad_q = grad_q + product_tn(grad_s, head_k)
             grad_queries.append(grad_q)
+            ring_work(block)
             acc[0, start : start + span, :] += grad_k[:span]
             acc[1, start : start + span, :] += grad_v[:span]
             acc[0, 2 * HALF + rows :, :] += grad_k[span:]
@@ -1091,43 +1365,61 @@
             out[rows:, pl.ds(column + shift, LANES)] = (
                 acc[which, 2 * HALF + rows :, :] * scale
             ).astype(jnp.bfloat16)
-        halo_copy(pair, 0).start()
-        halo_copy(pair, 1).start()
+
+        @pl.when(seq_index > 0)
+        def _():
+            halo_copy(pair, 0).start()
+
+        @pl.when(seq_index < seq_count - 1)
+        def _():
+            halo_copy(pair, 1).start()
 
     @pl.when(pair == pairs)
     def _():
+
+        @pl.when(seq_index < seq_count - 1)
+        def _():
+            for which in range(pairs):
+                halo_copy(which, 0).wait_recv()
+                own[which, :, rows - HALF :, :] += halo_land[which, 0].astype(jnp.float32)
+
+        @pl.when(seq_index > 0)
+        def _():
+            for which in range(pairs):
+                halo_copy(which, 1).wait_recv()
+                own[which, :, :HALF, :] += halo_land[which, 1].astype(jnp.float32)
+
         for which in range(pairs):
-            halo_copy(which, 0).wait_recv()
-            halo_copy(which, 1).wait_recv()
-            own[which, :, rows - HALF :, :] += halo_land[which, 0].astype(jnp.float32)
-            own[which, :, :HALF, :] += halo_land[which, 1].astype(jnp.float32)
             column = (pairs + which) * LANES
             out[:rows, column : column + LANES] = turned_back(own[which, 0], tables).astype(
                 jnp.bfloat16
             )
             column = (2 * pairs + which) * LANES
             out[:rows, column : column + LANES] = own[which, 1].astype(jnp.bfloat16)
-        if not ready:
-            shares[...] = jnp.zeros_like(shares)
-        for piece in range(ready_count):
-            shares[:, piece * ring.width : (piece + 1) * ring.width] = ring.total(piece)
-        if ready:
-            ring.close()
-        for which in range(pairs):
-            halo_copy(which, 0).wait_send()
-            halo_copy(which, 1).wait_send()
+        for piece in range(len(pieces)):
+            shares[piece] = ring.total(piece)
+        ring.close()
+        cores.close(0)
+
+        @pl.when(seq_index > 0)
+        def _():
+            for which in range(pairs):
+                halo_copy(which, 0).wait_send()
+
+        @pl.when(seq_index < seq_count - 1)
+        def _():
+            for which in range(pairs):
+                halo_copy(which, 1).wait_send()
 
 
 def self_back(
-    query, near, stamps, grad_out, logs, key_ids, query_ids, query_slots, tables, ready, score_scale, seq_count
+    query, near, stamps, grad_out, logs, key_ids, query_ids, query_slots, tables, ready, made_rows, made_columns, score_scale, seq_count
 ):
     rows, part = query.shape
     slots = stamps.shape[0]
     pairs = part // LANES
     window = near.shape[1]
-    half, width = ready[0].shape if ready else (8 * seq_count // 2, LANES)
-    seg = half // (seq_count // 2)
-    share_width = max(len(ready), 1) * width
+    ready_count, chips, seg, width = ready.shape
     span = QUERY_BLOCK + 2 * HALF
     blocks = rows // QUERY_BLOCK
     last = pairs - 1
@@ -1139,7 +1431,7 @@
         return pl.BlockSpec(shape, lambda i: (0,) * len(shape), pipeline_mode=pl.Buffered(1))
 
     return pl.pallas_call(
-        functools.partial(self_back_kernel, seq_count, pairs, score_scale, len(ready)),
+        functools.partial(self_back_kernel, seq_count, pairs, score_scale),
         grid=(pairs + 1,),
         in_specs=[
             at(0, (rows, LANES)),
@@ -1153,17 +1445,20 @@
             whole((1, rows)),
             whole((1, rows)),
             whole((3, rows, LANES)),
-            *(whole((half, width)) for _ in ready),
+            whole(ready.shape),
+            whole(made_rows.shape),
+            whole(made_columns.shape),
         ],
         out_specs=[
             pl.BlockSpec((rows + slots, 3 * part), lambda i: (0, 0)),
-            pl.BlockSpec((seg, share_width), lambda i: (0, 0)),
+            pl.BlockSpec((ready_count + 1, seg, width), lambda i: (0, 0, 0)),
         ],
         out_shape=[
             jax.ShapeDtypeStruct((rows + slots, 3 * part), jnp.bfloat16),
-            jax.ShapeDtypeStruct((seg, share_width), jnp.float32),
+            jax.ShapeDtypeStruct((ready_count + 1, seg, width), jnp.float32),
         ],
         scratch_shapes=[
+            pltpu.VMEM((chips, seg, width), jnp.bfloat16),
             pltpu.VMEM((blocks, span + slots, QUERY_BLOCK), jnp.float32),
             pltpu.VMEM((2, window + slots, LANES), jnp.float32),
             pltpu.VMEM((pairs, 2, rows, LANES), jnp.float32),
@@ -1171,14 +1466,15 @@
             pltpu.VMEM((pairs, 2, 2, HALF, LANES), jnp.bfloat16),
             pltpu.SemaphoreType.DMA((pairs, 2)),
             pltpu.SemaphoreType.DMA((pairs, 2)),
-            *(ring_scratch(seq_count, len(ready), seg, width) if ready else []),
+            *core_scratch(1, chips, seg, width, 1),
+            *ring_scratch(seq_count, ready_count + 1, seg, width),
         ],
         compiler_params=pltpu.CompilerParams(
             collective_id=3, has_side_effects=True, vmem_limit_bytes=VMEM_BYTES
         ),
         cost_estimate=pl.CostEstimate(
             flops=10 * rows * window * part,
-            bytes_accessed=16 * len(ready) * half * width,
+            bytes_accessed=16 * chips * seg * width * (ready_count + 1),
             transcendentals=rows * window * part // HD,
         ),
         name="self_back",
@@ -1194,19 +1490,283 @@
         query_ids[None],
         query_slots[None],
         tables,
-        *ready,
-    )
-
-
-def tail_or_rings(ready, rows_t, columns, small, split, last_terms, seq_count):
-    if rows_t.shape[0] // seq_count % 16 == 0:
-        return tail_sums(ready, rows_t, columns, small, split, last_terms, seq_count)
-    made = core_sum(rows_t, columns, seq_count)
-    ring = Ring(side_by_side([*ready, made], seq_count // 2), seq_count)
-    late = small.shape[0] // 2
-    small = all_sum(small, ("seq",))
-    small = jnp.concatenate([all_sum(small[:late], ("head",)), small[late:]], axis=0)
-    return ring.finish(), small, head_total(split), sum(each.astype(jnp.float32) for each in last_terms)
+        ready,
+        made_rows,
+        made_columns,
+    )
+
+
+def mid_kernel(seq_count, head_count, score_scale, ctx_tokens, *refs):
+    (
+        grad_low,
+        top,
+        normal_three,
+        inverse_three,
+        normal_two,
+        inverse_two,
+        gains,
+        c_out,
+        c_query,
+        w_out,
+        query,
+        key,
+        value,
+        logs,
+        query_slots,
+        cross_mixed,
+        normed_two,
+        context,
+        kept,
+        moving,
+        grad_h_one,
+        grad_two_low,
+        grad_one_low,
+        grad_attn,
+        grad_query,
+        ctx_grads,
+        gain_terms,
+        share,
+        core_sums,
+        grad_mix,
+        split,
+        split_land,
+        split_send,
+        split_recv,
+        third_land,
+        fourth_land,
+        third_sems,
+        fourth_sems,
+        keep,
+        keep_sems,
+        *core_refs,
+    ) = refs
+    seq_index = lax.axis_index("seq")
+    head_index = lax.axis_index("head")
+    others = [{"head": (head_index + 1 + step) % head_count} for step in range(head_count - 1)]
+    sides = ring_neighbours(seq_index, seq_count)
+    partner = {"seq": xor_place(seq_index, 1)}
+    cores = CoreSum(partner, *core_refs)
+    greet([*others, partner] + [{"seq": side} for side in sides])
+
+    def hop(side, which):
+        sems = fourth_sems if which else third_sems
+        return pltpu.make_async_remote_copy(
+            src_ref=third_land.at[side] if which else moving.at[side],
+            dst_ref=(fourth_land if which else third_land).at[side],
+            send_sem=sems.at[0, side],
+            recv_sem=sems.at[1, side],
+            device_id={"seq": sides[side]},
+            device_id_type=MESH,
+        )
+
+    def keep_copy(which):
+        at = (1, kept.shape[0] - 1, 0)[which]
+        return pltpu.make_async_copy(kept.at[at], keep.at[which % 2], keep_sems.at[which])
+
+    def third_to_fourth():
+        for side in range(2):
+            hop(side, 0).wait_recv()
+            keep_copy(side).wait()
+            term = keep[side].astype(jnp.float32) + third_land[side].astype(jnp.float32)
+            third_land[side] = term.astype(jnp.bfloat16)
+            hop(side, 1).start()
+        keep_copy(2).start()
+
+    def over_heads(which, step):
+        return pltpu.make_async_remote_copy(
+            src_ref=grad_low if which == 0 else split,
+            dst_ref=split_land.at[which, step],
+            send_sem=split_send.at[which, step],
+            recv_sem=split_recv.at[which, step],
+            device_id=others[step],
+            device_id_type=MESH,
+        )
+
+    def summed(which):
+        total = (grad_low if which == 0 else split)[...].astype(jnp.float32)
+        for step in range(head_count - 1):
+            over_heads(which, step).wait_recv()
+            total = total + split_land[which, step].astype(jnp.float32)
+        return total
+
+    for step in range(head_count - 1):
+        over_heads(0, step).start()
+    hop(0, 0).start()
+    hop(1, 0).start()
+    keep_copy(0).start()
+    keep_copy(1).start()
+    gain_terms[...] = jnp.zeros_like(gain_terms)
+    total = summed(0)
+    normal = normal_three[...]
+    gain_terms[0:1, :] = jnp.sum(total * normal, axis=0, keepdims=True)
+    grad_h_one[...] = top[...].astype(jnp.float32) + through_norm(
+        total, normal, inverse_three[...], gains[0:1, :]
+    )
+    grad_two_low[...] = grad_h_one[...].astype(jnp.bfloat16)
+    grad_mix[...] = product(grad_two_low[...], c_out[...]).astype(jnp.bfloat16)
+    cores.start(0, product_tn(grad_two_low[...], cross_mixed[...]))
+    rows = query.shape[0]
+    keys = key.shape[0]
+    pairs = query.shape[1] // LANES
+    token_slot = lax.broadcasted_iota(jnp.int32, (keys, 1), 0) // ctx_tokens
+    bias = jnp.where(token_slot == query_slots[...], 0.0, NEG)
+    lane = lax.broadcasted_iota(jnp.int32, (1, LANES), 1)
+    for pair in range(pairs):
+        columns = slice(pair * LANES, (pair + 1) * LANES)
+        pair_q, pair_g = query[:, columns], grad_mix[:, columns]
+        pair_k, pair_v = key[:, columns], value[:, columns]
+        grad_q = jnp.zeros((rows, LANES), jnp.float32)
+        grad_k = jnp.zeros((keys, LANES), jnp.float32)
+        grad_v = jnp.zeros((keys, LANES), jnp.float32)
+        for head in range(LANES // HD):
+            here = lane // HD == head
+            head_q = jnp.where(here, pair_q, jnp.zeros_like(pair_q))
+            head_g = jnp.where(here, pair_g, jnp.zeros_like(pair_g))
+            head_k = jnp.where(here, pair_k, jnp.zeros_like(pair_k))
+            at = pair * (LANES // HD) + head
+            scores = product_t(pair_k, head_q) * score_scale + bias
+            probs = jnp.exp(scores - logs[at : at + 1, :])
+            grad_p = product_t(pair_v, head_g)
+            dot = jnp.sum(probs * grad_p, axis=0, keepdims=True)
+            grad_s = (probs * (grad_p - dot)).astype(jnp.bfloat16)
+            grad_k = grad_k + product(grad_s, head_q)
+            grad_v = grad_v + product(probs.astype(jnp.bfloat16), head_g)
+            grad_q = grad_q + product_tn(grad_s, head_k)
+        grad_query[:, columns] = (grad_q * score_scale).astype(jnp.bfloat16)
+        ctx_grads[:, columns] = (grad_k * score_scale).astype(jnp.bfloat16)
+        second = slice((pairs + pair) * LANES, (pairs + pair + 1) * LANES)
+        ctx_grads[:, second] = grad_v.astype(jnp.bfloat16)
+        if pair == HOP_PAIR:
+            third_to_fourth()
+    split[...] = product_t(grad_query[...], c_query[...]).astype(jnp.bfloat16)
+    for step in range(head_count - 1):
+        over_heads(1, step).start()
+    cores.start(1, product_tn(normed_two[...], grad_query[...]))
+    part = query.shape[1]
+    core_sums[0] = cores.finish(0)
+    cores.close(0)
+    ctx_rows = cores.terms.shape[3] // 2
+    for which in range(2):
+        term = product_tn(context[...], ctx_grads[:, which * part : (which + 1) * part])
+        term = term.astype(jnp.bfloat16).reshape(-1, 2, ctx_rows, part)
+        cores.terms[0, :, :, which * ctx_rows : (which + 1) * ctx_rows, :] = term
+    cores.copy(2).start()
+    for piece in range(1, 3):
+        core_sums[piece] = cores.finish(piece)
+    total = summed(1)
+    normal = normal_two[...]
+    gain_terms[1:2, :] = jnp.sum(total * normal, axis=0, keepdims=True)
+    grad_h_one[...] += through_norm(
+        total, normal, inverse_two[...], gains[1:2, :]
+    )
+    grad_one_low[...] = grad_h_one[...].astype(jnp.bfloat16)
+    grad_attn[...] = product(grad_one_low[...], w_out[...]).astype(jnp.bfloat16)
+    keep_copy(2).wait()
+    whole = keep[0].astype(jnp.float32)
+    for side in range(2):
+        hop(side, 1).wait_recv()
+        whole = whole + fourth_land[side].astype(jnp.float32)
+    share[...] = whole
+    for side in range(2):
+        hop(side, 0).wait_send()
+        hop(side, 1).wait_send()
+    for piece in range(1, 3):
+        cores.close(piece)
+    for which in range(2):
+        for step in range(head_count - 1):
+            over_heads(which, step).wait_send()
+
+
+def mid_layer(
+    grad_low, top, thirds, seconds, gains, weights, query, key, value, logs, slots, cross_mixed, normed_two, context, kept, moving, ctx_tokens, seq_count
+):
+    rows, width = grad_low.shape
+    part = query.shape[1]
+    keys = key.shape[0]
+    head_count = lax.axis_size("head")
+    chips, moved = seq_count // 2, moving.shape
+    seg = moved[2]
+    bf, wide = jnp.bfloat16, jnp.float32
+    vmem = pl.BlockSpec(memory_space=pltpu.VMEM)
+
+    def weight_spec(which):
+        return pl.BlockSpec((width, part), lambda i: (0, which), pipeline_mode=pl.Buffered(1))
+
+    scratches = [
+        pltpu.VMEM((rows, part), bf),
+        pltpu.VMEM((rows, width), bf),
+        pltpu.VMEM((2, head_count - 1, rows, width), bf),
+        pltpu.SemaphoreType.DMA((2, head_count - 1)),
+        pltpu.SemaphoreType.DMA((2, head_count - 1)),
+    ]
+    out_shapes = [
+        jax.ShapeDtypeStruct((rows, width), wide),
+        jax.ShapeDtypeStruct((rows, width), bf),
+        jax.ShapeDtypeStruct((rows, width), bf),
+        jax.ShapeDtypeStruct((rows, part), bf),
+        jax.ShapeDtypeStruct((rows, part), bf),
+        jax.ShapeDtypeStruct((keys, 2 * part), bf),
+        jax.ShapeDtypeStruct((8, width), wide),
+    ]
+    scratches += [
+        pltpu.VMEM(moved, bf),
+        pltpu.VMEM(moved, bf),
+        pltpu.SemaphoreType.DMA((2, 2)),
+        pltpu.SemaphoreType.DMA((2, 2)),
+        pltpu.VMEM((2, *moved[1:]), bf),
+        pltpu.SemaphoreType.DMA((3,)),
+        *core_scratch(3, chips, seg, part, 2),
+    ]
+    out_shapes += [
+        jax.ShapeDtypeStruct(moved[1:], wide),
+        jax.ShapeDtypeStruct((3, chips, seg, part), bf),
+    ]
+    return pl.pallas_call(
+        functools.partial(
+            mid_kernel, seq_count, head_count, HD ** (-0.5), ctx_tokens
+        ),
+        grid=(1,),
+        in_specs=[
+            *[vmem] * 7,
+            weight_spec(5),
+            weight_spec(4),
+            weight_spec(3),
+            *[vmem] * 8,
+            pl.BlockSpec(memory_space=pl.ANY),
+            pl.BlockSpec(memory_space=pl.ANY),
+        ],
+        out_specs=[vmem] * len(out_shapes),
+        out_shape=out_shapes,
+        scratch_shapes=scratches,
+        compiler_params=pltpu.CompilerParams(
+            collective_id=6, has_side_effects=True, vmem_limit_bytes=VMEM_BYTES
+        ),
+        cost_estimate=pl.CostEstimate(
+            flops=10 * rows * keys * part + 6 * rows * width * part,
+            bytes_accessed=100 * rows * width,
+            transcendentals=rows * keys * part // HD,
+        ),
+        name="mid_layer",
+    )(
+        grad_low,
+        top,
+        *thirds,
+        *seconds,
+        gains,
+        weights,
+        weights,
+        weights,
+        query,
+        key,
+        value,
+        logs,
+        slots[None],
+        cross_mixed,
+        normed_two,
+        context,
+        kept,
+        moving,
+    )
 
 
 def head_total(partial_sum):
@@ -1264,20 +1824,13 @@
     ctx_rows = cross_key.shape[0]
     ctx_width = prompt.shape[2]
     head_count = part // HD
-    chips = seq_count // 2
     bias_rows = 2 * hidden_width // width
     small_rows = -(-max(clip_total + 1, bias_rows + 3) // 8) * 8
-    order = owner_matrix(width, seq_index, seq_count)
-
-    def ordered(matrix, by=order):
-        return product_t(by, matrix).astype(jnp.bfloat16)
-
     vectors = jnp.stack([norm1_gain, norm2_gain, norm3_gain, down_bias], axis=1)
     vectors = jnp.pad(vectors, ((0, 0), (0, LANES - 4)))
     ctx_pair = jnp.concatenate([cross_key, cross_value], axis=0)
     attn_local = jnp.concatenate(
         [
-            vectors,
             query_weight,
             key_weight,
             value_weight,
@@ -1285,24 +1838,25 @@
             cross_query,
             cross_out,
             ctx_pair,
+            vectors,
         ],
         axis=1,
     )
-    starts = [LANES + each * part for each in range(8)]
+    starts = [each * part for each in range(8)]
     attn_weights, token = ring_gather(
-        attn_local, (0, starts[1], *starts[2:]), seq_count, 4
+        attn_local, (*starts[:7], starts[7] + LANES), seq_count, 4
     )
     glu_local = jnp.concatenate([gate_weight, up_weight, down_weight], axis=1).astype(jnp.bfloat16)
     token, glu_local = lax.optimization_barrier((token, glu_local))
     glu_weights = low_gather(glu_local)
-    w_qkv = attn_weights[:, LANES : starts[3]]
+    w_qkv = attn_weights[:, : starts[3]]
     w_out = attn_weights[:, starts[3] : starts[4]]
     c_query = attn_weights[:, starts[4] : starts[5]]
     c_out = attn_weights[:, starts[5] : starts[6]]
-    ctx_weights = attn_weights[:, starts[6] :].reshape(seq_count, 2, ctx_rows, part)
+    ctx_weights = attn_weights[:, starts[6] : starts[7]].reshape(seq_count, 2, ctx_rows, part)
     c_key = ctx_weights[:, 0].reshape(ctx_width, part)
     c_value = ctx_weights[:, 1].reshape(ctx_width, part)
-    rows_of = attn_weights[:, :8].astype(jnp.float32).T + token[0, 0]
+    rows_of = attn_weights[:, starts[7] : starts[7] + 8].astype(jnp.float32).T + token[0, 0]
     gain_one_f, gain_two_f, gain_three_f, bias_f = rows_of[0], rows_of[1], rows_of[2], rows_of[3]
 
     positions = first_row + jnp.arange(local_rows, dtype=jnp.int32)
@@ -1348,14 +1902,15 @@
     h_one = frames_f + head_total(product_t(attn_mixed, w_out))
     middle_out, normal_two, inverse_two = layer_norm_parts(h_one, gain_two_f)
     normed_two = middle_out.astype(jnp.bfloat16)
-    cross_h = product(normed_two, c_query).astype(jnp.bfloat16).reshape(local_rows, head_count, HD)
+    cross_rows = product(normed_two, c_query).astype(jnp.bfloat16)
+    cross_h = cross_rows.reshape(local_rows, head_count, HD)
     context_rows = lax.dynamic_slice_in_dim(prompt, base_clip, slot_count, 0).reshape(
         slot_count * ctx_tokens, ctx_width
     )
-    ctx_key_h = product(context_rows, c_key).astype(jnp.bfloat16)
-    ctx_key_h = ctx_key_h.reshape(slot_count * ctx_tokens, head_count, HD)
-    ctx_value_h = product(context_rows, c_value).astype(jnp.bfloat16)
-    ctx_value_h = ctx_value_h.reshape(slot_count * ctx_tokens, head_count, HD)
+    ctx_keys = product(context_rows, c_key).astype(jnp.bfloat16)
+    ctx_key_h = ctx_keys.reshape(slot_count * ctx_tokens, head_count, HD)
+    ctx_values = product(context_rows, c_value).astype(jnp.bfloat16)
+    ctx_value_h = ctx_values.reshape(slot_count * ctx_tokens, head_count, HD)
     key_slot = jnp.arange(slot_count * ctx_tokens, dtype=jnp.int32) // ctx_tokens
     cross_keys = [(ctx_key_h, ctx_value_h, own_slot[:, None] == key_slot[None, :])]
     cross_mix_h, cross_logs = attend_forward(cross_h, cross_keys, score_scale)
@@ -1364,63 +1919,51 @@
     third_out, normal_three, inverse_three = layer_norm_parts(h_two, gain_three_f)
     normed_three = third_out.astype(jnp.bfloat16)
 
-    glu_out, grad_normed_low, bias_local, glu_left, *moving = glu_layer(
+    glu_out, grad_normed_low, bias_local, glu_kept, glu_moving = glu_layer(
         normed_three,
-        ordered(normed_three),
+        normed_three.T,
         out_grad,
-        ordered(out_grad),
+        out_grad.T,
         glu_weights,
         gate_bias,
         up_bias,
         seq_count,
     )
-    grad_normed_three = head_total(grad_normed_low)
-    if moving:
-        places = kept_places(seq_count)
-        glu_ring = Ring(lambda near: glu_left[places.index(near)], seq_count, moving[0])
-    else:
-        glu_ring = Ring(
-            lambda near: glu_left[:, near * gain_rows : (near + 1) * gain_rows], seq_count
-        )
-    grad_top = out_grad.astype(jnp.float32)
-    gain_three_term = jnp.sum(grad_normed_three * normal_three, axis=0)
-    down_bias_term = jnp.sum(grad_top, axis=0)
-
-    grad_h_two = grad_top + norm_back(grad_normed_three, normal_three, inverse_three, gain_three_f)
-    grad_two_low = grad_h_two.astype(jnp.bfloat16)
-    grad_cross_h = product(grad_two_low, c_out).astype(jnp.bfloat16)
-    grad_cross_h = grad_cross_h.reshape(local_rows, head_count, HD)
-    cross_out_sum = core_sum(ordered(grad_two_low), cross_mixed, seq_count)
-    grad_cross_q, ctx_key_grads, ctx_value_grads = attend_backward(
-        cross_h, cross_keys, score_scale, cross_logs, grad_cross_h
-    )
-    grad_cross_query = grad_cross_q.reshape(local_rows, part).astype(jnp.bfloat16)
-    ctx_grads = jnp.concatenate(
-        [ctx_key_grads[0].reshape(-1, part), ctx_value_grads[0].reshape(-1, part)], axis=1
-    ).astype(jnp.bfloat16)
-    grad_cross_query = glu_ring.after(grad_cross_query)
-    glu_ring.step()
-    grad_normed_two = head_total(product_t(grad_cross_query, c_query))
-    cross_query_sum = core_sum(ordered(normed_two), grad_cross_query, seq_count)
-    ctx_order = owner_matrix(ctx_width, seq_index, seq_count)
-    ctx_sum = core_sum(ordered(context_rows, ctx_order), ctx_grads, seq_count)
-    ctx_sum = jnp.transpose(ctx_sum.reshape(chips, ctx_rows, 2, part), (0, 2, 1, 3))
-    grad_normed_two, cross_out_sum, cross_query_sum, ctx_sum = lax.optimization_barrier(
-        (grad_normed_two, cross_out_sum, cross_query_sum, ctx_sum.reshape(width // 2, part))
-    )
-    gain_two_term = jnp.sum(grad_normed_two * normal_two, axis=0)
-    grad_h_one = grad_h_two + norm_back(grad_normed_two, normal_two, inverse_two, gain_two_f)
-    grad_one_low = grad_h_one.astype(jnp.bfloat16)
-    grad_attn = product(grad_one_low, w_out).astype(jnp.bfloat16)
+    (
+        grad_h_one,
+        grad_two_low,
+        grad_one_low,
+        grad_attn,
+        grad_cross_query,
+        ctx_grads,
+        gain_terms,
+        glu_share,
+        cross_sums,
+    ) = mid_layer(
+        grad_normed_low,
+        out_grad,
+        (normal_three, inverse_three),
+        (normal_two, inverse_two),
+        jnp.stack([gain_three_f, gain_two_f]),
+        attn_weights,
+        cross_rows,
+        ctx_keys,
+        ctx_values,
+        cross_logs,
+        own_slot,
+        cross_mixed,
+        normed_two,
+        context_rows,
+        glu_kept,
+        glu_moving,
+        ctx_tokens,
+        seq_count,
+    )
+    gain_three_term, gain_two_term = gain_terms[0], gain_terms[1]
+    down_bias_term = jnp.sum(out_grad.astype(jnp.float32), axis=0)
     grad_attn, glu_out = lax.optimization_barrier((grad_attn, glu_out))
-    glu_total = head_total(glu_out)
-    out_sum = core_sum(ordered(grad_one_low), attn_mixed, seq_count)
-    ready_sums = [cross_out_sum, cross_query_sum, out_sum, ctx_sum]
-
-    if gain_rows % 16 == 0:
-        early_sums, ready_sums = ready_sums[:SELF_PIECES], ready_sums[SELF_PIECES:]
-    else:
-        early_sums = []
+    head_pairs = [(index, index ^ 1) for index in range(lax.axis_size("head"))]
+    glu_other = lax.ppermute(glu_out, "head", head_pairs)
     ones = jnp.ones((local_rows, HD - ROT), jnp.float32)
     flat = jnp.zeros((local_rows, ROT // 2), jnp.float32)
     low_side = [sin_table, flat, 0 * ones]
@@ -1441,58 +1984,37 @@
         own_ids,
         own_slot,
         tables,
-        early_sums,
+        cross_sums,
+        grad_one_low,
+        attn_mixed,
         score_scale,
         seq_count,
     )
-    grad_qkv, glu_total = lax.optimization_barrier((grad_qkv, glu_total))
-    result = (h_two + glu_total + bias_f).astype(jnp.bfloat16)
-    grad_qkv = glu_ring.after(grad_qkv)
-    glu_terms = glu_ring.last_terms()
-    grad_normed_all = product_t(grad_qkv, w_qkv)
-    gain_one_term = jnp.sum(grad_normed_all[:local_rows] * normal_one[:local_rows], axis=0)
-    stamp_full = lax.dynamic_update_slice_in_dim(
-        jnp.zeros((clip_total, width), jnp.float32), grad_normed_all[local_rows:stamp_end], base_clip, 0
-    )
-    small = jnp.concatenate(
+    early_rows = jnp.concatenate(
         [
-            jnp.pad(
-                jnp.concatenate([stamp_full, gain_one_term[None]], axis=0),
-                ((0, small_rows - clip_total - 1), (0, 0)),
-            ),
-            jnp.pad(
-                jnp.concatenate(
-                    [
-                        bias_local.reshape(-1, width),
-                        jnp.stack([gain_two_term, gain_three_term, down_bias_term]),
-                    ],
-                    axis=0,
-                ),
-                ((0, small_rows - bias_rows - 3), (0, 0)),
-            ),
+            bias_local.reshape(-1, width),
+            jnp.stack([gain_two_term, gain_three_term, down_bias_term]),
         ],
         axis=0,
     )
-    shares, small, grad_normed_one, glu_share = tail_or_rings(
-        ready_sums,
-        ordered(normed_one),
+    early_rows = jnp.pad(early_rows, ((0, small_rows - bias_rows - 3), (0, 0)))
+    clip_range = jnp.arange(small_rows, dtype=jnp.int32)
+    placing = (clip_range[:, None] - base_clip == slot_range[None, :]).astype(jnp.float32)
+    qkv_share, small, frames_grad, result = tail_sums(
+        normed_one.T,
         grad_qkv,
-        small,
-        grad_normed_all[:local_rows].astype(jnp.bfloat16),
-        glu_terms,
+        attn_weights,
+        (normal_one[:local_rows], inverse_one[:local_rows], gain_one_f[None]),
+        grad_h_one,
+        placing,
+        early_rows,
+        h_two,
+        (glu_out, glu_other),
+        bias_f[None],
+        clip_total,
         seq_count,
     )
-    frames_grad = (
-        grad_h_one
-        + norm_back(grad_normed_one, normal_one[:local_rows], inverse_one[:local_rows], gain_one_f)
-    ).astype(jnp.bfloat16)
-    if gain_rows % 16 == 0:
-        shares = jnp.concatenate([early_share, shares], axis=1)
-    cross_out_share = shares[:, :part]
-    cross_query_share = shares[:, part : 2 * part]
-    out_share = shares[:, 2 * part : 3 * part]
-    ctx_share = shares[:, 3 * part : 4 * part]
-    qkv_share = shares[:, 4 * part :]
+    cross_out_share, cross_query_share, ctx_share, out_share = early_share
     late = small[: clip_total + 1]
     early = small[small_rows : small_rows + bias_rows + 3]
     stamp_sum = late[:clip_total]
@@ -1515,9 +2037,9 @@
         gains_own[0],
         gains_own[1],
         gains_own[2],
-        qkv_share[:, :part],
-        qkv_share[:, part : 2 * part],
-        qkv_share[:, 2 * part :],
+        qkv_share[0],
+        qkv_share[1],
+        qkv_share[2],
         out_share,
         cross_query_share,
         ctx_share[:ctx_rows],
@@ -1579,6 +2101,7 @@
         P("head"),
         P("seq"),
     )
+    fast = mesh.shape["seq"] == FAST_SEQ
     return jax.shard_map(
-        per_device, mesh=mesh, in_specs=in_specs, out_specs=out_specs, check_vma=False
-    )
+        per_device if fast else per_device_plain, mesh=mesh, in_specs=in_specs, out_specs=out_specs, check_vma=False
+    )

time: 646 us -> 626 us (0.969)
  Pallas kernels: 296 us -> 407 us
  matrix products: 101 us -> 36.7 us
  waiting for transfers between devices: 61.6 us -> 12.3 us
  other arithmetic: 75.3 us -> 50.3 us
  local copies, waits for them, and re-layouts: 70.5 us -> 85.3 us
  starting transfers between devices: 18.4 us -> 8.45 us
    pallas_call x2 -> x3, Pallas kernels: 140 us -> 257 us  [the longest x1 96.3 us: glu_layer(): pl.pallas_call(functools.partial(glu_kernel, blocks, seq_count), grid=(bl...]
    ppermute x5 -> x2, waiting for transfers between devices: 61.6 us -> 12.3 us  [head_total(): total = total + lax.ppermute(low, 'head', pairs).astype(jnp.float32)]
    dot_general x11 -> x2, matrix products: 41.9 us -> 8.34 us  [product_t(): lax.dot_general(matrix_a, matrix_b, (((1,), (1,)), ((), ())), preferred_e...]
    dot_general x14 -> x4, matrix products: 39.6 us -> 13.6 us  [product(): return jnp.dot(matrix_a, matrix_b, preferred_element_type=jnp.float32)]
    convert_element_type x4 -> x2, other arithmetic: 12.8 us -> 3.21 us  [the longest x1 1.89 us: per_device(): normed_two = middle_out.astype(jnp.bfloat16)]
    reduce_sum x5 -> x1, other arithmetic: 8.46 us -> 0.79 us  [per_device(): down_bias_term = jnp.sum(out_grad.astype(jnp.float32), axis=0)]
    add x6 -> x1, other arithmetic: 8.24 us -> 0.67 us  [per_device(): attn_weights[:, starts[7]:starts[7] + 8].astype(jnp.float32).T + token[0, 0]]
  transfers between devices with their start and end apart: 16 -> 6, of which waited for: 4 -> 1; matrix products, arithmetic and copies ran while one was open for 31% -> 23% of each run, Pallas kernels for 10% -> 10%
where the time goes in v5:
time: 626 us; the launch traced here: 616 us
  Pallas kernels  407 us (65%)
  local copies, waits for them, and re-layouts  85.3 us (14%)
  other arithmetic  50.3 us (8%)
  matrix products  36.7 us (6%)
  between operations  15.8 us (3%)
  waiting for transfers between devices  12.3 us (2%)
  starting transfers between devices  8.45 us (1%)
    pallas_call x1, Pallas kernels, glu_layer(): pl.pallas_call(functools.partial(glu_kernel, blocks, seq_count), grid=(bl...  96.3 us
    pallas_call x1, Pallas kernels, mid_layer(): pl.pallas_call(functools.partial(mid_kernel, seq_count, head_count, HD **...  92.1 us
    pallas_call x1, Pallas kernels, ring_gather(): pl.pallas_call(functools.partial(gather_kernel, seq_count, bounds), in_sp...  89.1 us
    pallas_call x1, Pallas kernels, tail_sums(): pl.pallas_call(functools.partial(tail_kernel, seq_count, head_count, made...  68.3 us
    pallas_call x1, Pallas kernels, self_back(): pl.pallas_call(functools.partial(self_back_kernel, seq_count, pairs, scor...  61.2 us
    dot_general x4, matrix products, product(): return jnp.dot(matrix_a, matrix_b, preferred_element_type=jnp.float32)  13.6 us
  transfers between devices with their start and end apart: 6, of which 1 were waited for; matrix products, arithmetic and copies ran while one was open for 23% of the time, Pallas kernels for 10%

profile of v5, /device:TPU:0, one launch (start us, length us, event | category | flops | bytes accessed | tf_op | source)
XLA Modules:
  0.0 615.9 jit_solution(534823460798675525)
XLA Ops:
  15.9 89.1 %ring_gather.1 = (bf16[8,2,96,5504]{3,2,1,0:T(8,128)(2,1)}, f32[8,128]{1,0:T(8,128)}) custom-call(bf16[96,5504]{1,0:T(8,128)(2,1)} %copy-done.14), custom_call_target="tpu_custom_call" | custom-call | bytes 270532608 | tf_op jit(solution)/shard_map/ring_gather/pallas_call | solution.py:630
  105.1 1.2 copy-done.18
  106.7 1.3 pad_maximum_fusion.1
  111.9 1.2 slice.185
  115.2 1.2 slice_reduce_fusion
  116.4 7.5 %fusion.56 = (bf16[400,2304]{1,0:T(8,128)(2,1)}, f32[400,2304]{1,0:T(8,128)S(1)}) fusion(bf16[1536,5504]{1,0:T(8,128)(2,1)} %bitcast.89, f32[1536]{0:T(1024)S(1)} %get-tuple-element.70, f32[400]{0:T(512)S(1)} %add_rsqrt_fusion.2, f32[400]{0:T(512)S(1)} %broadcast_multiply_fusion.2, bf16[2,1536]{1,0:T(2,128)(2,1)S(1)} %constant_dynamic-slice_fusion.1, ...), kind=kOutput, calls=%fused_computation.171 | convolution fusion | flops 2838220800 | bytes 13802624 | tf_op jit(solution)/shard_map/dot_general | solution.py:83
  123.9 1.2 fusion.50
  125.1 1.4 copy.108
  130.5 1.2 fusion.22
  131.7 3.3 collective-permute-start
  135.0 1.5 collective-permute-start.1
  136.5 3.4 slice.260
  139.9 2.7 copy.107
  142.6 1.8 slice.245
  144.4 1.3 fusion.53
  145.7 1.4 reshape.410
  147.1 1.4 reshape.411
  151.1 1.3 multiply_subtract_fusion
  156.8 1.2 convolution_convert_fusion.2.refs_11_
  158.1 1.2 convolution_convert_fusion.3.refs_12_
  159.3 1.5 pad_maximum_fusion.refs_1_.refs_2_
  160.9 1.8 fusion.51
  163.3 2.5 copy.111
  165.9 2.5 copy.110
  168.4 4.5 fusion
  173.0 4.5 fusion.1
  178.5 6.1 fusion.15
  184.7 4.1 convolution_convert_fusion.1
  188.8 1.5 collective-permute-start.2
  194.3 2.3 subtract_multiply_fusion
  196.6 12.3 %collective-permute-done.2 = bf16[384,1536]{1,0:T(8,128)(2,1)} collective-permute-done((bf16[384,1536]{1,0:T(8,128)(2,1)}, bf16[384,1536]{1,0:T(8,128)(2,1)}, u32[]{:S(2)}, u32[]{:S(2)}) %collective-permute-start.2) | collective-permute-done | bytes 1179680 | tf_op jit(solution)/shard_map/ppermute | solution.py:1780
  208.9 2.2 fusion.49
  211.7 1.9 multiply_convert_fusion.2
  214.6 3.6 fusion.17.refs_10_
  218.2 2.1 copy.115
  220.3 2.1 fusion.5
  223.5 1.4 fusion.16
  225.0 4.2 convolution_convert_fusion
  229.2 1.5 collective-permute-start.3
  231.2 1.4 copy.118
  233.2 1.5 slice.253.refs_3_.refs_4_
  234.7 1.2 broadcast_in_dim.62.refs_8_
  237.7 2.1 copy.126.refs_0_
  241.1 3.3 slice.267.refs_3_
  244.4 3.1 copy.129.refs_0_
  247.5 1.5 slice.238.refs_4_
  251.3 1.3 fusion.41.refs_7_
  252.7 1.3 pad_maximum_fusion.5.refs_6_
  255.1 1.4 add.166.refs_6_
  256.4 2.2 copy.122.refs_15_
  258.6 1.5 rsqrt.38.refs_5_
  260.7 2.1 fusion.48
  264.2 1.8 multiply_convert_fusion.1
  266.1 1.4 copy.119.normed_t
  267.5 96.3 %glu_layer.1 = (bf16[384,1536]{1,0:T(8,128)(2,1)}, bf16[384,1536]{1,0:T(8,128)(2,1)}, f32[2,3072]{1,0:T(2,128)}, bf16[3,3,96,3072]{3,2,1,0:T(8,128)(2,1)}, bf16[2,3,96,3072]{3,2,1,0:T(8,128)(2,1)}) custom-call(bf16[384,1536]{1,0:T(8,128)(2,1)} %copy-done.9, bf16[1536,384]{1,0:T(8,128)(2,1)} %copy.119.normed_t, bf16[384,1536]{1,0:T(8,128)(2,1)} %refs_1_.1, ...), custom_call_target="tpu_custom_call" | custom-call | flops 32614907904 | bytes 56623104 | tf_op jit(solution)/shard_map/glu_layer/pallas_call | solution.py:831
  363.8 92.1 %mid_layer.1 = (f32[384,1536]{1,0:T(8,128)}, bf16[384,1536]{1,0:T(8,128)(2,1)}, bf16[384,1536]{1,0:T(8,128)(2,1)}, bf16[384,768]{1,0:T(8,128)(2,1)}, bf16[384,76...) custom-call(bf16[384,1536]{1,0:T(8,128)(2,1)} %get-tuple-element.47., ...), custom_call_target="tpu_custom_call" | custom-call | flops 3472883712 | bytes 58982400 | tf_op jit(solution)/shard_map/mid_layer/pallas_call | solution.py:1724
  457.5 61.2 %self_back.1 = (bf16[400,2304]{1,0:T(8,128)(2,1)}, f32[4,96,768]{2,1,0:T(8,128)}) custom-call(bf16[384,768]{1,0:T(8,128)(2,1)} %copy.126.refs_0_, bf16[2,896,768]{2,1,0:T(8,128)(2,1)} %copy-done.2, bf16[2,896,768]{2,1,0:T(8,128)(2,1)} %copy-done.2, bf16[16,2304]{1,0:T(8,128)(2,1)} %slice.253.refs_3_.refs_4_, bf16[16,2304]{1,0:T(8,128)(2,1)} %slice.253.refs_3_.refs_4_, ...), custom_call_target="tpu_custom_call" | custom-call | flops 2642411520 | bytes 37748736 | tf_op jit(solution)/shard_map/self_back/pallas_call | solution.py:1433
  518.7 1.7 slice_bitcast_fusion.10
  521.0 2.1 slice_bitcast_fusion.4
  523.1 3.8 slice_bitcast_fusion
  528.0 68.3 %tail_sums.1 = (f32[3,96,768]{2,1,0:T(8,128)}, f32[16,1536]{1,0:T(8,128)}, bf16[384,1536]{1,0:T(8,128)(2,1)}, bf16[384,1536]{1,0:T(8,128)(2,1)}) custom-call(bf16[1536,400]{1,0:T(8,128)(2,1)} %copy.129.refs_0_, bf16[400,2304]{1,0:T(8,128)(2,1)} %get-tuple-element.55.refs_1_, bf16[1536,5504]{1,0:T(8,128)(2,1)} %bitcast.97, f32[384,1536]{1,0:T(8,128)} %slice.267.refs_3_, ...), custom_call_target="tpu_custom_call" | custom-call | flops 5662310400 | bytes 56623104 | tf_op jit(solution)/shard_map/tail_sums/pallas_call | solution.py:1170
  600.6 2.1 slice_bitcast_fusion.7
  603.9 1.5 fusion.31
  605.4 2.5 copy.148
  (218 shorter events, 52.8 us)
Async XLA Ops:
  7.2 143.8 %copy-start = (bf16[6,128,768]{2,1,0:T(8,128)(2,1)S(1)}, bf16[6,128,768]{2,1,0:T(8,128)(2,1)}, u32[]{:S(2)}) copy-start(bf16[6,128,768]{2,1,0:T(8,128)(2,1)} %param.24) | copy-start | bytes 3538948
  7.2 97.8 %copy-start.17 = (f32[96,3072]{1,0:T(8,128)S(1)}, f32[96,3072]{1,0:T(8,128)}, u32[]{:S(2)}) copy-start(f32[96,3072]{1,0:T(8,128)} %param.37) | copy-start | bytes 3538948
  7.2 260.2 %all-gather.2.cloned.1.call-start = ((), (), s32[]{:S(2)}) async-start(), calls=%async_computation | async-start | bytes 30081024 | tf_op jit(solution)/shard_map/all_gather | solution.py:1785
  8.9 5.9 copy-start.33
  8.9 5.9 copy-start.34
  14.9 1.0 copy-start.14
  105.0 1.3 copy-start.18
  105.0 1.6 copy-start.19
  108.0 5.8 copy-start.4
  108.9 0.6 copy-start.52
  114.0 9.9 %copy-start.50 = (f32[400]{0:T(512)}, f32[400]{0:T(512)S(1)}, u32[]{:S(2)}) copy-start(f32[400]{0:T(512)S(1)} %broadcast_multiply_fusion.2) | copy-start | bytes 4804
  114.5 9.4 %copy-start.48 = (f32[400]{0:T(512)}, f32[400]{0:T(512)S(1)}, u32[]{:S(2)}) copy-start(f32[400]{0:T(512)S(1)} %add_rsqrt_fusion.2) | copy-start | bytes 4804
  127.8 1.2 copy-start.29
  127.8 1.2 copy-start.31
  131.7 27.6 %collective-permute-start = (bf16[2,256,768]{2,1,0:T(8,128)(2,1)}, bf16[2,256,768]{2,1,0:T(8,128)(2,1)}, u32[]{:S(2)}, u32[]{:S(2)}) collective-permute-start(bf16[2,256,768]{2,1,0:T(8,128)(2,1)} %get-tuple-element.104), channel_id=1, source_target_pairs={{0,2},{2,4},{4,6},{6,8},{8,10},{10,12},{12,14},{14,16},{16,18},{18... | collective-permute-start | bytes 2359304 | tf_op jit(solution)/shard_map/ppermute | solution.py:25
  135.0 24.3 %collective-permute-start.1 = (bf16[2,256,768]{2,1,0:T(8,128)(2,1)}, bf16[2,256,768]{2,1,0:T(8,128)(2,1)}, u32[]{:S(2)}, u32[]{:S(2)}) collective-permute-start(bf16[2,256,768]{2,1,0:T(8,128)(2,1)} %get-tuple-element.105), channel_id=1, source_target_pairs={{2,0},{4,2},{6,4},{8,6},{10,8},{12,10},{14,12},{16,14},{18,16},{20... | collective-permute-start | bytes 2359304 | tf_op jit(solution)/shard_map/ppermute | solution.py:28
  148.5 7.4 %copy-start.6 = (bf16[1536,768]{1,0:T(8,128)(2,1)S(1)}, bf16[1536,768]{1,0:T(8,128)(2,1)}, u32[]{:S(2)}) copy-start(bf16[1536,768]{1,0:T(8,128)(2,1)} %slice.260) | copy-start | bytes 7077892
  149.4 6.5 %copy-start.43 = (s32[384]{0:T(512)}, s32[384]{0:T(512)S(1)}, u32[]{:S(2)}) copy-start(s32[384]{0:T(512)S(1)} %broadcast_subtract_fusion) | copy-start | bytes 4612
  150.2 5.7 copy-start.39
  151.1 7.0 %copy-start.7 = (bf16[2,128,768]{2,1,0:T(8,128)(2,1)}, bf16[2,128,768]{2,1,0:T(8,128)(2,1)S(1)}, u32[]{:S(2)}) copy-start(bf16[2,128,768]{2,1,0:T(8,128)(2,1)S(1)} %constant_dynamic-slice_fusion) | copy-start | bytes 1179652
  153.4 15.0 %copy-start.8 = (bf16[384,12,64]{0,2,1:T(8,128)(2,1)}, bf16[384,12,64]{0,2,1:T(8,128)(2,1)S(1)}, u32[]{:S(2)}) copy-start(bf16[384,12,64]{0,2,1:T(8,128)(2,1)S(1)} %maximum_convert_fusion) | copy-start | bytes 1769476
  155.9 0.7 copy-start.53
  160.9 2.4 copy-start.2
  173.0 5.2 copy-start.45
  173.0 5.5 copy-start.13
  184.7 4.1 copy-start.22
  184.7 5.7 copy-start.5
  184.7 6.4 %copy-start.11 = (bf16[256,768]{1,0:T(8,128)(2,1)S(1)}, bf16[256,768]{1,0:T(8,128)(2,1)}, u32[]{:S(2)}) copy-start(bf16[256,768]{1,0:T(8,128)(2,1)} %convolution_convert_fusion.2.refs_11_) | copy-start | bytes 1179652
  184.7 7.4 %copy-start.12 = (bf16[256,768]{1,0:T(8,128)(2,1)S(1)}, bf16[256,768]{1,0:T(8,128)(2,1)}, u32[]{:S(2)}) copy-start(bf16[256,768]{1,0:T(8,128)(2,1)} %convolution_convert_fusion.3.refs_12_) | copy-start | bytes 1179652
  188.8 4.3 copy-start.30
  188.8 4.3 copy-start.32
  188.8 20.0 %collective-permute-start.2 = (bf16[384,1536]{1,0:T(8,128)(2,1)}, bf16[384,1536]{1,0:T(8,128)(2,1)}, u32[]{:S(2)}, u32[]{:S(2)}) collective-permute-start(bf16[384,1536]{1,0:T(8,128)(2,1)} %convolution_convert_fusion.1), channel_id=1, source_target_pairs={{0,1},{1,0},{2,3},{3,2},{4,5},{5,4},{6,7},{7,6},{8,9},{9,8},{10,11... | collective-permute-start | bytes 3538952 | tf_op jit(solution)/shard_map/ppermute | solution.py:1780
  192.1 2.2 copy-start.49
  192.1 2.2 copy-start.51
  211.0 0.7 copy-start.42
  211.4 2.2 copy-start.47
  213.6 1.0 copy-start.10
  220.3 2.1 copy-start.21
  222.5 1.0 copy-start.35
  222.5 1.0 copy-start.26
  223.5 1.5 copy-start.37
  225.0 4.3 copy-start.24
  229.2 3.4 copy-start.44
  229.2 6.8 %copy-start.40 = (s32[896]{0:T(1024)S(1)}, s32[896]{0:T(1024)}, u32[]{:S(2)}) copy-start(s32[896]{0:T(1024)} %copy-done.39) | copy-start | bytes 10756
  229.2 31.5 %collective-permute-start.3 = (bf16[384,1536]{1,0:T(8,128)(2,1)}, bf16[384,1536]{1,0:T(8,128)(2,1)}, u32[]{:S(2)}, u32[]{:S(2)}) collective-permute-start(bf16[384,1536]{1,0:T(8,128)(2,1)} %convolution_convert_fusion), channel_id=1, source_target_pairs={{0,1},{1,0},{2,3},{3,2},{4,5},{5,4},{6,7},{7,6},{8,9},{9,8},{10,11... | collective-permute-start | bytes 3538952 | tf_op jit(solution)/shard_map/ppermute | solution.py:1780
  232.6 8.2 %copy-start.28 = (f32[384,64]{0,1:T(8,128)S(1)}, f32[384,64]{0,1:T(8,128)}, u32[]{:S(2)}) copy-start(f32[384,64]{0,1:T(8,128)} %get-tuple-element.111) | copy-start | bytes 294916
  232.6 8.3 %copy-start.27 = (f32[384,64]{0,1:T(8,128)S(1)}, f32[384,64]{0,1:T(8,128)}, u32[]{:S(2)}) copy-start(f32[384,64]{0,1:T(8,128)} %get-tuple-element.112) | copy-start | bytes 294916
  244.4 9.5 %copy-start.23 = (bf16[12,64,384]{2,1,0:T(8,128)(2,1)S(1)}, bf16[12,64,384]{2,1,0:T(8,128)(2,1)}, u32[]{:S(2)}) copy-start(bf16[12,64,384]{2,1,0:T(8,128)(2,1)} %copy-done.22) | copy-start | bytes 1769476
  250.8 9.2 %copy-start.36 = (f32[12,384]{1,0:T(8,128)S(1)}, f32[12,384]{1,0:T(8,128)}, u32[]{:S(2)}) copy-start(f32[12,384]{1,0:T(8,128)} %copy-done.35) | copy-start | bytes 55300
  250.8 9.2 %copy-start.38 = (f32[12,384]{1,0:T(8,128)S(1)}, f32[12,384]{1,0:T(8,128)}, u32[]{:S(2)}) copy-start(f32[12,384]{1,0:T(8,128)} %copy-done.37) | copy-start | bytes 55300
  262.8 3.3 copy-start.3
  262.8 1.5 copy-start.41
  266.1 1.4 copy-start.9
  363.8 93.0 %copy-start.46 = (f32[2,3072]{1,0:T(2,128)S(1)}, f32[2,3072]{1,0:T(2,128)}, u32[]{:S(2)}) copy-start(f32[2,3072]{1,0:T(2,128)} %get-tuple-element.57) | copy-start | bytes 73732
  363.8 93.0 %copy-start.15 = (bf16[384,1536]{1,0:T(8,128)(2,1)S(1)}, bf16[384,1536]{1,0:T(8,128)(2,1)}, u32[]{:S(2)}) copy-start(bf16[384,1536]{1,0:T(8,128)(2,1)} %get-tuple-element.59.refs_10_) | copy-start | bytes 3538948
  456.9 70.1 %collective-permute-start.4 = (bf16[384,1536]{1,0:T(8,128)(2,1)S(1)}, bf16[384,1536]{1,0:T(8,128)(2,1)S(1)}, u32[]{:S(2)}, u32[]{:S(2)}) collective-permute-start(bf16[384,1536]{1,0:T(8,128)(2,1)S(1)} %copy-done.15), channel_id=1, source_target_pairs={{0,1},{1,0},{2,3},{3,2},{4,5},{5,4},{6,7},{7,6},{8,9},{9,8},{10,11... | collective-permute-start | bytes 3538952 | tf_op jit(solution)/shard_map/ppermute | solution.py:1966
  527.0 1.0 copy-start.16
  528.0 70.1 %copy-start.25 = (bf16[6,1536]{1,0:T(8,128)(2,1)S(1)}, bf16[6,1536]{1,0:T(8,128)(2,1)}, u32[]{:S(2)}) copy-start(bf16[6,1536]{1,0:T(8,128)(2,1)} %param.23) | copy-start | bytes 55300
  528.0 70.2 %copy-start.54 = (f32[6]{0:T(128)S(1)}, f32[6]{0:T(128)}, u32[]{:S(2)}) copy-start(f32[6]{0:T(128)} %broadcast_multiply_fusion.4) | copy-start | bytes 76
  528.0 70.2 %copy-start.55 = (f32[6]{0:T(128)S(1)}, f32[6]{0:T(128)}, u32[]{:S(2)}) copy-start(f32[6]{0:T(128)} %add_rsqrt_fusion.3) | copy-start | bytes 76
  596.3 11.6 %copy-start.20 = (bf16[384,1536]{1,0:T(8,128)(2,1)S(1)}, bf16[384,1536]{1,0:T(8,128)(2,1)}, u32[]{:S(2)}) copy-start(bf16[384,1536]{1,0:T(8,128)(2,1)} %get-tuple-element.159) | copy-start | bytes 3538948
  605.4 3.5 copy-start.1
Sparse Core Ops, SparseCore 0:
  108.2 156.3 all-gather.1

commit v6 on v5

--- a/solution.py
+++ b/solution.py
@@ -525,7 +525,7 @@
 BLOCK = 256
 TAIL_WIDTH = 768
 QUERY_BLOCK = 128
-HOP_PAIR = 3
+HOP_CHUNK = 1
 MADE_AT = 1
 VMEM_BYTES = 60 * 1024 * 1024
 MESH = pl.DeviceIdType.MESH
@@ -549,10 +549,30 @@
     return [2 * chip_near(seq_index, seq_count, step) + seq_index % 2 for step in (1, -1)]
 
 
-def gather_kernel(
-    seq_count, bounds, local, out, token, own_sem, ring_send, ring_recv, core_send, core_recv
-):
-    token[...] = jnp.zeros_like(token)
+def gather_kernel(seq_count, bounds, count, later_count, *refs):
+    wides, refs = refs[:count], refs[count:]
+    later, refs = refs[:later_count], refs[later_count:]
+    out, later_out, refs = refs[0], refs[1], refs[2:]
+    wide_bufs, later_bufs, refs = refs[:count], refs[count : count + later_count], refs[count + later_count :]
+    (
+        local,
+        later_local,
+        in_sems,
+        later_sem,
+        own_sem,
+        ring_send,
+        ring_recv,
+        core_send,
+        core_recv,
+    ) = refs
+    loads = [
+        pltpu.make_async_copy(source, target, in_sems.at[at])
+        for at, (source, target) in enumerate(
+            zip([*wides, *later], [*wide_bufs, *later_bufs])
+        )
+    ]
+    for load in loads:
+        load.start()
     far = seq_count // 4
     seq_index = lax.axis_index("seq")
     core = seq_index % 2
@@ -599,15 +619,33 @@
             device_id_type=MESH,
         )
 
+    def wides_of(piece):
+        if piece < len(bounds) - 2:
+            return [(0, 0, piece)]
+        height, width = wides[piece].shape
+        return [(0, 0, piece), (height, 0, piece + 1), (0, width, piece + 2)]
+
     pieces = range(len(bounds) - 1)
     arrivals = [(piece, side, hop) for hop in range(far) for piece in pieces for side in range(2)]
     own_copy = pltpu.make_async_copy(local, out.at[seq_index // 2, core], own_sem)
     for piece in pieces:
+        for row, column, at in wides_of(piece):
+            height, width = wides[at].shape
+            column += bounds[piece]
+            loads[at].wait()
+            local[row : row + height, column : column + width] = wide_bufs[at][...].astype(
+                jnp.bfloat16
+            )
         for side in range(2):
             ring_copy(piece, side, 0).start()
+        core_copy(piece, 0, -1).start()
     own_copy.start()
-    for piece in pieces:
-        core_copy(piece, 0, -1).start()
+    for at, wide in enumerate(later_bufs):
+        width = wide.shape[1]
+        loads[count + at].wait()
+        later_local[:, at * width : (at + 1) * width] = wide[...].astype(jnp.bfloat16)
+    later_copy = pltpu.make_async_copy(later_local, later_out, later_sem)
+    later_copy.start()
     for piece, side, hop in arrivals:
         ring_copy(piece, side, hop).wait_recv()
         if hop + 1 < far:
@@ -617,41 +655,47 @@
     for piece, side, hop in crossed:
         core_copy(piece, side, hop).wait_recv()
     own_copy.wait()
+    later_copy.wait()
     for piece, side, hop in crossed:
         core_copy(piece, side, hop).wait_send()
     for piece, side, hop in arrivals:
         ring_copy(piece, side, hop).wait_send()
 
 
-def ring_gather(local, bounds, seq_count, collective_id):
-    rows, width = local.shape
-    local = local.astype(jnp.bfloat16)
+def ring_gather(wides, later, bounds, seq_count, collective_id):
+    rows, width = wides[0].shape[0], bounds[-1]
     pieces, far = len(bounds) - 1, seq_count // 4
-    gathered, token = pl.pallas_call(
-        functools.partial(gather_kernel, seq_count, bounds),
-        in_specs=[pl.BlockSpec(memory_space=pl.ANY)],
-        out_specs=[
-            pl.BlockSpec(memory_space=pl.ANY),
-            pl.BlockSpec(memory_space=pltpu.VMEM),
-        ],
+    later_width = sum(each.shape[1] for each in later)
+    hbm = pl.BlockSpec(memory_space=pltpu.HBM)
+    gathered, later = pl.pallas_call(
+        functools.partial(gather_kernel, seq_count, bounds, len(wides), len(later)),
+        in_specs=[hbm] * (len(wides) + len(later)),
+        out_specs=[hbm, hbm],
         out_shape=[
             jax.ShapeDtypeStruct((seq_count // 2, 2, rows, width), jnp.bfloat16),
-            jax.ShapeDtypeStruct((8, LANES), jnp.float32),
+            jax.ShapeDtypeStruct((rows, later_width), jnp.bfloat16),
         ],
         scratch_shapes=[
+            *(pltpu.VMEM(each.shape, jnp.float32) for each in (*wides, *later)),
+            pltpu.VMEM((rows, width), jnp.bfloat16),
+            pltpu.VMEM((rows, later_width), jnp.bfloat16),
+            pltpu.SemaphoreType.DMA((len(wides) + len(later),)),
+            pltpu.SemaphoreType.DMA,
             pltpu.SemaphoreType.DMA,
             pltpu.SemaphoreType.DMA((pieces, 2, far)),
             pltpu.SemaphoreType.DMA((pieces, 2, far)),
             pltpu.SemaphoreType.DMA((pieces, 2, far + 1)),
             pltpu.SemaphoreType.DMA((pieces, 2, far + 1)),
         ],
-        compiler_params=pltpu.CompilerParams(collective_id=collective_id, has_side_effects=True),
+        compiler_params=pltpu.CompilerParams(
+            collective_id=collective_id, has_side_effects=True, vmem_limit_bytes=VMEM_BYTES
+        ),
         cost_estimate=pl.CostEstimate(
             flops=0, bytes_accessed=32 * rows * seq_count * width, transcendentals=0
         ),
         name="ring_gather",
-    )(local)
-    return gathered.reshape(seq_count * rows, width), token
+    )(*wides, *later)
+    return gathered.reshape(seq_count * rows, width), later
 
 
 def kept_places(seq_count):
@@ -1036,6 +1080,7 @@
         glu_own,
         glu_other,
         down_bias,
+        ready,
         out,
         small_out,
         frames_grad,
@@ -1055,7 +1100,8 @@
     width = columns.shape[1] // made_count
     rows = grad_h_one.shape[0]
     late = placing.shape[0]
-    ring = ChipRing(seq_count, [mine.at[made] for made in range(made_count)], *ring_refs)
+    pieces = [ready, *(mine.at[made] for made in range(made_count))]
+    ring = ChipRing(seq_count, pieces, *ring_refs)
     seq_index = lax.axis_index("seq")
     head_index = lax.axis_index("head")
     partners = []
@@ -1112,6 +1158,7 @@
             device_id_type=MESH,
         )
 
+    ring.start(0)
     for made in range(made_count):
         cores.start(made, product(rows_t[...], columns[:, made * width : (made + 1) * width]))
     grad_normed = product_t(columns[...], weights[...])
@@ -1127,7 +1174,7 @@
     step_on(0)
     for made in range(made_count):
         mine[made] = cores.finish(made)
-        ring.start(made)
+        ring.start(made + 1)
     result[...] = (
         h_two[...]
         + (glu_own[...].astype(jnp.float32) + glu_other[...].astype(jnp.float32))
@@ -1135,8 +1182,8 @@
     ).astype(jnp.bfloat16)
     done = 1
     for hop in range(1, ring.far):
-        for made in range(made_count):
-            ring.advance(made, hop)
+        for piece in range(len(pieces)):
+            ring.advance(piece, hop)
         while done <= len(partners) * hop // (ring.far - 1):
             step_on(done)
             done += 1
@@ -1144,8 +1191,8 @@
     total = split[...].astype(jnp.float32) + split_land[...].astype(jnp.float32)
     back = through_norm(total, normal[...], inverse[...], gain[...])
     frames_grad[...] = (grad_h_one[...] + back).astype(jnp.bfloat16)
-    for made in range(made_count):
-        out[made] = ring.total(made)
+    for piece in range(len(pieces)):
+        out[piece] = ring.total(piece)
     split_copy().wait_send()
     for made in range(made_count):
         cores.close(made)
@@ -1155,7 +1202,7 @@
 
 
 def tail_sums(
-    rows_t, columns, weights, norm, grad_h_one, placing, early, h_two, glu_terms, down_bias, clip_total, seq_count
+    rows_t, columns, weights, norm, grad_h_one, placing, early, h_two, glu_terms, down_bias, ready, clip_total, seq_count
 ):
     head_count = lax.axis_size("head")
     chips = seq_count // 2
@@ -1174,11 +1221,11 @@
             vmem,
             vmem,
             pl.BlockSpec((wide, made_count * width), lambda i: (0, 0), pipeline_mode=pl.Buffered(1)),
-            *[vmem] * 10,
+            *[vmem] * 11,
         ],
         out_specs=[vmem] * 4,
         out_shape=[
-            jax.ShapeDtypeStruct((made_count, seg, width), jnp.float32),
+            jax.ShapeDtypeStruct((made_count + 1, seg, width), jnp.float32),
             jax.ShapeDtypeStruct(small, jnp.float32),
             jax.ShapeDtypeStruct((rows, wide), bf),
             jax.ShapeDtypeStruct((rows, wide), bf),
@@ -1194,7 +1241,7 @@
             pltpu.SemaphoreType.DMA,
             pltpu.SemaphoreType.DMA,
             *core_scratch(made_count, chips, seg, width, made_count),
-            *ring_scratch(seq_count, made_count, seg, width),
+            *ring_scratch(seq_count, made_count + 1, seg, width),
         ],
         compiler_params=pltpu.CompilerParams(
             collective_id=2, has_side_effects=True, vmem_limit_bytes=VMEM_BYTES
@@ -1216,6 +1263,7 @@
         h_two,
         *glu_terms,
         down_bias,
+        ready,
     )
 
 
@@ -1265,7 +1313,7 @@
     seq_index = lax.axis_index("seq")
     before = (seq_index + seq_count - 1) % seq_count
     behind = (seq_index + 1) % seq_count
-    pieces = [*(ready.at[piece] for piece in range(ready_count)), mine]
+    pieces = [ready.at[piece] for piece in range(ready_count)]
     ring = ChipRing(seq_count, pieces, *ring_refs)
     partner = {"seq": xor_place(seq_index, 1)}
     cores = CoreSum(partner, *core_refs)
@@ -1307,7 +1355,6 @@
         @pl.when(pair * blocks + block == MADE_AT)
         def _():
             mine[...] = cores.finish(0)
-            ring.start(ready_count)
 
         for moment, (piece, hop) in zip(due, order):
             if moment % blocks == block:
@@ -1451,14 +1498,15 @@
         ],
         out_specs=[
             pl.BlockSpec((rows + slots, 3 * part), lambda i: (0, 0)),
-            pl.BlockSpec((ready_count + 1, seg, width), lambda i: (0, 0, 0)),
+            pl.BlockSpec((ready_count, seg, width), lambda i: (0, 0, 0)),
+            pl.BlockSpec((chips, seg, width), lambda i: (0, 0, 0)),
         ],
         out_shape=[
             jax.ShapeDtypeStruct((rows + slots, 3 * part), jnp.bfloat16),
-            jax.ShapeDtypeStruct((ready_count + 1, seg, width), jnp.float32),
+            jax.ShapeDtypeStruct((ready_count, seg, width), jnp.float32),
+            jax.ShapeDtypeStruct((chips, seg, width), jnp.bfloat16),
         ],
         scratch_shapes=[
-            pltpu.VMEM((chips, seg, width), jnp.bfloat16),
             pltpu.VMEM((blocks, span + slots, QUERY_BLOCK), jnp.float32),
             pltpu.VMEM((2, window + slots, LANES), jnp.float32),
             pltpu.VMEM((pairs, 2, rows, LANES), jnp.float32),
@@ -1467,14 +1515,14 @@
             pltpu.SemaphoreType.DMA((pairs, 2)),
             pltpu.SemaphoreType.DMA((pairs, 2)),
             *core_scratch(1, chips, seg, width, 1),
-            *ring_scratch(seq_count, ready_count + 1, seg, width),
+            *ring_scratch(seq_count, ready_count, seg, width),
         ],
         compiler_params=pltpu.CompilerParams(
             collective_id=3, has_side_effects=True, vmem_limit_bytes=VMEM_BYTES
         ),
         cost_estimate=pl.CostEstimate(
             flops=10 * rows * window * part,
-            bytes_accessed=16 * chips * seg * width * (ready_count + 1),
+            bytes_accessed=16 * chips * seg * width * ready_count,
             transcendentals=rows * window * part // HD,
         ),
         name="self_back",
@@ -1527,7 +1575,7 @@
         gain_terms,
         share,
         core_sums,
-        grad_mix,
+        ctx_acc,
         split,
         split_land,
         split_send,
@@ -1548,13 +1596,13 @@
     cores = CoreSum(partner, *core_refs)
     greet([*others, partner] + [{"seq": side} for side in sides])
 
-    def hop(side, which):
+    def hop(side, which, slab):
         sems = fourth_sems if which else third_sems
         return pltpu.make_async_remote_copy(
-            src_ref=third_land.at[side] if which else moving.at[side],
-            dst_ref=(fourth_land if which else third_land).at[side],
-            send_sem=sems.at[0, side],
-            recv_sem=sems.at[1, side],
+            src_ref=third_land.at[side, slab] if which else moving.at[side, slab],
+            dst_ref=(fourth_land if which else third_land).at[side, slab],
+            send_sem=sems.at[0, side, slab],
+            recv_sem=sems.at[1, side, slab],
             device_id={"seq": sides[side]},
             device_id_type=MESH,
         )
@@ -1565,84 +1613,108 @@
 
     def third_to_fourth():
         for side in range(2):
-            hop(side, 0).wait_recv()
             keep_copy(side).wait()
-            term = keep[side].astype(jnp.float32) + third_land[side].astype(jnp.float32)
-            third_land[side] = term.astype(jnp.bfloat16)
-            hop(side, 1).start()
+        for slab in range(3):
+            for side in range(2):
+                hop(side, 0, slab).wait_recv()
+                term = keep[side, slab].astype(jnp.float32)
+                term = term + third_land[side, slab].astype(jnp.float32)
+                third_land[side, slab] = term.astype(jnp.bfloat16)
+                hop(side, 1, slab).start()
         keep_copy(2).start()
 
-    def over_heads(which, step):
+    def over_heads(which, chunk):
+        part = pl.ds(chunk * QUERY_BLOCK, QUERY_BLOCK)
         return pltpu.make_async_remote_copy(
-            src_ref=grad_low if which == 0 else split,
-            dst_ref=split_land.at[which, step],
-            send_sem=split_send.at[which, step],
-            recv_sem=split_recv.at[which, step],
-            device_id=others[step],
+            src_ref=(grad_low if which == 0 else split).at[part],
+            dst_ref=split_land.at[which, part],
+            send_sem=split_send.at[which, chunk],
+            recv_sem=split_recv.at[which, chunk],
+            device_id=others[0],
             device_id_type=MESH,
         )
 
-    def summed(which):
-        total = (grad_low if which == 0 else split)[...].astype(jnp.float32)
-        for step in range(head_count - 1):
-            over_heads(which, step).wait_recv()
-            total = total + split_land[which, step].astype(jnp.float32)
-        return total
-
-    for step in range(head_count - 1):
-        over_heads(0, step).start()
-    hop(0, 0).start()
-    hop(1, 0).start()
+    rows = query.shape[0]
+    keys = key.shape[0]
+    part = query.shape[1]
+    pairs = part // LANES
+    chunks = range(rows // QUERY_BLOCK)
+
+    def chunk_rows(chunk):
+        return slice(chunk * QUERY_BLOCK, (chunk + 1) * QUERY_BLOCK)
+
+    def summed(which, chunk):
+        over_heads(which, chunk).wait_recv()
+        here = chunk_rows(chunk)
+        own = (grad_low if which == 0 else split)[here, :].astype(jnp.float32)
+        return own + split_land[which, here, :].astype(jnp.float32)
+
+    for chunk in chunks:
+        over_heads(0, chunk).start()
+    for slab in range(3):
+        hop(0, 0, slab).start()
+        hop(1, 0, slab).start()
     keep_copy(0).start()
     keep_copy(1).start()
     gain_terms[...] = jnp.zeros_like(gain_terms)
-    total = summed(0)
-    normal = normal_three[...]
-    gain_terms[0:1, :] = jnp.sum(total * normal, axis=0, keepdims=True)
-    grad_h_one[...] = top[...].astype(jnp.float32) + through_norm(
-        total, normal, inverse_three[...], gains[0:1, :]
-    )
-    grad_two_low[...] = grad_h_one[...].astype(jnp.bfloat16)
-    grad_mix[...] = product(grad_two_low[...], c_out[...]).astype(jnp.bfloat16)
+    ctx_acc[...] = jnp.zeros_like(ctx_acc)
+    token_slot = lax.broadcasted_iota(jnp.int32, (keys, 1), 0) // ctx_tokens
+    lane = lax.broadcasted_iota(jnp.int32, (1, LANES), 1)
+    for chunk in chunks:
+        here = chunk_rows(chunk)
+        total = summed(0, chunk)
+        normal = normal_three[here, :]
+        gain_terms[0:1, :] += jnp.sum(total * normal, axis=0, keepdims=True)
+        grad_two = top[here, :].astype(jnp.float32) + through_norm(
+            total, normal, inverse_three[here, :], gains[0:1, :]
+        )
+        grad_h_one[here, :] = grad_two
+        grad_two_low[here, :] = grad_two.astype(jnp.bfloat16)
+        grad_mix = product(grad_two_low[here, :], c_out[...]).astype(jnp.bfloat16)
+        bias = jnp.where(token_slot == query_slots[:, here], 0.0, NEG)
+        for pair in range(pairs):
+            columns = slice(pair * LANES, (pair + 1) * LANES)
+            second = slice((pairs + pair) * LANES, (pairs + pair + 1) * LANES)
+            pair_q, pair_g = query[here, columns], grad_mix[:, columns]
+            pair_k, pair_v = key[:, columns], value[:, columns]
+            grad_q = jnp.zeros((QUERY_BLOCK, LANES), jnp.float32)
+            grad_k = jnp.zeros((keys, LANES), jnp.float32)
+            grad_v = jnp.zeros((keys, LANES), jnp.float32)
+            for head in range(LANES // HD):
+                mine = lane // HD == head
+                head_q = jnp.where(mine, pair_q, jnp.zeros_like(pair_q))
+                head_g = jnp.where(mine, pair_g, jnp.zeros_like(pair_g))
+                head_k = jnp.where(mine, pair_k, jnp.zeros_like(pair_k))
+                at = pair * (LANES // HD) + head
+                scores = product_t(pair_k, head_q) * score_scale + bias
+                probs = jnp.exp(scores - logs[at : at + 1, here])
+                grad_p = product_t(pair_v, head_g)
+                dot = jnp.sum(probs * grad_p, axis=0, keepdims=True)
+                grad_s = (probs * (grad_p - dot)).astype(jnp.bfloat16)
+                grad_k = grad_k + product(grad_s, head_q)
+                grad_v = grad_v + product(probs.astype(jnp.bfloat16), head_g)
+                grad_q = grad_q + product_tn(grad_s, head_k)
+            grad_query[here, columns] = (grad_q * score_scale).astype(jnp.bfloat16)
+            ctx_acc[:, columns] += grad_k * score_scale
+            ctx_acc[:, second] += grad_v
+        split[here, :] = product_t(grad_query[here, :], c_query[...]).astype(jnp.bfloat16)
+        over_heads(1, chunk).start()
+        if chunk == HOP_CHUNK:
+            third_to_fourth()
+    ctx_grads[...] = ctx_acc[...].astype(jnp.bfloat16)
     cores.start(0, product_tn(grad_two_low[...], cross_mixed[...]))
-    rows = query.shape[0]
-    keys = key.shape[0]
-    pairs = query.shape[1] // LANES
-    token_slot = lax.broadcasted_iota(jnp.int32, (keys, 1), 0) // ctx_tokens
-    bias = jnp.where(token_slot == query_slots[...], 0.0, NEG)
-    lane = lax.broadcasted_iota(jnp.int32, (1, LANES), 1)
-    for pair in range(pairs):
-        columns = slice(pair * LANES, (pair + 1) * LANES)
-        pair_q, pair_g = query[:, columns], grad_mix[:, columns]
-        pair_k, pair_v = key[:, columns], value[:, columns]
-        grad_q = jnp.zeros((rows, LANES), jnp.float32)
-        grad_k = jnp.zeros((keys, LANES), jnp.float32)
-        grad_v = jnp.zeros((keys, LANES), jnp.float32)
-        for head in range(LANES // HD):
-            here = lane // HD == head
-            head_q = jnp.where(here, pair_q, jnp.zeros_like(pair_q))
-            head_g = jnp.where(here, pair_g, jnp.zeros_like(pair_g))
-            head_k = jnp.where(here, pair_k, jnp.zeros_like(pair_k))
-            at = pair * (LANES // HD) + head
-            scores = product_t(pair_k, head_q) * score_scale + bias
-            probs = jnp.exp(scores - logs[at : at + 1, :])
-            grad_p = product_t(pair_v, head_g)
-            dot = jnp.sum(probs * grad_p, axis=0, keepdims=True)
-            grad_s = (probs * (grad_p - dot)).astype(jnp.bfloat16)
-            grad_k = grad_k + product(grad_s, head_q)
-            grad_v = grad_v + product(probs.astype(jnp.bfloat16), head_g)
-            grad_q = grad_q + product_tn(grad_s, head_k)
-        grad_query[:, columns] = (grad_q * score_scale).astype(jnp.bfloat16)
-        ctx_grads[:, columns] = (grad_k * score_scale).astype(jnp.bfloat16)
-        second = slice((pairs + pair) * LANES, (pairs + pair + 1) * LANES)
-        ctx_grads[:, second] = grad_v.astype(jnp.bfloat16)
-        if pair == HOP_PAIR:
-            third_to_fourth()
-    split[...] = product_t(grad_query[...], c_query[...]).astype(jnp.bfloat16)
-    for step in range(head_count - 1):
-        over_heads(1, step).start()
     cores.start(1, product_tn(normed_two[...], grad_query[...]))
-    part = query.shape[1]
+    for chunk in chunks:
+        here = chunk_rows(chunk)
+        total = summed(1, chunk)
+        normal = normal_two[here, :]
+        gain_terms[1:2, :] += jnp.sum(total * normal, axis=0, keepdims=True)
+        grad_one = grad_h_one[here, :] + through_norm(
+            total, normal, inverse_two[here, :], gains[1:2, :]
+        )
+        grad_h_one[here, :] = grad_one
+        grad_one_low[here, :] = grad_one.astype(jnp.bfloat16)
+        grad_attn[here, :] = product(grad_one_low[here, :], w_out[...]).astype(jnp.bfloat16)
     core_sums[0] = cores.finish(0)
     cores.close(0)
     ctx_rows = cores.terms.shape[3] // 2
@@ -1653,28 +1725,22 @@
     cores.copy(2).start()
     for piece in range(1, 3):
         core_sums[piece] = cores.finish(piece)
-    total = summed(1)
-    normal = normal_two[...]
-    gain_terms[1:2, :] = jnp.sum(total * normal, axis=0, keepdims=True)
-    grad_h_one[...] += through_norm(
-        total, normal, inverse_two[...], gains[1:2, :]
-    )
-    grad_one_low[...] = grad_h_one[...].astype(jnp.bfloat16)
-    grad_attn[...] = product(grad_one_low[...], w_out[...]).astype(jnp.bfloat16)
     keep_copy(2).wait()
     whole = keep[0].astype(jnp.float32)
     for side in range(2):
-        hop(side, 1).wait_recv()
+        for slab in range(3):
+            hop(side, 1, slab).wait_recv()
         whole = whole + fourth_land[side].astype(jnp.float32)
     share[...] = whole
     for side in range(2):
-        hop(side, 0).wait_send()
-        hop(side, 1).wait_send()
+        for slab in range(3):
+            hop(side, 0, slab).wait_send()
+            hop(side, 1, slab).wait_send()
     for piece in range(1, 3):
         cores.close(piece)
-    for which in range(2):
-        for step in range(head_count - 1):
-            over_heads(which, step).wait_send()
+    for chunk in chunks:
+        over_heads(0, chunk).wait_send()
+        over_heads(1, chunk).wait_send()
 
 
 def mid_layer(
@@ -1693,11 +1759,11 @@
         return pl.BlockSpec((width, part), lambda i: (0, which), pipeline_mode=pl.Buffered(1))
 
     scratches = [
-        pltpu.VMEM((rows, part), bf),
+        pltpu.VMEM((keys, 2 * part), wide),
         pltpu.VMEM((rows, width), bf),
-        pltpu.VMEM((2, head_count - 1, rows, width), bf),
-        pltpu.SemaphoreType.DMA((2, head_count - 1)),
-        pltpu.SemaphoreType.DMA((2, head_count - 1)),
+        pltpu.VMEM((2, rows, width), bf),
+        pltpu.SemaphoreType.DMA((2, rows // QUERY_BLOCK)),
+        pltpu.SemaphoreType.DMA((2, rows // QUERY_BLOCK)),
     ]
     out_shapes = [
         jax.ShapeDtypeStruct((rows, width), wide),
@@ -1711,8 +1777,8 @@
     scratches += [
         pltpu.VMEM(moved, bf),
         pltpu.VMEM(moved, bf),
-        pltpu.SemaphoreType.DMA((2, 2)),
-        pltpu.SemaphoreType.DMA((2, 2)),
+        pltpu.SemaphoreType.DMA((2, 2, 3)),
+        pltpu.SemaphoreType.DMA((2, 2, 3)),
         pltpu.VMEM((2, *moved[1:]), bf),
         pltpu.SemaphoreType.DMA((3,)),
         *core_scratch(3, chips, seg, part, 2),
@@ -1828,8 +1894,8 @@
     small_rows = -(-max(clip_total + 1, bias_rows + 3) // 8) * 8
     vectors = jnp.stack([norm1_gain, norm2_gain, norm3_gain, down_bias], axis=1)
     vectors = jnp.pad(vectors, ((0, 0), (0, LANES - 4)))
-    ctx_pair = jnp.concatenate([cross_key, cross_value], axis=0)
-    attn_local = jnp.concatenate(
+    starts = [each * part for each in range(8)]
+    attn_weights, glu_local = ring_gather(
         [
             query_weight,
             key_weight,
@@ -1837,17 +1903,15 @@
             out_weight,
             cross_query,
             cross_out,
-            ctx_pair,
+            cross_key,
+            cross_value,
             vectors,
         ],
-        axis=1,
-    )
-    starts = [each * part for each in range(8)]
-    attn_weights, token = ring_gather(
-        attn_local, (*starts[:7], starts[7] + LANES), seq_count, 4
-    )
-    glu_local = jnp.concatenate([gate_weight, up_weight, down_weight], axis=1).astype(jnp.bfloat16)
-    token, glu_local = lax.optimization_barrier((token, glu_local))
+        [gate_weight, up_weight, down_weight],
+        (*starts[:7], starts[7] + LANES),
+        seq_count,
+        4,
+    )
     glu_weights = low_gather(glu_local)
     w_qkv = attn_weights[:, : starts[3]]
     w_out = attn_weights[:, starts[3] : starts[4]]
@@ -1856,7 +1920,7 @@
     ctx_weights = attn_weights[:, starts[6] : starts[7]].reshape(seq_count, 2, ctx_rows, part)
     c_key = ctx_weights[:, 0].reshape(ctx_width, part)
     c_value = ctx_weights[:, 1].reshape(ctx_width, part)
-    rows_of = attn_weights[:, starts[7] : starts[7] + 8].astype(jnp.float32).T + token[0, 0]
+    rows_of = attn_weights[:, starts[7] : starts[7] + 8].astype(jnp.float32).T
     gain_one_f, gain_two_f, gain_three_f, bias_f = rows_of[0], rows_of[1], rows_of[2], rows_of[3]
 
     positions = first_row + jnp.arange(local_rows, dtype=jnp.int32)
@@ -1974,7 +2038,7 @@
             for each in ([cos_table, cos_table, ones], low_side, high_side)
         ]
     )
-    grad_qkv, early_share = self_back(
+    grad_qkv, early_share, out_sum = self_back(
         query_rows,
         near,
         stamps,
@@ -2011,10 +2075,12 @@
         h_two,
         (glu_out, glu_other),
         bias_f[None],
+        out_sum,
         clip_total,
         seq_count,
     )
-    cross_out_share, cross_query_share, ctx_share, out_share = early_share
+    cross_out_share, cross_query_share, ctx_share = early_share
+    out_share = qkv_share[0]
     late = small[: clip_total + 1]
     early = small[small_rows : small_rows + bias_rows + 3]
     stamp_sum = late[:clip_total]
@@ -2037,9 +2103,9 @@
         gains_own[0],
         gains_own[1],
         gains_own[2],
-        qkv_share[0],
         qkv_share[1],
         qkv_share[2],
+        qkv_share[3],
         out_share,
         cross_query_share,
         ctx_share[:ctx_rows],

time: 626 us -> 609 us (0.973)
  other arithmetic: 50.3 us -> 41.4 us
    pallas_call x1, Pallas kernels: 61.2 us -> 49.5 us  [self_back(): pl.pallas_call(functools.partial(self_back_kernel, seq_count, pairs, scor...]
    pallas_call x1, Pallas kernels: 68.3 us -> 78.7 us  [tail_sums(): pl.pallas_call(functools.partial(tail_kernel, seq_count, head_count, made...]
  transfers between devices with their start and end apart: 6 -> 6, of which waited for: 1 -> 1; matrix products, arithmetic and copies ran while one was open for 23% -> 24% of each run, Pallas kernels for 10% -> 8%
where the time goes in v6:
time: 609 us; the launch traced here: 600 us
  Pallas kernels  405 us (67%)
  local copies, waits for them, and re-layouts  80.4 us (13%)
  other arithmetic  41.4 us (7%)
  matrix products  37.2 us (6%)
  between operations  15.6 us (3%)
  waiting for transfers between devices  12.2 us (2%)
  starting transfers between devices  8.91 us (1%)
    pallas_call x1, Pallas kernels, glu_layer(): pl.pallas_call(functools.partial(glu_kernel, blocks, seq_count), grid=(bl...  96.4 us
    pallas_call x1, Pallas kernels, mid_layer(): pl.pallas_call(functools.partial(mid_kernel, seq_count, head_count, HD **...  91.6 us
    pallas_call x1, Pallas kernels, ring_gather(): pl.pallas_call(functools.partial(gather_kernel, seq_count, bounds, len(wi...  88.4 us
    pallas_call x1, Pallas kernels, tail_sums(): pl.pallas_call(functools.partial(tail_kernel, seq_count, head_count, made...  78.7 us
    pallas_call x1, Pallas kernels, self_back(): pl.pallas_call(functools.partial(self_back_kernel, seq_count, pairs, scor...  49.5 us
    dot_general x4, matrix products, product(): return jnp.dot(matrix_a, matrix_b, preferred_element_type=jnp.float32)  14.2 us
  transfers between devices with their start and end apart: 6, of which 1 were waited for; matrix products, arithmetic and copies ran while one was open for 24% of the time, Pallas kernels for 8%

profile of v6, /device:TPU:0, one launch (start us, length us, event | category | flops | bytes accessed | tf_op | source)
XLA Modules:
  0.0 600.5 jit_solution(14121353599769515255)
XLA Ops:
  8.8 88.4 %ring_gather.1 = (bf16[8,2,96,5504]{3,2,1,0:T(8,128)(2,1)}, bf16[96,9216]{1,0:T(8,128)(2,1)}) custom-call(f32[96,768]{1,0:T(8,128)} %refs_0_.1, f32[96,768]{1,0:T(8,128)} %refs_1_.2, f32[96,768]{1,0:T(8,128)} %refs_2_.1, f32[96,768]{1,0:T(8,128)} %refs_3_.1, f32[96,768]{1,0:T(8,128)} %refs_4_.1, f32[96,768]{1,0:T(8,128)} %refs_5_.1, f32[48,768]{1,0:T(8,128)} %refs_6_.1, ...), custom_call_target="tpu_custom_call" | custom-call | bytes 270532608 | tf_op jit(solution)/shard_map/ring_gather/pallas_call | solution.py:670
  102.6 1.2 slice_reduce_fusion
  103.8 8.2 %fusion.56 = (bf16[400,2304]{1,0:T(8,128)(2,1)}, f32[400,2304]{1,0:T(8,128)S(1)}) fusion(bf16[1536,5504]{1,0:T(8,128)(2,1)} %bitcast.84, f32[1536]{0:T(1024)S(1)} %get-tuple-element.68, f32[400]{0:T(512)S(1)} %add_rsqrt_fusion.2, f32[400]{0:T(512)S(1)} %broadcast_multiply_fusion.2, bf16[2,1536]{1,0:T(2,128)(2,1)S(1)} %constant_dynamic-slice_fusion.1, ...), kind=kOutput, calls=%fused_computation.158 | convolution fusion | flops 2838220800 | bytes 13802624 | tf_op jit(solution)/shard_map/dot_general | solution.py:83
  112.0 1.2 fusion.50
  113.1 1.4 copy.108
  114.5 1.1 slice.321
  115.8 1.1 subtract_convert_fusion
  117.3 1.1 slice_bitcast_fusion.3
  118.5 1.2 fusion.22
  119.7 3.2 collective-permute-start
  122.9 1.5 collective-permute-start.1
  124.4 3.3 slice.260
  127.6 2.7 copy.107
  130.3 1.8 slice.245
  132.1 1.3 fusion.53
  133.4 1.4 reshape.410
  134.8 1.4 reshape.411
  138.9 1.3 multiply_subtract_fusion
  143.3 1.1 fusion.13
  145.4 1.3 convolution_convert_fusion.2.refs_11_
  146.6 1.2 convolution_convert_fusion.3.refs_12_
  147.8 1.5 pad_maximum_fusion.refs_1_.refs_2_
  149.4 1.8 fusion.51
  151.7 2.5 copy.111
  154.2 2.5 copy.110
  156.7 4.5 fusion
  161.4 4.5 fusion.1
  166.9 6.1 %fusion.15 = bf16[12,64,384]{2,1,0:T(8,128)(2,1)S(1)} fusion(f32[12,64,384]{2,1,0:T(8,128)S(1)} %fusion.36, bf16[896,12,64]{0,2,1:T(8,128)(2,1)S(1)} %bitcast.109, f32[12,384,896]{2,1,0:T(8,128)S(1)} %get-tuple-element.126, f32[12,384]{1,0:T(8,128)S(1)} %get-tuple-element.71, f32[12,384]{1,0:T(8,128)S(1)} %max.9, pred[384,896]{1,0:T(8,128)(4,1)S(1)} %fusion.13), kind=kOutput, calls=%fused_computation.39 | convolution fusion | flops 549715968 | bytes 20041728 | tf_op jit(solution)/shard_map/hqk,khd->qhd/dot_general | solution.py:138
  173.1 4.1 convolution_convert_fusion.1
  177.2 1.7 collective-permute-start.2
  182.7 2.3 subtract_multiply_fusion
  185.0 12.2 %collective-permute-done.2 = bf16[384,1536]{1,0:T(8,128)(2,1)} collective-permute-done((bf16[384,1536]{1,0:T(8,128)(2,1)}, bf16[384,1536]{1,0:T(8,128)(2,1)}, u32[]{:S(2)}, u32[]{:S(2)}) %collective-permute-start.2) | collective-permute-done | bytes 1179680 | tf_op jit(solution)/shard_map/ppermute | solution.py:1846
  197.2 2.2 fusion.49
  200.1 1.9 multiply_convert_fusion.2
  203.0 3.5 fusion.17.refs_10_
  206.5 2.1 copy.115
  208.7 2.1 fusion.5
  211.8 1.4 fusion.16
  213.3 4.1 convolution_convert_fusion
  217.4 1.8 collective-permute-start.3
  219.7 1.4 copy.118
  221.7 1.5 slice.253.refs_3_.refs_4_
  223.2 1.2 broadcast_in_dim.62.refs_8_
  226.0 2.1 copy.126.refs_0_
  229.5 3.3 slice.267.refs_3_
  232.8 3.0 copy.129.refs_0_
  235.8 1.5 slice.238.refs_4_
  239.6 1.3 fusion.41.refs_7_
  240.9 1.3 pad_maximum_fusion.4.refs_6_
  242.3 1.1 copy.128.refs_13_
  243.3 1.4 add.154.refs_6_
  244.7 2.2 copy.122.refs_15_
  246.8 1.5 rsqrt.38.refs_5_
  248.9 2.1 fusion.48
  252.5 1.8 multiply_convert_fusion.1
  254.3 1.4 copy.119.normed_t
  255.7 96.4 %glu_layer.1 = (bf16[384,1536]{1,0:T(8,128)(2,1)}, bf16[384,1536]{1,0:T(8,128)(2,1)}, f32[2,3072]{1,0:T(2,128)}, bf16[3,3,96,3072]{3,2,1,0:T(8,128)(2,1)}, bf16[2,3,96,3072]{3,2,1,0:T(8,128)(2,1)}) custom-call(bf16[384,1536]{1,0:T(8,128)(2,1)} %copy-done.9, bf16[1536,384]{1,0:T(8,128)(2,1)} %copy.119.normed_t, bf16[384,1536]{1,0:T(8,128)(2,1)} %refs_1_.3, ...), custom_call_target="tpu_custom_call" | custom-call | flops 32614907904 | bytes 56623104 | tf_op jit(solution)/shard_map/glu_layer/pallas_call | solution.py:875
  352.1 91.6 %mid_layer.1 = (f32[384,1536]{1,0:T(8,128)}, bf16[384,1536]{1,0:T(8,128)(2,1)}, bf16[384,1536]{1,0:T(8,128)(2,1)}, bf16[384,768]{1,0:T(8,128)(2,1)}, bf16[384,76...) custom-call(bf16[384,1536]{1,0:T(8,128)(2,1)} %get-tuple-element.44., ...), custom_call_target="tpu_custom_call" | custom-call | flops 3472883712 | bytes 58982400 | tf_op jit(solution)/shard_map/mid_layer/pallas_call | solution.py:1790
  445.4 49.5 %self_back.1 = (bf16[400,2304]{1,0:T(8,128)(2,1)}, f32[3,96,768]{2,1,0:T(8,128)}, bf16[8,96,768]{2,1,0:T(8,128)(2,1)}) custom-call(bf16[384,768]{1,0:T(8,128)(2,1)} %copy.126.refs_0_, bf16[2,896,768]{2,1,0:T(8,128)(2,1)} %copy-done.2, bf16[2,896,768]{2,1,0:T(8,128)(2,1)} %copy-done.2, bf16[16,2304]{1,0:T(8,128)(2,1)} %slice.253.refs_3_.refs_4_, ...), custom_call_target="tpu_custom_call" | custom-call | flops 2642411520 | bytes 28311552 | tf_op jit(solution)/shard_map/self_back/pallas_call | solution.py:1480
  494.9 1.7 slice_bitcast_fusion.10
  497.3 1.9 slice_bitcast_fusion.4
  499.2 3.8 slice_bitcast_fusion
  504.1 78.7 %tail_sums.1 = (f32[4,96,768]{2,1,0:T(8,128)}, f32[16,1536]{1,0:T(8,128)}, bf16[384,1536]{1,0:T(8,128)(2,1)}, bf16[384,1536]{1,0:T(8,128)(2,1)}) custom-call(bf16[1536,400]{1,0:T(8,128)(2,1)} %copy.129.refs_0_, bf16[400,2304]{1,0:T(8,128)(2,1)} %get-tuple-element.52.refs_1_, bf16[1536,5504]{1,0:T(8,128)(2,1)} %bitcast.92, f32[384,1536]{1,0:T(8,128)} %slice.267.refs_3_, ...), custom_call_target="tpu_custom_call" | custom-call | flops 5662310400 | bytes 56623104 | tf_op jit(solution)/shard_map/tail_sums/pallas_call | solution.py:1217
  587.1 2.3 slice_bitcast_fusion.6
  (194 shorter events, 41.4 us)
Async XLA Ops:
  7.2 131.6 %copy-start = (bf16[6,128,768]{2,1,0:T(8,128)(2,1)S(1)}, bf16[6,128,768]{2,1,0:T(8,128)(2,1)}, u32[]{:S(2)}) copy-start(bf16[6,128,768]{2,1,0:T(8,128)(2,1)} %param.24) | copy-start | bytes 3538948
  7.2 248.5 %all-gather.2.cloned.1.call-start = ((), (), s32[]{:S(2)}) async-start(), calls=%async_computation | async-start | bytes 30081024 | tf_op jit(solution)/shard_map/all_gather | solution.py:1851
  97.2 4.6 copy-start.4
  98.1 0.6 copy-start.48
  102.1 9.9 %copy-start.46 = (f32[400]{0:T(512)}, f32[400]{0:T(512)S(1)}, u32[]{:S(2)}) copy-start(f32[400]{0:T(512)S(1)} %broadcast_multiply_fusion.2) | copy-start | bytes 4804
  102.5 9.4 %copy-start.44 = (f32[400]{0:T(512)}, f32[400]{0:T(512)S(1)}, u32[]{:S(2)}) copy-start(f32[400]{0:T(512)S(1)} %add_rsqrt_fusion.2) | copy-start | bytes 4804
  115.8 1.2 copy-start.26
  115.8 1.2 copy-start.28
  119.7 28.1 %collective-permute-start = (bf16[2,256,768]{2,1,0:T(8,128)(2,1)}, bf16[2,256,768]{2,1,0:T(8,128)(2,1)}, u32[]{:S(2)}, u32[]{:S(2)}) collective-permute-start(bf16[2,256,768]{2,1,0:T(8,128)(2,1)} %get-tuple-element.101), channel_id=1, source_target_pairs={{0,2},{2,4},{4,6},{6,8},{8,10},{10,12},{12,14},{14,16},{16,18},{18... | collective-permute-start | bytes 2359304 | tf_op jit(solution)/shard_map/ppermute | solution.py:25
  122.9 24.9 %collective-permute-start.1 = (bf16[2,256,768]{2,1,0:T(8,128)(2,1)}, bf16[2,256,768]{2,1,0:T(8,128)(2,1)}, u32[]{:S(2)}, u32[]{:S(2)}) collective-permute-start(bf16[2,256,768]{2,1,0:T(8,128)(2,1)} %get-tuple-element.102), channel_id=1, source_target_pairs={{2,0},{4,2},{6,4},{8,6},{10,8},{12,10},{14,12},{16,14},{18,16},{20... | collective-permute-start | bytes 2359304 | tf_op jit(solution)/shard_map/ppermute | solution.py:28
  136.2 5.6 copy-start.27
  136.2 8.3 %copy-start.6 = (bf16[1536,768]{1,0:T(8,128)(2,1)S(1)}, bf16[1536,768]{1,0:T(8,128)(2,1)}, u32[]{:S(2)}) copy-start(bf16[1536,768]{1,0:T(8,128)(2,1)} %slice.260) | copy-start | bytes 7077892
  137.2 7.2 %copy-start.39 = (s32[384]{0:T(512)}, s32[384]{0:T(512)S(1)}, u32[]{:S(2)}) copy-start(s32[384]{0:T(512)S(1)} %broadcast_subtract_fusion) | copy-start | bytes 4612
  138.0 6.5 %copy-start.35 = (s32[896]{0:T(1024)}, s32[896]{0:T(1024)S(1)}, u32[]{:S(2)}) copy-start(s32[896]{0:T(1024)S(1)} %pad_dynamic-slice_fusion) | copy-start | bytes 10756
  138.9 7.7 %copy-start.7 = (bf16[2,128,768]{2,1,0:T(8,128)(2,1)}, bf16[2,128,768]{2,1,0:T(8,128)(2,1)S(1)}, u32[]{:S(2)}) copy-start(bf16[2,128,768]{2,1,0:T(8,128)(2,1)S(1)} %constant_dynamic-slice_fusion) | copy-start | bytes 1179652
  141.2 15.5 %copy-start.8 = (bf16[384,12,64]{0,2,1:T(8,128)(2,1)}, bf16[384,12,64]{0,2,1:T(8,128)(2,1)S(1)}, u32[]{:S(2)}) copy-start(bf16[384,12,64]{0,2,1:T(8,128)(2,1)S(1)} %maximum_convert_fusion) | copy-start | bytes 1769476
  144.4 0.7 copy-start.49
  149.4 2.3 copy-start.2
  161.3 5.2 copy-start.41
  161.3 5.5 copy-start.13
  173.0 4.2 copy-start.19
  173.0 5.8 copy-start.5
  173.0 6.6 %copy-start.11 = (bf16[256,768]{1,0:T(8,128)(2,1)S(1)}, bf16[256,768]{1,0:T(8,128)(2,1)}, u32[]{:S(2)}) copy-start(bf16[256,768]{1,0:T(8,128)(2,1)} %convolution_convert_fusion.2.refs_11_) | copy-start | bytes 1179652
  173.0 7.5 %copy-start.12 = (bf16[256,768]{1,0:T(8,128)(2,1)S(1)}, bf16[256,768]{1,0:T(8,128)(2,1)}, u32[]{:S(2)}) copy-start(bf16[256,768]{1,0:T(8,128)(2,1)} %convolution_convert_fusion.3.refs_12_) | copy-start | bytes 1179652
  177.2 4.4 copy-start.29
  177.2 20.0 %collective-permute-start.2 = (bf16[384,1536]{1,0:T(8,128)(2,1)}, bf16[384,1536]{1,0:T(8,128)(2,1)}, u32[]{:S(2)}, u32[]{:S(2)}) collective-permute-start(bf16[384,1536]{1,0:T(8,128)(2,1)} %convolution_convert_fusion.1), channel_id=1, source_target_pairs={{0,1},{1,0},{2,3},{3,2},{4,5},{5,4},{6,7},{7,6},{8,9},{9,8},{10,11... | collective-permute-start | bytes 3538952 | tf_op jit(solution)/shard_map/ppermute | solution.py:1846
  180.6 2.1 copy-start.45
  180.6 2.1 copy-start.47
  199.4 0.7 copy-start.38
  199.8 2.2 copy-start.43
  202.0 1.0 copy-start.10
  208.7 2.1 copy-start.18
  210.8 1.0 copy-start.31
  210.8 1.0 copy-start.23
  211.8 1.5 copy-start.33
  213.3 4.1 copy-start.21
  217.4 3.7 copy-start.40
  217.4 7.0 %copy-start.36 = (s32[896]{0:T(1024)S(1)}, s32[896]{0:T(1024)}, u32[]{:S(2)}) copy-start(s32[896]{0:T(1024)} %copy-done.35) | copy-start | bytes 10756
  217.4 31.6 %collective-permute-start.3 = (bf16[384,1536]{1,0:T(8,128)(2,1)}, bf16[384,1536]{1,0:T(8,128)(2,1)}, u32[]{:S(2)}, u32[]{:S(2)}) collective-permute-start(bf16[384,1536]{1,0:T(8,128)(2,1)} %convolution_convert_fusion), channel_id=1, source_target_pairs={{0,1},{1,0},{2,3},{3,2},{4,5},{5,4},{6,7},{7,6},{8,9},{9,8},{10,11... | collective-permute-start | bytes 3538952 | tf_op jit(solution)/shard_map/ppermute | solution.py:1846
  221.1 8.1 %copy-start.25 = (f32[384,64]{0,1:T(8,128)S(1)}, f32[384,64]{0,1:T(8,128)}, u32[]{:S(2)}) copy-start(f32[384,64]{0,1:T(8,128)} %get-tuple-element.110) | copy-start | bytes 294916
  221.1 8.3 %copy-start.24 = (f32[384,64]{0,1:T(8,128)S(1)}, f32[384,64]{0,1:T(8,128)}, u32[]{:S(2)}) copy-start(f32[384,64]{0,1:T(8,128)} %maximum_maximum_fusion) | copy-start | bytes 294916
  232.8 9.4 %copy-start.20 = (bf16[12,64,384]{2,1,0:T(8,128)(2,1)S(1)}, bf16[12,64,384]{2,1,0:T(8,128)(2,1)}, u32[]{:S(2)}) copy-start(bf16[12,64,384]{2,1,0:T(8,128)(2,1)} %copy-done.19) | copy-start | bytes 1769476
  239.1 9.2 %copy-start.32 = (f32[12,384]{1,0:T(8,128)S(1)}, f32[12,384]{1,0:T(8,128)}, u32[]{:S(2)}) copy-start(f32[12,384]{1,0:T(8,128)} %copy-done.31) | copy-start | bytes 55300
  239.1 9.2 %copy-start.34 = (f32[12,384]{1,0:T(8,128)S(1)}, f32[12,384]{1,0:T(8,128)}, u32[]{:S(2)}) copy-start(f32[12,384]{1,0:T(8,128)} %copy-done.33) | copy-start | bytes 55300
  251.0 3.3 copy-start.3
  251.0 1.5 copy-start.37
  254.3 1.4 copy-start.9
  352.1 92.5 %copy-start.42 = (f32[2,3072]{1,0:T(2,128)S(1)}, f32[2,3072]{1,0:T(2,128)}, u32[]{:S(2)}) copy-start(f32[2,3072]{1,0:T(2,128)} %get-tuple-element.54) | copy-start | bytes 73732
  352.1 92.6 %copy-start.14 = (bf16[384,1536]{1,0:T(8,128)(2,1)S(1)}, bf16[384,1536]{1,0:T(8,128)(2,1)}, u32[]{:S(2)}) copy-start(bf16[384,1536]{1,0:T(8,128)(2,1)} %get-tuple-element.56.refs_10_) | copy-start | bytes 3538948
  444.7 58.4 %collective-permute-start.4 = (bf16[384,1536]{1,0:T(8,128)(2,1)S(1)}, bf16[384,1536]{1,0:T(8,128)(2,1)S(1)}, u32[]{:S(2)}, u32[]{:S(2)}) collective-permute-start(bf16[384,1536]{1,0:T(8,128)(2,1)S(1)} %copy-done.14), channel_id=1, source_target_pairs={{0,1},{1,0},{2,3},{3,2},{4,5},{5,4},{6,7},{7,6},{8,9},{9,8},{10,11... | collective-permute-start | bytes 3538952 | tf_op jit(solution)/shard_map/ppermute | solution.py:2030
  503.1 1.0 copy-start.15
  504.1 80.6 %copy-start.22 = (bf16[6,1536]{1,0:T(8,128)(2,1)S(1)}, bf16[6,1536]{1,0:T(8,128)(2,1)}, u32[]{:S(2)}) copy-start(bf16[6,1536]{1,0:T(8,128)(2,1)} %param.23) | copy-start | bytes 55300
  504.1 80.6 %copy-start.50 = (f32[6]{0:T(128)S(1)}, f32[6]{0:T(128)}, u32[]{:S(2)}) copy-start(f32[6]{0:T(128)} %broadcast_multiply_fusion.4) | copy-start | bytes 76
  504.1 80.6 %copy-start.51 = (f32[6]{0:T(128)S(1)}, f32[6]{0:T(128)}, u32[]{:S(2)}) copy-start(f32[6]{0:T(128)} %add_rsqrt_fusion.3) | copy-start | bytes 76
  582.8 7.9 %copy-start.30 = (f32[16,1536]{1,0:T(8,128)S(1)}, f32[16,1536]{1,0:T(8,128)}, u32[]{:S(2)}) copy-start(f32[16,1536]{1,0:T(8,128)} %get-tuple-element.60) | copy-start | bytes 294916
  582.8 8.6 %copy-start.17 = (bf16[384,1536]{1,0:T(8,128)(2,1)S(1)}, bf16[384,1536]{1,0:T(8,128)(2,1)}, u32[]{:S(2)}) copy-start(bf16[384,1536]{1,0:T(8,128)(2,1)} %get-tuple-element.153) | copy-start | bytes 3538948
  587.1 5.3 copy-start.16
  591.4 2.0 copy-start.1
Sparse Core Ops, SparseCore 0:
  97.4 156.3 all-gather.1

commit v7 on v6

--- a/solution.py
+++ b/solution.py
@@ -1161,6 +1161,9 @@
     ring.start(0)
     for made in range(made_count):
         cores.start(made, product(rows_t[...], columns[:, made * width : (made + 1) * width]))
+    for made in range(made_count):
+        mine[made] = cores.finish(made)
+        ring.start(made + 1)
     grad_normed = product_t(columns[...], weights[...])
     split[...] = grad_normed[:rows].astype(jnp.bfloat16)
     split_copy().start()
@@ -1172,18 +1175,16 @@
     small_send[0, :late, :] = first
     small_send[0, late:, :] = early[...]
     step_on(0)
-    for made in range(made_count):
-        mine[made] = cores.finish(made)
-        ring.start(made + 1)
-    result[...] = (
-        h_two[...]
-        + (glu_own[...].astype(jnp.float32) + glu_other[...].astype(jnp.float32))
-        + down_bias[...]
-    ).astype(jnp.bfloat16)
     done = 1
     for hop in range(1, ring.far):
         for piece in range(len(pieces)):
             ring.advance(piece, hop)
+        if hop == 1:
+            result[...] = (
+                h_two[...]
+                + (glu_own[...].astype(jnp.float32) + glu_other[...].astype(jnp.float32))
+                + down_bias[...]
+            ).astype(jnp.bfloat16)
         while done <= len(partners) * hop // (ring.far - 1):
             step_on(done)
             done += 1

time: 609 us -> 607 us (level)
  no operation moved by 1% of the time
where the time goes in v7:
time: 607 us; the launch traced here: 598 us
  Pallas kernels  402 us (66%)
  local copies, waits for them, and re-layouts  80.4 us (13%)
  other arithmetic  41.4 us (7%)
  matrix products  37.2 us (6%)
  between operations  15.6 us (3%)
  waiting for transfers between devices  12.2 us (2%)
  starting transfers between devices  8.91 us (1%)
    pallas_call x1, Pallas kernels, glu_layer(): pl.pallas_call(functools.partial(glu_kernel, blocks, seq_count), grid=(bl...  96.4 us
    pallas_call x1, Pallas kernels, mid_layer(): pl.pallas_call(functools.partial(mid_kernel, seq_count, head_count, HD **...  91.6 us
    pallas_call x1, Pallas kernels, ring_gather(): pl.pallas_call(functools.partial(gather_kernel, seq_count, bounds, len(wi...  88.4 us
    pallas_call x1, Pallas kernels, tail_sums(): pl.pallas_call(functools.partial(tail_kernel, seq_count, head_count, made...  76.1 us
    pallas_call x1, Pallas kernels, self_back(): pl.pallas_call(functools.partial(self_back_kernel, seq_count, pairs, scor...  49.5 us
    dot_general x4, matrix products, product(): return jnp.dot(matrix_a, matrix_b, preferred_element_type=jnp.float32)  14.2 us
    ppermute x2, waiting for transfers between devices, head_total(): total = total + lax.ppermute(low, 'head', pairs).astype(jnp.float32)  12.2 us
  transfers between devices with their start and end apart: 6, of which 1 were waited for; matrix products, arithmetic and copies ran while one was open for 24% of the time, Pallas kernels for 8%

profile of v7, /device:TPU:0, one launch (start us, length us, event | category | flops | bytes accessed | tf_op | source)
XLA Modules:
  0.0 597.8 jit_solution(14836889765286419824)
XLA Ops:
  8.8 88.4 %ring_gather.1 = (bf16[8,2,96,5504]{3,2,1,0:T(8,128)(2,1)}, bf16[96,9216]{1,0:T(8,128)(2,1)}) custom-call(f32[96,768]{1,0:T(8,128)} %refs_0_.1, f32[96,768]{1,0:T(8,128)} %refs_1_.2, f32[96,768]{1,0:T(8,128)} %refs_2_.1, f32[96,768]{1,0:T(8,128)} %refs_3_.1, f32[96,768]{1,0:T(8,128)} %refs_4_.1, f32[96,768]{1,0:T(8,128)} %refs_5_.1, f32[48,768]{1,0:T(8,128)} %refs_6_.1, ...), custom_call_target="tpu_custom_call" | custom-call | bytes 270532608 | tf_op jit(solution)/shard_map/ring_gather/pallas_call | solution.py:670
  102.6 1.2 slice_reduce_fusion
  103.8 8.2 %fusion.56 = (bf16[400,2304]{1,0:T(8,128)(2,1)}, f32[400,2304]{1,0:T(8,128)S(1)}) fusion(bf16[1536,5504]{1,0:T(8,128)(2,1)} %bitcast.84, f32[1536]{0:T(1024)S(1)} %get-tuple-element.68, f32[400]{0:T(512)S(1)} %add_rsqrt_fusion.2, f32[400]{0:T(512)S(1)} %broadcast_multiply_fusion.2, bf16[2,1536]{1,0:T(2,128)(2,1)S(1)} %constant_dynamic-slice_fusion.1, ...), kind=kOutput, calls=%fused_computation.158 | convolution fusion | flops 2838220800 | bytes 13802624 | tf_op jit(solution)/shard_map/dot_general | solution.py:83
  112.0 1.2 fusion.50
  113.1 1.4 copy.108
  114.5 1.1 slice.321
  115.8 1.1 subtract_convert_fusion
  117.3 1.1 slice_bitcast_fusion.3
  118.5 1.2 fusion.22
  119.7 3.2 collective-permute-start
  122.9 1.5 collective-permute-start.1
  124.4 3.3 slice.260
  127.6 2.7 copy.107
  130.3 1.8 slice.245
  132.1 1.3 fusion.53
  133.4 1.4 reshape.410
  134.8 1.4 reshape.411
  138.9 1.3 multiply_subtract_fusion
  143.3 1.1 fusion.13
  145.4 1.3 convolution_convert_fusion.2.refs_11_
  146.6 1.2 convolution_convert_fusion.3.refs_12_
  147.8 1.5 pad_maximum_fusion.refs_1_.refs_2_
  149.4 1.8 fusion.51
  151.7 2.5 copy.111
  154.2 2.5 copy.110
  156.7 4.5 fusion
  161.4 4.5 fusion.1
  166.9 6.1 %fusion.15 = bf16[12,64,384]{2,1,0:T(8,128)(2,1)S(1)} fusion(f32[12,64,384]{2,1,0:T(8,128)S(1)} %fusion.36, bf16[896,12,64]{0,2,1:T(8,128)(2,1)S(1)} %bitcast.109, f32[12,384,896]{2,1,0:T(8,128)S(1)} %get-tuple-element.126, f32[12,384]{1,0:T(8,128)S(1)} %get-tuple-element.71, f32[12,384]{1,0:T(8,128)S(1)} %max.9, pred[384,896]{1,0:T(8,128)(4,1)S(1)} %fusion.13), kind=kOutput, calls=%fused_computation.39 | convolution fusion | flops 549715968 | bytes 20041728 | tf_op jit(solution)/shard_map/hqk,khd->qhd/dot_general | solution.py:138
  173.1 4.1 convolution_convert_fusion.1
  177.2 1.7 collective-permute-start.2
  182.7 2.3 subtract_multiply_fusion
  185.0 12.2 %collective-permute-done.2 = bf16[384,1536]{1,0:T(8,128)(2,1)} collective-permute-done((bf16[384,1536]{1,0:T(8,128)(2,1)}, bf16[384,1536]{1,0:T(8,128)(2,1)}, u32[]{:S(2)}, u32[]{:S(2)}) %collective-permute-start.2) | collective-permute-done | bytes 1179680 | tf_op jit(solution)/shard_map/ppermute | solution.py:1847
  197.2 2.2 fusion.49
  200.1 1.9 multiply_convert_fusion.2
  203.0 3.5 fusion.17.refs_10_
  206.5 2.1 copy.115
  208.7 2.1 fusion.5
  211.8 1.4 fusion.16
  213.3 4.1 convolution_convert_fusion
  217.4 1.8 collective-permute-start.3
  219.7 1.4 copy.118
  221.7 1.5 slice.253.refs_3_.refs_4_
  223.2 1.2 broadcast_in_dim.62.refs_8_
  226.0 2.1 copy.126.refs_0_
  229.5 3.3 slice.267.refs_3_
  232.8 3.0 copy.129.refs_0_
  235.8 1.5 slice.238.refs_4_
  239.6 1.3 fusion.41.refs_7_
  240.9 1.3 pad_maximum_fusion.4.refs_6_
  242.3 1.1 copy.128.refs_13_
  243.3 1.4 add.154.refs_6_
  244.7 2.2 copy.122.refs_15_
  246.8 1.5 rsqrt.38.refs_5_
  248.9 2.1 fusion.48
  252.5 1.8 multiply_convert_fusion.1
  254.3 1.4 copy.119.normed_t
  255.7 96.4 %glu_layer.1 = (bf16[384,1536]{1,0:T(8,128)(2,1)}, bf16[384,1536]{1,0:T(8,128)(2,1)}, f32[2,3072]{1,0:T(2,128)}, bf16[3,3,96,3072]{3,2,1,0:T(8,128)(2,1)}, bf16[2,3,96,3072]{3,2,1,0:T(8,128)(2,1)}) custom-call(bf16[384,1536]{1,0:T(8,128)(2,1)} %copy-done.9, bf16[1536,384]{1,0:T(8,128)(2,1)} %copy.119.normed_t, bf16[384,1536]{1,0:T(8,128)(2,1)} %refs_1_.3, ...), custom_call_target="tpu_custom_call" | custom-call | flops 32614907904 | bytes 56623104 | tf_op jit(solution)/shard_map/glu_layer/pallas_call | solution.py:875
  352.1 91.6 %mid_layer.1 = (f32[384,1536]{1,0:T(8,128)}, bf16[384,1536]{1,0:T(8,128)(2,1)}, bf16[384,1536]{1,0:T(8,128)(2,1)}, bf16[384,768]{1,0:T(8,128)(2,1)}, bf16[384,76...) custom-call(bf16[384,1536]{1,0:T(8,128)(2,1)} %get-tuple-element.44., ...), custom_call_target="tpu_custom_call" | custom-call | flops 3472883712 | bytes 58982400 | tf_op jit(solution)/shard_map/mid_layer/pallas_call | solution.py:1791
  445.4 49.5 %self_back.1 = (bf16[400,2304]{1,0:T(8,128)(2,1)}, f32[3,96,768]{2,1,0:T(8,128)}, bf16[8,96,768]{2,1,0:T(8,128)(2,1)}) custom-call(bf16[384,768]{1,0:T(8,128)(2,1)} %copy.126.refs_0_, bf16[2,896,768]{2,1,0:T(8,128)(2,1)} %copy-done.2, bf16[2,896,768]{2,1,0:T(8,128)(2,1)} %copy-done.2, bf16[16,2304]{1,0:T(8,128)(2,1)} %slice.253.refs_3_.refs_4_, ...), custom_call_target="tpu_custom_call" | custom-call | flops 2642411520 | bytes 28311552 | tf_op jit(solution)/shard_map/self_back/pallas_call | solution.py:1481
  494.9 1.7 slice_bitcast_fusion.10
  497.3 1.9 slice_bitcast_fusion.4
  499.2 3.8 slice_bitcast_fusion
  504.1 76.1 %tail_sums.1 = (f32[4,96,768]{2,1,0:T(8,128)}, f32[16,1536]{1,0:T(8,128)}, bf16[384,1536]{1,0:T(8,128)(2,1)}, bf16[384,1536]{1,0:T(8,128)(2,1)}) custom-call(bf16[1536,400]{1,0:T(8,128)(2,1)} %copy.129.refs_0_, bf16[400,2304]{1,0:T(8,128)(2,1)} %get-tuple-element.52.refs_1_, bf16[1536,5504]{1,0:T(8,128)(2,1)} %bitcast.92, f32[384,1536]{1,0:T(8,128)} %slice.267.refs_3_, ...), custom_call_target="tpu_custom_call" | custom-call | flops 5662310400 | bytes 56623104 | tf_op jit(solution)/shard_map/tail_sums/pallas_call | solution.py:1218
  584.5 2.3 slice_bitcast_fusion.6
  (194 shorter events, 41.4 us)
Async XLA Ops:
  7.2 131.6 %copy-start = (bf16[6,128,768]{2,1,0:T(8,128)(2,1)S(1)}, bf16[6,128,768]{2,1,0:T(8,128)(2,1)}, u32[]{:S(2)}) copy-start(bf16[6,128,768]{2,1,0:T(8,128)(2,1)} %param.24) | copy-start | bytes 3538948
  7.2 248.5 %all-gather.2.cloned.1.call-start = ((), (), s32[]{:S(2)}) async-start(), calls=%async_computation | async-start | bytes 30081024 | tf_op jit(solution)/shard_map/all_gather | solution.py:1852
  97.2 4.6 copy-start.4
  98.1 0.6 copy-start.48
  102.1 9.9 %copy-start.46 = (f32[400]{0:T(512)}, f32[400]{0:T(512)S(1)}, u32[]{:S(2)}) copy-start(f32[400]{0:T(512)S(1)} %broadcast_multiply_fusion.2) | copy-start | bytes 4804
  102.5 9.4 %copy-start.44 = (f32[400]{0:T(512)}, f32[400]{0:T(512)S(1)}, u32[]{:S(2)}) copy-start(f32[400]{0:T(512)S(1)} %add_rsqrt_fusion.2) | copy-start | bytes 4804
  115.8 1.2 copy-start.26
  115.8 1.2 copy-start.28
  119.7 28.1 %collective-permute-start = (bf16[2,256,768]{2,1,0:T(8,128)(2,1)}, bf16[2,256,768]{2,1,0:T(8,128)(2,1)}, u32[]{:S(2)}, u32[]{:S(2)}) collective-permute-start(bf16[2,256,768]{2,1,0:T(8,128)(2,1)} %get-tuple-element.101), channel_id=1, source_target_pairs={{0,2},{2,4},{4,6},{6,8},{8,10},{10,12},{12,14},{14,16},{16,18},{18... | collective-permute-start | bytes 2359304 | tf_op jit(solution)/shard_map/ppermute | solution.py:25
  122.9 24.9 %collective-permute-start.1 = (bf16[2,256,768]{2,1,0:T(8,128)(2,1)}, bf16[2,256,768]{2,1,0:T(8,128)(2,1)}, u32[]{:S(2)}, u32[]{:S(2)}) collective-permute-start(bf16[2,256,768]{2,1,0:T(8,128)(2,1)} %get-tuple-element.102), channel_id=1, source_target_pairs={{2,0},{4,2},{6,4},{8,6},{10,8},{12,10},{14,12},{16,14},{18,16},{20... | collective-permute-start | bytes 2359304 | tf_op jit(solution)/shard_map/ppermute | solution.py:28
  136.2 5.6 copy-start.27
  136.2 8.3 %copy-start.6 = (bf16[1536,768]{1,0:T(8,128)(2,1)S(1)}, bf16[1536,768]{1,0:T(8,128)(2,1)}, u32[]{:S(2)}) copy-start(bf16[1536,768]{1,0:T(8,128)(2,1)} %slice.260) | copy-start | bytes 7077892
  137.2 7.2 %copy-start.39 = (s32[384]{0:T(512)}, s32[384]{0:T(512)S(1)}, u32[]{:S(2)}) copy-start(s32[384]{0:T(512)S(1)} %broadcast_subtract_fusion) | copy-start | bytes 4612
  138.0 6.5 %copy-start.35 = (s32[896]{0:T(1024)}, s32[896]{0:T(1024)S(1)}, u32[]{:S(2)}) copy-start(s32[896]{0:T(1024)S(1)} %pad_dynamic-slice_fusion) | copy-start | bytes 10756
  138.9 7.7 %copy-start.7 = (bf16[2,128,768]{2,1,0:T(8,128)(2,1)}, bf16[2,128,768]{2,1,0:T(8,128)(2,1)S(1)}, u32[]{:S(2)}) copy-start(bf16[2,128,768]{2,1,0:T(8,128)(2,1)S(1)} %constant_dynamic-slice_fusion) | copy-start | bytes 1179652
  141.2 15.5 %copy-start.8 = (bf16[384,12,64]{0,2,1:T(8,128)(2,1)}, bf16[384,12,64]{0,2,1:T(8,128)(2,1)S(1)}, u32[]{:S(2)}) copy-start(bf16[384,12,64]{0,2,1:T(8,128)(2,1)S(1)} %maximum_convert_fusion) | copy-start | bytes 1769476
  144.4 0.7 copy-start.49
  149.4 2.3 copy-start.2
  161.3 5.2 copy-start.41
  161.3 5.5 copy-start.13
  173.0 4.2 copy-start.19
  173.0 5.8 copy-start.5
  173.0 6.6 %copy-start.11 = (bf16[256,768]{1,0:T(8,128)(2,1)S(1)}, bf16[256,768]{1,0:T(8,128)(2,1)}, u32[]{:S(2)}) copy-start(bf16[256,768]{1,0:T(8,128)(2,1)} %convolution_convert_fusion.2.refs_11_) | copy-start | bytes 1179652
  173.0 7.5 %copy-start.12 = (bf16[256,768]{1,0:T(8,128)(2,1)S(1)}, bf16[256,768]{1,0:T(8,128)(2,1)}, u32[]{:S(2)}) copy-start(bf16[256,768]{1,0:T(8,128)(2,1)} %convolution_convert_fusion.3.refs_12_) | copy-start | bytes 1179652
  177.2 4.4 copy-start.29
  177.2 20.0 %collective-permute-start.2 = (bf16[384,1536]{1,0:T(8,128)(2,1)}, bf16[384,1536]{1,0:T(8,128)(2,1)}, u32[]{:S(2)}, u32[]{:S(2)}) collective-permute-start(bf16[384,1536]{1,0:T(8,128)(2,1)} %convolution_convert_fusion.1), channel_id=1, source_target_pairs={{0,1},{1,0},{2,3},{3,2},{4,5},{5,4},{6,7},{7,6},{8,9},{9,8},{10,11... | collective-permute-start | bytes 3538952 | tf_op jit(solution)/shard_map/ppermute | solution.py:1847
  180.6 2.1 copy-start.45
  180.6 2.1 copy-start.47
  199.4 0.7 copy-start.38
  199.8 2.2 copy-start.43
  202.0 1.0 copy-start.10
  208.7 2.1 copy-start.18
  210.8 1.0 copy-start.31
  210.8 1.0 copy-start.23
  211.8 1.5 copy-start.33
  213.3 4.1 copy-start.21
  217.4 3.7 copy-start.40
  217.4 7.0 %copy-start.36 = (s32[896]{0:T(1024)S(1)}, s32[896]{0:T(1024)}, u32[]{:S(2)}) copy-start(s32[896]{0:T(1024)} %copy-done.35) | copy-start | bytes 10756
  217.4 31.6 %collective-permute-start.3 = (bf16[384,1536]{1,0:T(8,128)(2,1)}, bf16[384,1536]{1,0:T(8,128)(2,1)}, u32[]{:S(2)}, u32[]{:S(2)}) collective-permute-start(bf16[384,1536]{1,0:T(8,128)(2,1)} %convolution_convert_fusion), channel_id=1, source_target_pairs={{0,1},{1,0},{2,3},{3,2},{4,5},{5,4},{6,7},{7,6},{8,9},{9,8},{10,11... | collective-permute-start | bytes 3538952 | tf_op jit(solution)/shard_map/ppermute | solution.py:1847
  221.1 8.1 %copy-start.25 = (f32[384,64]{0,1:T(8,128)S(1)}, f32[384,64]{0,1:T(8,128)}, u32[]{:S(2)}) copy-start(f32[384,64]{0,1:T(8,128)} %get-tuple-element.110) | copy-start | bytes 294916
  221.1 8.3 %copy-start.24 = (f32[384,64]{0,1:T(8,128)S(1)}, f32[384,64]{0,1:T(8,128)}, u32[]{:S(2)}) copy-start(f32[384,64]{0,1:T(8,128)} %maximum_maximum_fusion) | copy-start | bytes 294916
  232.8 9.4 %copy-start.20 = (bf16[12,64,384]{2,1,0:T(8,128)(2,1)S(1)}, bf16[12,64,384]{2,1,0:T(8,128)(2,1)}, u32[]{:S(2)}) copy-start(bf16[12,64,384]{2,1,0:T(8,128)(2,1)} %copy-done.19) | copy-start | bytes 1769476
  239.1 9.2 %copy-start.32 = (f32[12,384]{1,0:T(8,128)S(1)}, f32[12,384]{1,0:T(8,128)}, u32[]{:S(2)}) copy-start(f32[12,384]{1,0:T(8,128)} %copy-done.31) | copy-start | bytes 55300
  239.1 9.2 %copy-start.34 = (f32[12,384]{1,0:T(8,128)S(1)}, f32[12,384]{1,0:T(8,128)}, u32[]{:S(2)}) copy-start(f32[12,384]{1,0:T(8,128)} %copy-done.33) | copy-start | bytes 55300
  251.0 3.3 copy-start.3
  251.0 1.5 copy-start.37
  254.3 1.4 copy-start.9
  352.1 92.5 %copy-start.42 = (f32[2,3072]{1,0:T(2,128)S(1)}, f32[2,3072]{1,0:T(2,128)}, u32[]{:S(2)}) copy-start(f32[2,3072]{1,0:T(2,128)} %get-tuple-element.54) | copy-start | bytes 73732
  352.1 92.6 %copy-start.14 = (bf16[384,1536]{1,0:T(8,128)(2,1)S(1)}, bf16[384,1536]{1,0:T(8,128)(2,1)}, u32[]{:S(2)}) copy-start(bf16[384,1536]{1,0:T(8,128)(2,1)} %get-tuple-element.56.refs_10_) | copy-start | bytes 3538948
  444.7 58.4 %collective-permute-start.4 = (bf16[384,1536]{1,0:T(8,128)(2,1)S(1)}, bf16[384,1536]{1,0:T(8,128)(2,1)S(1)}, u32[]{:S(2)}, u32[]{:S(2)}) collective-permute-start(bf16[384,1536]{1,0:T(8,128)(2,1)S(1)} %copy-done.14), channel_id=1, source_target_pairs={{0,1},{1,0},{2,3},{3,2},{4,5},{5,4},{6,7},{7,6},{8,9},{9,8},{10,11... | collective-permute-start | bytes 3538952 | tf_op jit(solution)/shard_map/ppermute | solution.py:2031
  503.1 1.0 copy-start.15
  504.1 77.9 %copy-start.22 = (bf16[6,1536]{1,0:T(8,128)(2,1)S(1)}, bf16[6,1536]{1,0:T(8,128)(2,1)}, u32[]{:S(2)}) copy-start(bf16[6,1536]{1,0:T(8,128)(2,1)} %param.23) | copy-start | bytes 55300
  504.1 77.9 %copy-start.50 = (f32[6]{0:T(128)S(1)}, f32[6]{0:T(128)}, u32[]{:S(2)}) copy-start(f32[6]{0:T(128)} %broadcast_multiply_fusion.4) | copy-start | bytes 76
  504.1 77.9 %copy-start.51 = (f32[6]{0:T(128)S(1)}, f32[6]{0:T(128)}, u32[]{:S(2)}) copy-start(f32[6]{0:T(128)} %add_rsqrt_fusion.3) | copy-start | bytes 76
  580.1 7.9 %copy-start.30 = (f32[16,1536]{1,0:T(8,128)S(1)}, f32[16,1536]{1,0:T(8,128)}, u32[]{:S(2)}) copy-start(f32[16,1536]{1,0:T(8,128)} %get-tuple-element.60) | copy-start | bytes 294916
  580.2 8.6 %copy-start.17 = (bf16[384,1536]{1,0:T(8,128)(2,1)S(1)}, bf16[384,1536]{1,0:T(8,128)(2,1)}, u32[]{:S(2)}) copy-start(bf16[384,1536]{1,0:T(8,128)(2,1)} %get-tuple-element.153) | copy-start | bytes 3538948
  584.5 5.3 copy-start.16
  588.7 2.0 copy-start.1
Sparse Core Ops, SparseCore 0:
  97.4 156.3 all-gather.1
